TPU v7x, 256 devices: a whole 4x4x8 slice. The times are simulated.
256 devices in a mesh: ax: 64 (over y_lo, z, x), sec: 4 (over y_hi, core).
Axes of the slice: x: 4, y: 4 (y_hi: 2, y_lo: 2; y = y_hi * 2 + y_lo), z: 8, core: 2. Of those that a mesh axis runs over, the one named last changes fastest.
Arguments:
- load: float32 [8192, 6, 1024], P('ax', None, 'sec'), may hold values from -6 to 6
- disp: float32 [8192, 6, 1024], P('ax', None, 'sec'), may hold values from -1.5 to 1.5
- stiff: float32 [8192, 6, 1024], P('ax', None, 'sec'), may hold values from 0.5 to 2
- hole: int32 [8192, 1024], P('ax', 'sec'), may hold values 0 or 1
- section_class: int32 [8192], P('ax'), may hold values from 0 to 3
- class_table: float32 [4, 6], replicated, may hold values from 0.5 to 2
- precond: float32 [6, 6, 1024], replicated, may hold values from -0.5 to 0.5, as said below
Outputs:
- disp_new: float32 [8192, 6, 1024], P('ax', None, 'sec')
- residual_new: float32 [8192, 6, 1024], P('ax', None, 'sec')
- stats: float32 [3], replicated
Inputs may be any that keep to these rules, and one draw needn't show every extreme that they name: `precond`: for each harmonic the matrix over the first two dimensions is symmetric and positive definite.
All inputs are finite; a program needn't handle non-finite values. No bound on the sum of `hole` on one device may be relied on, other than what follows from the above.
Results may differ from a plain program's by a relative error of at most 0.0075.
Values sent between devices are 32-bit elements; how exact they have to be, the bound alone decides.
A program may use at most 64 MiB of HBM per device.

v0:
```python
import math

import jax
import jax.numpy as jnp
from jax import lax
from jax.sharding import PartitionSpec as P


def with_halo(x, sides, width, wrap):
    for axis, dim in sides:
        size, length = (lax.axis_size(axis), x.shape[dim])
        up = [(i, (i + 1) % size) for i in range(size if wrap else size - 1)]
        down = [(j, i) for i, j in up]
        last = lax.slice_in_dim(x, length - width, length, axis=dim)
        first = lax.slice_in_dim(x, 0, width, axis=dim)
        before = lax.ppermute(last, axis, up)
        after = lax.ppermute(first, axis, down)
        x = jnp.concatenate([before, x, after], axis=dim)
    return x


def swap_radial(field):
    extent = field.shape
    folded = field.reshape(extent[0], extent[1] // 2, 2, extent[2])
    return jnp.flip(folded, axis=2).reshape(extent)


def apply_operator(field, stiffness):
    axial_pad = with_halo(field, (("ax", 0),), 1, False)
    sector_pad = with_halo(field, (("sec", 2),), 1, True)
    beside = axial_pad[2:] + axial_pad[:-2]
    beside = beside + sector_pad[:, :, 2:] + sector_pad[:, :, :-2]
    return (stiffness + 4.5) * field - beside - 0.5 * swap_radial(field)


def harmonic_table(row_index, col_index, length):
    product = row_index[:, None] * col_index[None, :] % length
    angle = 2.0 * math.pi / length * product.astype(jnp.float32)
    return jnp.concatenate([jnp.cos(angle), jnp.sin(angle)], axis=1)


def scale_harmonics(block_inverse, spectrum):
    doubled = jnp.concatenate([block_inverse, block_inverse], axis=2)
    return jnp.sum(doubled[None] * spectrum[:, None], axis=2)


def shards(load, disp, stiff, hole, section_class, class_table, precond):
    slab_count, comp_count, sector_width = disp.shape
    sector_count = lax.axis_size("sec")
    around_cells = sector_width * sector_count
    total_axial = slab_count * lax.axis_size("ax")
    position = lax.axis_index("ax") * slab_count + jnp.arange(slab_count)
    taper = 1.0 + 2.0 * position.astype(jnp.float32) / (total_axial - 1)
    one_hot = (section_class[:, None] == jnp.arange(class_table.shape[0])[None, :]).astype(
        jnp.float32
    )
    factors = jnp.dot(one_hot, class_table, precision=lax.Precision.HIGHEST)
    stiffness = stiff * (factors * taper[:, None])[:, :, None]
    solid = (1 - hole).astype(jnp.float32)[:, None, :]
    residual = solid * (load - apply_operator(disp, stiffness))
    sector = lax.axis_index("sec")
    own_index = sector * sector_width + jnp.arange(sector_width)
    table = harmonic_table(jnp.arange(around_cells), own_index, around_cells)
    own_inverse = lax.dynamic_slice_in_dim(precond, sector * sector_width, sector_width, 2)
    initial = jnp.zeros((slab_count, comp_count, 2 * sector_width), jnp.float32)
    piece = lax.all_gather(residual, "sec", axis=2, tiled=True)
    span = piece.shape[2]
    table_rows = table
    flat = piece.reshape(-1, span)
    spectrum = jnp.dot(flat, table_rows, precision=lax.Precision.HIGHEST).reshape(initial.shape)
    scaled = scale_harmonics(own_inverse, spectrum).reshape(-1, 2 * sector_width)
    table_rows = table
    shares = lax.psum_scatter(
        lax.dot_general(
            table_rows, scaled, (((1,), (1,)), ((), ())), precision=lax.Precision.HIGHEST
        )
        / around_cells,
        "sec",
        scatter_dimension=0,
        tiled=True,
    )
    smoothed = shares.T.reshape(slab_count, comp_count, sector_width)
    prec = solid * smoothed
    image = solid * apply_operator(prec, stiffness)
    cell_total = slab_count * lax.axis_size("ax") * comp_count * around_cells
    inner_rz = lax.psum(jnp.sum(residual * prec), ("ax", "sec")) / cell_total
    inner_zq = lax.psum(jnp.sum(prec * image), ("ax", "sec")) / cell_total
    alpha = inner_rz / inner_zq
    residual_new = residual - alpha * image
    square_new = lax.psum(jnp.sum(residual_new * residual_new), ("ax", "sec")) / cell_total
    disp_new = disp + alpha * prec
    return (disp_new, residual_new, jnp.stack([inner_rz, inner_zq, square_new]))


def solution(mesh):
    in_specs = (
        P("ax", None, "sec"),
        P("ax", None, "sec"),
        P("ax", None, "sec"),
        P("ax", "sec"),
        P("ax"),
        P(),
        P(),
    )
    out_specs = (P("ax", None, "sec"), P("ax", None, "sec"), P())
    return jax.shard_map(shards, mesh=mesh, in_specs=in_specs, out_specs=out_specs, check_vma=False)
```

profile of v0, /device:TPU:4, one launch (start us, length us, event | category | flops | bytes accessed | tf_op | source)
XLA Modules:
  0.0 316.7 jit_solution(832956261714137729)
XLA Ops:
  7.3 2.3 fusion.30
  9.5 2.6 collective-permute-start.2
  12.2 0.8 fusion.29
  13.0 2.4 collective-permute-start
  15.4 3.4 %collective-permute-start.1 = (f32[1,6,256]{2,0,1:T(1,128)S(1)}, f32[1,6,256]{2,0,1:T(1,128)S(1)}, u32[]{:S(2)}, u32[]{:S(2)}) collective-permute-start(f32[1,6,256]{2,0,1:T(1,128)S(1)} %get-tuple-element.15), channel_id=1, source_target_pairs={{0,4},{4,8},{8,12},{12,16},{16,20},{20,24},{24,28},{28,32},{32,36}... | collective-permute-start | bytes 18440 | tf_op jit(solution)/shard_map/ppermute | solution.py:16
  18.8 0.9 subtract_convert_fusion
  19.8 0.9 convolution_multiply_fusion.1
  20.8 1.1 collective-permute-done.2
  22.0 0.9 collective-permute-done.3
  22.9 1.6 fusion.18
  24.8 4.1 %fusion.22 = (f32[1024,256]{1,0:T(8,128)S(1)}, f32[1024,256]{1,0:T(8,128)S(1)}) fusion(s32[256]{0:T(256)S(1)} %iota_add_fusion), kind=kLoop, calls=%fused_computation.47 | loop fusion | flops 3670016 | bytes 2098176 | tf_op jit(solution)/shard_map/cos | solution.py:39
  28.9 34.0 %all-gather.2.cloned.1.call-done = f32[128,6,1024]{2,0,1:T(8,128)} async-done(((f32[128,6,256]{2,0,1:T(8,128)}), f32[128,6,1024]{2,0,1:T(8,128)}) %all-gather.2.cloned.1.call-update) | async-done | bytes 3145744 | tf_op jit(solution)/shard_map/all_gather | solution.py:66
  62.9 7.0 %fusion = f32[128,6,512]{2,0,1:T(8,128)S(1)} fusion(f32[128,6,1024]{2,0,1:T(8,128)} %all-gather.2.cloned.1.call-done, f32[1024,256]{1,0:T(8,128)S(1)} %get-tuple-element.19, f32[1024,256]{1,0:T(8,128)S(1)} %get-tuple-element.18), kind=kOutput, calls=%fused_computation.2 | convolution fusion | flops 4832362496 | bytes 6815744 | tf_op jit(solution)/shard_map/dot_general | solution.py:70
  69.8 0.7 multiply_reduce_fusion
  70.5 2.3 copy.24
  72.8 2.6 reshape.48
  75.4 8.3 %convolution_multiply_fusion = f32[1024,768]{1,0:T(8,128)} fusion(f32[768,512]{1,0:T(8,128)} %reshape.48, f32[1024,256]{1,0:T(8,128)S(1)} %get-tuple-element.19, f32[1024,256]{1,0:T(8,128)S(1)} %get-tuple-element.18), kind=kOutput, calls=%fused_computation.4 | convolution fusion | flops 4833148928 | bytes 6815744 | tf_op jit(solution)/shard_map/dot_general | solution.py:74
  83.6 49.6 %reduce-scatter.2.cloned.1.call-done = f32[256,768]{1,0:T(8,128)} async-done(((f32[1024,768]{1,0:T(8,128)}), f32[256,768]{1,0:T(8,128)}) %reduce-scatter.2.cloned.1.call-update) | async-done | bytes 786448 | tf_op jit(solution)/shard_map/reduce_scatter | solution.py:73
  133.3 1.4 copy.25
  135.1 1.0 fusion.28
  136.1 2.6 reshape.50
  138.7 0.5 collective-permute-start.7
  139.2 2.5 collective-permute-start.4
  141.7 3.4 %collective-permute-start.5 = (f32[1,6,256]{2,0,1:T(1,128)S(1)}, f32[1,6,256]{2,0,1:T(1,128)S(1)}, u32[]{:S(2)}, u32[]{:S(2)}) collective-permute-start(f32[1,6,256]{2,0,1:T(1,128)S(1)} %get-tuple-element.11), channel_id=1, source_target_pairs={{0,4},{4,8},{8,12},{12,16},{16,20},{20,24},{24,28},{28,32},{32,36}... | collective-permute-start | bytes 18440 | tf_op jit(solution)/shard_map/ppermute | solution.py:16
  145.1 1.2 copy_multiply_fusion
  146.4 5.2 %collective-permute-done.7 = f32[128,6,1]{2,0,1:T(8,128)S(1)} collective-permute-done((f32[128,6,1]{2,0,1:T(8,128)S(1)}, f32[128,6,1]{2,0,1:T(8,128)S(1)}, u32[]{:S(2)}, u32[]{:S(2)}) %collective-permute-start.7) | collective-permute-done | bytes 3104 | tf_op jit(solution)/shard_map/ppermute | solution.py:16
  151.6 2.2 multiply_reduce_fusion.2
  153.8 76.5 %all-reduce = (f32[]{:T(128)}, f32[]{:T(128)}) all-reduce(f32[]{:T(128)} %get-tuple-element.4, f32[]{:T(128)} %get-tuple-element.3), channel_id=1, replica_groups=mesh['ax'=64,'sec'=4] {'ax','sec'}, use_global_device_ids=true, to_apply=%region_3.4 | all-reduce | flops 2 | bytes 16 | tf_op jit(solution)/shard_map/psum | solution.py:86
  231.6 1.2 multiply_add_fusion
  232.8 1.6 multiply_reduce_fusion.1
  234.4 74.2 %psum.23 = f32[]{:T(128)} all-reduce(f32[]{:T(128)} %get-tuple-element.7), channel_id=1, replica_groups=mesh['ax'=64,'sec'=4] {'ax','sec'}, use_global_device_ids=true, to_apply=%region_7.8 | all-reduce | flops 1 | bytes 8 | tf_op jit(solution)/shard_map/psum | solution.py:90
  309.3 0.6 pad_maximum_fusion.12
  (40 shorter events, 1.0 us)
Async XLA Ops:
  7.2 17.6 %copy-start = (f32[6,6,1024]{2,1,0:T(8,128)S(1)}, f32[6,6,1024]{2,1,0:T(8,128)}, u32[]{:S(2)}) copy-start(f32[6,6,1024]{2,1,0:T(8,128)} %param.13) | copy-start | bytes 442372
  7.2 13.5 %copy-start.1 = (f32[128,6,256]{2,0,1:T(8,128)S(1)}, f32[128,6,256]{2,0,1:T(8,128)}, u32[]{:S(2)}) copy-start(f32[128,6,256]{2,0,1:T(8,128)} %param.8) | copy-start | bytes 2359300
  7.2 15.7 %copy-start.9 = (f32[128,6,256]{2,0,1:T(8,128)S(1)}, f32[128,6,256]{2,0,1:T(8,128)}, u32[]{:S(2)}) copy-start(f32[128,6,256]{2,0,1:T(8,128)} %param.7) | copy-start | bytes 2359300
  7.2 15.7 %copy-start.6 = (f32[128,6,256]{2,0,1:T(8,128)S(1)}, f32[128,6,256]{2,0,1:T(8,128)}, u32[]{:S(2)}) copy-start(f32[128,6,256]{2,0,1:T(8,128)} %param.9) | copy-start | bytes 2359300
  7.2 55.6 %all-gather.2.cloned.1.call-start = ((), (), s32[]{:S(2)}) async-start(), calls=%async_computation.1 | async-start | bytes 3932160 | tf_op jit(solution)/shard_map/all_gather | solution.py:66
  9.5 12.4 %collective-permute-start.2 = (f32[128,6,1]{2,0,1:T(8,128)}, f32[128,6,1]{2,0,1:T(8,128)S(1)}, u32[]{:S(2)}, u32[]{:S(2)}) collective-permute-start(f32[128,6,1]{2,0,1:T(8,128)} %get-tuple-element.16), channel_id=1, source_target_pairs={{1,0},{2,1},{3,2},{0,3},{5,4},{6,5},{7,6},{4,7},{9,8},{10,9},{11,1... | collective-permute-start | bytes 9224 | tf_op jit(solution)/shard_map/ppermute | solution.py:17
  12.1 10.7 %collective-permute-start.3 = (f32[128,6,1]{2,0,1:T(8,128)}, f32[128,6,1]{2,0,1:T(8,128)S(1)}, u32[]{:S(2)}, u32[]{:S(2)}) collective-permute-start(f32[128,6,1]{2,0,1:T(8,128)} %get-tuple-element.17), channel_id=1, source_target_pairs={{0,1},{1,2},{2,3},{3,0},{4,5},{5,6},{6,7},{7,4},{8,9},{9,10},{10,1... | collective-permute-start | bytes 9224 | tf_op jit(solution)/shard_map/ppermute | solution.py:16
  13.0 9.9 %collective-permute-start = (f32[1,6,256]{2,0,1:T(1,128)S(1)}, f32[1,6,256]{2,0,1:T(1,128)S(1)}, u32[]{:S(2)}, u32[]{:S(2)}) collective-permute-start(f32[1,6,256]{2,0,1:T(1,128)S(1)} %get-tuple-element.14), channel_id=1, source_target_pairs={{4,0},{8,4},{12,8},{16,12},{20,16},{24,20},{28,24},{32,28},{36,32}... | collective-permute-start | bytes 18440 | tf_op jit(solution)/shard_map/ppermute | solution.py:17
  15.4 7.5 %collective-permute-start.1 = (f32[1,6,256]{2,0,1:T(1,128)S(1)}, f32[1,6,256]{2,0,1:T(1,128)S(1)}, u32[]{:S(2)}, u32[]{:S(2)}) collective-permute-start(f32[1,6,256]{2,0,1:T(1,128)S(1)} %get-tuple-element.15), channel_id=1, source_target_pairs={{0,4},{4,8},{8,12},{12,16},{16,20},{20,24},{24,28},{28,32},{32,36}... | collective-permute-start | bytes 18440 | tf_op jit(solution)/shard_map/ppermute | solution.py:16
  24.5 108.8 %reduce-scatter.2.cloned.1.call-start = ((), (), s32[]{:S(2)}) async-start(), calls=%async_computation.2 | async-start | bytes 3932160 | tf_op jit(solution)/shard_map/reduce_scatter | solution.py:73
  134.7 1.4 copy-start.5
  135.1 1.1 copy-start.3
  136.1 15.5 %copy-start.2 = (f32[128,6,256]{2,0,1:T(8,128)S(1)}, f32[128,6,256]{2,0,1:T(8,128)}, u32[]{:S(2)}) copy-start(f32[128,6,256]{2,0,1:T(8,128)} %fusion.18) | copy-start | bytes 2359300
  138.7 12.9 %copy-start.4 = (f32[128,6,256]{2,0,1:T(8,128)S(1)}, f32[128,6,256]{2,0,1:T(8,128)}, u32[]{:S(2)}) copy-start(f32[128,6,256]{2,0,1:T(8,128)} %copy-done.3) | copy-start | bytes 2359300
  138.7 12.9 %copy-start.7 = (f32[128,6,256]{2,0,1:T(8,128)S(1)}, f32[128,6,256]{2,0,1:T(8,128)}, u32[]{:S(2)}) copy-start(f32[128,6,256]{2,0,1:T(8,128)} %param.9) | copy-start | bytes 2359300
  138.7 7.6 %collective-permute-start.6 = (f32[128,6,1]{2,0,1:T(8,128)}, f32[128,6,1]{2,0,1:T(8,128)S(1)}, u32[]{:S(2)}, u32[]{:S(2)}) collective-permute-start(f32[128,6,1]{2,0,1:T(8,128)} %get-tuple-element.12), channel_id=1, source_target_pairs={{1,0},{2,1},{3,2},{0,3},{5,4},{6,5},{7,6},{4,7},{9,8},{10,9},{11,1... | collective-permute-start | bytes 9224 | tf_op jit(solution)/shard_map/ppermute | solution.py:17
  138.7 12.8 %collective-permute-start.7 = (f32[128,6,1]{2,0,1:T(8,128)S(1)}, f32[128,6,1]{2,0,1:T(8,128)S(1)}, u32[]{:S(2)}, u32[]{:S(2)}) collective-permute-start(f32[128,6,1]{2,0,1:T(8,128)S(1)} %get-tuple-element.13), channel_id=1, source_target_pairs={{0,1},{1,2},{2,3},{3,0},{4,5},{5,6},{6,7},{7,4},{8,9},{9,10},{10,1... | collective-permute-start | bytes 9224 | tf_op jit(solution)/shard_map/ppermute | solution.py:16
  139.2 12.3 %collective-permute-start.4 = (f32[1,6,256]{2,0,1:T(1,128)S(1)}, f32[1,6,256]{2,0,1:T(1,128)S(1)}, u32[]{:S(2)}, u32[]{:S(2)}) collective-permute-start(f32[1,6,256]{2,0,1:T(1,128)S(1)} %get-tuple-element.10), channel_id=1, source_target_pairs={{4,0},{8,4},{12,8},{16,12},{20,16},{24,20},{28,24},{32,28},{36,32}... | collective-permute-start | bytes 18440 | tf_op jit(solution)/shard_map/ppermute | solution.py:17
  141.7 9.9 %collective-permute-start.5 = (f32[1,6,256]{2,0,1:T(1,128)S(1)}, f32[1,6,256]{2,0,1:T(1,128)S(1)}, u32[]{:S(2)}, u32[]{:S(2)}) collective-permute-start(f32[1,6,256]{2,0,1:T(1,128)S(1)} %get-tuple-element.11), channel_id=1, source_target_pairs={{0,4},{4,8},{8,12},{12,16},{16,20},{20,24},{24,28},{28,32},{32,36}... | collective-permute-start | bytes 18440 | tf_op jit(solution)/shard_map/ppermute | solution.py:16
  231.6 1.2 copy-start.8
Sparse Core Ops, SparseCore 0:
  24.6 38.1 all-gather.1
  83.8 49.4 reduce-scatter.1
where the time goes:
time: 320 us; the launch traced here: 317 us
  blocking collectives  151 us (47%)
  waiting for transfers between devices  90.9 us (28%)
  between operations  16.3 us (5%)
  matrix products  16.1 us (5%)
  starting transfers between devices  15.1 us (5%)
  other arithmetic  14.5 us (5%)
  local copies, waits for them, and re-layouts  13.1 us (4%)
    psum x1, blocking collectives, shards(): inner_rz = lax.psum(jnp.sum(residual * prec), ('ax', 'sec')) / cell_total  76.5 us
    psum x1, blocking collectives, shards(): lax.psum(jnp.sum(residual_new * residual_new), ('ax', 'sec')) / cell_total  74.2 us
    reduce_scatter x1, waiting for transfers between devices, shards(): lax.psum_scatter(lax.dot_general(table_rows, scaled, (((1,), (1,)), ((),...  49.6 us
    all_gather x1, waiting for transfers between devices, shards(): piece = lax.all_gather(residual, 'sec', axis=2, tiled=True)  34 us
    dot_general x1, matrix products, shards(): lax.dot_general(table_rows, scaled, (((1,), (1,)), ((), ())), precision=l...  8.26 us
    ppermute x4, starting transfers between devices, with_halo(): after = lax.ppermute(first, axis, down)  7.53 us
    ppermute x4, starting transfers between devices, with_halo(): before = lax.ppermute(last, axis, up)  7.29 us
    dot_general x1, matrix products, shards(): jnp.dot(flat, table_rows, precision=lax.Precision.HIGHEST)  6.95 us
  transfers between devices with their start and end apart: 10, of which 5 were waited for; matrix products, arithmetic and copies ran while one was open for 3% of the time, Pallas kernels for 0%

commit v1 on v0

--- a/solution.py
+++ b/solution.py
@@ -3,7 +3,92 @@
 import jax
 import jax.numpy as jnp
 from jax import lax
+from jax.experimental import pallas as pl
+from jax.experimental.pallas import tpu as pltpu
 from jax.sharding import PartitionSpec as P
+
+
+MESH = pl.DeviceIdType.MESH
+
+
+def _lines():
+    me_ax = lax.axis_index("ax")
+    me_sec = lax.axis_index("sec")
+    x = me_ax % 4
+    z = (me_ax // 4) % 8
+    ylo = me_ax // 32
+    core = me_sec % 2
+    yhi = me_sec // 2
+    y = yhi * 2 + ylo
+    return [
+        (2, core, lambda c: (me_ax, yhi * 2 + c)),
+        (4, x, lambda c: (me_ax - x + c, me_sec)),
+        (4, y, lambda c: (me_ax - ylo * 32 + (c % 2) * 32, (c // 2) * 2 + core)),
+        (8, z, lambda c: (me_ax - z * 4 + c * 4, me_sec)),
+    ]
+
+
+def _ar_kernel(x_ref, o_ref, r0, r1, r2, r3, own, send_sems, recv_sems):
+    recvs = (r0, r1, r2, r3)
+    lines = _lines()
+    for r in recvs:
+        r[...] = jnp.zeros_like(r)
+    barrier = pltpu.get_barrier_semaphore()
+    count = 0
+    for n, mine, dev in lines:
+        for d in range(1, n):
+            pl.semaphore_signal(barrier, inc=1, device_id=dev((mine + d) % n), device_id_type=MESH)
+            count += 1
+    pl.semaphore_wait(barrier, count)
+    src = x_ref
+    base = 0
+    for r, (n, mine, dev) in enumerate(lines):
+        copies = []
+        for d in range(1, n):
+            cp = pltpu.make_async_remote_copy(
+                src_ref=src,
+                dst_ref=recvs[r].at[mine],
+                send_sem=send_sems.at[base + d],
+                recv_sem=recv_sems.at[base + d],
+                device_id=dev((mine + d) % n),
+                device_id_type=MESH,
+            )
+            cp.start()
+            copies.append(cp)
+        mine_val = src[...]
+        for cp in copies:
+            cp.wait_recv()
+        total = None
+        for c in range(n):
+            v = jnp.where(mine == c, mine_val, recvs[r][c])
+            total = v if total is None else total + v
+        for cp in copies:
+            cp.wait_send()
+        base += n
+        if r + 1 < len(lines):
+            own[r] = total
+            src = own.at[r]
+        else:
+            o_ref[...] = total
+
+
+def all_sum(part, cid):
+    return pl.pallas_call(
+        _ar_kernel,
+        out_shape=jax.ShapeDtypeStruct(part.shape, jnp.float32),
+        in_specs=[pl.BlockSpec(memory_space=pltpu.VMEM)],
+        out_specs=pl.BlockSpec(memory_space=pltpu.VMEM),
+        scratch_shapes=[
+            pltpu.VMEM((2,) + part.shape, jnp.float32),
+            pltpu.VMEM((4,) + part.shape, jnp.float32),
+            pltpu.VMEM((4,) + part.shape, jnp.float32),
+            pltpu.VMEM((8,) + part.shape, jnp.float32),
+            pltpu.VMEM((3,) + part.shape, jnp.float32),
+            pltpu.SemaphoreType.DMA((18,)),
+            pltpu.SemaphoreType.DMA((18,)),
+        ],
+        compiler_params=pltpu.CompilerParams(collective_id=cid, has_side_effects=True),
+    )(part)
 
 
 def with_halo(x, sides, width, wrap):
@@ -83,11 +168,22 @@
     prec = solid * smoothed
     image = solid * apply_operator(prec, stiffness)
     cell_total = slab_count * lax.axis_size("ax") * comp_count * around_cells
-    inner_rz = lax.psum(jnp.sum(residual * prec), ("ax", "sec")) / cell_total
-    inner_zq = lax.psum(jnp.sum(prec * image), ("ax", "sec")) / cell_total
+    parts = jnp.stack(
+        [
+            jnp.sum(residual * prec),
+            jnp.sum(prec * image),
+            jnp.sum(residual * residual),
+            jnp.sum(residual * image),
+            jnp.sum(image * image),
+        ]
+    )
+    packed = jnp.zeros((8, 128), jnp.float32).at[0, :5].set(parts)
+    totals = all_sum(packed, 0)[0]
+    inner_rz = totals[0] / cell_total
+    inner_zq = totals[1] / cell_total
     alpha = inner_rz / inner_zq
     residual_new = residual - alpha * image
-    square_new = lax.psum(jnp.sum(residual_new * residual_new), ("ax", "sec")) / cell_total
+    square_new = (totals[2] - alpha * (2.0 * totals[3] - alpha * totals[4])) / cell_total
     disp_new = disp + alpha * prec
     return (disp_new, residual_new, jnp.stack([inner_rz, inner_zq, square_new]))
 

time: 320 us -> 195 us (0.61)
  blocking collectives: 151 us -> 0 us
  Pallas kernels: 0 us -> 21.3 us
  local copies, waits for them, and re-layouts: 13.1 us -> 18.5 us
    psum x2 -> x0, blocking collectives: 151 us -> none  [the longest x1 76.5 us: shards(): inner_rz = lax.psum(jnp.sum(residual * prec), ('ax', 'sec')) / cell_total]
    pallas_call x0 -> x1, Pallas kernels: none -> 21.3 us  [all_sum(): pl.pallas_call(_ar_kernel, out_shape=jax.ShapeDtypeStruct(part.shape, jnp...]
    another operation x0 -> x1, local copies, waits for them, and re-layouts: none -> 3.26 us  [shards(): jnp.stack([jnp.sum(residual * prec), jnp.sum(prec * image), jnp.sum(resid...]
  transfers between devices with their start and end apart: 10 -> 10, of which waited for: 5 -> 5; matrix products, arithmetic and copies ran while one was open for 3% -> 4% of each run, Pallas kernels for 0% -> 0%
where the time goes in v1:
time: 195 us; the launch traced here: 194 us
  waiting for transfers between devices  90.9 us (47%)
  Pallas kernels  21.3 us (11%)
  local copies, waits for them, and re-layouts  18.5 us (9%)
  between operations  17.5 us (9%)
  matrix products  16.1 us (8%)
  starting transfers between devices  15.1 us (8%)
  other arithmetic  14.5 us (7%)
    reduce_scatter x1, waiting for transfers between devices, shards(): lax.psum_scatter(lax.dot_general(table_rows, scaled, (((1,), (1,)), ((),...  49.6 us
    all_gather x1, waiting for transfers between devices, shards(): piece = lax.all_gather(residual, 'sec', axis=2, tiled=True)  34 us
    pallas_call x1, Pallas kernels, all_sum(): pl.pallas_call(_ar_kernel, out_shape=jax.ShapeDtypeStruct(part.shape, jnp...  21.3 us
    dot_general x1, matrix products, shards(): lax.dot_general(table_rows, scaled, (((1,), (1,)), ((), ())), precision=l...  8.26 us
    ppermute x4, starting transfers between devices, with_halo(): after = lax.ppermute(first, axis, down)  7.53 us
    ppermute x4, starting transfers between devices, with_halo(): before = lax.ppermute(last, axis, up)  7.29 us
    dot_general x1, matrix products, shards(): jnp.dot(flat, table_rows, precision=lax.Precision.HIGHEST)  6.95 us
    ppermute x4, waiting for transfers between devices, with_halo(): before = lax.ppermute(last, axis, up)  6.12 us
  transfers between devices with their start and end apart: 10, of which 5 were waited for; matrix products, arithmetic and copies ran while one was open for 4% of the time, Pallas kernels for 0%

profile of v1, /device:TPU:4, one launch (start us, length us, event | category | flops | bytes accessed | tf_op | source)
XLA Modules:
  0.0 193.8 jit_solution(17260886811694644641)
XLA Ops:
  7.3 2.3 %fusion.30 = (f32[128,6,1]{2,0,1:T(8,128)}, f32[128,6,1]{2,0,1:T(8,128)}) fusion(f32[128,6,256]{2,0,1:T(8,128)} %param.10), kind=kLoop, calls=%fused_computation.63 | loop fusion | bytes 12288 | tf_op jit(solution)/shard_map/slice | solution.py:100
  9.5 2.6 %collective-permute-start.2 = (f32[128,6,1]{2,0,1:T(8,128)}, f32[128,6,1]{2,0,1:T(8,128)S(1)}, u32[]{:S(2)}, u32[]{:S(2)}) collective-permute-start(f32[128,6,1]{2,0,1:T(8,128)} %get-tuple-element.27), channel_id=1, source_target_pairs={{1,0},{2,1},{3,2},{0,3},{5,4},{6,5},{7,6},{4,7},{9,8},{10,9},{11,1... | collective-permute-start | bytes 9224 | tf_op jit(solution)/shard_map/ppermute | solution.py:102
  12.2 0.8 fusion.29
  13.0 2.4 %collective-permute-start = (f32[1,6,256]{2,0,1:T(1,128)S(1)}, f32[1,6,256]{2,0,1:T(1,128)S(1)}, u32[]{:S(2)}, u32[]{:S(2)}) collective-permute-start(f32[1,6,256]{2,0,1:T(1,128)S(1)} %get-tuple-element.25), channel_id=1, source_target_pairs={{4,0},{8,4},{12,8},{16,12},{20,16},{24,20},{28,24},{32,28},{36,32}... | collective-permute-start | bytes 18440 | tf_op jit(solution)/shard_map/ppermute | solution.py:102
  15.4 3.4 %collective-permute-start.1 = (f32[1,6,256]{2,0,1:T(1,128)S(1)}, f32[1,6,256]{2,0,1:T(1,128)S(1)}, u32[]{:S(2)}, u32[]{:S(2)}) collective-permute-start(f32[1,6,256]{2,0,1:T(1,128)S(1)} %get-tuple-element.26), channel_id=1, source_target_pairs={{0,4},{4,8},{8,12},{12,16},{16,20},{20,24},{24,28},{28,32},{32,36}... | collective-permute-start | bytes 18440 | tf_op jit(solution)/shard_map/ppermute | solution.py:101
  18.8 0.9 subtract_convert_fusion
  19.8 0.9 convolution_multiply_fusion.1
  20.8 1.1 collective-permute-done.2
  22.0 0.9 collective-permute-done.3
  22.9 1.6 fusion.18
  24.8 4.1 %fusion.22 = (f32[1024,256]{1,0:T(8,128)S(1)}, f32[1024,256]{1,0:T(8,128)S(1)}) fusion(s32[256]{0:T(256)S(1)} %iota_add_fusion), kind=kLoop, calls=%fused_computation.49 | loop fusion | flops 3670016 | bytes 2098176 | tf_op jit(solution)/shard_map/cos | solution.py:124
  28.9 34.0 %all-gather.2.cloned.1.call-done = f32[128,6,1024]{2,0,1:T(8,128)} async-done(((f32[128,6,256]{2,0,1:T(8,128)}), f32[128,6,1024]{2,0,1:T(8,128)}) %all-gather.2.cloned.1.call-update) | async-done | bytes 3145744 | tf_op jit(solution)/shard_map/all_gather | solution.py:151
  62.9 7.0 %fusion = f32[128,6,512]{2,0,1:T(8,128)S(1)} fusion(f32[128,6,1024]{2,0,1:T(8,128)} %all-gather.2.cloned.1.call-done, f32[1024,256]{1,0:T(8,128)S(1)} %get-tuple-element.35, f32[1024,256]{1,0:T(8,128)S(1)} %get-tuple-element.34), kind=kOutput, calls=%fused_computation.2 | convolution fusion | flops 4832362496 | bytes 6815744 | tf_op jit(solution)/shard_map/dot_general | solution.py:155
  69.8 0.7 multiply_reduce_fusion
  70.5 2.3 %copy.24 = f32[128,6,512]{2,1,0:T(8,128)} copy(f32[128,6,512]{2,0,1:T(8,128)S(1)} %multiply_reduce_fusion) | data formatting | bytes 3145728 | tf_op jit(solution)/shard_map/reduce_sum | solution.py:129
  72.8 2.6 %reshape.97 = f32[768,512]{1,0:T(8,128)} reshape(f32[128,6,512]{2,1,0:T(8,128)} %copy.24) | data formatting | bytes 3145728 | tf_op jit(solution)/shard_map/reshape | solution.py:156
  75.4 8.3 %convolution_multiply_fusion = f32[1024,768]{1,0:T(8,128)} fusion(f32[768,512]{1,0:T(8,128)} %reshape.97, f32[1024,256]{1,0:T(8,128)S(1)} %get-tuple-element.35, f32[1024,256]{1,0:T(8,128)S(1)} %get-tuple-element.34), kind=kOutput, calls=%fused_computation.4 | convolution fusion | flops 4833148928 | bytes 6815744 | tf_op jit(solution)/shard_map/dot_general | solution.py:159
  83.7 49.6 %reduce-scatter.2.cloned.1.call-done = f32[256,768]{1,0:T(8,128)} async-done(((f32[1024,768]{1,0:T(8,128)}), f32[256,768]{1,0:T(8,128)}) %reduce-scatter.2.cloned.1.call-update) | async-done | bytes 786448 | tf_op jit(solution)/shard_map/reduce_scatter | solution.py:158
  133.3 1.4 copy.25
  135.1 1.0 fusion.28
  136.1 2.6 %reshape.99 = f32[128,3,2,256]{3,2,1,0:T(2,128)} reshape(f32[768,256]{1,0:T(8,128)} %copy-done.5) | data formatting | bytes 1572864 | tf_op jit(solution)/shard_map/reshape | solution.py:167
  139.2 2.5 %collective-permute-start.4 = (f32[1,6,256]{2,0,1:T(1,128)S(1)}, f32[1,6,256]{2,0,1:T(1,128)S(1)}, u32[]{:S(2)}, u32[]{:S(2)}) collective-permute-start(f32[1,6,256]{2,0,1:T(1,128)S(1)} %get-tuple-element.21), channel_id=1, source_target_pairs={{4,0},{8,4},{12,8},{16,12},{20,16},{24,20},{28,24},{32,28},{36,32}... | collective-permute-start | bytes 18440 | tf_op jit(solution)/shard_map/ppermute | solution.py:102
  141.7 3.4 %collective-permute-start.5 = (f32[1,6,256]{2,0,1:T(1,128)S(1)}, f32[1,6,256]{2,0,1:T(1,128)S(1)}, u32[]{:S(2)}, u32[]{:S(2)}) collective-permute-start(f32[1,6,256]{2,0,1:T(1,128)S(1)} %get-tuple-element.22), channel_id=1, source_target_pairs={{0,4},{4,8},{8,12},{12,16},{16,20},{20,24},{24,28},{28,32},{32,36}... | collective-permute-start | bytes 18440 | tf_op jit(solution)/shard_map/ppermute | solution.py:101
  145.1 1.2 copy_multiply_fusion
  146.4 5.2 %collective-permute-done.7 = f32[128,6,1]{2,0,1:T(8,128)S(1)} collective-permute-done((f32[128,6,1]{2,0,1:T(8,128)S(1)}, f32[128,6,1]{2,0,1:T(8,128)S(1)}, u32[]{:S(2)}, u32[]{:S(2)}) %collective-permute-start.7) | collective-permute-done | bytes 3104 | tf_op jit(solution)/shard_map/ppermute | solution.py:101
  151.6 2.3 %multiply_reduce_fusion.1 = (f32[]{:T(128)}, f32[]{:T(128)}, f32[]{:T(128)}, f32[]{:T(128)}, f32[]{:T(128)}, /*index=5*/f32[128,6,256]{2,0,1:T(8,128)}) fusion(f32[128,6,256]{2,0,1:T(8,128)S(1)} %copy-done.2, f32[128,6,256]{2,0,1:T(8,128)S(1)} %copy-done.4, f32[128,3,2,256]{3,0,2,1:T(8,128)S(1)} %reverse_multiply_fusion, ...), kind=kLoop, calls=%fused_computation.40 | loop fusion | flops 4521979 | bytes 4084756 | tf_op jit(solution)/shard_map/reduce_sum | solution.py:177
  153.9 3.3 %stack.35 = f32[5]{0:T(128)S(1)} concatenate(f32[1]{0:T(128)} %bitcast.4, f32[1]{0:T(128)} %bitcast.6, f32[1]{0:T(128)} %bitcast.7, f32[1]{0:T(128)} %bitcast.8, f32[1]{0:T(128)} %bitcast.9), dimensions={0} | concatenate | bytes 40 | tf_op jit(solution)/shard_map/stack | solution.py:171
  157.2 0.6 scatter.4.x_ref
  157.8 21.3 %shard_map.94 = f32[8,128]{1,0:T(8,128)} custom-call(f32[8,128]{1,0:T(8,128)} %scatter.4.x_ref), custom_call_target="tpu_custom_call" | custom-call | tf_op jit(solution)/shard_map/pallas_call | solution.py:76
  179.1 1.5 fusion.31
  183.1 2.7 %multiply_subtract_fusion = (f32[128,6,256]{2,0,1:T(8,128)}, f32[128,6,256]{2,0,1:T(8,128)}) fusion(f32[128,6,256]{2,0,1:T(8,128)S(1)} %copy-done.2, f32[128,6,256]{2,0,1:T(8,128)} %get-tuple-element.20, f32[]{:T(128)} %bitcast.11, f32[128,6,256]{2,0,1:T(8,128)S(1)} %copy-done.1, f32[128,6,256]{2,1,0:T(8,128)S(1)} %reshape.98, ...), kind=kLoop, calls=%fused_computation.38 | loop fusion | flops 983040 | bytes 4849668 | tf_op jit(solution)/shard_map/sub | solution.py:185
  186.4 0.6 pad_maximum_fusion.12
  (39 shorter events, 1.5 us)
Async XLA Ops:
  7.2 17.6 %copy-start = (f32[6,6,1024]{2,1,0:T(8,128)S(1)}, f32[6,6,1024]{2,1,0:T(8,128)}, u32[]{:S(2)}) copy-start(f32[6,6,1024]{2,1,0:T(8,128)} %param.15) | copy-start | bytes 442372
  7.2 13.5 %copy-start.1 = (f32[128,6,256]{2,0,1:T(8,128)S(1)}, f32[128,6,256]{2,0,1:T(8,128)}, u32[]{:S(2)}) copy-start(f32[128,6,256]{2,0,1:T(8,128)} %param.10) | copy-start | bytes 2359300
  7.2 15.7 %copy-start.6 = (f32[128,6,256]{2,0,1:T(8,128)S(1)}, f32[128,6,256]{2,0,1:T(8,128)}, u32[]{:S(2)}) copy-start(f32[128,6,256]{2,0,1:T(8,128)} %param.11) | copy-start | bytes 2359300
  7.2 15.7 %copy-start.8 = (f32[128,6,256]{2,0,1:T(8,128)S(1)}, f32[128,6,256]{2,0,1:T(8,128)}, u32[]{:S(2)}) copy-start(f32[128,6,256]{2,0,1:T(8,128)} %param.9) | copy-start | bytes 2359300
  7.2 55.6 %all-gather.2.cloned.1.call-start = ((), (), s32[]{:S(2)}) async-start(), calls=%async_computation.1 | async-start | bytes 3932160 | tf_op jit(solution)/shard_map/all_gather | solution.py:151
  9.5 12.4 %collective-permute-start.2 = (f32[128,6,1]{2,0,1:T(8,128)}, f32[128,6,1]{2,0,1:T(8,128)S(1)}, u32[]{:S(2)}, u32[]{:S(2)}) collective-permute-start(f32[128,6,1]{2,0,1:T(8,128)} %get-tuple-element.27), channel_id=1, source_target_pairs={{1,0},{2,1},{3,2},{0,3},{5,4},{6,5},{7,6},{4,7},{9,8},{10,9},{11,1... | collective-permute-start | bytes 9224 | tf_op jit(solution)/shard_map/ppermute | solution.py:102
  12.1 10.7 %collective-permute-start.3 = (f32[128,6,1]{2,0,1:T(8,128)}, f32[128,6,1]{2,0,1:T(8,128)S(1)}, u32[]{:S(2)}, u32[]{:S(2)}) collective-permute-start(f32[128,6,1]{2,0,1:T(8,128)} %get-tuple-element.28), channel_id=1, source_target_pairs={{0,1},{1,2},{2,3},{3,0},{4,5},{5,6},{6,7},{7,4},{8,9},{9,10},{10,1... | collective-permute-start | bytes 9224 | tf_op jit(solution)/shard_map/ppermute | solution.py:101
  13.0 9.9 %collective-permute-start = (f32[1,6,256]{2,0,1:T(1,128)S(1)}, f32[1,6,256]{2,0,1:T(1,128)S(1)}, u32[]{:S(2)}, u32[]{:S(2)}) collective-permute-start(f32[1,6,256]{2,0,1:T(1,128)S(1)} %get-tuple-element.25), channel_id=1, source_target_pairs={{4,0},{8,4},{12,8},{16,12},{20,16},{24,20},{28,24},{32,28},{36,32}... | collective-permute-start | bytes 18440 | tf_op jit(solution)/shard_map/ppermute | solution.py:102
  15.4 7.5 %collective-permute-start.1 = (f32[1,6,256]{2,0,1:T(1,128)S(1)}, f32[1,6,256]{2,0,1:T(1,128)S(1)}, u32[]{:S(2)}, u32[]{:S(2)}) collective-permute-start(f32[1,6,256]{2,0,1:T(1,128)S(1)} %get-tuple-element.26), channel_id=1, source_target_pairs={{0,4},{4,8},{8,12},{12,16},{16,20},{20,24},{24,28},{28,32},{32,36}... | collective-permute-start | bytes 18440 | tf_op jit(solution)/shard_map/ppermute | solution.py:101
  24.5 108.8 %reduce-scatter.2.cloned.1.call-start = ((), (), s32[]{:S(2)}) async-start(), calls=%async_computation.2 | async-start | bytes 3932160 | tf_op jit(solution)/shard_map/reduce_scatter | solution.py:158
  134.7 1.4 copy-start.5
  135.1 1.0 copy-start.3
  136.1 15.5 %copy-start.2 = (f32[128,6,256]{2,0,1:T(8,128)S(1)}, f32[128,6,256]{2,0,1:T(8,128)}, u32[]{:S(2)}) copy-start(f32[128,6,256]{2,0,1:T(8,128)} %fusion.18) | copy-start | bytes 2359300
  138.7 12.9 %copy-start.4 = (f32[128,6,256]{2,0,1:T(8,128)S(1)}, f32[128,6,256]{2,0,1:T(8,128)}, u32[]{:S(2)}) copy-start(f32[128,6,256]{2,0,1:T(8,128)} %copy-done.3) | copy-start | bytes 2359300
  138.7 12.9 %copy-start.7 = (f32[128,6,256]{2,0,1:T(8,128)S(1)}, f32[128,6,256]{2,0,1:T(8,128)}, u32[]{:S(2)}) copy-start(f32[128,6,256]{2,0,1:T(8,128)} %param.11) | copy-start | bytes 2359300
  138.7 7.7 %collective-permute-start.6 = (f32[128,6,1]{2,0,1:T(8,128)}, f32[128,6,1]{2,0,1:T(8,128)S(1)}, u32[]{:S(2)}, u32[]{:S(2)}) collective-permute-start(f32[128,6,1]{2,0,1:T(8,128)} %get-tuple-element.23), channel_id=1, source_target_pairs={{1,0},{2,1},{3,2},{0,3},{5,4},{6,5},{7,6},{4,7},{9,8},{10,9},{11,1... | collective-permute-start | bytes 9224 | tf_op jit(solution)/shard_map/ppermute | solution.py:102
  138.7 12.9 %collective-permute-start.7 = (f32[128,6,1]{2,0,1:T(8,128)S(1)}, f32[128,6,1]{2,0,1:T(8,128)S(1)}, u32[]{:S(2)}, u32[]{:S(2)}) collective-permute-start(f32[128,6,1]{2,0,1:T(8,128)S(1)} %get-tuple-element.24), channel_id=1, source_target_pairs={{0,1},{1,2},{2,3},{3,0},{4,5},{5,6},{6,7},{7,4},{8,9},{9,10},{10,1... | collective-permute-start | bytes 9224 | tf_op jit(solution)/shard_map/ppermute | solution.py:101
  139.2 12.3 %collective-permute-start.4 = (f32[1,6,256]{2,0,1:T(1,128)S(1)}, f32[1,6,256]{2,0,1:T(1,128)S(1)}, u32[]{:S(2)}, u32[]{:S(2)}) collective-permute-start(f32[1,6,256]{2,0,1:T(1,128)S(1)} %get-tuple-element.21), channel_id=1, source_target_pairs={{4,0},{8,4},{12,8},{16,12},{20,16},{24,20},{28,24},{32,28},{36,32}... | collective-permute-start | bytes 18440 | tf_op jit(solution)/shard_map/ppermute | solution.py:102
  141.7 9.9 %collective-permute-start.5 = (f32[1,6,256]{2,0,1:T(1,128)S(1)}, f32[1,6,256]{2,0,1:T(1,128)S(1)}, u32[]{:S(2)}, u32[]{:S(2)}) collective-permute-start(f32[1,6,256]{2,0,1:T(1,128)S(1)} %get-tuple-element.22), channel_id=1, source_target_pairs={{0,4},{4,8},{8,12},{12,16},{16,20},{20,24},{24,28},{28,32},{32,36}... | collective-permute-start | bytes 18440 | tf_op jit(solution)/shard_map/ppermute | solution.py:101
Sparse Core Ops, SparseCore 0:
  24.6 38.1 all-gather.1
  83.8 49.4 reduce-scatter.1

commit v2 on v1

--- a/solution.py
+++ b/solution.py
@@ -1,3 +1,4 @@
+import functools
 import math
 
 import jax
@@ -91,6 +92,118 @@
     )(part)
 
 
+def _to_lines_kernel(n, x_ref, o_ref, send_sems, recv_sems, local_sem):
+    me = lax.axis_index("sec")
+    ax = lax.axis_index("ax")
+    rows, width = o_ref.shape[1], x_ref.shape[2]
+    barrier = pltpu.get_barrier_semaphore()
+    for d in range(1, n):
+        pl.semaphore_signal(barrier, inc=1, device_id=(ax, (me + d) % n), device_id_type=MESH)
+    pl.semaphore_wait(barrier, n - 1)
+    dst = o_ref.at[:, :, pl.ds(pl.multiple_of(me * width, width), width)]
+    copies = []
+    for d in range(1, n):
+        peer = (me + d) % n
+        cp = pltpu.make_async_remote_copy(
+            src_ref=x_ref.at[:, pl.ds(pl.multiple_of(peer * rows, rows), rows), :],
+            dst_ref=dst,
+            send_sem=send_sems.at[d],
+            recv_sem=recv_sems.at[d],
+            device_id=(ax, peer),
+            device_id_type=MESH,
+        )
+        cp.start()
+        copies.append(cp)
+    local = pltpu.make_async_copy(
+        x_ref.at[:, pl.ds(pl.multiple_of(me * rows, rows), rows), :], dst, local_sem
+    )
+    local.start()
+    local.wait()
+    for cp in copies:
+        cp.wait()
+
+
+def _from_lines_kernel(n, x_ref, o_ref, send_sems, recv_sems, local_sem):
+    me = lax.axis_index("sec")
+    ax = lax.axis_index("ax")
+    rows, width = x_ref.shape[1], o_ref.shape[2]
+    barrier = pltpu.get_barrier_semaphore()
+    for d in range(1, n):
+        pl.semaphore_signal(barrier, inc=1, device_id=(ax, (me + d) % n), device_id_type=MESH)
+    pl.semaphore_wait(barrier, n - 1)
+    dst = o_ref.at[:, pl.ds(pl.multiple_of(me * rows, rows), rows), :]
+    copies = []
+    for d in range(1, n):
+        peer = (me + d) % n
+        cp = pltpu.make_async_remote_copy(
+            src_ref=x_ref.at[:, :, pl.ds(pl.multiple_of(peer * width, width), width)],
+            dst_ref=dst,
+            send_sem=send_sems.at[d],
+            recv_sem=recv_sems.at[d],
+            device_id=(ax, peer),
+            device_id_type=MESH,
+        )
+        cp.start()
+        copies.append(cp)
+    local = pltpu.make_async_copy(
+        x_ref.at[:, :, pl.ds(pl.multiple_of(me * width, width), width)], dst, local_sem
+    )
+    local.start()
+    local.wait()
+    for cp in copies:
+        cp.wait()
+
+
+def _exchange(body, out_shape, cid, n, x):
+    return pl.pallas_call(
+        functools.partial(body, n),
+        out_shape=jax.ShapeDtypeStruct(out_shape, x.dtype),
+        in_specs=[pl.BlockSpec(memory_space=pltpu.VMEM)],
+        out_specs=pl.BlockSpec(memory_space=pltpu.VMEM),
+        scratch_shapes=[
+            pltpu.SemaphoreType.DMA((n,)),
+            pltpu.SemaphoreType.DMA((n,)),
+            pltpu.SemaphoreType.DMA,
+        ],
+        compiler_params=pltpu.CompilerParams(collective_id=cid, has_side_effects=True),
+    )(x)
+
+
+def to_lines(x, n):
+    comps, rows, width = x.shape
+    return _exchange(_to_lines_kernel, (comps, rows // n, width * n), 1, n, x)
+
+
+def from_lines(x, n):
+    comps, rows, around = x.shape
+    return _exchange(_from_lines_kernel, (comps, rows * n, around // n), 2, n, x)
+
+
+def dft_table(length):
+    half = length // 2
+    root = int(round(math.sqrt(length)))
+    cols = jnp.concatenate([jnp.arange(half + 1), jnp.arange(1, half)])
+    is_sin = jnp.arange(length) > half
+    step = 2.0 * math.pi / length
+    coarse = (root * jnp.arange(length // root)[:, None] * cols[None, :]) % length
+    fine = (jnp.arange(root)[:, None] * cols[None, :]) % length
+    coarse_c, coarse_s = jnp.cos(step * coarse.astype(jnp.float32)), jnp.sin(step * coarse.astype(jnp.float32))
+    fine_c, fine_s = jnp.cos(step * fine.astype(jnp.float32)), jnp.sin(step * fine.astype(jnp.float32))
+    cos_part = coarse_c[:, None] * fine_c[None] - coarse_s[:, None] * fine_s[None]
+    sin_part = coarse_s[:, None] * fine_c[None] + coarse_c[:, None] * fine_s[None]
+    return jnp.where(is_sin[None, None], sin_part, cos_part).reshape(length, length)
+
+
+def paired_inverse(precond):
+    length = precond.shape[2]
+    half = length // 2
+    low = precond[:, :, : half + 1]
+    mirror = jnp.flip(precond[:, :, half + 1 :], axis=2)
+    inner = jnp.concatenate([jnp.zeros_like(low[:, :, :1]), mirror, jnp.zeros_like(low[:, :, :1])], axis=2)
+    paired = low + inner
+    return jnp.concatenate([paired, paired[:, :, 1:half]], axis=2)
+
+
 def with_halo(x, sides, width, wrap):
     for axis, dim in sides:
         size, length = (lax.axis_size(axis), x.shape[dim])
@@ -118,17 +231,6 @@
     return (stiffness + 4.5) * field - beside - 0.5 * swap_radial(field)
 
 
-def harmonic_table(row_index, col_index, length):
-    product = row_index[:, None] * col_index[None, :] % length
-    angle = 2.0 * math.pi / length * product.astype(jnp.float32)
-    return jnp.concatenate([jnp.cos(angle), jnp.sin(angle)], axis=1)
-
-
-def scale_harmonics(block_inverse, spectrum):
-    doubled = jnp.concatenate([block_inverse, block_inverse], axis=2)
-    return jnp.sum(doubled[None] * spectrum[:, None], axis=2)
-
-
 def shards(load, disp, stiff, hole, section_class, class_table, precond):
     slab_count, comp_count, sector_width = disp.shape
     sector_count = lax.axis_size("sec")
@@ -143,28 +245,20 @@
     stiffness = stiff * (factors * taper[:, None])[:, :, None]
     solid = (1 - hole).astype(jnp.float32)[:, None, :]
     residual = solid * (load - apply_operator(disp, stiffness))
-    sector = lax.axis_index("sec")
-    own_index = sector * sector_width + jnp.arange(sector_width)
-    table = harmonic_table(jnp.arange(around_cells), own_index, around_cells)
-    own_inverse = lax.dynamic_slice_in_dim(precond, sector * sector_width, sector_width, 2)
-    initial = jnp.zeros((slab_count, comp_count, 2 * sector_width), jnp.float32)
-    piece = lax.all_gather(residual, "sec", axis=2, tiled=True)
-    span = piece.shape[2]
-    table_rows = table
-    flat = piece.reshape(-1, span)
-    spectrum = jnp.dot(flat, table_rows, precision=lax.Precision.HIGHEST).reshape(initial.shape)
-    scaled = scale_harmonics(own_inverse, spectrum).reshape(-1, 2 * sector_width)
-    table_rows = table
-    shares = lax.psum_scatter(
-        lax.dot_general(
-            table_rows, scaled, (((1,), (1,)), ((), ())), precision=lax.Precision.HIGHEST
-        )
-        / around_cells,
-        "sec",
-        scatter_dimension=0,
-        tiled=True,
-    )
-    smoothed = shares.T.reshape(slab_count, comp_count, sector_width)
+    lines = to_lines(jnp.transpose(residual, (1, 0, 2)), sector_count)
+    spectrum = jnp.dot(
+        lines.reshape(-1, around_cells), dft_table(around_cells), precision=lax.Precision.HIGH
+    ).reshape(lines.shape)
+    mixed = jnp.sum(paired_inverse(precond)[:, :, None] * spectrum[None], axis=1)
+    smoothed_lines = lax.dot_general(
+        mixed.reshape(-1, around_cells),
+        dft_table(around_cells),
+        (((1,), (1,)), ((), ())),
+        precision=lax.Precision.HIGH,
+    ) / around_cells
+    smoothed = jnp.transpose(
+        from_lines(smoothed_lines.reshape(lines.shape), sector_count), (1, 0, 2)
+    )
     prec = solid * smoothed
     image = solid * apply_operator(prec, stiffness)
     cell_total = slab_count * lax.axis_size("ax") * comp_count * around_cells

time: 195 us -> 125 us (0.64)
  waiting for transfers between devices: 90.9 us -> 3.62 us
  Pallas kernels: 21.3 us -> 57.2 us
  between operations: 17.5 us -> 4.23 us
  local copies, waits for them, and re-layouts: 18.5 us -> 10 us
  matrix products: 16.1 us -> 7.66 us
  other arithmetic: 14.5 us -> 22.5 us
  starting transfers between devices: 15.1 us -> 19.1 us
    reduce_scatter x1 -> x0, waiting for transfers between devices: 49.6 us -> none  [shards(): lax.psum_scatter(lax.dot_general(table_rows, scaled, (((1,), (1,)), ((),...]
    all_gather x1 -> x0, waiting for transfers between devices: 34 us -> none  [shards(): piece = lax.all_gather(residual, 'sec', axis=2, tiled=True)]
    pallas_call x0 -> x2, Pallas kernels: none -> 28.3 us  [_exchange(): pl.pallas_call(functools.partial(body, n), out_shape=jax.ShapeDtypeStruct...]
    dot_general x2, matrix products: 15.2 us -> 7.47 us  [the longest x1 4.22 us: shards(): jnp.dot(lines.reshape(-1, around_cells), dft_table(around_cells), precisi...]
    pallas_call x1, Pallas kernels: 21.3 us -> 28.9 us  [all_sum(): pl.pallas_call(_ar_kernel, out_shape=jax.ShapeDtypeStruct(part.shape, jnp...]
    select_n x0 -> x2, other arithmetic: none -> 7.05 us  [dft_table(): jnp.where(is_sin[None, None], sin_part, cos_part).reshape(length, length)]
    reshape x3 -> x0, local copies, waits for them, and re-layouts: 5.28 us -> none  [the longest x2 2.69 us: shards(): smoothed = shares.T.reshape(slab_count, comp_count, sector_width)]
    ppermute x4, waiting for transfers between devices: 6.12 us -> 1.58 us  [with_halo(): before = lax.ppermute(last, axis, up)]
  transfers between devices with their start and end apart: 10 -> 8, of which waited for: 5 -> 2; matrix products, arithmetic and copies ran while one was open for 4% -> 11% of each run, Pallas kernels for 0% -> 0%
where the time goes in v2:
time: 125 us; the launch traced here: 124 us
  Pallas kernels  57.2 us (46%)
  other arithmetic  22.5 us (18%)
  starting transfers between devices  19.1 us (15%)
  local copies, waits for them, and re-layouts  10 us (8%)
  matrix products  7.66 us (6%)
  between operations  4.23 us (3%)
  waiting for transfers between devices  3.62 us (3%)
    pallas_call x1, Pallas kernels, all_sum(): pl.pallas_call(_ar_kernel, out_shape=jax.ShapeDtypeStruct(part.shape, jnp...  28.9 us
    pallas_call x2, Pallas kernels, _exchange(): pl.pallas_call(functools.partial(body, n), out_shape=jax.ShapeDtypeStruct...  28.3 us
    ppermute x4, starting transfers between devices, with_halo(): after = lax.ppermute(first, axis, down)  11 us
    ppermute x4, starting transfers between devices, with_halo(): before = lax.ppermute(last, axis, up)  8.09 us
    select_n x2, other arithmetic, dft_table(): jnp.where(is_sin[None, None], sin_part, cos_part).reshape(length, length)  7.05 us
    dot_general x1, matrix products, shards(): jnp.dot(lines.reshape(-1, around_cells), dft_table(around_cells), precisi...  4.22 us
    dot_general x1, matrix products, shards(): lax.dot_general(mixed.reshape(-1, around_cells), dft_table(around_cells),...  3.25 us
    another operation x1, local copies, waits for them, and re-layouts, shards(): jnp.stack([jnp.sum(residual * prec), jnp.sum(prec * image), jnp.sum(resid...  3.24 us
  transfers between devices with their start and end apart: 8, of which 2 were waited for; matrix products, arithmetic and copies ran while one was open for 11% of the time, Pallas kernels for 0%

profile of v2, /device:TPU:4, one launch (start us, length us, event | category | flops | bytes accessed | tf_op | source)
XLA Modules:
  0.0 124.4 jit_solution(919889168161101909)
XLA Ops:
  0.6 2.1 %fusion.33 = (f32[128,6,1]{2,0,1:T(8,128)}, f32[128,6,1]{2,0,1:T(8,128)}) fusion(f32[128,6,256]{2,0,1:T(8,128)} %param.10), kind=kLoop, calls=%fused_computation.76 | loop fusion | bytes 12288 | tf_op jit(solution)/shard_map/slice | solution.py:213
  2.8 2.6 %collective-permute-start.2 = (f32[128,6,1]{2,0,1:T(8,128)}, f32[128,6,1]{2,0,1:T(8,128)S(1)}, u32[]{:S(2)}, u32[]{:S(2)}) collective-permute-start(f32[128,6,1]{2,0,1:T(8,128)} %get-tuple-element.27), channel_id=1, source_target_pairs={{1,0},{2,1},{3,2},{0,3},{5,4},{6,5},{7,6},{4,7},{9,8},{10,9},{11,1... | collective-permute-start | bytes 9224 | tf_op jit(solution)/shard_map/ppermute | solution.py:215
  5.4 0.8 fusion.32
  6.2 2.4 %collective-permute-start = (f32[1,6,256]{2,0,1:T(1,128)S(1)}, f32[1,6,256]{2,0,1:T(1,128)S(1)}, u32[]{:S(2)}, u32[]{:S(2)}) collective-permute-start(f32[1,6,256]{2,0,1:T(1,128)S(1)} %get-tuple-element.25), channel_id=1, source_target_pairs={{4,0},{8,4},{12,8},{16,12},{20,16},{24,20},{28,24},{32,28},{36,32}... | collective-permute-start | bytes 18440 | tf_op jit(solution)/shard_map/ppermute | solution.py:215
  8.7 3.4 %collective-permute-start.1 = (f32[1,6,256]{2,0,1:T(1,128)S(1)}, f32[1,6,256]{2,0,1:T(1,128)S(1)}, u32[]{:S(2)}, u32[]{:S(2)}) collective-permute-start(f32[1,6,256]{2,0,1:T(1,128)S(1)} %get-tuple-element.26), channel_id=1, source_target_pairs={{0,4},{4,8},{8,12},{12,16},{16,20},{20,24},{24,28},{28,32},{32,36}... | collective-permute-start | bytes 18440 | tf_op jit(solution)/shard_map/ppermute | solution.py:214
  12.1 0.9 subtract_convert_fusion
  13.1 1.2 reverse_multiply_fusion.1
  14.3 1.0 slice.116
  15.7 1.0 maximum_add_fusion
  16.9 1.1 fusion.27
  17.9 3.8 %broadcast_select_fusion = (f32[32,32,1024]{2,1,0:T(8,128)}, f32[32,32,1024]{2,1,0:T(8,128)S(1)}, f32[32,32,1024]{2,1,0:T(8,128)S(1)}) fusion(pred[1024]{0:T(1024)(128)(4,1)S(1)} %iota_compare_fusion.2, f32[32,1024]{1,0:T(8,128)S(1)} %get-tuple-element.39, f32[32,1024]{1,0:T(8,128)S(1)} %get-tuple-element.33, f32[32,1024]{1,0:T(8,128)S(1)} %get-tuple-element.40, ...), kind=kLoop, calls=%fused_computation.6 | loop fusion | flops 7340032 | bytes 13108224 | tf_op jit(solution)/shard_map/jit(_where)/select_n | solution.py:194
  21.7 3.3 %bitcast_select_fusion = f32[1024,1024]{1,0:T(8,128)} fusion(f32[32,32,1024]{2,1,0:T(8,128)S(1)} %get-tuple-element.30, f32[32,32,1024]{2,1,0:T(8,128)S(1)} %get-tuple-element.31, pred[1024]{0:T(1024)(128)(4,1)S(1)} %iota_compare_fusion.2), kind=kLoop, calls=%fused_computation.3 | loop fusion | flops 1048576 | bytes 12583936 | tf_op jit(solution)/shard_map/jit(_where)/select_n | solution.py:194
  25.4 2.6 %fusion.12 = f32[128,6,256]{2,0,1:T(8,128)} fusion(f32[128,6,256]{2,0,1:T(8,128)S(1)} %copy-done.6, f32[128,6,256]{2,0,1:T(8,128)S(1)} %copy-done.3, f32[128,6,1]{2,0,1:T(8,128)} %collective-permute-done.3, f32[128,6,1]{2,0,1:T(8,128)S(1)} %collective-permute-done.2, f32[1,6,256]{2,0,1:T(1,128)S(1)} %collective-permute-done.1, ...), kind=kLoop, calls=%fused_computation.24 | loop fusion | flops 2752512 | bytes 4084736 | tf_op jit(solution)/shard_map/mul | solution.py:247
  28.1 13.8 %shard_map.94 = f32[6,32,1024]{2,1,0:T(8,128)} custom-call(f32[6,128,256]{2,1,0:T(8,128)} %bitcast.44), custom_call_target="tpu_custom_call" | custom-call | tf_op jit(solution)/shard_map/pallas_call | solution.py:158
  41.9 4.2 %fusion = f32[6,32,1024]{2,1,0:T(8,128)S(1)} fusion(f32[6,32,1024]{2,1,0:T(8,128)} %shard_map.94, f32[1024,1024]{1,0:T(8,128)} %bitcast_select_fusion), kind=kOutput, calls=%fused_computation.1 | convolution fusion | flops 1207959552 | bytes 5767168 | tf_op jit(solution)/shard_map/dot_general | solution.py:249
  46.1 0.3 multiply_reduce_fusion
  46.5 3.2 %convolution_multiply_fusion = f32[192,1024]{1,0:T(8,128)} fusion(f32[192,1024]{1,0:T(8,128)S(1)} %bitcast.46, f32[1024,1024]{1,0:T(8,128)S(1)} %bitcast.42), kind=kOutput, calls=%fused_computation.7 | convolution fusion | flops 1208156160 | bytes 5767168 | tf_op jit(solution)/shard_map/dot_general | solution.py:253
  49.7 14.5 %shard_map.95 = f32[6,128,256]{2,1,0:T(8,128)} custom-call(f32[6,32,1024]{2,1,0:T(8,128)} %bitcast.47), custom_call_target="tpu_custom_call" | custom-call | tf_op jit(solution)/shard_map/pallas_call | solution.py:158
  64.3 1.3 %fusion.39 = f32[128,6,256]{2,0,1:T(8,128)S(1)} fusion(f32[6,128,256]{2,1,0:T(8,128)} %shard_map.95, f32[128,256]{1,0:T(8,128)S(1)} %subtract_convert_fusion), kind=kLoop, calls=%fused_computation.78 | loop fusion | flops 196608 | bytes 1703936 | tf_op jit(solution)/shard_map/mul | solution.py:262
  65.7 1.2 broadcast_multiply_fusion
  67.0 3.5 %collective-permute-start.6 = (f32[128,6,1]{2,0,1:T(8,128)S(1)}, f32[128,6,1]{2,0,1:T(8,128)S(1)}, u32[]{:S(2)}, u32[]{:S(2)}) collective-permute-start(f32[128,6,1]{2,0,1:T(8,128)S(1)} %get-tuple-element.23), channel_id=1, source_target_pairs={{1,0},{2,1},{3,2},{0,3},{5,4},{6,5},{7,6},{4,7},{9,8},{10,9},{11,1... | collective-permute-start | bytes 9224 | tf_op jit(solution)/shard_map/ppermute | solution.py:215
  70.5 2.4 %collective-permute-start.4 = (f32[1,6,256]{2,0,1:T(1,128)S(1)}, f32[1,6,256]{2,0,1:T(1,128)S(1)}, u32[]{:S(2)}, u32[]{:S(2)}) collective-permute-start(f32[1,6,256]{2,0,1:T(1,128)S(1)} %get-tuple-element.21), channel_id=1, source_target_pairs={{4,0},{8,4},{12,8},{16,12},{20,16},{24,20},{28,24},{32,28},{36,32}... | collective-permute-start | bytes 18440 | tf_op jit(solution)/shard_map/ppermute | solution.py:215
  72.9 4.7 %collective-permute-start.5 = (f32[1,6,256]{2,0,1:T(1,128)S(1)}, f32[1,6,256]{2,0,1:T(1,128)S(1)}, u32[]{:S(2)}, u32[]{:S(2)}) collective-permute-start(f32[1,6,256]{2,0,1:T(1,128)S(1)} %get-tuple-element.22), channel_id=1, source_target_pairs={{0,4},{4,8},{8,12},{12,16},{16,20},{20,24},{24,28},{28,32},{32,36}... | collective-permute-start | bytes 18440 | tf_op jit(solution)/shard_map/ppermute | solution.py:214
  77.7 2.0 %collective-permute-done.6 = f32[128,6,1]{2,0,1:T(8,128)S(1)} collective-permute-done((f32[128,6,1]{2,0,1:T(8,128)S(1)}, f32[128,6,1]{2,0,1:T(8,128)S(1)}, u32[]{:S(2)}, u32[]{:S(2)}) %collective-permute-start.6) | collective-permute-done | bytes 3104 | tf_op jit(solution)/shard_map/ppermute | solution.py:215
  79.7 1.6 %collective-permute-done.7 = f32[128,6,1]{2,0,1:T(8,128)S(1)} collective-permute-done((f32[128,6,1]{2,0,1:T(8,128)S(1)}, f32[128,6,1]{2,0,1:T(8,128)S(1)}, u32[]{:S(2)}, u32[]{:S(2)}) %collective-permute-start.7) | collective-permute-done | bytes 3104 | tf_op jit(solution)/shard_map/ppermute | solution.py:214
  81.3 2.4 %multiply_reduce_fusion.1 = (f32[]{:T(128)}, f32[]{:T(128)}, f32[]{:T(128)}, f32[]{:T(128)}, f32[]{:T(128)}, /*index=5*/f32[128,6,256]{2,0,1:T(8,128)}) fusion(f32[128,6,256]{2,0,1:T(8,128)S(1)} %copy-done.4, f32[128,3,2,256]{3,0,2,1:T(8,128)S(1)} %reverse_multiply_fusion, f32[128,6,256]{2,0,1:T(8,128)S(1)} %fusion.39, ...), kind=kLoop, calls=%fused_computation.32 | loop fusion | flops 4718587 | bytes 4871188 | tf_op jit(solution)/shard_map/reduce_sum | solution.py:271
  83.7 3.2 %stack.35 = f32[5]{0:T(128)S(1)} concatenate(f32[1]{0:T(128)} %bitcast.10, f32[1]{0:T(128)} %bitcast.13, f32[1]{0:T(128)} %bitcast.14, f32[1]{0:T(128)} %bitcast.15, f32[1]{0:T(128)} %bitcast.16), dimensions={0} | concatenate | bytes 40 | tf_op jit(solution)/shard_map/stack | solution.py:265
  86.9 0.6 scatter.4.x_ref
  87.5 28.9 %shard_map.96 = f32[8,128]{1,0:T(8,128)} custom-call(f32[8,128]{1,0:T(8,128)} %scatter.4.x_ref), custom_call_target="tpu_custom_call" | custom-call | tf_op jit(solution)/shard_map/pallas_call | solution.py:77
  116.4 1.5 %fusion.34 = (f32[1,1]{1,0:T(1,128)}, f32[1,1]{1,0:T(1,128)}, f32[1,1]{1,0:T(1,128)}, f32[1,1]{1,0:T(1,128)}, f32[1,1]{1,0:T(1,128)}) fusion(f32[8,128]{1,0:T(8,128)} %shard_map.96), kind=kLoop, calls=%fused_computation.77 | loop fusion | bytes 40 | tf_op jit(solution)/shard_map/slice | solution.py:280
  120.6 2.5 %multiply_subtract_fusion.1 = (f32[128,6,256]{2,0,1:T(8,128)}, f32[128,6,256]{2,0,1:T(8,128)}) fusion(f32[128,6,256]{2,0,1:T(8,128)S(1)} %copy-done.4, f32[128,6,256]{2,0,1:T(8,128)} %get-tuple-element.20, f32[]{:T(128)} %bitcast.18, f32[128,6,256]{2,0,1:T(8,128)S(1)} %copy-done.3, f32[6,128,256]{2,1,0:T(8,128)S(1)} %copy-done.1, ...), kind=kLoop, calls=%fused_computation.30 | loop fusion | flops 983040 | bytes 4849668 | tf_op jit(solution)/shard_map/sub | solution.py:279
  123.8 0.6 pad_maximum_fusion.9
  (39 shorter events, 1.2 us)
Async XLA Ops:
  0.6 24.4 %copy-start = (f32[4,6]{1,0:T(4,128)S(1)}, f32[4,6]{1,0:T(4,128)}, u32[]{:S(2)}) copy-start(f32[4,6]{1,0:T(4,128)} %param.14) | copy-start | bytes 292
  2.8 22.6 %collective-permute-start.2 = (f32[128,6,1]{2,0,1:T(8,128)}, f32[128,6,1]{2,0,1:T(8,128)S(1)}, u32[]{:S(2)}, u32[]{:S(2)}) collective-permute-start(f32[128,6,1]{2,0,1:T(8,128)} %get-tuple-element.27), channel_id=1, source_target_pairs={{1,0},{2,1},{3,2},{0,3},{5,4},{6,5},{7,6},{4,7},{9,8},{10,9},{11,1... | collective-permute-start | bytes 9224 | tf_op jit(solution)/shard_map/ppermute | solution.py:215
  5.4 20.0 %collective-permute-start.3 = (f32[128,6,1]{2,0,1:T(8,128)}, f32[128,6,1]{2,0,1:T(8,128)}, u32[]{:S(2)}, u32[]{:S(2)}) collective-permute-start(f32[128,6,1]{2,0,1:T(8,128)} %get-tuple-element.28), channel_id=1, source_target_pairs={{0,1},{1,2},{2,3},{3,0},{4,5},{5,6},{6,7},{7,4},{8,9},{9,10},{10,1... | collective-permute-start | bytes 9224 | tf_op jit(solution)/shard_map/ppermute | solution.py:214
  6.2 19.1 %collective-permute-start = (f32[1,6,256]{2,0,1:T(1,128)S(1)}, f32[1,6,256]{2,0,1:T(1,128)S(1)}, u32[]{:S(2)}, u32[]{:S(2)}) collective-permute-start(f32[1,6,256]{2,0,1:T(1,128)S(1)} %get-tuple-element.25), channel_id=1, source_target_pairs={{4,0},{8,4},{12,8},{16,12},{20,16},{24,20},{28,24},{32,28},{36,32}... | collective-permute-start | bytes 18440 | tf_op jit(solution)/shard_map/ppermute | solution.py:215
  8.7 16.7 %collective-permute-start.1 = (f32[1,6,256]{2,0,1:T(1,128)S(1)}, f32[1,6,256]{2,0,1:T(1,128)S(1)}, u32[]{:S(2)}, u32[]{:S(2)}) collective-permute-start(f32[1,6,256]{2,0,1:T(1,128)S(1)} %get-tuple-element.26), channel_id=1, source_target_pairs={{0,4},{4,8},{8,12},{12,16},{16,20},{20,24},{24,28},{28,32},{32,36}... | collective-permute-start | bytes 18440 | tf_op jit(solution)/shard_map/ppermute | solution.py:214
  21.7 3.3 %copy-start.7 = (s32[128]{0:T(128)S(1)}, s32[128]{0:T(128)}, u32[]{:S(2)}) copy-start(s32[128]{0:T(128)} %param.13) | copy-start | bytes 1540
  21.7 3.7 %copy-start.3 = (f32[128,6,256]{2,0,1:T(8,128)S(1)}, f32[128,6,256]{2,0,1:T(8,128)}, u32[]{:S(2)}) copy-start(f32[128,6,256]{2,0,1:T(8,128)} %param.10) | copy-start | bytes 2359300
  21.7 3.7 %copy-start.5 = (f32[128,6,256]{2,0,1:T(8,128)S(1)}, f32[128,6,256]{2,0,1:T(8,128)}, u32[]{:S(2)}) copy-start(f32[128,6,256]{2,0,1:T(8,128)} %param.11) | copy-start | bytes 2359300
  21.7 3.7 %copy-start.6 = (f32[128,6,256]{2,0,1:T(8,128)S(1)}, f32[128,6,256]{2,0,1:T(8,128)}, u32[]{:S(2)}) copy-start(f32[128,6,256]{2,0,1:T(8,128)} %param.9) | copy-start | bytes 2359300
  41.9 4.6 %copy-start.2 = (f32[32,32,1024]{2,1,0:T(8,128)S(1)}, f32[32,32,1024]{2,1,0:T(8,128)}, u32[]{:S(2)}) copy-start(f32[32,32,1024]{2,1,0:T(8,128)} %get-tuple-element.29) | copy-start | bytes 12582916
  49.7 31.6 %copy-start.4 = (f32[128,6,256]{2,0,1:T(8,128)S(1)}, f32[128,6,256]{2,0,1:T(8,128)}, u32[]{:S(2)}) copy-start(f32[128,6,256]{2,0,1:T(8,128)} %fusion.12) | copy-start | bytes 2359300
  64.3 17.0 %copy-start.1 = (f32[6,128,256]{2,1,0:T(8,128)S(1)}, f32[6,128,256]{2,1,0:T(8,128)}, u32[]{:S(2)}) copy-start(f32[6,128,256]{2,1,0:T(8,128)} %shard_map.95) | copy-start | bytes 2359300
  67.0 12.7 %collective-permute-start.6 = (f32[128,6,1]{2,0,1:T(8,128)S(1)}, f32[128,6,1]{2,0,1:T(8,128)S(1)}, u32[]{:S(2)}, u32[]{:S(2)}) collective-permute-start(f32[128,6,1]{2,0,1:T(8,128)S(1)} %get-tuple-element.23), channel_id=1, source_target_pairs={{1,0},{2,1},{3,2},{0,3},{5,4},{6,5},{7,6},{4,7},{9,8},{10,9},{11,1... | collective-permute-start | bytes 9224 | tf_op jit(solution)/shard_map/ppermute | solution.py:215
  70.5 10.8 %collective-permute-start.7 = (f32[128,6,1]{2,0,1:T(8,128)S(1)}, f32[128,6,1]{2,0,1:T(8,128)S(1)}, u32[]{:S(2)}, u32[]{:S(2)}) collective-permute-start(f32[128,6,1]{2,0,1:T(8,128)S(1)} %get-tuple-element.24), channel_id=1, source_target_pairs={{0,1},{1,2},{2,3},{3,0},{4,5},{5,6},{6,7},{7,4},{8,9},{9,10},{10,1... | collective-permute-start | bytes 9224 | tf_op jit(solution)/shard_map/ppermute | solution.py:214
  70.5 10.8 %collective-permute-start.4 = (f32[1,6,256]{2,0,1:T(1,128)S(1)}, f32[1,6,256]{2,0,1:T(1,128)S(1)}, u32[]{:S(2)}, u32[]{:S(2)}) collective-permute-start(f32[1,6,256]{2,0,1:T(1,128)S(1)} %get-tuple-element.21), channel_id=1, source_target_pairs={{4,0},{8,4},{12,8},{16,12},{20,16},{24,20},{28,24},{32,28},{36,32}... | collective-permute-start | bytes 18440 | tf_op jit(solution)/shard_map/ppermute | solution.py:215
  72.9 8.4 %collective-permute-start.5 = (f32[1,6,256]{2,0,1:T(1,128)S(1)}, f32[1,6,256]{2,0,1:T(1,128)S(1)}, u32[]{:S(2)}, u32[]{:S(2)}) collective-permute-start(f32[1,6,256]{2,0,1:T(1,128)S(1)} %get-tuple-element.22), channel_id=1, source_target_pairs={{0,4},{4,8},{8,12},{12,16},{16,20},{20,24},{24,28},{28,32},{32,36}... | collective-permute-start | bytes 18440 | tf_op jit(solution)/shard_map/ppermute | solution.py:214

commit v3 on v2

--- a/solution.py
+++ b/solution.py
@@ -204,17 +204,65 @@
     return jnp.concatenate([paired, paired[:, :, 1:half]], axis=2)
 
 
-def with_halo(x, sides, width, wrap):
-    for axis, dim in sides:
-        size, length = (lax.axis_size(axis), x.shape[dim])
-        up = [(i, (i + 1) % size) for i in range(size if wrap else size - 1)]
-        down = [(j, i) for i, j in up]
-        last = lax.slice_in_dim(x, length - width, length, axis=dim)
-        first = lax.slice_in_dim(x, 0, width, axis=dim)
-        before = lax.ppermute(last, axis, up)
-        after = lax.ppermute(first, axis, down)
-        x = jnp.concatenate([before, x, after], axis=dim)
-    return x
+def _halo_kernel(sizes, x_ref, o_ref, send_sems, recv_sems):
+    n_ax, n_sec = sizes
+    ax = lax.axis_index("ax")
+    sec = lax.axis_index("sec")
+    peers = [
+        ((ax + n_ax - 1) % n_ax, sec),
+        ((ax + 1) % n_ax, sec),
+        (ax, (sec + n_sec - 1) % n_sec),
+        (ax, (sec + 1) % n_sec),
+    ]
+    barrier = pltpu.get_barrier_semaphore()
+    for peer in peers:
+        pl.semaphore_signal(barrier, inc=1, device_id=peer, device_id_type=MESH)
+    pl.semaphore_wait(barrier, len(peers))
+    copies = []
+    for i, peer in enumerate(peers):
+        cp = pltpu.make_async_remote_copy(
+            src_ref=x_ref.at[i],
+            dst_ref=o_ref.at[i],
+            send_sem=send_sems.at[i],
+            recv_sem=recv_sems.at[i],
+            device_id=peer,
+            device_id_type=MESH,
+        )
+        cp.start()
+        copies.append(cp)
+    for cp in copies:
+        cp.wait()
+
+
+def halo_exchange(field, cid):
+    rows, comps, width = field.shape
+    lanes = max(width, rows)
+    subl = -(-comps // 8) * 8
+
+    def fit(plane):
+        return jnp.pad(plane, ((0, subl - plane.shape[0]), (0, lanes - plane.shape[1])))
+
+    edges = jnp.stack(
+        [fit(field[0]), fit(field[-1]), fit(field[:, :, 0].T), fit(field[:, :, -1].T)]
+    )
+    got = pl.pallas_call(
+        functools.partial(_halo_kernel, (lax.axis_size("ax"), lax.axis_size("sec"))),
+        out_shape=jax.ShapeDtypeStruct(edges.shape, edges.dtype),
+        in_specs=[pl.BlockSpec(memory_space=pltpu.VMEM)],
+        out_specs=pl.BlockSpec(memory_space=pltpu.VMEM),
+        scratch_shapes=[pltpu.SemaphoreType.DMA((4,)), pltpu.SemaphoreType.DMA((4,))],
+        compiler_params=pltpu.CompilerParams(collective_id=cid, has_side_effects=True),
+    )(edges)
+    ax = lax.axis_index("ax")
+    after_row = jnp.where(ax == lax.axis_size("ax") - 1, 0.0, got[0, :comps, :width])
+    before_row = jnp.where(ax == 0, 0.0, got[1, :comps, :width])
+    after_col = got[2, :comps, :rows].T
+    before_col = got[3, :comps, :rows].T
+    down = jnp.concatenate([field[1:], after_row[None]], axis=0)
+    up = jnp.concatenate([before_row[None], field[:-1]], axis=0)
+    right = jnp.concatenate([field[:, :, 1:], after_col[:, :, None]], axis=2)
+    left = jnp.concatenate([before_col[:, :, None], field[:, :, :-1]], axis=2)
+    return up + down + left + right
 
 
 def swap_radial(field):
@@ -223,11 +271,8 @@
     return jnp.flip(folded, axis=2).reshape(extent)
 
 
-def apply_operator(field, stiffness):
-    axial_pad = with_halo(field, (("ax", 0),), 1, False)
-    sector_pad = with_halo(field, (("sec", 2),), 1, True)
-    beside = axial_pad[2:] + axial_pad[:-2]
-    beside = beside + sector_pad[:, :, 2:] + sector_pad[:, :, :-2]
+def apply_operator(field, stiffness, cid):
+    beside = halo_exchange(field, cid)
     return (stiffness + 4.5) * field - beside - 0.5 * swap_radial(field)
 
 
@@ -244,7 +289,7 @@
     factors = jnp.dot(one_hot, class_table, precision=lax.Precision.HIGHEST)
     stiffness = stiff * (factors * taper[:, None])[:, :, None]
     solid = (1 - hole).astype(jnp.float32)[:, None, :]
-    residual = solid * (load - apply_operator(disp, stiffness))
+    residual = solid * (load - apply_operator(disp, stiffness, 3))
     lines = to_lines(jnp.transpose(residual, (1, 0, 2)), sector_count)
     spectrum = jnp.dot(
         lines.reshape(-1, around_cells), dft_table(around_cells), precision=lax.Precision.HIGH
@@ -260,7 +305,7 @@
         from_lines(smoothed_lines.reshape(lines.shape), sector_count), (1, 0, 2)
     )
     prec = solid * smoothed
-    image = solid * apply_operator(prec, stiffness)
+    image = solid * apply_operator(prec, stiffness, 4)
     cell_total = slab_count * lax.axis_size("ax") * comp_count * around_cells
     parts = jnp.stack(
         [

time: 125 us -> 147 us (1.18)
  local copies, waits for them, and re-layouts: 10 us -> 42.6 us
  starting transfers between devices: 19.1 us -> 0 us
  Pallas kernels: 57.2 us -> 68.5 us
  waiting for transfers between devices: 3.62 us -> 0 us
    pallas_call x0 -> x2, Pallas kernels: none -> 20.3 us  [halo_exchange(): pl.pallas_call(functools.partial(_halo_kernel, (lax.axis_size('ax'), lax....]
    ppermute x8 -> x0, starting transfers between devices: 19.1 us -> none  [the longest x4 11 us: with_halo(): after = lax.ppermute(first, axis, down)]
    unnamed x18 -> x35, local copies, waits for them, and re-layouts: 0.45 us -> 11.9 us
    pallas_call x1, Pallas kernels: 28.9 us -> 20.3 us  [all_sum(): pl.pallas_call(_ar_kernel, out_shape=jax.ShapeDtypeStruct(part.shape, jnp...]
    mul x0 -> x3, local copies, waits for them, and re-layouts: none -> 6.12 us  [the longest x2 4.92 us: apply_operator(): return (stiffness + 4.5) * field - beside - 0.5 * swap_radial(field)]
    slice x4 -> x8, local copies, waits for them, and re-layouts: 3.13 us -> 9.25 us  [the longest x3 4.06 us: halo_exchange(): field[0]]
    select_n x0 -> x4, local copies, waits for them, and re-layouts: none -> 5.46 us  [the longest x2 2.73 us: halo_exchange(): before_row = jnp.where(ax == 0, 0.0, got[1, :comps, :width])]
    ppermute x8 -> x0, waiting for transfers between devices: 3.62 us -> none  [the longest x4 2.03 us: with_halo(): after = lax.ppermute(first, axis, down)]
  transfers between devices with their start and end apart: 8 -> 0, of which waited for: 2 -> 0; matrix products, arithmetic and copies ran while one was open for 11% -> 0% of each run, Pallas kernels for 0% -> 0%
where the time goes in v3:
time: 147 us; the launch traced here: 146 us
  Pallas kernels  68.5 us (47%)
  local copies, waits for them, and re-layouts  42.6 us (29%)
  other arithmetic  23.1 us (16%)
  matrix products  7.39 us (5%)
  between operations  4.24 us (3%)
    pallas_call x2, Pallas kernels, _exchange(): pl.pallas_call(functools.partial(body, n), out_shape=jax.ShapeDtypeStruct...  27.9 us
    pallas_call x1, Pallas kernels, all_sum(): pl.pallas_call(_ar_kernel, out_shape=jax.ShapeDtypeStruct(part.shape, jnp...  20.3 us
    pallas_call x2, Pallas kernels, halo_exchange(): pl.pallas_call(functools.partial(_halo_kernel, (lax.axis_size('ax'), lax....  20.3 us
    unnamed x35, local copies, waits for them, and re-layouts  11.9 us
    dot_general x1, matrix products, shards(): lax.dot_general(mixed.reshape(-1, around_cells), dft_table(around_cells),...  5.3 us
    mul x2, local copies, waits for them, and re-layouts, apply_operator(): return (stiffness + 4.5) * field - beside - 0.5 * swap_radial(field)  4.92 us
    select_n x2, other arithmetic, dft_table(): jnp.where(is_sin[None, None], sin_part, cos_part).reshape(length, length)  4.77 us
    mul x1, other arithmetic, shards(): residual = solid * (load - apply_operator(disp, stiffness, 3))  4.46 us

profile of v3, /device:TPU:4, one launch (start us, length us, event | category | flops | bytes accessed | tf_op | source)
XLA Modules:
  0.0 145.8 jit_solution(14099880901049468152)
XLA Ops:
  0.6 1.6 %copy.141 = f32[128,6,256]{0,1,2:T(8,128)S(1)} copy(f32[128,6,256]{2,0,1:T(8,128)} %param.10) | data formatting | bytes 1572864 | tf_op args[1]
  3.7 7.0 %shard_map.94 = f32[4,8,256]{2,1,0:T(8,128)} custom-call(f32[4,8,256]{2,1,0:T(8,128)} %pad_maximum_fusion.1.x_ref), custom_call_target="tpu_custom_call" | custom-call | tf_op jit(solution)/shard_map/pallas_call | solution.py:248
  11.4 1.4 copy.122
  12.8 1.4 copy.125
  14.9 1.6 %fusion.32 = (f32[127,6,256]{0,1,2:T(8,128)}, f32[127,6,256]{0,1,2:T(8,128)}) fusion(f32[128,6,256]{0,1,2:T(8,128)S(1)} %copy.141), kind=kLoop, calls=%fused_computation.93 | loop fusion | bytes 3121152 | tf_op jit(solution)/shard_map/slice | solution.py:261
  16.5 1.5 %fusion.31 = (f32[128,6,255]{0,1,2:T(8,128)}, f32[128,6,255]{0,1,2:T(8,128)}) fusion(f32[128,6,256]{0,1,2:T(8,128)S(1)} %copy.141), kind=kLoop, calls=%fused_computation.92 | loop fusion | bytes 3133440 | tf_op jit(solution)/shard_map/slice | solution.py:263
  18.4 1.6 %copy.114 = f32[128,6,256]{0,1,2:T(8,128)S(1)} copy(f32[128,6,256]{2,0,1:T(8,128)} %param.11) | data formatting | bytes 1572864 | tf_op args[2]
  21.1 2.5 %copy.128 = f32[128,6,256]{0,1,2:T(8,128)} copy(f32[128,6,256]{2,0,1:T(8,128)} %bitcast.105) | data formatting | bytes 1572864 | tf_op jit(solution)/shard_map/mul | solution.py:276
  23.5 2.4 %copy.129 = f32[128,6,256]{0,1,2:T(8,128)} copy(f32[128,6,256]{2,0,1:T(8,128)} %param.9) | data formatting | bytes 1572864 | tf_op args[0]
  26.0 4.5 %fusion.7 = f32[128,6,256]{0,1,2:T(8,128)S(1)} fusion(f32[128,6,256]{0,1,2:T(8,128)} %copy.129, f32[128,6,256]{0,1,2:T(8,128)} %copy.128, f32[127,6,256]{0,1,2:T(8,128)} %get-tuple-element.44, f32[1,6,256]{0,1,2:T(8,128)} %copy.122, f32[1,6,256]{0,1,2:T(8,128)} %copy.125, f32[127,6,256]{0,1,2:T(8,128)} %get-tuple-element.43, ...), kind=kLoop, calls=%fused_computation.15 | loop fusion | flops 2752512 | bytes 7212032 | tf_op jit(solution)/shard_map/mul | solution.py:292
  30.5 1.2 copy.131.x_ref
  31.7 13.4 %shard_map.95 = f32[6,32,1024]{2,1,0:T(8,128)} custom-call(f32[6,128,256]{2,1,0:T(8,128)} %copy.131.x_ref), custom_call_target="tpu_custom_call" | custom-call | tf_op jit(solution)/shard_map/pallas_call | solution.py:158
  46.3 3.9 %broadcast_select_fusion = (f32[32,32,1024]{2,1,0:T(8,128)}, f32[32,32,1024]{2,1,0:T(8,128)S(1)}, f32[32,32,1024]{2,1,0:T(8,128)S(1)}) fusion(pred[1024]{0:T(1024)(128)(4,1)S(1)} %iota_compare_fusion.2, f32[32,1024]{1,0:T(8,128)S(1)} %get-tuple-element.67, f32[32,1024]{1,0:T(8,128)S(1)} %get-tuple-element.61, f32[32,1024]{1,0:T(8,128)S(1)} %get-tuple-element.68, ...), kind=kLoop, calls=%fused_computation.6 | loop fusion | flops 7340032 | bytes 13108224 | tf_op jit(solution)/shard_map/jit(_where)/select_n | solution.py:194
  51.3 1.9 %fusion = f32[6,32,1024]{2,1,0:T(8,128)S(1)} fusion(f32[6,32,1024]{2,1,0:T(8,128)S(1)} %copy-done.10, f32[1024,1024]{1,0:T(8,128)S(1)} %bitcast_select_fusion), kind=kOutput, calls=%fused_computation.1 | convolution fusion | flops 1207959552 | bytes 5767168 | tf_op jit(solution)/shard_map/dot_general | solution.py:294
  54.4 5.3 %convolution_multiply_fusion = f32[192,1024]{1,0:T(8,128)} fusion(f32[192,1024]{1,0:T(8,128)S(1)} %bitcast.107, f32[1024,1024]{1,0:T(8,128)} %bitcast.101), kind=kOutput, calls=%fused_computation.7 | convolution fusion | flops 1208156160 | bytes 5767168 | tf_op jit(solution)/shard_map/dot_general | solution.py:298
  59.7 14.5 %shard_map.96 = f32[6,128,256]{2,1,0:T(8,128)} custom-call(f32[6,32,1024]{2,1,0:T(8,128)} %bitcast.108), custom_call_target="tpu_custom_call" | custom-call | tf_op jit(solution)/shard_map/pallas_call | solution.py:158
  74.2 1.6 %copy.132 = f32[6,128,256]{1,0,2:T(8,128)S(1)} copy(f32[6,128,256]{2,1,0:T(8,128)} %shard_map.96) | data formatting | bytes 1572864 | tf_op jit(solution)/shard_map/pallas_call | solution.py:158
  75.9 1.7 %fusion.30 = (f32[1,6,256]{0,1,2:T(8,128)}, f32[1,6,256]{0,1,2:T(8,128)}) fusion(f32[128,6,256]{0,1,2:T(8,128)S(1)} %multiply_bitcast_fusion), kind=kLoop, calls=%fused_computation.91 | loop fusion | bytes 24576 | tf_op jit(solution)/shard_map/slice | solution.py:246
  77.5 1.5 %copy.134 = f32[1,6,256]{2,1,0:T(8,128)S(1)} copy(f32[1,6,256]{0,1,2:T(8,128)} %get-tuple-element.38) | data formatting | bytes 12288 | tf_op jit(solution)/shard_map/slice | solution.py:246
  79.1 1.6 %copy.133 = f32[1,6,256]{2,1,0:T(8,128)S(1)} copy(f32[1,6,256]{0,1,2:T(8,128)} %get-tuple-element.37) | data formatting | bytes 12288 | tf_op jit(solution)/shard_map/slice | solution.py:246
  81.3 13.3 %shard_map.97 = f32[4,8,256]{2,1,0:T(8,128)} custom-call(f32[4,8,256]{2,1,0:T(8,128)} %pad_maximum_fusion.2.x_ref), custom_call_target="tpu_custom_call" | custom-call | tf_op jit(solution)/shard_map/pallas_call | solution.py:248
  95.3 1.4 copy.136
  96.7 1.4 copy.138
  99.9 2.1 %reverse_multiply_fusion = f32[128,3,2,256]{3,0,2,1:T(8,128)} fusion(f32[128,3,2,256]{3,0,2,1:T(8,128)} %bitcast.106), kind=kLoop, calls=%fused_computation.31 | loop fusion | flops 196608 | bytes 1572864 | tf_op jit(solution)/shard_map/mul | solution.py:276
  102.0 2.4 %copy.140 = f32[128,6,256]{0,1,2:T(8,128)} copy(f32[128,6,256]{2,0,1:T(8,128)} %bitcast.104) | data formatting | bytes 1572864 | tf_op jit(solution)/shard_map/mul | solution.py:276
  107.0 3.1 %multiply_reduce_fusion.1 = (f32[]{:T(128)}, f32[]{:T(128)}, f32[]{:T(128)}, f32[]{:T(128)}, f32[]{:T(128)}, /*index=5*/f32[128,6,256]{0,1,2:T(8,128)}) fusion(f32[128,6,256]{0,1,2:T(8,128)S(1)} %copy-done.2, f32[128,6,256]{0,1,2:T(8,128)S(1)} %copy-done.6, f32[128,6,1]{0,1,2:T(8,128)S(1)} %get-tuple-element.55, f32[128,6,255]{0,1,2:T(8,128)S(1)} %get-tuple-element.36, ...), kind=kLoop, calls=%fused_computation.24 | loop fusion | flops 4718587 | bytes 7212052 | tf_op jit(solution)/shard_map/reduce_sum | solution.py:316
  110.1 3.3 %stack.75 = f32[5]{0:T(128)S(1)} concatenate(f32[1]{0:T(128)} %bitcast.26, f32[1]{0:T(128)} %bitcast.45, f32[1]{0:T(128)} %bitcast.46, f32[1]{0:T(128)} %bitcast.47, f32[1]{0:T(128)} %bitcast.48), dimensions={0} | concatenate | bytes 40 | tf_op jit(solution)/shard_map/stack | solution.py:310
  114.0 20.3 %shard_map.98 = f32[8,128]{1,0:T(8,128)} custom-call(f32[8,128]{1,0:T(8,128)} %scatter.4.x_ref), custom_call_target="tpu_custom_call" | custom-call | tf_op jit(solution)/shard_map/pallas_call | solution.py:77
  134.3 1.5 %fusion.34 = (f32[1,1]{1,0:T(1,128)}, f32[1,1]{1,0:T(1,128)}, f32[1,1]{1,0:T(1,128)}, f32[1,1]{1,0:T(1,128)}, f32[1,1]{1,0:T(1,128)}) fusion(f32[8,128]{1,0:T(8,128)} %shard_map.98), kind=kLoop, calls=%fused_computation.95 | loop fusion | bytes 40 | tf_op jit(solution)/shard_map/slice | solution.py:325
  139.7 2.4 %multiply_subtract_fusion.1 = f32[128,6,256]{0,1,2:T(8,128)} fusion(f32[128,6,256]{0,1,2:T(8,128)S(1)} %copy-done.3, f32[128,6,256]{0,1,2:T(8,128)} %get-tuple-element.32, f32[]{:T(128)} %bitcast.50), kind=kLoop, calls=%fused_computation.22 | loop fusion | flops 393216 | bytes 2359300 | tf_op jit(solution)/shard_map/sub | solution.py:324
  142.1 2.4 %copy.143 = f32[128,6,256]{2,0,1:T(8,128)} copy(f32[128,6,256]{0,1,2:T(8,128)} %multiply_subtract_fusion.1) | data formatting | bytes 1572864
  144.6 1.2 copy.142
  (72 shorter events, 14.8 us)
Async XLA Ops:
  0.6 17.6 %copy-start = (f32[4,6]{1,0:T(4,128)S(1)}, f32[4,6]{1,0:T(4,128)}, u32[]{:S(2)}) copy-start(f32[4,6]{1,0:T(4,128)} %param.14) | copy-start | bytes 292
  14.9 3.2 %copy-start.12 = (s32[128,256]{1,0:T(8,128)S(1)}, s32[128,256]{1,0:T(8,128)}, u32[]{:S(2)}) copy-start(s32[128,256]{1,0:T(8,128)} %param.12) | copy-start | bytes 393220
  14.9 3.3 %copy-start.13 = (s32[128]{0:T(128)S(1)}, s32[128]{0:T(128)}, u32[]{:S(2)}) copy-start(s32[128]{0:T(128)} %param.13) | copy-start | bytes 1540
  16.5 3.5 %copy-start.9 = (f32[128,6,256]{2,0,1:T(8,128)S(1)}, f32[128,6,256]{2,0,1:T(8,128)}, u32[]{:S(2)}) copy-start(f32[128,6,256]{2,0,1:T(8,128)} %param.10) | copy-start | bytes 2359300
  20.0 10.4 %copy-start.4 = (f32[128,6,256]{0,1,2:T(8,128)}, f32[128,6,256]{0,1,2:T(8,128)S(1)}, u32[]{:S(2)}) copy-start(f32[128,6,256]{0,1,2:T(8,128)S(1)} %copy.114) | copy-start | bytes 2359300
  30.5 19.7 %copy-start.1 = (f32[128,6,256]{0,1,2:T(8,128)}, f32[128,6,256]{0,1,2:T(8,128)S(1)}, u32[]{:S(2)}) copy-start(f32[128,6,256]{0,1,2:T(8,128)S(1)} %fusion.7) | copy-start | bytes 2359300
  50.2 1.1 copy-start.10
  51.3 1.9 %copy-start.11 = (f32[6,6,1024]{2,1,0:T(8,128)S(1)}, f32[6,6,1024]{2,1,0:T(8,128)}, u32[]{:S(2)}) copy-start(f32[6,6,1024]{2,1,0:T(8,128)} %param.15) | copy-start | bytes 442372
  104.5 1.2 copy-start.2
  104.5 1.5 %copy-start.5 = (f32[128,6,256]{0,1,2:T(8,128)S(1)}, f32[128,6,256]{0,1,2:T(8,128)}, u32[]{:S(2)}) copy-start(f32[128,6,256]{0,1,2:T(8,128)} %copy-done.4) | copy-start | bytes 2359300
  104.5 1.9 %copy-start.6 = (f32[128,6,256]{0,1,2:T(8,128)S(1)}, f32[128,6,256]{0,1,2:T(8,128)}, u32[]{:S(2)}) copy-start(f32[128,6,256]{0,1,2:T(8,128)} %copy.140) | copy-start | bytes 2359300
  104.5 2.2 %copy-start.7 = (f32[1,6,256]{0,1,2:T(8,128)S(1)}, f32[1,6,256]{0,1,2:T(8,128)}, u32[]{:S(2)}) copy-start(f32[1,6,256]{0,1,2:T(8,128)} %copy.136) | copy-start | bytes 18436
  104.5 2.5 %copy-start.8 = (f32[1,6,256]{0,1,2:T(8,128)S(1)}, f32[1,6,256]{0,1,2:T(8,128)}, u32[]{:S(2)}) copy-start(f32[1,6,256]{0,1,2:T(8,128)} %copy.138) | copy-start | bytes 18436
  107.0 32.7 %copy-start.3 = (f32[128,6,256]{0,1,2:T(8,128)S(1)}, f32[128,6,256]{0,1,2:T(8,128)}, u32[]{:S(2)}) copy-start(f32[128,6,256]{0,1,2:T(8,128)} %copy-done.1) | copy-start | bytes 2359300

commit v4 on v2

--- a/solution.py
+++ b/solution.py
@@ -12,7 +12,7 @@
 MESH = pl.DeviceIdType.MESH
 
 
-def _lines():
+def _groups():
     me_ax = lax.axis_index("ax")
     me_sec = lax.axis_index("sec")
     x = me_ax % 4
@@ -20,35 +20,56 @@
     ylo = me_ax // 32
     core = me_sec % 2
     yhi = me_sec // 2
-    y = yhi * 2 + ylo
+
+    def plane_peer(c):
+        y = c % 4
+        return ((y % 2) * 32 + z * 4 + (c // 4) % 4, (y // 2) * 2 + c // 16)
+
     return [
-        (2, core, lambda c: (me_ax, yhi * 2 + c)),
-        (4, x, lambda c: (me_ax - x + c, me_sec)),
-        (4, y, lambda c: (me_ax - ylo * 32 + (c % 2) * 32, (c // 2) * 2 + core)),
+        (32, (core * 4 + x) * 4 + yhi * 2 + ylo, plane_peer),
         (8, z, lambda c: (me_ax - z * 4 + c * 4, me_sec)),
     ]
 
 
-def _ar_kernel(x_ref, o_ref, r0, r1, r2, r3, own, send_sems, recv_sems):
-    recvs = (r0, r1, r2, r3)
-    lines = _lines()
+def _local_sums(r_ref, p_ref, i_ref):
+    rows = r_ref.shape[0]
+    plane = r_ref.shape[1:]
+
+    def body(k, acc):
+        r, p, i = r_ref[k], p_ref[k], i_ref[k]
+        return (acc[0] + r * p, acc[1] + p * i, acc[2] + r * r, acc[3] + r * i, acc[4] + i * i)
+
+    zero = jnp.zeros(plane, jnp.float32)
+    acc = lax.fori_loop(0, rows, body, (zero,) * 5, unroll=8)
+    lane = lax.broadcasted_iota(jnp.int32, (8, 128), 1)
+    row = lax.broadcasted_iota(jnp.int32, (8, 128), 0)
+    packed = jnp.zeros((8, 128), jnp.float32)
+    for k, a in enumerate(acc):
+        packed = jnp.where((row == 0) & (lane == k), jnp.sum(a), packed)
+    return packed
+
+
+def _ar_kernel(r_ref, p_ref, i_ref, o_ref, recv_a, recv_b, own, send_sems, recv_sems):
+    recvs = (recv_a, recv_b)
+    groups = _groups()
     for r in recvs:
         r[...] = jnp.zeros_like(r)
     barrier = pltpu.get_barrier_semaphore()
     count = 0
-    for n, mine, dev in lines:
+    for n, mine, dev in groups:
         for d in range(1, n):
             pl.semaphore_signal(barrier, inc=1, device_id=dev((mine + d) % n), device_id_type=MESH)
             count += 1
+    own[0] = _local_sums(r_ref, p_ref, i_ref)
     pl.semaphore_wait(barrier, count)
-    src = x_ref
     base = 0
-    for r, (n, mine, dev) in enumerate(lines):
+    for g, (n, mine, dev) in enumerate(groups):
+        src = own.at[g]
         copies = []
         for d in range(1, n):
             cp = pltpu.make_async_remote_copy(
                 src_ref=src,
-                dst_ref=recvs[r].at[mine],
+                dst_ref=recvs[g].at[mine],
                 send_sem=send_sems.at[base + d],
                 recv_sem=recv_sems.at[base + d],
                 device_id=dev((mine + d) % n),
@@ -61,35 +82,32 @@
             cp.wait_recv()
         total = None
         for c in range(n):
-            v = jnp.where(mine == c, mine_val, recvs[r][c])
+            v = jnp.where(mine == c, mine_val, recvs[g][c])
             total = v if total is None else total + v
         for cp in copies:
             cp.wait_send()
         base += n
-        if r + 1 < len(lines):
-            own[r] = total
-            src = own.at[r]
+        if g + 1 < len(groups):
+            own[g + 1] = total
         else:
             o_ref[...] = total
 
 
-def all_sum(part, cid):
+def all_sums(residual, prec, image, cid):
     return pl.pallas_call(
         _ar_kernel,
-        out_shape=jax.ShapeDtypeStruct(part.shape, jnp.float32),
-        in_specs=[pl.BlockSpec(memory_space=pltpu.VMEM)],
+        out_shape=jax.ShapeDtypeStruct((8, 128), jnp.float32),
+        in_specs=[pl.BlockSpec(memory_space=pltpu.VMEM)] * 3,
         out_specs=pl.BlockSpec(memory_space=pltpu.VMEM),
         scratch_shapes=[
-            pltpu.VMEM((2,) + part.shape, jnp.float32),
-            pltpu.VMEM((4,) + part.shape, jnp.float32),
-            pltpu.VMEM((4,) + part.shape, jnp.float32),
-            pltpu.VMEM((8,) + part.shape, jnp.float32),
-            pltpu.VMEM((3,) + part.shape, jnp.float32),
-            pltpu.SemaphoreType.DMA((18,)),
-            pltpu.SemaphoreType.DMA((18,)),
+            pltpu.VMEM((32, 8, 128), jnp.float32),
+            pltpu.VMEM((8, 8, 128), jnp.float32),
+            pltpu.VMEM((2, 8, 128), jnp.float32),
+            pltpu.SemaphoreType.DMA((40,)),
+            pltpu.SemaphoreType.DMA((40,)),
         ],
         compiler_params=pltpu.CompilerParams(collective_id=cid, has_side_effects=True),
-    )(part)
+    )(residual, prec, image)
 
 
 def _to_lines_kernel(n, x_ref, o_ref, send_sems, recv_sems, local_sem):
@@ -262,17 +280,7 @@
     prec = solid * smoothed
     image = solid * apply_operator(prec, stiffness)
     cell_total = slab_count * lax.axis_size("ax") * comp_count * around_cells
-    parts = jnp.stack(
-        [
-            jnp.sum(residual * prec),
-            jnp.sum(prec * image),
-            jnp.sum(residual * residual),
-            jnp.sum(residual * image),
-            jnp.sum(image * image),
-        ]
-    )
-    packed = jnp.zeros((8, 128), jnp.float32).at[0, :5].set(parts)
-    totals = all_sum(packed, 0)[0]
+    totals = all_sums(residual, prec, image, 0)[0]
     inner_rz = totals[0] / cell_total
     inner_zq = totals[1] / cell_total
     alpha = inner_rz / inner_zq

time: 125 us -> 125 us (level)
  Pallas kernels: 57.2 us -> 54.1 us
  waiting for transfers between devices: 3.62 us -> 6.42 us
    unnamed x18 -> x23, local copies, waits for them, and re-layouts: 0.45 us -> 5.63 us
    another operation x2 -> x1, local copies, waits for them, and re-layouts: 3.24 us -> 0.01 us  [the longest x1 3.24 us: shards(): jnp.stack([jnp.sum(residual * prec), jnp.sum(prec * image), jnp.sum(resid...]
    pallas_call x1, Pallas kernels: 28.9 us -> 25.9 us  [all_sums(): pl.pallas_call(_ar_kernel, out_shape=jax.ShapeDtypeStruct((8, 128), jnp.f...]
    ppermute x4, waiting for transfers between devices: 2.03 us -> 4.82 us  [with_halo(): after = lax.ppermute(first, axis, down)]
    slice x4, local copies, waits for them, and re-layouts: 3.13 us -> 0.41 us  [with_halo(): first = lax.slice_in_dim(x, 0, width, axis=dim)]
    mul x0 -> x1, other arithmetic: none -> 2.55 us  [shards(): image = solid * apply_operator(prec, stiffness)]
    reduce_sum x1 -> x0, other arithmetic: 2.41 us -> none  [shards(): jnp.sum(image * image)]
    mul x1, other arithmetic: 2.65 us -> 4.02 us  [shards(): residual = solid * (load - apply_operator(disp, stiffness))]
  transfers between devices with their start and end apart: 8 -> 8, of which waited for: 2 -> 2; matrix products, arithmetic and copies ran while one was open for 11% -> 9% of each run, Pallas kernels for 0% -> 0%
where the time goes in v4:
time: 125 us
  Pallas kernels  54.1 us (43%)
  other arithmetic  23.5 us (19%)
  starting transfers between devices  19.3 us (15%)
  local copies, waits for them, and re-layouts  9.31 us (7%)
  matrix products  7.66 us (6%)
  waiting for transfers between devices  6.42 us (5%)
  between operations  4.27 us (3%)
    pallas_call x2, Pallas kernels, _exchange(): pl.pallas_call(functools.partial(body, n), out_shape=jax.ShapeDtypeStruct...  28.2 us
    pallas_call x1, Pallas kernels, all_sums(): pl.pallas_call(_ar_kernel, out_shape=jax.ShapeDtypeStruct((8, 128), jnp.f...  25.9 us
    ppermute x4, starting transfers between devices, with_halo(): after = lax.ppermute(first, axis, down)  11.1 us
    ppermute x4, starting transfers between devices, with_halo(): before = lax.ppermute(last, axis, up)  8.27 us
    select_n x2, other arithmetic, dft_table(): jnp.where(is_sin[None, None], sin_part, cos_part).reshape(length, length)  7.06 us
    unnamed x23, local copies, waits for them, and re-layouts  5.63 us
    ppermute x4, waiting for transfers between devices, with_halo(): after = lax.ppermute(first, axis, down)  4.82 us
    dot_general x1, matrix products, shards(): jnp.dot(lines.reshape(-1, around_cells), dft_table(around_cells), precisi...  4.21 us
  transfers between devices with their start and end apart: 8, of which 2 were waited for; matrix products, arithmetic and copies ran while one was open for 9% of the time, Pallas kernels for 0%

profile of v4, /device:TPU:4, one launch (start us, length us, event | category | flops | bytes accessed | tf_op | source)
XLA Modules:
  0.0 124.7 jit_solution(15984338764490864143)
XLA Ops:
  0.7 1.7 %copy.65 = f32[128,6,256]{2,1,0:T(8,128)S(1)} copy(f32[128,6,256]{2,0,1:T(8,128)} %param.8) | data formatting | bytes 1572864 | tf_op args[1]
  2.4 0.2 fusion.34
  2.6 2.7 %collective-permute-start.2 = (f32[128,6,1]{2,1,0:T(8,128)S(1)}, f32[128,6,1]{2,1,0:T(8,128)}, u32[]{:S(2)}, u32[]{:S(2)}) collective-permute-start(f32[128,6,1]{2,1,0:T(8,128)S(1)} %get-tuple-element.18), channel_id=1, source_target_pairs={{1,0},{2,1},{3,2},{0,3},{5,4},{6,5},{7,6},{4,7},{9,8},{10,9},{11,1... | collective-permute-start | bytes 9224 | tf_op jit(solution)/shard_map/ppermute | solution.py:233
  5.3 2.4 %collective-permute-start = (f32[1,6,256]{2,1,0:T(8,128)S(1)}, f32[1,6,256]{2,1,0:T(8,128)S(1)}, u32[]{:S(2)}, u32[]{:S(2)}) collective-permute-start(f32[1,6,256]{2,1,0:T(8,128)S(1)} %get-tuple-element.16), channel_id=1, source_target_pairs={{4,0},{8,4},{12,8},{16,12},{20,16},{24,20},{28,24},{32,28},{36,32}... | collective-permute-start | bytes 18440 | tf_op jit(solution)/shard_map/ppermute | solution.py:233
  7.7 3.6 %collective-permute-start.1 = (f32[1,6,256]{2,1,0:T(8,128)S(1)}, f32[1,6,256]{2,1,0:T(8,128)S(1)}, u32[]{:S(2)}, u32[]{:S(2)}) collective-permute-start(f32[1,6,256]{2,1,0:T(8,128)S(1)} %get-tuple-element.17), channel_id=1, source_target_pairs={{0,4},{4,8},{8,12},{12,16},{16,20},{20,24},{24,28},{28,32},{32,36}... | collective-permute-start | bytes 18440 | tf_op jit(solution)/shard_map/ppermute | solution.py:232
  11.3 0.9 subtract_convert_fusion
  12.3 1.0 reverse_multiply_fusion.1
  13.3 0.3 reverse
  14.1 1.1 fusion.29
  15.1 3.8 %broadcast_select_fusion = (f32[32,32,1024]{2,1,0:T(8,128)}, f32[32,32,1024]{2,1,0:T(8,128)S(1)}, f32[32,32,1024]{2,1,0:T(8,128)S(1)}) fusion(pred[1024]{0:T(1024)(128)(4,1)S(1)} %iota_compare_fusion.2, f32[32,1024]{1,0:T(8,128)S(1)} %get-tuple-element.30, f32[32,1024]{1,0:T(8,128)S(1)} %get-tuple-element.24, f32[32,1024]{1,0:T(8,128)S(1)} %get-tuple-element.31, ...), kind=kLoop, calls=%fused_computation.6 | loop fusion | flops 7340032 | bytes 13108224 | tf_op jit(solution)/shard_map/jit(_where)/select_n | solution.py:212
  18.9 3.3 %bitcast_select_fusion = f32[1024,1024]{1,0:T(8,128)} fusion(f32[32,32,1024]{2,1,0:T(8,128)S(1)} %get-tuple-element.21, f32[32,32,1024]{2,1,0:T(8,128)S(1)} %get-tuple-element.22, pred[1024]{0:T(1024)(128)(4,1)S(1)} %iota_compare_fusion.2), kind=kLoop, calls=%fused_computation.3 | loop fusion | flops 1048576 | bytes 12583936 | tf_op jit(solution)/shard_map/jit(_where)/select_n | solution.py:212
  22.7 4.0 %fusion.12.r_ref = f32[128,6,256]{2,1,0:T(8,128)S(1)} fusion(f32[128,6,256]{2,1,0:T(8,128)S(1)} %copy.65, f32[128,6,1]{2,1,0:T(8,128)} %collective-permute-done.3, f32[128,6,1]{2,1,0:T(8,128)} %collective-permute-done.2, f32[1,6,256]{2,1,0:T(8,128)S(1)} %collective-permute-done.1, f32[1,6,256]{2,1,0:T(8,128)S(1)} %collective-permute-done, ...), kind=kLoop, calls=%fused_computation.24 | loop fusion | flops 2752512 | bytes 4084736 | tf_op jit(solution)/shard_map/mul | solution.py:265
  26.7 1.2 copy.61.x_ref
  27.9 13.7 %shard_map.94 = f32[6,32,1024]{2,1,0:T(8,128)} custom-call(f32[6,128,256]{2,1,0:T(8,128)} %copy.61.x_ref), custom_call_target="tpu_custom_call" | custom-call | tf_op jit(solution)/shard_map/pallas_call | solution.py:176
  41.7 4.2 %fusion = f32[6,32,1024]{2,1,0:T(8,128)S(1)} fusion(f32[6,32,1024]{2,1,0:T(8,128)} %shard_map.94, f32[1024,1024]{1,0:T(8,128)} %bitcast_select_fusion), kind=kOutput, calls=%fused_computation.1 | convolution fusion | flops 1207959552 | bytes 5767168 | tf_op jit(solution)/shard_map/dot_general | solution.py:267
  45.9 0.3 multiply_reduce_fusion
  46.3 3.2 %convolution_multiply_fusion = f32[192,1024]{1,0:T(8,128)} fusion(f32[192,1024]{1,0:T(8,128)S(1)} %bitcast.36, f32[1024,1024]{1,0:T(8,128)S(1)} %bitcast.31), kind=kOutput, calls=%fused_computation.7 | convolution fusion | flops 1208156160 | bytes 5767168 | tf_op jit(solution)/shard_map/dot_general | solution.py:271
  49.5 14.5 %shard_map.95 = f32[6,128,256]{2,1,0:T(8,128)} custom-call(f32[6,32,1024]{2,1,0:T(8,128)} %bitcast.38), custom_call_target="tpu_custom_call" | custom-call | tf_op jit(solution)/shard_map/pallas_call | solution.py:176
  64.0 1.8 %fusion.15.p_ref = f32[128,6,256]{2,1,0:T(8,128)S(1)} fusion(f32[6,128,256]{2,1,0:T(8,128)} %shard_map.95, f32[128,256]{1,0:T(8,128)S(1)} %subtract_convert_fusion), kind=kLoop, calls=%fused_computation.31 | loop fusion | flops 196608 | bytes 1703936 | tf_op jit(solution)/shard_map/mul | solution.py:280
  66.1 0.3 copy.63
  66.3 3.5 %collective-permute-start.6 = (f32[128,6,1]{2,1,0:T(8,128)S(1)}, f32[128,6,1]{2,1,0:T(8,128)S(1)}, u32[]{:S(2)}, u32[]{:S(2)}) collective-permute-start(f32[128,6,1]{2,1,0:T(8,128)S(1)} %get-tuple-element.14), channel_id=1, source_target_pairs={{1,0},{2,1},{3,2},{0,3},{5,4},{6,5},{7,6},{4,7},{9,8},{10,9},{11,1... | collective-permute-start | bytes 9224 | tf_op jit(solution)/shard_map/ppermute | solution.py:233
  69.8 2.4 %collective-permute-start.4 = (f32[1,6,256]{2,1,0:T(8,128)S(1)}, f32[1,6,256]{2,1,0:T(8,128)S(1)}, u32[]{:S(2)}, u32[]{:S(2)}) collective-permute-start(f32[1,6,256]{2,1,0:T(8,128)S(1)} %get-tuple-element.12), channel_id=1, source_target_pairs={{4,0},{8,4},{12,8},{16,12},{20,16},{24,20},{28,24},{32,28},{36,32}... | collective-permute-start | bytes 18440 | tf_op jit(solution)/shard_map/ppermute | solution.py:233
  72.3 4.7 %collective-permute-start.5 = (f32[1,6,256]{2,1,0:T(8,128)S(1)}, f32[1,6,256]{2,1,0:T(8,128)S(1)}, u32[]{:S(2)}, u32[]{:S(2)}) collective-permute-start(f32[1,6,256]{2,1,0:T(8,128)S(1)} %get-tuple-element.13), channel_id=1, source_target_pairs={{0,4},{4,8},{8,12},{12,16},{16,20},{20,24},{24,28},{28,32},{32,36}... | collective-permute-start | bytes 18440 | tf_op jit(solution)/shard_map/ppermute | solution.py:232
  77.0 4.8 %collective-permute-done.6 = f32[128,6,1]{2,1,0:T(8,128)S(1)} collective-permute-done((f32[128,6,1]{2,1,0:T(8,128)S(1)}, f32[128,6,1]{2,1,0:T(8,128)S(1)}, u32[]{:S(2)}, u32[]{:S(2)}) %collective-permute-start.6) | collective-permute-done | bytes 3104 | tf_op jit(solution)/shard_map/ppermute | solution.py:233
  81.8 1.6 %collective-permute-done.7 = f32[128,6,1]{2,1,0:T(8,128)S(1)} collective-permute-done((f32[128,6,1]{2,1,0:T(8,128)S(1)}, f32[128,6,1]{2,1,0:T(8,128)S(1)}, u32[]{:S(2)}, u32[]{:S(2)}) %collective-permute-start.7) | collective-permute-done | bytes 3104 | tf_op jit(solution)/shard_map/ppermute | solution.py:232
  83.4 2.5 %fusion.5.i_ref = f32[128,6,256]{2,1,0:T(8,128)} fusion(f32[128,6,256]{2,1,0:T(8,128)S(1)} %fusion.15.p_ref, f32[128,6,1]{2,1,0:T(8,128)S(1)} %collective-permute-done.7, f32[128,6,1]{2,1,0:T(8,128)S(1)} %collective-permute-done.6, f32[1,6,256]{2,1,0:T(8,128)S(1)} %collective-permute-done.5, f32[1,6,256]{2,1,0:T(8,128)S(1)} %collective-permute-done.4, ...), kind=kLoop, calls=%fused_computation.13 | loop fusion | flops 2555904 | bytes 3298304 | tf_op jit(solution)/shard_map/mul | solution.py:281
  86.0 25.9 %shard_map.96 = f32[8,128]{1,0:T(8,128)} custom-call(f32[128,6,256]{2,1,0:T(8,128)} %copy-done.3, f32[128,6,256]{2,1,0:T(8,128)} %copy-done.1, f32[128,6,256]{2,1,0:T(8,128)} %fusion.5.i_ref), custom_call_target="tpu_custom_call" | custom-call | tf_op jit(solution)/shard_map/pallas_call | solution.py:97
  111.9 1.5 %fusion.35 = (f32[1,1]{1,0:T(1,128)}, f32[1,1]{1,0:T(1,128)}, f32[1,1]{1,0:T(1,128)}, f32[1,1]{1,0:T(1,128)}, f32[1,1]{1,0:T(1,128)}) fusion(f32[8,128]{1,0:T(8,128)} %shard_map.96), kind=kLoop, calls=%fused_computation.74 | loop fusion | bytes 40 | tf_op jit(solution)/shard_map/slice | solution.py:288
  114.8 3.9 %multiply_subtract_fusion.1 = (f32[128,6,256]{2,1,0:T(8,128)S(1)}, f32[128,6,256]{2,1,0:T(8,128)}) fusion(f32[128,6,256]{2,1,0:T(8,128)S(1)} %copy-done.4, f32[128,6,256]{2,1,0:T(8,128)} %fusion.5.i_ref, f32[]{:T(128)} %bitcast.12, f32[6,128,256]{2,1,0:T(8,128)} %shard_map.95, f32[128,256]{1,0:T(8,128)S(1)} %subtract_convert_fusion, ...), kind=kLoop, calls=%fused_computation.34 | loop fusion | flops 983040 | bytes 4849668 | tf_op jit(solution)/shard_map/sub | solution.py:287
  119.9 2.4 %copy.66 = f32[128,6,256]{2,0,1:T(8,128)} copy(f32[128,6,256]{2,1,0:T(8,128)} %get-tuple-element.33) | data formatting | bytes 1572864
  122.3 1.1 copy.67
  124.1 0.6 pad_maximum_fusion.9
  (44 shorter events, 1.2 us)
Async XLA Ops:
  0.6 21.6 %copy-start = (f32[4,6]{1,0:T(4,128)S(1)}, f32[4,6]{1,0:T(4,128)}, u32[]{:S(2)}) copy-start(f32[4,6]{1,0:T(4,128)} %param.12) | copy-start | bytes 292
  0.6 11.6 %copy-start.5 = (f32[128,6,256]{2,0,1:T(8,128)S(1)}, f32[128,6,256]{2,0,1:T(8,128)}, u32[]{:S(2)}) copy-start(f32[128,6,256]{2,0,1:T(8,128)} %param.8) | copy-start | bytes 2359300
  0.7 12.6 %copy-start.7 = (f32[6,6,1024]{2,1,0:T(8,128)S(1)}, f32[6,6,1024]{2,1,0:T(8,128)}, u32[]{:S(2)}) copy-start(f32[6,6,1024]{2,1,0:T(8,128)} %param.13) | copy-start | bytes 442372
  2.6 20.1 %collective-permute-start.2 = (f32[128,6,1]{2,1,0:T(8,128)S(1)}, f32[128,6,1]{2,1,0:T(8,128)}, u32[]{:S(2)}, u32[]{:S(2)}) collective-permute-start(f32[128,6,1]{2,1,0:T(8,128)S(1)} %get-tuple-element.18), channel_id=1, source_target_pairs={{1,0},{2,1},{3,2},{0,3},{5,4},{6,5},{7,6},{4,7},{9,8},{10,9},{11,1... | collective-permute-start | bytes 9224 | tf_op jit(solution)/shard_map/ppermute | solution.py:233
  5.3 17.4 %collective-permute-start.3 = (f32[128,6,1]{2,1,0:T(8,128)S(1)}, f32[128,6,1]{2,1,0:T(8,128)}, u32[]{:S(2)}, u32[]{:S(2)}) collective-permute-start(f32[128,6,1]{2,1,0:T(8,128)S(1)} %get-tuple-element.19), channel_id=1, source_target_pairs={{0,1},{1,2},{2,3},{3,0},{4,5},{5,6},{6,7},{7,4},{8,9},{9,10},{10,1... | collective-permute-start | bytes 9224 | tf_op jit(solution)/shard_map/ppermute | solution.py:232
  5.3 17.4 %collective-permute-start = (f32[1,6,256]{2,1,0:T(8,128)S(1)}, f32[1,6,256]{2,1,0:T(8,128)S(1)}, u32[]{:S(2)}, u32[]{:S(2)}) collective-permute-start(f32[1,6,256]{2,1,0:T(8,128)S(1)} %get-tuple-element.16), channel_id=1, source_target_pairs={{4,0},{8,4},{12,8},{16,12},{20,16},{24,20},{28,24},{32,28},{36,32}... | collective-permute-start | bytes 18440 | tf_op jit(solution)/shard_map/ppermute | solution.py:233
  7.7 15.0 %collective-permute-start.1 = (f32[1,6,256]{2,1,0:T(8,128)S(1)}, f32[1,6,256]{2,1,0:T(8,128)S(1)}, u32[]{:S(2)}, u32[]{:S(2)}) collective-permute-start(f32[1,6,256]{2,1,0:T(8,128)S(1)} %get-tuple-element.17), channel_id=1, source_target_pairs={{0,4},{4,8},{8,12},{12,16},{16,20},{20,24},{24,28},{28,32},{32,36}... | collective-permute-start | bytes 18440 | tf_op jit(solution)/shard_map/ppermute | solution.py:232
  18.9 3.3 %copy-start.8 = (s32[128]{0:T(128)S(1)}, s32[128]{0:T(128)}, u32[]{:S(2)}) copy-start(s32[128]{0:T(128)} %param.11) | copy-start | bytes 1540
  26.7 19.2 %copy-start.3 = (f32[128,6,256]{2,1,0:T(8,128)}, f32[128,6,256]{2,1,0:T(8,128)S(1)}, u32[]{:S(2)}) copy-start(f32[128,6,256]{2,1,0:T(8,128)S(1)} %fusion.12.r_ref) | copy-start | bytes 2359300
  41.7 4.6 %copy-start.2 = (f32[32,32,1024]{2,1,0:T(8,128)S(1)}, f32[32,32,1024]{2,1,0:T(8,128)}, u32[]{:S(2)}) copy-start(f32[32,32,1024]{2,1,0:T(8,128)} %get-tuple-element.20) | copy-start | bytes 12582916
  64.0 19.4 %copy-start.6 = (f32[128,6,256]{2,0,1:T(8,128)S(1)}, f32[128,6,256]{2,0,1:T(8,128)}, u32[]{:S(2)}) copy-start(f32[128,6,256]{2,0,1:T(8,128)} %param.9) | copy-start | bytes 2359300
  65.8 20.2 %copy-start.1 = (f32[128,6,256]{2,1,0:T(8,128)}, f32[128,6,256]{2,1,0:T(8,128)S(1)}, u32[]{:S(2)}) copy-start(f32[128,6,256]{2,1,0:T(8,128)S(1)} %fusion.15.p_ref) | copy-start | bytes 2359300
  66.3 15.5 %collective-permute-start.6 = (f32[128,6,1]{2,1,0:T(8,128)S(1)}, f32[128,6,1]{2,1,0:T(8,128)S(1)}, u32[]{:S(2)}, u32[]{:S(2)}) collective-permute-start(f32[128,6,1]{2,1,0:T(8,128)S(1)} %get-tuple-element.14), channel_id=1, source_target_pairs={{1,0},{2,1},{3,2},{0,3},{5,4},{6,5},{7,6},{4,7},{9,8},{10,9},{11,1... | collective-permute-start | bytes 9224 | tf_op jit(solution)/shard_map/ppermute | solution.py:233
  69.8 13.6 %collective-permute-start.7 = (f32[128,6,1]{2,1,0:T(8,128)S(1)}, f32[128,6,1]{2,1,0:T(8,128)S(1)}, u32[]{:S(2)}, u32[]{:S(2)}) collective-permute-start(f32[128,6,1]{2,1,0:T(8,128)S(1)} %get-tuple-element.15), channel_id=1, source_target_pairs={{0,1},{1,2},{2,3},{3,0},{4,5},{5,6},{6,7},{7,4},{8,9},{9,10},{10,1... | collective-permute-start | bytes 9224 | tf_op jit(solution)/shard_map/ppermute | solution.py:232
  69.8 13.6 %collective-permute-start.4 = (f32[1,6,256]{2,1,0:T(8,128)S(1)}, f32[1,6,256]{2,1,0:T(8,128)S(1)}, u32[]{:S(2)}, u32[]{:S(2)}) collective-permute-start(f32[1,6,256]{2,1,0:T(8,128)S(1)} %get-tuple-element.12), channel_id=1, source_target_pairs={{4,0},{8,4},{12,8},{16,12},{20,16},{24,20},{28,24},{32,28},{36,32}... | collective-permute-start | bytes 18440 | tf_op jit(solution)/shard_map/ppermute | solution.py:233
  72.3 11.2 %collective-permute-start.5 = (f32[1,6,256]{2,1,0:T(8,128)S(1)}, f32[1,6,256]{2,1,0:T(8,128)S(1)}, u32[]{:S(2)}, u32[]{:S(2)}) collective-permute-start(f32[1,6,256]{2,1,0:T(8,128)S(1)} %get-tuple-element.13), channel_id=1, source_target_pairs={{0,4},{4,8},{8,12},{12,16},{16,20},{20,24},{24,28},{28,32},{32,36}... | collective-permute-start | bytes 18440 | tf_op jit(solution)/shard_map/ppermute | solution.py:232
  77.0 37.7 %copy-start.4 = (f32[128,6,256]{2,1,0:T(8,128)S(1)}, f32[128,6,256]{2,1,0:T(8,128)}, u32[]{:S(2)}) copy-start(f32[128,6,256]{2,1,0:T(8,128)} %copy-done.3) | copy-start | bytes 2359300

commit v5 on v4

--- a/solution.py
+++ b/solution.py
@@ -141,35 +141,118 @@
         cp.wait()
 
 
-def _from_lines_kernel(n, x_ref, o_ref, send_sems, recv_sems, local_sem):
+def _from_lines_kernel(sizes, x_ref, cpk_ref, last_ref, first_ref, o_ref, cols_ref, before_ref,
+                       after_ref, send_sems, recv_sems, local_sems):
+    n_ax, n = sizes
     me = lax.axis_index("sec")
     ax = lax.axis_index("ax")
     rows, width = x_ref.shape[1], o_ref.shape[2]
+    up_ax, down_ax = (ax + 1) % n_ax, (ax + n_ax - 1) % n_ax
+    peers = [(ax, (me + d) % n) for d in range(1, n)]
+    peers += [(up_ax, s) for s in range(n)] + [(down_ax, s) for s in range(n)]
     barrier = pltpu.get_barrier_semaphore()
-    for d in range(1, n):
-        pl.semaphore_signal(barrier, inc=1, device_id=(ax, (me + d) % n), device_id_type=MESH)
-    pl.semaphore_wait(barrier, n - 1)
+    for peer in peers:
+        pl.semaphore_signal(barrier, inc=1, device_id=peer, device_id_type=MESH)
+    pl.semaphore_wait(barrier, len(peers))
     dst = o_ref.at[:, pl.ds(pl.multiple_of(me * rows, rows), rows), :]
-    copies = []
+    sends, recvs = [], []
     for d in range(1, n):
         peer = (me + d) % n
-        cp = pltpu.make_async_remote_copy(
-            src_ref=x_ref.at[:, :, pl.ds(pl.multiple_of(peer * width, width), width)],
-            dst_ref=dst,
-            send_sem=send_sems.at[d],
-            recv_sem=recv_sems.at[d],
-            device_id=(ax, peer),
-            device_id_type=MESH,
-        )
+        for k, (src, out) in enumerate(
+            (
+                (x_ref.at[:, :, pl.ds(pl.multiple_of(peer * width, width), width)], dst),
+                (cpk_ref.at[peer], cols_ref.at[me]),
+            )
+        ):
+            cp = pltpu.make_async_remote_copy(
+                src_ref=src,
+                dst_ref=out,
+                send_sem=send_sems.at[k * n + d],
+                recv_sem=recv_sems.at[k * n + d],
+                device_id=(ax, peer),
+                device_id_type=MESH,
+            )
+            cp.start()
+            sends.append(cp)
+        origin = (me + n - d) % n
+        for k, (src, out) in enumerate(
+            (
+                (x_ref.at[:, :, pl.ds(0, width)], o_ref.at[:, pl.ds(pl.multiple_of(origin * rows, rows), rows), :]),
+                (cpk_ref.at[0], cols_ref.at[origin]),
+            )
+        ):
+            recvs.append(
+                pltpu.make_async_remote_copy(
+                    src_ref=src,
+                    dst_ref=out,
+                    send_sem=send_sems.at[k * n + d],
+                    recv_sem=recv_sems.at[k * n + d],
+                    device_id=(ax, origin),
+                    device_id_type=MESH,
+                )
+            )
+    for s in range(n):
+        for k, (src, out, target) in enumerate(
+            ((last_ref.at[s], before_ref.at[me], up_ax), (first_ref.at[s], after_ref.at[me], down_ax))
+        ):
+            base = (2 + k) * n
+            cp = pltpu.make_async_remote_copy(
+                src_ref=src,
+                dst_ref=out,
+                send_sem=send_sems.at[base + s],
+                recv_sem=recv_sems.at[base + me],
+                device_id=(target, s),
+                device_id_type=MESH,
+            )
+            cp.start()
+            sends.append(cp)
+            recvs.append(
+                pltpu.make_async_remote_copy(
+                    src_ref=src,
+                    dst_ref=(before_ref, after_ref)[k].at[s],
+                    send_sem=send_sems.at[base + s],
+                    recv_sem=recv_sems.at[base + s],
+                    device_id=(target, s),
+                    device_id_type=MESH,
+                )
+            )
+    local = [
+        pltpu.make_async_copy(
+            x_ref.at[:, :, pl.ds(pl.multiple_of(me * width, width), width)], dst, local_sems.at[0]
+        ),
+        pltpu.make_async_copy(cpk_ref.at[me], cols_ref.at[me], local_sems.at[1]),
+    ]
+    for cp in local:
         cp.start()
-        copies.append(cp)
-    local = pltpu.make_async_copy(
-        x_ref.at[:, :, pl.ds(pl.multiple_of(me * width, width), width)], dst, local_sem
-    )
-    local.start()
-    local.wait()
-    for cp in copies:
+    for cp in local:
         cp.wait()
+    for cp in recvs:
+        cp.wait_recv()
+    for cp in sends:
+        cp.wait_send()
+
+
+def from_lines_with_halo(x, cpk, last, first, n):
+    comps, rows, around = x.shape
+    n_ax = lax.axis_size("ax")
+    shapes = [
+        (comps, rows * n, around // n),
+        cpk.shape,
+        (n,) + last.shape[1:],
+        (n,) + first.shape[1:],
+    ]
+    return pl.pallas_call(
+        functools.partial(_from_lines_kernel, (n_ax, n)),
+        out_shape=[jax.ShapeDtypeStruct(s, x.dtype) for s in shapes],
+        in_specs=[pl.BlockSpec(memory_space=pltpu.VMEM)] * 4,
+        out_specs=[pl.BlockSpec(memory_space=pltpu.VMEM)] * 4,
+        scratch_shapes=[
+            pltpu.SemaphoreType.DMA((4 * n,)),
+            pltpu.SemaphoreType.DMA((4 * n,)),
+            pltpu.SemaphoreType.DMA((2,)),
+        ],
+        compiler_params=pltpu.CompilerParams(collective_id=2, has_side_effects=True),
+    )(x, cpk, last, first)
 
 
 def _exchange(body, out_shape, cid, n, x):
@@ -192,11 +275,6 @@
     return _exchange(_to_lines_kernel, (comps, rows // n, width * n), 1, n, x)
 
 
-def from_lines(x, n):
-    comps, rows, around = x.shape
-    return _exchange(_from_lines_kernel, (comps, rows * n, around // n), 2, n, x)
-
-
 def dft_table(length):
     half = length // 2
     root = int(round(math.sqrt(length)))
@@ -233,6 +311,20 @@
         after = lax.ppermute(first, axis, down)
         x = jnp.concatenate([before, x, after], axis=dim)
     return x
+
+
+def stencil_from_halo(field, before_row, after_row, before_col, after_col):
+    down = jnp.concatenate([field[:, 1:], after_row[:, None]], axis=1)
+    up = jnp.concatenate([before_row[:, None], field[:, :-1]], axis=1)
+    right = jnp.concatenate([field[:, :, 1:], after_col[:, :, None]], axis=2)
+    left = jnp.concatenate([before_col[:, :, None], field[:, :, :-1]], axis=2)
+    return down + up + right + left
+
+
+def swap_channels(field):
+    extent = field.shape
+    folded = field.reshape((extent[0] // 2, 2) + extent[1:])
+    return jnp.flip(folded, axis=1).reshape(extent)
 
 
 def swap_radial(field):
@@ -263,7 +355,10 @@
     stiffness = stiff * (factors * taper[:, None])[:, :, None]
     solid = (1 - hole).astype(jnp.float32)[:, None, :]
     residual = solid * (load - apply_operator(disp, stiffness))
-    lines = to_lines(jnp.transpose(residual, (1, 0, 2)), sector_count)
+    residual_t = jnp.transpose(residual, (1, 0, 2))
+    solid_t = jnp.transpose(solid, (1, 0, 2))
+    lines_all = to_lines(jnp.concatenate([residual_t, solid_t], axis=0), sector_count)
+    lines = lines_all[:comp_count]
     spectrum = jnp.dot(
         lines.reshape(-1, around_cells), dft_table(around_cells), precision=lax.Precision.HIGH
     ).reshape(lines.shape)
@@ -274,19 +369,43 @@
         (((1,), (1,)), ((), ())),
         precision=lax.Precision.HIGH,
     ) / around_cells
-    smoothed = jnp.transpose(
-        from_lines(smoothed_lines.reshape(lines.shape), sector_count), (1, 0, 2)
+    prec_lines = lines_all[comp_count:] * smoothed_lines.reshape(lines.shape)
+    group_rows = lines.shape[1]
+    lanes = -(-2 * group_rows // 128) * 128
+    subl = -(-comp_count // 8) * 8
+    edge_b = [(p * sector_width - 1) % around_cells for p in range(sector_count)]
+    edge_a = [((p + 1) * sector_width) % around_cells for p in range(sector_count)]
+    cols = jnp.concatenate([prec_lines[:, :, edge_b], prec_lines[:, :, edge_a]], axis=1)
+    cpk = jnp.pad(
+        jnp.transpose(cols.reshape(comp_count, 2 * group_rows, sector_count), (2, 0, 1)),
+        ((0, 0), (0, subl - comp_count), (0, lanes - 2 * group_rows)),
     )
-    prec = solid * smoothed
-    image = solid * apply_operator(prec, stiffness)
+
+    def row_pack(row):
+        split = jnp.transpose(row.reshape(comp_count, sector_count, sector_width), (1, 0, 2))
+        return jnp.pad(split, ((0, 0), (0, subl - comp_count), (0, 0)))
+
+    prec_t, halo_cols, before_rows, after_rows = from_lines_with_halo(
+        prec_lines, cpk, row_pack(prec_lines[:, -1]), row_pack(prec_lines[:, 0]), sector_count
+    )
+    ax = lax.axis_index("ax")
+    before_row = jnp.where(ax == 0, 0.0, before_rows[sector_count - 1, :comp_count])
+    after_row = jnp.where(ax == lax.axis_size("ax") - 1, 0.0, after_rows[0, :comp_count])
+    got_cols = jnp.transpose(halo_cols[:, :comp_count, : 2 * group_rows], (1, 0, 2))
+    got_cols = got_cols.reshape(comp_count, sector_count, 2, group_rows)
+    before_col = got_cols[:, :, 0].reshape(comp_count, slab_count)
+    after_col = got_cols[:, :, 1].reshape(comp_count, slab_count)
+    beside = stencil_from_halo(prec_t, before_row, after_row, before_col, after_col)
+    stiffness_t = jnp.transpose(stiffness, (1, 0, 2))
+    image_t = solid_t * ((stiffness_t + 4.5) * prec_t - beside - 0.5 * swap_channels(prec_t))
     cell_total = slab_count * lax.axis_size("ax") * comp_count * around_cells
-    totals = all_sums(residual, prec, image, 0)[0]
+    totals = all_sums(residual_t, prec_t, image_t, 0)[0]
     inner_rz = totals[0] / cell_total
     inner_zq = totals[1] / cell_total
     alpha = inner_rz / inner_zq
-    residual_new = residual - alpha * image
+    residual_new = residual - alpha * jnp.transpose(image_t, (1, 0, 2))
     square_new = (totals[2] - alpha * (2.0 * totals[3] - alpha * totals[4])) / cell_total
-    disp_new = disp + alpha * prec
+    disp_new = disp + alpha * jnp.transpose(prec_t, (1, 0, 2))
     return (disp_new, residual_new, jnp.stack([inner_rz, inner_zq, square_new]))
 
 

time: 125 us -> 127 us (1.016)
  local copies, waits for them, and re-layouts: 9.31 us -> 23.9 us
  starting transfers between devices: 19.3 us -> 8.48 us
  waiting for transfers between devices: 6.42 us -> 0.01 us
  Pallas kernels: 54.1 us -> 58.1 us
  other arithmetic: 23.5 us -> 25 us
    pallas_call x0 -> x1, Pallas kernels: none -> 18 us  [from_lines_with_halo(): pl.pallas_call(functools.partial(_from_lines_kernel, (n_ax, n)), out_shap...]
    pallas_call x2 -> x1, Pallas kernels: 28.2 us -> 15.2 us  [_exchange(): pl.pallas_call(functools.partial(body, n), out_shape=jax.ShapeDtypeStruct...]
    ppermute x4 -> x2, starting transfers between devices: 11.1 us -> 5.08 us  [with_halo(): after = lax.ppermute(first, axis, down)]
    gather x0 -> x2, local copies, waits for them, and re-layouts: none -> 5.47 us  [the longest x1 2.74 us: shards(): prec_lines[:, :, edge_b]]
    ppermute x4 -> x2, starting transfers between devices: 8.27 us -> 3.4 us  [with_halo(): before = lax.ppermute(last, axis, up)]
    ppermute x4 -> x2, waiting for transfers between devices: 4.82 us -> 0.01 us  [with_halo(): after = lax.ppermute(first, axis, down)]
    unnamed x23 -> x40, local copies, waits for them, and re-layouts: 5.63 us -> 1.33 us
    slice x0 -> x4, local copies, waits for them, and re-layouts: none -> 4.27 us  [the longest x1 2.82 us: stencil_from_halo(): left = jnp.concatenate([before_col[:, :, None], field[:, :, :-1]], axis=2)]
  transfers between devices with their start and end apart: 8 -> 4, of which waited for: 2 -> 0; matrix products, arithmetic and copies ran while one was open for 9% -> 11% of each run, Pallas kernels for 0% -> 0%
where the time goes in v5:
time: 127 us
  Pallas kernels  58.1 us (46%)
  other arithmetic  25 us (20%)
  local copies, waits for them, and re-layouts  23.9 us (19%)
  starting transfers between devices  8.48 us (7%)
  matrix products  6.85 us (5%)
  between operations  4.32 us (3%)
    pallas_call x1, Pallas kernels, all_sums(): pl.pallas_call(_ar_kernel, out_shape=jax.ShapeDtypeStruct((8, 128), jnp.f...  24.8 us
    pallas_call x1, Pallas kernels, from_lines_with_halo(): pl.pallas_call(functools.partial(_from_lines_kernel, (n_ax, n)), out_shap...  18 us
    pallas_call x1, Pallas kernels, _exchange(): pl.pallas_call(functools.partial(body, n), out_shape=jax.ShapeDtypeStruct...  15.2 us
    select_n x2, other arithmetic, dft_table(): jnp.where(is_sin[None, None], sin_part, cos_part).reshape(length, length)  7.17 us
    ppermute x2, starting transfers between devices, with_halo(): after = lax.ppermute(first, axis, down)  5.08 us
    dot_general x1, matrix products, shards(): jnp.dot(lines.reshape(-1, around_cells), dft_table(around_cells), precisi...  4.31 us
    mul x1, other arithmetic, shards(): solid_t * ((stiffness_t + 4.5) * prec_t - beside - 0.5 * swap_channels(pr...  4.12 us
    mul x2, local copies, waits for them, and re-layouts, shards(): prec_lines = lines_all[comp_count:] * smoothed_lines.reshape(lines.shape)  3.77 us
  transfers between devices with their start and end apart: 4, of which 0 were waited for; matrix products, arithmetic and copies ran while one was open for 11% of the time, Pallas kernels for 0%

profile of v5, /device:TPU:4, one launch (start us, length us, event | category | flops | bytes accessed | tf_op | source)
XLA Modules:
  0.0 126.7 jit_solution(9707130584099597570)
XLA Ops:
  0.7 2.1 %fusion.34 = (f32[128,6,1]{2,0,1:T(8,128)}, f32[128,6,1]{2,0,1:T(8,128)}) fusion(f32[128,6,256]{2,0,1:T(8,128)} %param.10), kind=kLoop, calls=%fused_computation.85 | loop fusion | bytes 12288 | tf_op jit(solution)/shard_map/slice | solution.py:309
  2.8 2.6 %collective-permute-start.2 = (f32[128,6,1]{2,0,1:T(8,128)}, f32[128,6,1]{2,0,1:T(8,128)S(1)}, u32[]{:S(2)}, u32[]{:S(2)}) collective-permute-start(f32[128,6,1]{2,0,1:T(8,128)} %get-tuple-element.21), channel_id=1, source_target_pairs={{1,0},{2,1},{3,2},{0,3},{5,4},{6,5},{7,6},{4,7},{9,8},{10,9},{11,1... | collective-permute-start | bytes 9224 | tf_op jit(solution)/shard_map/ppermute | solution.py:311
  5.5 0.8 fusion.33
  6.3 2.4 %collective-permute-start = (f32[1,6,256]{2,0,1:T(1,128)S(1)}, f32[1,6,256]{2,0,1:T(1,128)S(1)}, u32[]{:S(2)}, u32[]{:S(2)}) collective-permute-start(f32[1,6,256]{2,0,1:T(1,128)S(1)} %get-tuple-element.19), channel_id=1, source_target_pairs={{4,0},{8,4},{12,8},{16,12},{20,16},{24,20},{28,24},{32,28},{36,32}... | collective-permute-start | bytes 18440 | tf_op jit(solution)/shard_map/ppermute | solution.py:311
  8.7 3.4 %collective-permute-start.1 = (f32[1,6,256]{2,0,1:T(1,128)S(1)}, f32[1,6,256]{2,0,1:T(1,128)S(1)}, u32[]{:S(2)}, u32[]{:S(2)}) collective-permute-start(f32[1,6,256]{2,0,1:T(1,128)S(1)} %get-tuple-element.20), channel_id=1, source_target_pairs={{0,4},{4,8},{8,12},{12,16},{16,20},{20,24},{24,28},{28,32},{32,36}... | collective-permute-start | bytes 18440 | tf_op jit(solution)/shard_map/ppermute | solution.py:310
  12.2 1.6 %subtract_convert_fusion = (f32[128,256]{1,0:T(8,128)S(1)}, f32[1,128,256]{2,1,0:T(8,128)}) fusion(s32[128,256]{1,0:T(8,128)} %param.12), kind=kLoop, calls=%fused_computation.54 | loop fusion | flops 65536 | bytes 393216 | tf_op jit(solution)/shard_map/convert_element_type | solution.py:356
  13.8 1.2 reverse_multiply_fusion.1
  15.0 1.0 slice.112
  16.9 1.1 fusion.26
  17.9 3.9 %broadcast_select_fusion = (f32[32,32,1024]{2,1,0:T(8,128)}, f32[32,32,1024]{2,1,0:T(8,128)S(1)}, f32[32,32,1024]{2,1,0:T(8,128)S(1)}) fusion(pred[1024]{0:T(1024)(128)(4,1)S(1)} %iota_compare_fusion.2, f32[32,1024]{1,0:T(8,128)S(1)} %get-tuple-element.35, f32[32,1024]{1,0:T(8,128)S(1)} %get-tuple-element.29, f32[32,1024]{1,0:T(8,128)S(1)} %get-tuple-element.36, ...), kind=kLoop, calls=%fused_computation.8 | loop fusion | flops 7340032 | bytes 13108224 | tf_op jit(solution)/shard_map/jit(_where)/select_n | solution.py:290
  21.8 3.3 %bitcast_select_fusion = f32[1024,1024]{1,0:T(8,128)} fusion(f32[32,32,1024]{2,1,0:T(8,128)S(1)} %get-tuple-element.24, f32[32,32,1024]{2,1,0:T(8,128)S(1)} %get-tuple-element.25, pred[1024]{0:T(1024)(128)(4,1)S(1)} %iota_compare_fusion.2), kind=kLoop, calls=%fused_computation.5 | loop fusion | flops 1048576 | bytes 12583936 | tf_op jit(solution)/shard_map/jit(_where)/select_n | solution.py:290
  25.4 0.7 copy-done.10
  26.3 2.1 %fusion.6 = f32[128,6,256]{2,0,1:T(8,128)S(1)} fusion(f32[128,6,256]{2,0,1:T(8,128)} %param.9, f32[128,6,256]{2,0,1:T(8,128)S(1)} %copy-done.4, f32[128,6,1]{2,0,1:T(8,128)} %copy-done.11, f32[128,6,1]{2,0,1:T(8,128)} %copy-done.10, f32[1,6,256]{2,0,1:T(1,128)S(1)} %collective-permute-done.1, f32[1,6,256]{2,0,1:T(1,128)S(1)} %collective-permute-done, ...), kind=kLoop, calls=%fused_computation.17 | loop fusion | flops 2752512 | bytes 4084736 | tf_op jit(solution)/shard_map/mul | solution.py:357
  28.4 2.2 %pad_maximum_fusion.x_ref = f32[7,128,256]{2,1,0:T(8,128)} fusion(f32[1,128,256]{2,1,0:T(8,128)} %get-tuple-element.27, f32[6,128,256]{2,1,0:T(8,128)S(1)} %bitcast.60), kind=kLoop, calls=%fused_computation.11 | loop fusion | flops 229376 | bytes 1835008 | tf_op jit(solution)/shard_map/concatenate | solution.py:360
  30.6 15.2 %shard_map.112 = f32[7,32,1024]{2,1,0:T(8,128)} custom-call(f32[7,128,256]{2,1,0:T(8,128)} %pad_maximum_fusion.x_ref), custom_call_target="tpu_custom_call" | custom-call | tf_op jit(solution)/shard_map/pallas_call | solution.py:259
  45.8 1.1 slice_bitcast_fusion
  46.9 4.3 %fusion = f32[6,32,1024]{2,1,0:T(8,128)S(1)} fusion(f32[7,32,1024]{2,1,0:T(8,128)} %shard_map.112, f32[1024,1024]{1,0:T(8,128)} %bitcast_select_fusion), kind=kOutput, calls=%fused_computation.3 | convolution fusion | flops 1207959552 | bytes 5898240 | tf_op jit(solution)/shard_map/dot_general | solution.py:362
  51.6 2.4 %convolution_multiply_fusion = f32[192,1024]{1,0:T(8,128)S(1)} fusion(f32[192,1024]{1,0:T(8,128)S(1)} %bitcast.62, f32[1024,1024]{1,0:T(8,128)S(1)} %bitcast.58), kind=kOutput, calls=%fused_computation.9 | convolution fusion | flops 1208156160 | bytes 5767168 | tf_op jit(solution)/shard_map/dot_general | solution.py:366
  54.0 2.7 %copy.25 = f32[6,32,1024]{1,0,2:T(8,128)} copy(f32[6,32,1024]{2,1,0:T(8,128)S(1)} %broadcast_multiply_fusion.x_ref) | data formatting | bytes 1572864 | tf_op jit(solution)/shard_map/mul | solution.py:372
  56.9 2.7 %gather_fusion = f32[4,6,32]{2,1,0:T(8,128)S(1)} fusion(f32[6,32,1024]{1,0,2:T(8,128)} %copy.25, s32[1024]{0:T(1024)S(1)} %pad_clamp_fusion.1), kind=kCustom, calls=%fused_computation | custom fusion | bytes 6160 | tf_op jit(solution)/shard_map/gather | solution.py:378
  59.6 2.7 %gather_fusion.1 = f32[4,6,32]{2,1,0:T(8,128)S(1)} fusion(f32[6,32,1024]{1,0,2:T(8,128)} %copy.25, s32[1024]{0:T(1024)S(1)} %pad_clamp_fusion), kind=kCustom, calls=%fused_computation.1 | custom fusion | bytes 6160 | tf_op jit(solution)/shard_map/gather | solution.py:378
  63.7 0.6 pad.13.first_ref
  64.3 18.0 %shard_map.113 = (f32[6,128,256]{2,1,0:T(8,128)}, f32[4,8,128]{2,1,0:T(8,128)}, f32[4,8,256]{2,1,0:T(8,128)}, f32[4,8,256]{2,1,0:T(8,128)}) custom-call(f32[6,32,1024]{2,1,0:T(8,128)} %copy-done.7, f32[4,8,128]{2,1,0:T(8,128)} %pad.11.cpk_ref, f32[4,8,256]{2,1,0:T(8,128)} %pad.12.last_ref, f32[4,8,256]{2,1,0:T(8,128)} %pad.13.first_ref), custom_call_target="tpu_custom_call" | custom-call | tf_op jit(solution)/shard_map/pallas_call | solution.py:244
  82.3 2.8 %fusion.31 = (f32[6,128,255]{2,1,0:T(8,128)}, f32[6,128,255]{2,1,0:T(8,128)}) fusion(f32[6,128,256]{2,1,0:T(8,128)} %get-tuple-element.7.p_ref), kind=kLoop, calls=%fused_computation.82 | loop fusion | bytes 3133440 | tf_op jit(solution)/shard_map/slice | solution.py:320
  85.2 1.2 fusion.32
  86.4 1.0 reverse_multiply_fusion
  88.0 1.2 broadcast_in_dim_reshape_squeeze.9
  89.2 4.1 %fusion.13.i_ref = f32[6,128,256]{2,1,0:T(8,128)} fusion(f32[6,1,256]{2,1,0:T(1,128)S(1)} %get-tuple-element.37, f32[6,127,256]{2,1,0:T(8,128)} %get-tuple-element.18, f32[6,127,256]{2,1,0:T(8,128)} %get-tuple-element.17, f32[6,1,256]{2,1,0:T(1,128)S(1)} %get-tuple-element.38, f32[6,128,1]{2,1,0:T(8,128)S(1)} %broadcast_in_dim_reshape_squeeze.8, ...), kind=kLoop, calls=%fused_computation.28 | loop fusion | flops 2555904 | bytes 6425600 | tf_op jit(solution)/shard_map/mul | solution.py:400
  93.3 24.8 %shard_map.114 = f32[8,128]{1,0:T(8,128)} custom-call(f32[6,128,256]{2,1,0:T(8,128)} %bitcast.61, f32[6,128,256]{2,1,0:T(8,128)} %get-tuple-element.7.p_ref, f32[6,128,256]{2,1,0:T(8,128)} %fusion.13.i_ref), custom_call_target="tpu_custom_call" | custom-call | tf_op jit(solution)/shard_map/pallas_call | solution.py:97
  118.2 1.5 %fusion.35 = (f32[1,1]{1,0:T(1,128)}, f32[1,1]{1,0:T(1,128)}, f32[1,1]{1,0:T(1,128)}, f32[1,1]{1,0:T(1,128)}, f32[1,1]{1,0:T(1,128)}) fusion(f32[8,128]{1,0:T(8,128)} %shard_map.114), kind=kLoop, calls=%fused_computation.86 | loop fusion | bytes 40 | tf_op jit(solution)/shard_map/slice | solution.py:407
  121.0 2.2 %bitcast_subtract_fusion = f32[128,6,256]{2,0,1:T(8,128)} fusion(f32[128,6,256]{2,0,1:T(8,128)S(1)} %copy-done.6, f32[6,128,256]{2,1,0:T(8,128)} %fusion.13.i_ref, f32[]{:T(128)} %bitcast.22), kind=kLoop, calls=%fused_computation.29 | loop fusion | flops 393216 | bytes 2359300 | tf_op jit(solution)/shard_map/sub | solution.py:406
  123.2 1.0 bitcast_add_fusion
  (72 shorter events, 4.3 us)
Async XLA Ops:
  0.6 24.5 %copy-start = (f32[4,6]{1,0:T(4,128)S(1)}, f32[4,6]{1,0:T(4,128)}, u32[]{:S(2)}) copy-start(f32[4,6]{1,0:T(4,128)} %param.14) | copy-start | bytes 292
  0.6 16.1 %copy-start.17 = (s32[4]{0:T(128)S(1)}, s32[4]{0:T(128)}, u32[]{:S(2)}) copy-start(s32[4]{0:T(128)} %constant.99) | copy-start | bytes 52
  0.7 15.8 %copy-start.12 = (f32[6,6,1024]{2,1,0:T(8,128)S(1)}, f32[6,6,1024]{2,1,0:T(8,128)}, u32[]{:S(2)}) copy-start(f32[6,6,1024]{2,1,0:T(8,128)} %param.15) | copy-start | bytes 442372
  2.8 22.6 %collective-permute-start.2 = (f32[128,6,1]{2,0,1:T(8,128)}, f32[128,6,1]{2,0,1:T(8,128)S(1)}, u32[]{:S(2)}, u32[]{:S(2)}) collective-permute-start(f32[128,6,1]{2,0,1:T(8,128)} %get-tuple-element.21), channel_id=1, source_target_pairs={{1,0},{2,1},{3,2},{0,3},{5,4},{6,5},{7,6},{4,7},{9,8},{10,9},{11,1... | collective-permute-start | bytes 9224 | tf_op jit(solution)/shard_map/ppermute | solution.py:311
  5.4 20.0 %collective-permute-start.3 = (f32[128,6,1]{2,0,1:T(8,128)}, f32[128,6,1]{2,0,1:T(8,128)S(1)}, u32[]{:S(2)}, u32[]{:S(2)}) collective-permute-start(f32[128,6,1]{2,0,1:T(8,128)} %get-tuple-element.22), channel_id=1, source_target_pairs={{0,1},{1,2},{2,3},{3,0},{4,5},{5,6},{6,7},{7,4},{8,9},{9,10},{10,1... | collective-permute-start | bytes 9224 | tf_op jit(solution)/shard_map/ppermute | solution.py:310
  6.3 19.1 %collective-permute-start = (f32[1,6,256]{2,0,1:T(1,128)S(1)}, f32[1,6,256]{2,0,1:T(1,128)S(1)}, u32[]{:S(2)}, u32[]{:S(2)}) collective-permute-start(f32[1,6,256]{2,0,1:T(1,128)S(1)} %get-tuple-element.19), channel_id=1, source_target_pairs={{4,0},{8,4},{12,8},{16,12},{20,16},{24,20},{28,24},{32,28},{36,32}... | collective-permute-start | bytes 18440 | tf_op jit(solution)/shard_map/ppermute | solution.py:311
  8.7 16.7 %collective-permute-start.1 = (f32[1,6,256]{2,0,1:T(1,128)S(1)}, f32[1,6,256]{2,0,1:T(1,128)S(1)}, u32[]{:S(2)}, u32[]{:S(2)}) collective-permute-start(f32[1,6,256]{2,0,1:T(1,128)S(1)} %get-tuple-element.20), channel_id=1, source_target_pairs={{0,4},{4,8},{8,12},{12,16},{16,20},{20,24},{24,28},{28,32},{32,36}... | collective-permute-start | bytes 18440 | tf_op jit(solution)/shard_map/ppermute | solution.py:310
  13.8 12.5 %copy-start.9 = (f32[128,256]{1,0:T(8,128)}, f32[128,256]{1,0:T(8,128)S(1)}, u32[]{:S(2)}) copy-start(f32[128,256]{1,0:T(8,128)S(1)} %get-tuple-element.26) | copy-start | bytes 393220
  21.8 3.3 %copy-start.18 = (s32[128]{0:T(128)S(1)}, s32[128]{0:T(128)}, u32[]{:S(2)}) copy-start(s32[128]{0:T(128)} %param.13) | copy-start | bytes 1540
  21.8 3.5 %copy-start.16 = (s32[4]{0:T(128)S(1)}, s32[4]{0:T(128)}, u32[]{:S(2)}) copy-start(s32[4]{0:T(128)} %constant.100) | copy-start | bytes 52
  21.8 4.5 %copy-start.4 = (f32[128,6,256]{2,0,1:T(8,128)S(1)}, f32[128,6,256]{2,0,1:T(8,128)}, u32[]{:S(2)}) copy-start(f32[128,6,256]{2,0,1:T(8,128)} %param.10) | copy-start | bytes 2359300
  21.8 4.5 %copy-start.8 = (f32[128,6,256]{2,0,1:T(8,128)S(1)}, f32[128,6,256]{2,0,1:T(8,128)}, u32[]{:S(2)}) copy-start(f32[128,6,256]{2,0,1:T(8,128)} %param.11) | copy-start | bytes 2359300
  25.4 0.8 copy-start.10
  25.4 0.9 copy-start.11
  28.4 22.8 %copy-start.5 = (f32[128,6,256]{2,0,1:T(8,128)}, f32[128,6,256]{2,0,1:T(8,128)S(1)}, u32[]{:S(2)}) copy-start(f32[128,6,256]{2,0,1:T(8,128)S(1)} %fusion.6) | copy-start | bytes 2359300
  45.8 5.8 %copy-start.3 = (f32[32,32,1024]{2,1,0:T(8,128)S(1)}, f32[32,32,1024]{2,1,0:T(8,128)}, u32[]{:S(2)}) copy-start(f32[32,32,1024]{2,1,0:T(8,128)} %get-tuple-element.23) | copy-start | bytes 12582916
  54.0 10.3 %copy-start.7 = (f32[6,32,1024]{2,1,0:T(8,128)}, f32[6,32,1024]{2,1,0:T(8,128)S(1)}, u32[]{:S(2)}) copy-start(f32[6,32,1024]{2,1,0:T(8,128)S(1)} %broadcast_multiply_fusion.x_ref) | copy-start | bytes 2359300
  82.3 2.9 %copy-start.1 = (f32[6,128,256]{2,1,0:T(8,128)S(1)}, f32[6,128,256]{2,1,0:T(8,128)}, u32[]{:S(2)}) copy-start(f32[6,128,256]{2,1,0:T(8,128)} %get-tuple-element.7.p_ref) | copy-start | bytes 2359300
  82.3 5.1 %copy-start.15 = (f32[4,8,128]{2,1,0:T(8,128)S(1)}, f32[4,8,128]{2,1,0:T(8,128)}, u32[]{:S(2)}) copy-start(f32[4,8,128]{2,1,0:T(8,128)} %get-tuple-element.10) | copy-start | bytes 49156
  82.3 6.8 %copy-start.14 = (f32[4,8,256]{2,1,0:T(8,128)S(1)}, f32[4,8,256]{2,1,0:T(8,128)}, u32[]{:S(2)}) copy-start(f32[4,8,256]{2,1,0:T(8,128)} %get-tuple-element.8) | copy-start | bytes 98308
  82.3 6.8 %copy-start.13 = (f32[4,8,256]{2,1,0:T(8,128)S(1)}, f32[4,8,256]{2,1,0:T(8,128)}, u32[]{:S(2)}) copy-start(f32[4,8,256]{2,1,0:T(8,128)} %get-tuple-element.9) | copy-start | bytes 98308
  89.2 31.8 %copy-start.6 = (f32[128,6,256]{2,0,1:T(8,128)S(1)}, f32[128,6,256]{2,0,1:T(8,128)}, u32[]{:S(2)}) copy-start(f32[128,6,256]{2,0,1:T(8,128)} %copy-done.5) | copy-start | bytes 2359300
  89.2 34.0 %copy-start.2 = (f32[6,128,256]{2,1,0:T(8,128)S(1)}, f32[6,128,256]{2,1,0:T(8,128)}, u32[]{:S(2)}) copy-start(f32[6,128,256]{2,1,0:T(8,128)} %get-tuple-element.7.p_ref) | copy-start | bytes 2359300

commit v6 on v5

--- a/solution.py
+++ b/solution.py
@@ -279,15 +279,12 @@
     half = length // 2
     root = int(round(math.sqrt(length)))
     cols = jnp.concatenate([jnp.arange(half + 1), jnp.arange(1, half)])
-    is_sin = jnp.arange(length) > half
+    phase = jnp.where(jnp.arange(length) > half, 0.5 * math.pi, 0.0).astype(jnp.float32)
     step = 2.0 * math.pi / length
-    coarse = (root * jnp.arange(length // root)[:, None] * cols[None, :]) % length
-    fine = (jnp.arange(root)[:, None] * cols[None, :]) % length
-    coarse_c, coarse_s = jnp.cos(step * coarse.astype(jnp.float32)), jnp.sin(step * coarse.astype(jnp.float32))
-    fine_c, fine_s = jnp.cos(step * fine.astype(jnp.float32)), jnp.sin(step * fine.astype(jnp.float32))
-    cos_part = coarse_c[:, None] * fine_c[None] - coarse_s[:, None] * fine_s[None]
-    sin_part = coarse_s[:, None] * fine_c[None] + coarse_c[:, None] * fine_s[None]
-    return jnp.where(is_sin[None, None], sin_part, cos_part).reshape(length, length)
+    coarse = step * ((root * jnp.arange(length // root)[:, None] * cols[None, :]) % length).astype(jnp.float32)
+    fine = step * ((jnp.arange(root)[:, None] * cols[None, :]) % length).astype(jnp.float32) - phase
+    table = jnp.cos(coarse)[:, None] * jnp.cos(fine)[None] - jnp.sin(coarse)[:, None] * jnp.sin(fine)[None]
+    return table.reshape(length, length)
 
 
 def paired_inverse(precond):
@@ -373,9 +370,10 @@
     group_rows = lines.shape[1]
     lanes = -(-2 * group_rows // 128) * 128
     subl = -(-comp_count // 8) * 8
-    edge_b = [(p * sector_width - 1) % around_cells for p in range(sector_count)]
-    edge_a = [((p + 1) * sector_width) % around_cells for p in range(sector_count)]
-    cols = jnp.concatenate([prec_lines[:, :, edge_b], prec_lines[:, :, edge_a]], axis=1)
+    blocks = prec_lines.reshape(comp_count, group_rows, sector_count, sector_width)
+    cols = jnp.concatenate(
+        [jnp.roll(blocks[..., -1], 1, axis=2), jnp.roll(blocks[..., 0], -1, axis=2)], axis=1
+    )
     cpk = jnp.pad(
         jnp.transpose(cols.reshape(comp_count, 2 * group_rows, sector_count), (2, 0, 1)),
         ((0, 0), (0, subl - comp_count), (0, lanes - 2 * group_rows)),

time: 127 us -> 123 us (0.969)
  local copies, waits for them, and re-layouts: 23.9 us -> 20.8 us
  other arithmetic: 25 us -> 23.1 us
  waiting for transfers between devices: 0.01 us -> 1.65 us
    select_n x2 -> x1, other arithmetic: 7.17 us -> 0.01 us  [dft_table(): jnp.where(jnp.arange(length) > half, 0.5 * math.pi, 0.0).astype(jnp.float32)]
    gather x2 -> x0, local copies, waits for them, and re-layouts: 5.47 us -> none  [the longest x1 2.74 us: shards(): prec_lines[:, :, edge_b]]
    reshape x0 -> x2, local copies, waits for them, and re-layouts: none -> 4.84 us  [shards(): prec_lines = lines_all[comp_count:] * smoothed_lines.reshape(lines.shape)]
    mul x2, local copies, waits for them, and re-layouts: 3.77 us -> 0.3 us  [shards(): prec_lines = lines_all[comp_count:] * smoothed_lines.reshape(lines.shape)]
    mul x1 -> x2, other arithmetic: 0.06 us -> 2.95 us  [shards(): prec_lines = lines_all[comp_count:] * smoothed_lines.reshape(lines.shape)]
    sub x0 -> x1, other arithmetic: none -> 2.61 us  [dft_table(): jnp.cos(coarse)[:, None] * jnp.cos(fine)[None]]
    ppermute x2, waiting for transfers between devices: 0.01 us -> 1.65 us  [with_halo(): before = lax.ppermute(last, axis, up)]
  transfers between devices with their start and end apart: 4 -> 4, of which waited for: 0 -> 1; matrix products, arithmetic and copies ran while one was open for 11% -> 9% of each run, Pallas kernels for 0% -> 0%
where the time goes in v6:
time: 123 us; the launch traced here: 122 us
  Pallas kernels  57.9 us (47%)
  other arithmetic  23.1 us (19%)
  local copies, waits for them, and re-layouts  20.8 us (17%)
  starting transfers between devices  7.92 us (6%)
  matrix products  6.76 us (5%)
  between operations  4.3 us (3%)
  waiting for transfers between devices  1.65 us (1%)
    pallas_call x1, Pallas kernels, all_sums(): pl.pallas_call(_ar_kernel, out_shape=jax.ShapeDtypeStruct((8, 128), jnp.f...  24.8 us
    pallas_call x1, Pallas kernels, from_lines_with_halo(): pl.pallas_call(functools.partial(_from_lines_kernel, (n_ax, n)), out_shap...  18 us
    pallas_call x1, Pallas kernels, _exchange(): pl.pallas_call(functools.partial(body, n), out_shape=jax.ShapeDtypeStruct...  15 us
    reshape x2, local copies, waits for them, and re-layouts, shards(): prec_lines = lines_all[comp_count:] * smoothed_lines.reshape(lines.shape)  4.84 us
    ppermute x2, starting transfers between devices, with_halo(): after = lax.ppermute(first, axis, down)  4.52 us
    dot_general x1, matrix products, shards(): jnp.dot(lines.reshape(-1, around_cells), dft_table(around_cells), precisi...  4.22 us
    mul x1, other arithmetic, shards(): solid_t * ((stiffness_t + 4.5) * prec_t - beside - 0.5 * swap_channels(pr...  3.87 us
    ppermute x2, starting transfers between devices, with_halo(): before = lax.ppermute(last, axis, up)  3.4 us
  transfers between devices with their start and end apart: 4, of which 1 were waited for; matrix products, arithmetic and copies ran while one was open for 9% of the time, Pallas kernels for 0%

profile of v6, /device:TPU:4, one launch (start us, length us, event | category | flops | bytes accessed | tf_op | source)
XLA Modules:
  0.0 122.3 jit_solution(1578482168348696278)
XLA Ops:
  0.7 0.8 fusion.34
  1.5 2.4 %collective-permute-start = (f32[1,6,256]{2,0,1:T(1,128)S(1)}, f32[1,6,256]{2,0,1:T(1,128)S(1)}, u32[]{:S(2)}, u32[]{:S(2)}) collective-permute-start(f32[1,6,256]{2,0,1:T(1,128)S(1)} %get-tuple-element.23), channel_id=1, source_target_pairs={{4,0},{8,4},{12,8},{16,12},{20,16},{24,20},{28,24},{32,28},{36,32}... | collective-permute-start | bytes 18440 | tf_op jit(solution)/shard_map/ppermute | solution.py:308
  4.0 3.4 %collective-permute-start.1 = (f32[1,6,256]{2,0,1:T(1,128)S(1)}, f32[1,6,256]{2,0,1:T(1,128)S(1)}, u32[]{:S(2)}, u32[]{:S(2)}) collective-permute-start(f32[1,6,256]{2,0,1:T(1,128)S(1)} %get-tuple-element.24), channel_id=1, source_target_pairs={{0,4},{4,8},{8,12},{12,16},{16,20},{20,24},{24,28},{28,32},{32,36}... | collective-permute-start | bytes 18440 | tf_op jit(solution)/shard_map/ppermute | solution.py:307
  7.4 2.1 %fusion.35 = (f32[128,6,1]{2,0,1:T(8,128)}, f32[128,6,1]{2,0,1:T(8,128)}) fusion(f32[128,6,256]{2,0,1:T(8,128)} %param.8), kind=kLoop, calls=%fused_computation.82 | loop fusion | bytes 12288 | tf_op jit(solution)/shard_map/slice | solution.py:306
  9.5 2.1 %collective-permute-start.2 = (f32[128,6,1]{2,0,1:T(8,128)}, f32[128,6,1]{2,0,1:T(8,128)S(1)}, u32[]{:S(2)}, u32[]{:S(2)}) collective-permute-start(f32[128,6,1]{2,0,1:T(8,128)} %get-tuple-element.25), channel_id=1, source_target_pairs={{1,0},{2,1},{3,2},{0,3},{5,4},{6,5},{7,6},{4,7},{9,8},{10,9},{11,1... | collective-permute-start | bytes 9224 | tf_op jit(solution)/shard_map/ppermute | solution.py:308
  11.6 1.0 slice.134
  13.0 1.1 maximum_add_fusion.1
  14.2 1.6 %subtract_convert_fusion = (f32[128,256]{1,0:T(8,128)S(1)}, f32[1,128,256]{2,1,0:T(8,128)}) fusion(s32[128,256]{1,0:T(8,128)} %param.10), kind=kLoop, calls=%fused_computation.48 | loop fusion | flops 65536 | bytes 393216 | tf_op jit(solution)/shard_map/convert_element_type | solution.py:353
  15.8 1.2 %reverse_multiply_fusion.1 = f32[128,3,2,256]{3,0,2,1:T(8,128)S(1)} fusion(f32[128,3,2,256]{3,0,2,1:T(8,128)} %bitcast.58), kind=kLoop, calls=%fused_computation.27 | loop fusion | flops 196608 | bytes 1572864 | tf_op jit(solution)/shard_map/mul | solution.py:338
  17.3 1.1 fusion.25
  18.5 2.6 %multiply_subtract_fusion = f32[32,32,1024]{2,1,0:T(8,128)} fusion(f32[32,1024]{1,0:T(8,128)S(1)} %get-tuple-element.38, f32[32,1024]{1,0:T(8,128)S(1)} %get-tuple-element.32, f32[32,1024]{1,0:T(8,128)S(1)} %get-tuple-element.39, f32[32,1024]{1,0:T(8,128)S(1)} %get-tuple-element.31), kind=kLoop, calls=%fused_computation.1 | loop fusion | flops 3145728 | bytes 4718592 | tf_op jit(solution)/shard_map/sub | solution.py:286
  21.2 1.6 %collective-permute-done.3 = f32[128,6,1]{2,0,1:T(8,128)S(1)} collective-permute-done((f32[128,6,1]{2,0,1:T(8,128)}, f32[128,6,1]{2,0,1:T(8,128)S(1)}, u32[]{:S(2)}, u32[]{:S(2)}) %collective-permute-start.3) | collective-permute-done | bytes 3104 | tf_op jit(solution)/shard_map/ppermute | solution.py:307
  22.9 0.7 copy-done.11
  23.6 2.1 %fusion.4 = f32[128,6,256]{2,0,1:T(8,128)S(1)} fusion(f32[128,6,256]{2,0,1:T(8,128)} %param.7, f32[128,6,256]{2,0,1:T(8,128)S(1)} %copy-done.4, f32[128,6,1]{2,0,1:T(8,128)} %copy-done.11, f32[128,6,1]{2,0,1:T(8,128)} %copy-done.10, f32[1,6,256]{2,0,1:T(1,128)S(1)} %collective-permute-done.1, f32[1,6,256]{2,0,1:T(1,128)S(1)} %collective-permute-done, ...), kind=kLoop, calls=%fused_computation.11 | loop fusion | flops 2752512 | bytes 4084736 | tf_op jit(solution)/shard_map/mul | solution.py:354
  25.7 2.1 %pad_maximum_fusion.x_ref = f32[7,128,256]{2,1,0:T(8,128)} fusion(f32[1,128,256]{2,1,0:T(8,128)} %get-tuple-element.28, f32[6,128,256]{2,1,0:T(8,128)S(1)} %bitcast.59), kind=kLoop, calls=%fused_computation.5 | loop fusion | flops 229376 | bytes 1835008 | tf_op jit(solution)/shard_map/concatenate | solution.py:357
  27.8 15.0 %shard_map.94 = f32[7,32,1024]{2,1,0:T(8,128)} custom-call(f32[7,128,256]{2,1,0:T(8,128)} %pad_maximum_fusion.x_ref), custom_call_target="tpu_custom_call" | custom-call | tf_op jit(solution)/shard_map/pallas_call | solution.py:259
  42.8 0.9 fusion.31
  44.1 4.2 %fusion.37 = f32[6,32,1024]{2,1,0:T(8,128)S(1)} fusion(f32[7,32,1024]{2,1,0:T(8,128)} %shard_map.94, f32[1024,1024,1]{1,0,2:T(8,128)} %bitcast.56), kind=kOutput, calls=%fused_computation.84 | convolution fusion | flops 1207959552 | bytes 5898240 | tf_op jit(solution)/shard_map/dot_general | solution.py:359
  48.7 2.4 %convolution_multiply_fusion = f32[192,1024]{1,0:T(8,128)S(1)} fusion(f32[192,1024]{1,0:T(8,128)S(1)} %bitcast.62, f32[1024,1024]{1,0:T(8,128)S(1)} %bitcast.57), kind=kOutput, calls=%fused_computation.3 | convolution fusion | flops 1208156160 | bytes 5767168 | tf_op jit(solution)/shard_map/dot_general | solution.py:363
  51.4 4.5 %copy.25 = f32[6,32,4,256]{1,0,2,3:T(8,128)} copy(f32[6,32,4,256]{3,2,1,0:T(4,128)S(1)} %reshape.274) | data formatting | bytes 1572864 | tf_op jit(solution)/shard_map/reshape | solution.py:369
  55.9 2.9 %broadcast_multiply_fusion = f32[6,32,4,256]{1,0,2,3:T(8,128)S(1)} fusion(f32[6,32,4,256]{1,0,2,3:T(8,128)} %copy.25, f32[32,4,256]{0,1,2:T(4,128)S(1)} %copy.24), kind=kLoop, calls=%fused_computation.2 | loop fusion | flops 196608 | bytes 1703936 | tf_op jit(solution)/shard_map/mul | solution.py:369
  59.0 0.7 pad.13.first_ref
  59.8 0.6 pad.12.last_ref
  61.1 18.0 %shard_map.95 = (f32[6,128,256]{2,1,0:T(8,128)}, f32[4,8,128]{2,1,0:T(8,128)}, f32[4,8,256]{2,1,0:T(8,128)}, f32[4,8,256]{2,1,0:T(8,128)}) custom-call(f32[6,32,1024]{2,1,0:T(8,128)} %copy-done.7, f32[4,8,128]{2,1,0:T(8,128)} %pad.11.cpk_ref, f32[4,8,256]{2,1,0:T(8,128)} %pad.12.last_ref, f32[4,8,256]{2,1,0:T(8,128)} %pad.13.first_ref), custom_call_target="tpu_custom_call" | custom-call | tf_op jit(solution)/shard_map/pallas_call | solution.py:244
  79.2 2.8 %fusion.32 = (f32[6,128,255]{2,1,0:T(8,128)}, f32[6,128,255]{2,1,0:T(8,128)}) fusion(f32[6,128,256]{2,1,0:T(8,128)} %get-tuple-element.7.p_ref), kind=kLoop, calls=%fused_computation.79 | loop fusion | bytes 3133440 | tf_op jit(solution)/shard_map/slice | solution.py:317
  82.0 1.3 %fusion.33 = (f32[6,127,256]{2,1,0:T(8,128)}, f32[6,127,256]{2,1,0:T(8,128)}) fusion(f32[6,128,256]{2,1,0:T(8,128)S(1)} %copy-done.1), kind=kLoop, calls=%fused_computation.80 | loop fusion | bytes 3121152 | tf_op jit(solution)/shard_map/slice | solution.py:315
  83.9 1.1 broadcast_in_dim_reshape_squeeze.8
  85.2 3.9 %fusion.11.i_ref = f32[6,128,256]{2,1,0:T(8,128)} fusion(f32[6,1,256]{2,1,0:T(1,128)S(1)} %get-tuple-element.40, f32[6,127,256]{2,1,0:T(8,128)} %get-tuple-element.22, f32[6,127,256]{2,1,0:T(8,128)} %get-tuple-element.21, f32[6,1,256]{2,1,0:T(1,128)S(1)} %get-tuple-element.41, f32[6,128,1]{2,1,0:T(8,128)} %broadcast_in_dim_reshape_squeeze.8, ...), kind=kLoop, calls=%fused_computation.22 | loop fusion | flops 2555904 | bytes 6425600 | tf_op jit(solution)/shard_map/mul | solution.py:398
  89.0 24.8 %shard_map.96 = f32[8,128]{1,0:T(8,128)} custom-call(f32[6,128,256]{2,1,0:T(8,128)} %bitcast.60, f32[6,128,256]{2,1,0:T(8,128)} %get-tuple-element.7.p_ref, f32[6,128,256]{2,1,0:T(8,128)} %fusion.11.i_ref), custom_call_target="tpu_custom_call" | custom-call | tf_op jit(solution)/shard_map/pallas_call | solution.py:97
  113.9 1.5 %fusion.36 = (f32[1,1]{1,0:T(1,128)}, f32[1,1]{1,0:T(1,128)}, f32[1,1]{1,0:T(1,128)}, f32[1,1]{1,0:T(1,128)}, f32[1,1]{1,0:T(1,128)}) fusion(f32[8,128]{1,0:T(8,128)} %shard_map.96), kind=kLoop, calls=%fused_computation.83 | loop fusion | bytes 40 | tf_op jit(solution)/shard_map/slice | solution.py:405
  116.7 2.2 %bitcast_subtract_fusion = f32[128,6,256]{2,0,1:T(8,128)} fusion(f32[128,6,256]{2,0,1:T(8,128)S(1)} %copy-done.6, f32[6,128,256]{2,1,0:T(8,128)} %fusion.11.i_ref, f32[]{:T(128)} %bitcast.20), kind=kLoop, calls=%fused_computation.23 | loop fusion | flops 393216 | bytes 2359300 | tf_op jit(solution)/shard_map/sub | solution.py:404
  118.9 1.0 bitcast_add_fusion
  (70 shorter events, 4.2 us)
Async XLA Ops:
  0.6 16.5 %copy-start = (f32[4,6]{1,0:T(4,128)S(1)}, f32[4,6]{1,0:T(4,128)}, u32[]{:S(2)}) copy-start(f32[4,6]{1,0:T(4,128)} %param.12) | copy-start | bytes 292
  0.6 16.5 %copy-start.15 = (s32[128]{0:T(128)S(1)}, s32[128]{0:T(128)}, u32[]{:S(2)}) copy-start(s32[128]{0:T(128)} %param.11) | copy-start | bytes 1540
  1.5 21.3 %collective-permute-start = (f32[1,6,256]{2,0,1:T(1,128)S(1)}, f32[1,6,256]{2,0,1:T(1,128)S(1)}, u32[]{:S(2)}, u32[]{:S(2)}) collective-permute-start(f32[1,6,256]{2,0,1:T(1,128)S(1)} %get-tuple-element.23), channel_id=1, source_target_pairs={{4,0},{8,4},{12,8},{16,12},{20,16},{24,20},{28,24},{32,28},{36,32}... | collective-permute-start | bytes 18440 | tf_op jit(solution)/shard_map/ppermute | solution.py:308
  4.0 18.9 %collective-permute-start.1 = (f32[1,6,256]{2,0,1:T(1,128)S(1)}, f32[1,6,256]{2,0,1:T(1,128)S(1)}, u32[]{:S(2)}, u32[]{:S(2)}) collective-permute-start(f32[1,6,256]{2,0,1:T(1,128)S(1)} %get-tuple-element.24), channel_id=1, source_target_pairs={{0,4},{4,8},{8,12},{12,16},{16,20},{20,24},{24,28},{28,32},{32,36}... | collective-permute-start | bytes 18440 | tf_op jit(solution)/shard_map/ppermute | solution.py:307
  9.5 11.7 %collective-permute-start.2 = (f32[128,6,1]{2,0,1:T(8,128)}, f32[128,6,1]{2,0,1:T(8,128)S(1)}, u32[]{:S(2)}, u32[]{:S(2)}) collective-permute-start(f32[128,6,1]{2,0,1:T(8,128)} %get-tuple-element.25), channel_id=1, source_target_pairs={{1,0},{2,1},{3,2},{0,3},{5,4},{6,5},{7,6},{4,7},{9,8},{10,9},{11,1... | collective-permute-start | bytes 9224 | tf_op jit(solution)/shard_map/ppermute | solution.py:308
  11.5 11.3 %collective-permute-start.3 = (f32[128,6,1]{2,0,1:T(8,128)}, f32[128,6,1]{2,0,1:T(8,128)S(1)}, u32[]{:S(2)}, u32[]{:S(2)}) collective-permute-start(f32[128,6,1]{2,0,1:T(8,128)} %get-tuple-element.26), channel_id=1, source_target_pairs={{0,1},{1,2},{2,3},{3,0},{4,5},{5,6},{6,7},{7,4},{8,9},{9,10},{10,1... | collective-permute-start | bytes 9224 | tf_op jit(solution)/shard_map/ppermute | solution.py:307
  13.0 10.6 %copy-start.4 = (f32[128,6,256]{2,0,1:T(8,128)S(1)}, f32[128,6,256]{2,0,1:T(8,128)}, u32[]{:S(2)}) copy-start(f32[128,6,256]{2,0,1:T(8,128)} %param.8) | copy-start | bytes 2359300
  13.0 10.6 %copy-start.8 = (f32[128,6,256]{2,0,1:T(8,128)S(1)}, f32[128,6,256]{2,0,1:T(8,128)}, u32[]{:S(2)}) copy-start(f32[128,6,256]{2,0,1:T(8,128)} %param.9) | copy-start | bytes 2359300
  15.8 9.9 %copy-start.9 = (f32[128,256]{1,0:T(8,128)}, f32[128,256]{1,0:T(8,128)S(1)}, u32[]{:S(2)}) copy-start(f32[128,256]{1,0:T(8,128)S(1)} %get-tuple-element.27) | copy-start | bytes 393220
  21.2 1.7 %copy-start.10 = (f32[128,6,1]{2,0,1:T(8,128)}, f32[128,6,1]{2,0,1:T(8,128)S(1)}, u32[]{:S(2)}) copy-start(f32[128,6,1]{2,0,1:T(8,128)S(1)} %collective-permute-done.2) | copy-start | bytes 9220
  22.8 0.7 copy-start.11
  25.7 22.6 %copy-start.5 = (f32[128,6,256]{2,0,1:T(8,128)}, f32[128,6,256]{2,0,1:T(8,128)S(1)}, u32[]{:S(2)}) copy-start(f32[128,6,256]{2,0,1:T(8,128)S(1)} %fusion.4) | copy-start | bytes 2359300
  44.1 4.6 %copy-start.3 = (f32[32,32,1024]{2,1,0:T(8,128)S(1)}, f32[32,32,1024]{2,1,0:T(8,128)}, u32[]{:S(2)}) copy-start(f32[32,32,1024]{2,1,0:T(8,128)} %multiply_subtract_fusion) | copy-start | bytes 12582916
  58.9 2.2 %copy-start.7 = (f32[6,32,1024]{2,1,0:T(8,128)}, f32[6,32,1024]{2,1,0:T(8,128)S(1)}, u32[]{:S(2)}) copy-start(f32[6,32,1024]{2,1,0:T(8,128)S(1)} %broadcast_multiply_fusion.1.x_ref) | copy-start | bytes 2359300
  79.1 2.9 %copy-start.1 = (f32[6,128,256]{2,1,0:T(8,128)S(1)}, f32[6,128,256]{2,1,0:T(8,128)}, u32[]{:S(2)}) copy-start(f32[6,128,256]{2,1,0:T(8,128)} %get-tuple-element.7.p_ref) | copy-start | bytes 2359300
  79.1 4.1 %copy-start.13 = (f32[4,8,256]{2,1,0:T(8,128)S(1)}, f32[4,8,256]{2,1,0:T(8,128)}, u32[]{:S(2)}) copy-start(f32[4,8,256]{2,1,0:T(8,128)} %get-tuple-element.8) | copy-start | bytes 98308
  79.1 4.1 %copy-start.14 = (f32[4,8,128]{2,1,0:T(8,128)S(1)}, f32[4,8,128]{2,1,0:T(8,128)}, u32[]{:S(2)}) copy-start(f32[4,8,128]{2,1,0:T(8,128)} %get-tuple-element.10) | copy-start | bytes 49156
  79.1 4.3 %copy-start.12 = (f32[4,8,256]{2,1,0:T(8,128)S(1)}, f32[4,8,256]{2,1,0:T(8,128)}, u32[]{:S(2)}) copy-start(f32[4,8,256]{2,1,0:T(8,128)} %get-tuple-element.9) | copy-start | bytes 98308
  85.1 31.6 %copy-start.6 = (f32[128,6,256]{2,0,1:T(8,128)S(1)}, f32[128,6,256]{2,0,1:T(8,128)}, u32[]{:S(2)}) copy-start(f32[128,6,256]{2,0,1:T(8,128)} %copy-done.5) | copy-start | bytes 2359300
  85.2 33.7 %copy-start.2 = (f32[6,128,256]{2,1,0:T(8,128)S(1)}, f32[6,128,256]{2,1,0:T(8,128)}, u32[]{:S(2)}) copy-start(f32[6,128,256]{2,1,0:T(8,128)} %get-tuple-element.7.p_ref) | copy-start | bytes 2359300

commit v7 on v6

--- a/solution.py
+++ b/solution.py
@@ -49,7 +49,24 @@
     return packed
 
 
-def _ar_kernel(r_ref, p_ref, i_ref, o_ref, recv_a, recv_b, own, send_sems, recv_sems):
+def _finish(total, cell_total):
+    lane = lax.broadcasted_iota(jnp.int32, total.shape, 1)
+    row = lax.broadcasted_iota(jnp.int32, total.shape, 0)
+
+    def pick(k):
+        return jnp.sum(jnp.where((row == 0) & (lane == k), total, 0.0), keepdims=True)
+
+    inner_rz = pick(0) / cell_total
+    inner_zq = pick(1) / cell_total
+    alpha = inner_rz / inner_zq
+    square_new = (pick(2) - alpha * (2.0 * pick(3) - alpha * pick(4))) / cell_total
+    out = jnp.zeros(total.shape, jnp.float32)
+    for k, v in enumerate((alpha, inner_rz, inner_zq, square_new)):
+        out = jnp.where((row == 0) & (lane == k), v, out)
+    return out
+
+
+def _ar_kernel(cell_total, r_ref, p_ref, i_ref, o_ref, recv_a, recv_b, own, send_sems, recv_sems):
     recvs = (recv_a, recv_b)
     groups = _groups()
     for r in recvs:
@@ -90,12 +107,12 @@
         if g + 1 < len(groups):
             own[g + 1] = total
         else:
-            o_ref[...] = total
-
-
-def all_sums(residual, prec, image, cid):
+            o_ref[...] = _finish(total, cell_total)
+
+
+def all_sums(residual, prec, image, cell_total, cid):
     return pl.pallas_call(
-        _ar_kernel,
+        functools.partial(_ar_kernel, float(cell_total)),
         out_shape=jax.ShapeDtypeStruct((8, 128), jnp.float32),
         in_specs=[pl.BlockSpec(memory_space=pltpu.VMEM)] * 3,
         out_specs=pl.BlockSpec(memory_space=pltpu.VMEM),
@@ -370,12 +387,17 @@
     group_rows = lines.shape[1]
     lanes = -(-2 * group_rows // 128) * 128
     subl = -(-comp_count // 8) * 8
-    blocks = prec_lines.reshape(comp_count, group_rows, sector_count, sector_width)
-    cols = jnp.concatenate(
-        [jnp.roll(blocks[..., -1], 1, axis=2), jnp.roll(blocks[..., 0], -1, axis=2)], axis=1
-    )
+    edge_at = [(p * sector_width - 1) % around_cells for p in range(sector_count)]
+    edge_at += [((p + 1) * sector_width) % around_cells for p in range(sector_count)]
+    pick = (jnp.arange(around_cells)[None, :] == jnp.array(edge_at)[:, None]).astype(jnp.float32)
+    edges = lax.dot_general(
+        pick,
+        prec_lines.reshape(-1, around_cells),
+        (((1,), (1,)), ((), ())),
+        precision=lax.Precision.HIGHEST,
+    ).reshape(2, sector_count, comp_count, group_rows)
     cpk = jnp.pad(
-        jnp.transpose(cols.reshape(comp_count, 2 * group_rows, sector_count), (2, 0, 1)),
+        jnp.transpose(edges, (1, 2, 0, 3)).reshape(sector_count, comp_count, 2 * group_rows),
         ((0, 0), (0, subl - comp_count), (0, lanes - 2 * group_rows)),
     )
 
@@ -397,14 +419,11 @@
     stiffness_t = jnp.transpose(stiffness, (1, 0, 2))
     image_t = solid_t * ((stiffness_t + 4.5) * prec_t - beside - 0.5 * swap_channels(prec_t))
     cell_total = slab_count * lax.axis_size("ax") * comp_count * around_cells
-    totals = all_sums(residual_t, prec_t, image_t, 0)[0]
-    inner_rz = totals[0] / cell_total
-    inner_zq = totals[1] / cell_total
-    alpha = inner_rz / inner_zq
+    finished = all_sums(residual_t, prec_t, image_t, cell_total, 0)[0]
+    alpha = finished[0]
     residual_new = residual - alpha * jnp.transpose(image_t, (1, 0, 2))
-    square_new = (totals[2] - alpha * (2.0 * totals[3] - alpha * totals[4])) / cell_total
     disp_new = disp + alpha * jnp.transpose(prec_t, (1, 0, 2))
-    return (disp_new, residual_new, jnp.stack([inner_rz, inner_zq, square_new]))
+    return (disp_new, residual_new, finished[1:4])
 
 
 def solution(mesh):

time: 123 us -> 111 us (0.902); the launches traced: 122 us -> 109 us
  local copies, waits for them, and re-layouts: 20.8 us -> 16.1 us
  other arithmetic: 23.1 us -> 18.6 us
  between operations: 4.3 us -> 1.1 us
  Pallas kernels: 57.9 us -> 55.9 us
  waiting for transfers between devices: 1.65 us -> 0.01 us
    reshape x2, local copies, waits for them, and re-layouts: 4.84 us -> 0.11 us  [shards(): jnp.transpose(edges, (1, 2, 0, 3))]
    mul x2 -> x1, other arithmetic: 2.95 us -> 0.07 us  [shards(): prec_lines = lines_all[comp_count:] * smoothed_lines.reshape(lines.shape)]
    pallas_call x1, Pallas kernels: 18 us -> 16.3 us  [from_lines_with_halo(): pl.pallas_call(functools.partial(_from_lines_kernel, (n_ax, n)), out_shap...]
    ppermute x2, waiting for transfers between devices: 1.65 us -> 0.01 us  [with_halo(): before = lax.ppermute(last, axis, up)]
    slice x1, local copies, waits for them, and re-layouts: 1.26 us -> 2.73 us  [stencil_from_halo(): up = jnp.concatenate([before_row[:, None], field[:, :-1]], axis=1)]
    ppermute x2, starting transfers between devices: 4.52 us -> 5.98 us  [with_halo(): after = lax.ppermute(first, axis, down)]
    slice x1, local copies, waits for them, and re-layouts: 2.83 us -> 1.44 us  [stencil_from_halo(): left = jnp.concatenate([before_col[:, :, None], field[:, :, :-1]], axis=2)]
  transfers between devices with their start and end apart: 4 -> 4, of which waited for: 1 -> 0; matrix products, arithmetic and copies ran while one was open for 9% -> 9% of each run, Pallas kernels for 0% -> 0%
where the time goes in v7:
time: 111 us; the launch traced here: 109 us
  Pallas kernels  55.9 us (50%)
  other arithmetic  18.6 us (17%)
  local copies, waits for them, and re-layouts  16.1 us (15%)
  starting transfers between devices  9.09 us (8%)
  matrix products  7.83 us (7%)
    pallas_call x1, Pallas kernels, all_sums(): pl.pallas_call(functools.partial(_ar_kernel, float(cell_total)), out_shap...  23.9 us
    pallas_call x1, Pallas kernels, from_lines_with_halo(): pl.pallas_call(functools.partial(_from_lines_kernel, (n_ax, n)), out_shap...  16.3 us
    pallas_call x1, Pallas kernels, _exchange(): pl.pallas_call(functools.partial(body, n), out_shape=jax.ShapeDtypeStruct...  15.8 us
    ppermute x2, starting transfers between devices, with_halo(): after = lax.ppermute(first, axis, down)  5.98 us
    dot_general x1, matrix products, shards(): jnp.dot(lines.reshape(-1, around_cells), dft_table(around_cells), precisi...  4.31 us
    mul x1, other arithmetic, shards(): solid_t * ((stiffness_t + 4.5) * prec_t - beside - 0.5 * swap_channels(pr...  3.84 us
    ppermute x2, starting transfers between devices, with_halo(): before = lax.ppermute(last, axis, up)  3.11 us
    slice x2, local copies, waits for them, and re-layouts, with_halo(): first = lax.slice_in_dim(x, 0, width, axis=dim)  2.97 us
  transfers between devices with their start and end apart: 4, of which 0 were waited for; matrix products, arithmetic and copies ran while one was open for 9% of the time, Pallas kernels for 0%

profile of v7, /device:TPU:4, one launch (start us, length us, event | category | flops | bytes accessed | tf_op | source)
XLA Modules:
  0.0 108.7 jit_solution(8154545318858743290)
XLA Ops:
  0.7 2.1 %fusion.37 = (f32[128,6,1]{2,0,1:T(8,128)}, f32[128,6,1]{2,0,1:T(8,128)}) fusion(f32[128,6,256]{2,0,1:T(8,128)} %param.9), kind=kLoop, calls=%fused_computation.82 | loop fusion | bytes 12288 | tf_op jit(solution)/shard_map/slice | solution.py:323
  2.8 3.2 %collective-permute-start.2 = (f32[128,6,1]{2,0,1:T(8,128)}, f32[128,6,1]{2,0,1:T(8,128)}, u32[]{:S(2)}, u32[]{:S(2)}) collective-permute-start(f32[128,6,1]{2,0,1:T(8,128)} %get-tuple-element.21), channel_id=1, source_target_pairs={{1,0},{2,1},{3,2},{0,3},{5,4},{6,5},{7,6},{4,7},{9,8},{10,9},{11,1... | collective-permute-start | bytes 9224 | tf_op jit(solution)/shard_map/ppermute | solution.py:325
  6.1 0.8 fusion.36
  6.9 3.1 %collective-permute-start.1 = (f32[1,6,256]{2,0,1:T(1,128)S(1)}, f32[1,6,256]{2,0,1:T(1,128)S(1)}, u32[]{:S(2)}, u32[]{:S(2)}) collective-permute-start(f32[1,6,256]{2,0,1:T(1,128)S(1)} %get-tuple-element.20), channel_id=1, source_target_pairs={{0,4},{4,8},{8,12},{12,16},{16,20},{20,24},{24,28},{28,32},{32,36}... | collective-permute-start | bytes 18440 | tf_op jit(solution)/shard_map/ppermute | solution.py:324
  10.0 2.7 %collective-permute-start = (f32[1,6,256]{2,0,1:T(1,128)S(1)}, f32[1,6,256]{2,0,1:T(1,128)S(1)}, u32[]{:S(2)}, u32[]{:S(2)}) collective-permute-start(f32[1,6,256]{2,0,1:T(1,128)S(1)} %get-tuple-element.19), channel_id=1, source_target_pairs={{4,0},{8,4},{12,8},{16,12},{20,16},{24,20},{28,24},{32,28},{36,32}... | collective-permute-start | bytes 18440 | tf_op jit(solution)/shard_map/ppermute | solution.py:325
  12.8 1.6 %subtract_convert_fusion = (f32[128,256]{1,0:T(8,128)S(1)}, f32[1,128,256]{2,1,0:T(8,128)}) fusion(s32[128,256]{1,0:T(8,128)} %param.11), kind=kLoop, calls=%fused_computation.50 | loop fusion | flops 65536 | bytes 393216 | tf_op jit(solution)/shard_map/convert_element_type | solution.py:370
  14.4 1.3 %reverse_multiply_fusion.1 = f32[128,3,2,256]{3,0,2,1:T(8,128)S(1)} fusion(f32[128,3,2,256]{3,0,2,1:T(8,128)} %bitcast.62), kind=kLoop, calls=%fused_computation.28 | loop fusion | flops 196608 | bytes 1572864 | tf_op jit(solution)/shard_map/mul | solution.py:355
  15.7 1.0 slice.99
  17.6 1.1 %fusion.25 = (f32[32,1024]{1,0:T(8,128)S(1)}, f32[32,1024]{1,0:T(8,128)S(1)}, f32[32,1024]{1,0:T(8,128)S(1)}, f32[32,1024]{1,0:T(8,128)S(1)}) fusion(s32[1024]{0:T(1024)S(1)} %pad_add_fusion, s32[32]{0:T(128)S(1)} %iota_multiply_fusion, f32[1024]{0:T(1024)S(1)} %fusion.32), kind=kLoop, calls=%fused_computation.56 | loop fusion | flops 950272 | bytes 532608 | tf_op jit(solution)/shard_map/cos | solution.py:303
  18.7 2.6 %multiply_subtract_fusion = f32[32,32,1024]{2,1,0:T(8,128)} fusion(f32[32,1024]{1,0:T(8,128)S(1)} %get-tuple-element.29, f32[32,1024]{1,0:T(8,128)S(1)} %get-tuple-element.28, f32[32,1024]{1,0:T(8,128)S(1)} %get-tuple-element.30, f32[32,1024]{1,0:T(8,128)S(1)} %get-tuple-element.27), kind=kLoop, calls=%fused_computation.1 | loop fusion | flops 3145728 | bytes 4718592 | tf_op jit(solution)/shard_map/sub | solution.py:303
  21.5 2.1 %fusion.4 = f32[128,6,256]{2,0,1:T(8,128)S(1)} fusion(f32[128,6,256]{2,0,1:T(8,128)} %param.8, f32[128,6,256]{2,0,1:T(8,128)S(1)} %copy-done.4, f32[128,6,1]{2,0,1:T(8,128)} %collective-permute-done.3, f32[128,6,1]{2,0,1:T(8,128)} %collective-permute-done.2, f32[1,6,256]{2,0,1:T(1,128)S(1)} %collective-permute-done.1, ...), kind=kLoop, calls=%fused_computation.11 | loop fusion | flops 2752512 | bytes 4084736 | tf_op jit(solution)/shard_map/mul | solution.py:371
  23.7 2.1 %pad_maximum_fusion.x_ref = f32[7,128,256]{2,1,0:T(8,128)} fusion(f32[1,128,256]{2,1,0:T(8,128)} %get-tuple-element.24, f32[6,128,256]{2,1,0:T(8,128)S(1)} %bitcast.63), kind=kLoop, calls=%fused_computation.5 | loop fusion | flops 229376 | bytes 1835008 | tf_op jit(solution)/shard_map/concatenate | solution.py:374
  25.7 15.8 %shard_map.103 = f32[7,32,1024]{2,1,0:T(8,128)} custom-call(f32[7,128,256]{2,1,0:T(8,128)} %pad_maximum_fusion.x_ref), custom_call_target="tpu_custom_call" | custom-call | tf_op jit(solution)/shard_map/pallas_call | solution.py:276
  41.5 1.1 slice_bitcast_fusion
  42.6 4.3 %fusion.38 = f32[6,32,1024]{2,1,0:T(8,128)S(1)} fusion(f32[7,32,1024]{2,1,0:T(8,128)} %shard_map.103, f32[1024,1024,1]{1,0,2:T(8,128)} %bitcast.60), kind=kOutput, calls=%fused_computation.83 | convolution fusion | flops 1207959552 | bytes 5898240 | tf_op jit(solution)/shard_map/dot_general | solution.py:376
  46.9 0.3 multiply_reduce_fusion
  47.3 2.4 %bitcast_multiply_fusion.1 = (f32[192,1024]{1,0:T(8,128)S(1)}, f32[192,1024]{1,0:T(8,128)S(1)}) fusion(f32[32,1024]{1,0:T(8,128)S(1)} %slice_bitcast_fusion, f32[192,1024]{1,0:T(8,128)S(1)} %bitcast.65, f32[1024,1024]{1,0:T(8,128)S(1)} %bitcast.61), kind=kOutput, calls=%fused_computation.26 | convolution fusion | flops 1208352768 | bytes 6684672 | tf_op jit(solution)/shard_map/dot_general | solution.py:380
  49.8 0.9 convolution_bitcast_fusion
  50.8 0.6 pad.11.cpk_ref
  51.6 0.6 pad.12.last_ref
  52.2 0.6 pad.13.first_ref
  52.8 16.3 %shard_map.104 = (f32[6,128,256]{2,1,0:T(8,128)}, f32[4,8,128]{2,1,0:T(8,128)}, f32[4,8,256]{2,1,0:T(8,128)}, f32[4,8,256]{2,1,0:T(8,128)}) custom-call(f32[6,32,1024]{2,1,0:T(8,128)} %copy-done.8, f32[4,8,128]{2,1,0:T(8,128)} %pad.11.cpk_ref, f32[4,8,256]{2,1,0:T(8,128)} %pad.12.last_ref, f32[4,8,256]{2,1,0:T(8,128)} %pad.13.first_ref), custom_call_target="tpu_custom_call" | custom-call | tf_op jit(solution)/shard_map/pallas_call | solution.py:261
  69.2 2.7 %fusion.35 = (f32[6,127,256]{2,1,0:T(8,128)}, f32[6,127,256]{2,1,0:T(8,128)}) fusion(f32[6,128,256]{2,1,0:T(8,128)} %get-tuple-element.7.p_ref), kind=kLoop, calls=%fused_computation.80 | loop fusion | bytes 3121152 | tf_op jit(solution)/shard_map/slice | solution.py:332
  71.9 1.4 %fusion.34 = (f32[6,128,255]{2,1,0:T(8,128)}, f32[6,128,255]{2,1,0:T(8,128)}) fusion(f32[6,128,256]{2,1,0:T(8,128)S(1)} %copy-done.1), kind=kLoop, calls=%fused_computation.79 | loop fusion | bytes 3133440 | tf_op jit(solution)/shard_map/slice | solution.py:334
  73.6 0.4 broadcast_in_dim_reshape_squeeze.8
  74.0 1.2 %broadcast_in_dim_reshape_squeeze.9 = f32[6,128,1]{2,1,0:T(8,128)} reshape(f32[6,4,32]{2,1,0:T(4,128)S(1)} %get-tuple-element.13) | data formatting | bytes 6144 | tf_op jit(solution)/shard_map/broadcast_in_dim;reshape;squeeze | solution.py:334
  75.3 3.8 %fusion.11.i_ref = f32[6,128,256]{2,1,0:T(8,128)} fusion(f32[6,1,256]{2,1,0:T(1,128)S(1)} %get-tuple-element.33, f32[6,127,256]{2,1,0:T(8,128)} %get-tuple-element.18, f32[6,127,256]{2,1,0:T(8,128)} %get-tuple-element.17, f32[6,1,256]{2,1,0:T(1,128)S(1)} %get-tuple-element.34, f32[6,128,1]{2,1,0:T(8,128)S(1)} %broadcast_in_dim_reshape_squeeze.8, ...), kind=kLoop, calls=%fused_computation.22 | loop fusion | flops 2555904 | bytes 6425600 | tf_op jit(solution)/shard_map/mul | solution.py:420
  79.1 23.9 %shard_map.105 = f32[8,128]{1,0:T(8,128)} custom-call(f32[6,128,256]{2,1,0:T(8,128)} %bitcast.64, f32[6,128,256]{2,1,0:T(8,128)} %get-tuple-element.7.p_ref, f32[6,128,256]{2,1,0:T(8,128)} %fusion.11.i_ref), custom_call_target="tpu_custom_call" | custom-call | tf_op jit(solution)/shard_map/pallas_call | solution.py:114
  103.0 1.2 %slice.113 = f32[1,1]{1,0:T(1,128)} slice(f32[8,128]{1,0:T(8,128)} %shard_map.105), slice={[0:1], [0:1]} | slice | bytes 8 | tf_op jit(solution)/shard_map/slice | solution.py:423
  104.2 1.6 %bitcast_add_fusion = f32[128,6,256]{2,0,1:T(8,128)} fusion(f32[128,6,256]{2,0,1:T(8,128)S(1)} %copy-done.4, f32[6,128,256]{2,1,0:T(8,128)S(1)} %copy-done.2, f32[]{:T(128)} %bitcast.24), kind=kLoop, calls=%fused_computation.24 | loop fusion | flops 393216 | bytes 2359300 | tf_op jit(solution)/shard_map/add | solution.py:425
  105.8 1.6 %bitcast_subtract_fusion = f32[128,6,256]{2,0,1:T(8,128)} fusion(f32[128,6,256]{2,0,1:T(8,128)S(1)} %copy-done.6, f32[6,128,256]{2,1,0:T(8,128)S(1)} %copy-done.7, f32[]{:T(128)} %bitcast.24), kind=kLoop, calls=%fused_computation.23 | loop fusion | flops 393216 | bytes 2359300 | tf_op jit(solution)/shard_map/sub | solution.py:424
  107.4 1.3 %slice_bitcast_fusion.2 = f32[3]{0:T(128)} fusion(f32[8,128]{1,0:T(8,128)} %shard_map.105), kind=kLoop, calls=%fused_computation.75 | loop fusion | bytes 24 | tf_op jit(solution)/shard_map/slice | solution.py:426
  (64 shorter events, 1.7 us)
Async XLA Ops:
  0.6 16.8 %copy-start = (f32[4,6]{1,0:T(4,128)S(1)}, f32[4,6]{1,0:T(4,128)}, u32[]{:S(2)}) copy-start(f32[4,6]{1,0:T(4,128)} %param.13) | copy-start | bytes 292
  0.6 16.5 %copy-start.11 = (f32[6,6,1024]{2,1,0:T(8,128)S(1)}, f32[6,6,1024]{2,1,0:T(8,128)}, u32[]{:S(2)}) copy-start(f32[6,6,1024]{2,1,0:T(8,128)} %param.14) | copy-start | bytes 442372
  0.7 16.8 %copy-start.16 = (s32[128]{0:T(128)S(1)}, s32[128]{0:T(128)}, u32[]{:S(2)}) copy-start(s32[128]{0:T(128)} %param.12) | copy-start | bytes 1540
  2.8 18.6 %collective-permute-start.3 = (f32[128,6,1]{2,0,1:T(8,128)}, f32[128,6,1]{2,0,1:T(8,128)}, u32[]{:S(2)}, u32[]{:S(2)}) collective-permute-start(f32[128,6,1]{2,0,1:T(8,128)} %get-tuple-element.22), channel_id=1, source_target_pairs={{0,1},{1,2},{2,3},{3,0},{4,5},{5,6},{6,7},{7,4},{8,9},{9,10},{10,1... | collective-permute-start | bytes 9224 | tf_op jit(solution)/shard_map/ppermute | solution.py:324
  2.8 18.6 %collective-permute-start.2 = (f32[128,6,1]{2,0,1:T(8,128)}, f32[128,6,1]{2,0,1:T(8,128)}, u32[]{:S(2)}, u32[]{:S(2)}) collective-permute-start(f32[128,6,1]{2,0,1:T(8,128)} %get-tuple-element.21), channel_id=1, source_target_pairs={{1,0},{2,1},{3,2},{0,3},{5,4},{6,5},{7,6},{4,7},{9,8},{10,9},{11,1... | collective-permute-start | bytes 9224 | tf_op jit(solution)/shard_map/ppermute | solution.py:325
  6.9 14.6 %collective-permute-start.1 = (f32[1,6,256]{2,0,1:T(1,128)S(1)}, f32[1,6,256]{2,0,1:T(1,128)S(1)}, u32[]{:S(2)}, u32[]{:S(2)}) collective-permute-start(f32[1,6,256]{2,0,1:T(1,128)S(1)} %get-tuple-element.20), channel_id=1, source_target_pairs={{0,4},{4,8},{8,12},{12,16},{16,20},{20,24},{24,28},{28,32},{32,36}... | collective-permute-start | bytes 18440 | tf_op jit(solution)/shard_map/ppermute | solution.py:324
  10.0 11.5 %collective-permute-start = (f32[1,6,256]{2,0,1:T(1,128)S(1)}, f32[1,6,256]{2,0,1:T(1,128)S(1)}, u32[]{:S(2)}, u32[]{:S(2)}) collective-permute-start(f32[1,6,256]{2,0,1:T(1,128)S(1)} %get-tuple-element.19), channel_id=1, source_target_pairs={{4,0},{8,4},{12,8},{16,12},{20,16},{24,20},{28,24},{32,28},{36,32}... | collective-permute-start | bytes 18440 | tf_op jit(solution)/shard_map/ppermute | solution.py:325
  14.4 7.1 %copy-start.10 = (f32[128,256]{1,0:T(8,128)}, f32[128,256]{1,0:T(8,128)S(1)}, u32[]{:S(2)}) copy-start(f32[128,256]{1,0:T(8,128)S(1)} %get-tuple-element.23) | copy-start | bytes 393220
  14.4 7.1 %copy-start.4 = (f32[128,6,256]{2,0,1:T(8,128)S(1)}, f32[128,6,256]{2,0,1:T(8,128)}, u32[]{:S(2)}) copy-start(f32[128,6,256]{2,0,1:T(8,128)} %param.9) | copy-start | bytes 2359300
  14.4 7.1 %copy-start.9 = (f32[128,6,256]{2,0,1:T(8,128)S(1)}, f32[128,6,256]{2,0,1:T(8,128)}, u32[]{:S(2)}) copy-start(f32[128,6,256]{2,0,1:T(8,128)} %param.10) | copy-start | bytes 2359300
  23.6 23.3 %copy-start.5 = (f32[128,6,256]{2,0,1:T(8,128)}, f32[128,6,256]{2,0,1:T(8,128)S(1)}, u32[]{:S(2)}) copy-start(f32[128,6,256]{2,0,1:T(8,128)S(1)} %fusion.4) | copy-start | bytes 2359300
  41.5 5.8 %copy-start.3 = (f32[32,32,1024]{2,1,0:T(8,128)S(1)}, f32[32,32,1024]{2,1,0:T(8,128)}, u32[]{:S(2)}) copy-start(f32[32,32,1024]{2,1,0:T(8,128)} %multiply_subtract_fusion) | copy-start | bytes 12582916
  47.3 2.5 %copy-start.15 = (s32[2,4]{1,0:T(2,128)S(1)}, s32[2,4]{1,0:T(2,128)}, u32[]{:S(2)}) copy-start(s32[2,4]{1,0:T(2,128)} %constant.77) | copy-start | bytes 100
  49.8 3.1 %copy-start.8 = (f32[6,32,1024]{2,1,0:T(8,128)}, f32[6,32,1024]{2,1,0:T(8,128)S(1)}, u32[]{:S(2)}) copy-start(f32[6,32,1024]{2,1,0:T(8,128)S(1)} %broadcast_multiply_fusion.x_ref) | copy-start | bytes 2359300
  69.1 2.8 %copy-start.1 = (f32[6,128,256]{2,1,0:T(8,128)S(1)}, f32[6,128,256]{2,1,0:T(8,128)}, u32[]{:S(2)}) copy-start(f32[6,128,256]{2,1,0:T(8,128)} %get-tuple-element.7.p_ref) | copy-start | bytes 2359300
  69.1 4.2 %copy-start.13 = (f32[4,8,256]{2,1,0:T(8,128)S(1)}, f32[4,8,256]{2,1,0:T(8,128)}, u32[]{:S(2)}) copy-start(f32[4,8,256]{2,1,0:T(8,128)} %get-tuple-element.8) | copy-start | bytes 98308
  69.1 4.2 %copy-start.12 = (f32[4,8,256]{2,1,0:T(8,128)S(1)}, f32[4,8,256]{2,1,0:T(8,128)}, u32[]{:S(2)}) copy-start(f32[4,8,256]{2,1,0:T(8,128)} %get-tuple-element.9) | copy-start | bytes 98308
  69.1 4.2 %copy-start.14 = (f32[4,8,128]{2,1,0:T(8,128)S(1)}, f32[4,8,128]{2,1,0:T(8,128)}, u32[]{:S(2)}) copy-start(f32[4,8,128]{2,1,0:T(8,128)} %get-tuple-element.10) | copy-start | bytes 49156
  75.2 28.9 %copy-start.2 = (f32[6,128,256]{2,1,0:T(8,128)S(1)}, f32[6,128,256]{2,1,0:T(8,128)}, u32[]{:S(2)}) copy-start(f32[6,128,256]{2,1,0:T(8,128)} %get-tuple-element.7.p_ref) | copy-start | bytes 2359300
  75.3 30.5 %copy-start.6 = (f32[128,6,256]{2,0,1:T(8,128)S(1)}, f32[128,6,256]{2,0,1:T(8,128)}, u32[]{:S(2)}) copy-start(f32[128,6,256]{2,0,1:T(8,128)} %copy-done.5) | copy-start | bytes 2359300
  79.1 26.7 %copy-start.7 = (f32[6,128,256]{2,1,0:T(8,128)S(1)}, f32[6,128,256]{2,1,0:T(8,128)}, u32[]{:S(2)}) copy-start(f32[6,128,256]{2,1,0:T(8,128)} %fusion.11.i_ref) | copy-start | bytes 2359300

commit v8 on v7

--- a/solution.py
+++ b/solution.py
@@ -31,21 +31,29 @@
     ]
 
 
-def _local_sums(r_ref, p_ref, i_ref):
-    rows = r_ref.shape[0]
-    plane = r_ref.shape[1:]
-
-    def body(k, acc):
-        r, p, i = r_ref[k], p_ref[k], i_ref[k]
-        return (acc[0] + r * p, acc[1] + p * i, acc[2] + r * r, acc[3] + r * i, acc[4] + i * i)
-
-    zero = jnp.zeros(plane, jnp.float32)
-    acc = lax.fori_loop(0, rows, body, (zero,) * 5, unroll=8)
-    lane = lax.broadcasted_iota(jnp.int32, (8, 128), 1)
-    row = lax.broadcasted_iota(jnp.int32, (8, 128), 0)
+def _image_and_sums(r_ref, p_ref, s_ref, m_ref, hr_ref, hc_ref, img_ref):
+    comps, rows, width = p_ref.shape
+    row = lax.broadcasted_iota(jnp.int32, (rows, width), 0)
+    lane = lax.broadcasted_iota(jnp.int32, (rows, width), 1)
+    solid = m_ref[...]
+    acc = [jnp.zeros((1, width), jnp.float32) for _ in range(5)]
+    for q in range(comps):
+        field = p_ref[q]
+        up = jnp.where(row == 0, hr_ref[0, q : q + 1, :], pltpu.roll(field, 1, 0))
+        down = jnp.where(row == rows - 1, hr_ref[1, q : q + 1, :], pltpu.roll(field, rows - 1, 0))
+        left = jnp.where(lane == 0, hc_ref[0, q], pltpu.roll(field, 1, 1))
+        right = jnp.where(lane == width - 1, hc_ref[1, q], pltpu.roll(field, width - 1, 1))
+        beside = down + up + right + left
+        image = solid * ((s_ref[q] + 4.5) * field - beside - 0.5 * p_ref[q ^ 1])
+        img_ref[q] = image
+        res = r_ref[q]
+        for k, prod in enumerate((res * field, field * image, res * res, res * image, image * image)):
+            acc[k] = acc[k] + jnp.sum(prod, axis=0, keepdims=True)
+    lane8 = lax.broadcasted_iota(jnp.int32, (8, 128), 1)
+    row8 = lax.broadcasted_iota(jnp.int32, (8, 128), 0)
     packed = jnp.zeros((8, 128), jnp.float32)
     for k, a in enumerate(acc):
-        packed = jnp.where((row == 0) & (lane == k), jnp.sum(a), packed)
+        packed = jnp.where((row8 == 0) & (lane8 == k), jnp.sum(a), packed)
     return packed
 
 
@@ -66,7 +74,7 @@
     return out
 
 
-def _ar_kernel(cell_total, r_ref, p_ref, i_ref, o_ref, recv_a, recv_b, own, send_sems, recv_sems):
+def _ar_kernel(cell_total, r_ref, p_ref, s_ref, m_ref, hr_ref, hc_ref, o_ref, img_ref, recv_a, recv_b, own, send_sems, recv_sems):
     recvs = (recv_a, recv_b)
     groups = _groups()
     for r in recvs:
@@ -77,7 +85,7 @@
         for d in range(1, n):
             pl.semaphore_signal(barrier, inc=1, device_id=dev((mine + d) % n), device_id_type=MESH)
             count += 1
-    own[0] = _local_sums(r_ref, p_ref, i_ref)
+    own[0] = _image_and_sums(r_ref, p_ref, s_ref, m_ref, hr_ref, hc_ref, img_ref)
     pl.semaphore_wait(barrier, count)
     base = 0
     for g, (n, mine, dev) in enumerate(groups):
@@ -110,12 +118,15 @@
             o_ref[...] = _finish(total, cell_total)
 
 
-def all_sums(residual, prec, image, cell_total, cid):
+def image_and_totals(residual, prec, stiffness, solid, halo_rows, halo_cols, cell_total, cid):
     return pl.pallas_call(
         functools.partial(_ar_kernel, float(cell_total)),
-        out_shape=jax.ShapeDtypeStruct((8, 128), jnp.float32),
-        in_specs=[pl.BlockSpec(memory_space=pltpu.VMEM)] * 3,
-        out_specs=pl.BlockSpec(memory_space=pltpu.VMEM),
+        out_shape=[
+            jax.ShapeDtypeStruct((8, 128), jnp.float32),
+            jax.ShapeDtypeStruct(prec.shape, jnp.float32),
+        ],
+        in_specs=[pl.BlockSpec(memory_space=pltpu.VMEM)] * 6,
+        out_specs=[pl.BlockSpec(memory_space=pltpu.VMEM)] * 2,
         scratch_shapes=[
             pltpu.VMEM((32, 8, 128), jnp.float32),
             pltpu.VMEM((8, 8, 128), jnp.float32),
@@ -124,7 +135,7 @@
             pltpu.SemaphoreType.DMA((40,)),
         ],
         compiler_params=pltpu.CompilerParams(collective_id=cid, has_side_effects=True),
-    )(residual, prec, image)
+    )(residual, prec, stiffness, solid, halo_rows, halo_cols)
 
 
 def _to_lines_kernel(n, x_ref, o_ref, send_sems, recv_sems, local_sem):
@@ -325,14 +336,6 @@
         after = lax.ppermute(first, axis, down)
         x = jnp.concatenate([before, x, after], axis=dim)
     return x
-
-
-def stencil_from_halo(field, before_row, after_row, before_col, after_col):
-    down = jnp.concatenate([field[:, 1:], after_row[:, None]], axis=1)
-    up = jnp.concatenate([before_row[:, None], field[:, :-1]], axis=1)
-    right = jnp.concatenate([field[:, :, 1:], after_col[:, :, None]], axis=2)
-    left = jnp.concatenate([before_col[:, :, None], field[:, :, :-1]], axis=2)
-    return down + up + right + left
 
 
 def swap_channels(field):
@@ -415,11 +418,14 @@
     got_cols = got_cols.reshape(comp_count, sector_count, 2, group_rows)
     before_col = got_cols[:, :, 0].reshape(comp_count, slab_count)
     after_col = got_cols[:, :, 1].reshape(comp_count, slab_count)
-    beside = stencil_from_halo(prec_t, before_row, after_row, before_col, after_col)
     stiffness_t = jnp.transpose(stiffness, (1, 0, 2))
-    image_t = solid_t * ((stiffness_t + 4.5) * prec_t - beside - 0.5 * swap_channels(prec_t))
+    halo_rows = jnp.pad(jnp.stack([before_row, after_row]), ((0, 0), (0, subl - comp_count), (0, 0)))
+    halo_cols = jnp.stack([before_col, after_col])[..., None]
     cell_total = slab_count * lax.axis_size("ax") * comp_count * around_cells
-    finished = all_sums(residual_t, prec_t, image_t, cell_total, 0)[0]
+    finished, image_t = image_and_totals(
+        residual_t, prec_t, stiffness_t, solid_t[0], halo_rows, halo_cols, cell_total, 0
+    )
+    finished = finished[0]
     alpha = finished[0]
     residual_new = residual - alpha * jnp.transpose(image_t, (1, 0, 2))
     disp_new = disp + alpha * jnp.transpose(prec_t, (1, 0, 2))

time: 111 us -> 107 us (0.964)
  local copies, waits for them, and re-layouts: 16.1 us -> 11.6 us
    mul x3 -> x0, other arithmetic: 6.02 us -> none  [the longest x1 3.84 us: shards(): solid_t * ((stiffness_t + 4.5) * prec_t - beside - 0.5 * swap_channels(pr...]
    slice x2 -> x0, local copies, waits for them, and re-layouts: 4.17 us -> none  [the longest x1 2.73 us: stencil_from_halo(): up = jnp.concatenate([before_row[:, None], field[:, :-1]], axis=1)]
    transpose x0 -> x1, other arithmetic: none -> 2.7 us  [shards(): stiffness_t = jnp.transpose(stiffness, (1, 0, 2))]
    another operation x3, local copies, waits for them, and re-layouts: 1.56 us -> 0.18 us  [the longest x2 0.18 us: shards(): halo_cols = jnp.stack([before_col, after_col])[..., None]]
    broadcast_in_dim x0 -> x1, local copies, waits for them, and re-layouts: none -> 1.19 us  [shards(): halo_cols = jnp.stack([before_col, after_col])[..., None]]
    sub x1, other arithmetic: 1.63 us -> 2.79 us  [shards(): residual_new = residual - alpha * jnp.transpose(image_t, (1, 0, 2))]
  transfers between devices with their start and end apart: 4 -> 4, of which waited for: 0 -> 0; matrix products, arithmetic and copies ran while one was open for 9% -> 10% of each run, Pallas kernels for 0% -> 0%
where the time goes in v8:
time: 107 us; the launch traced here: 105 us
  Pallas kernels  56.3 us (53%)
  other arithmetic  18.7 us (17%)
  local copies, waits for them, and re-layouts  11.6 us (11%)
  starting transfers between devices  9.16 us (9%)
  matrix products  7.83 us (7%)
    pallas_call x1, Pallas kernels, image_and_totals(): pl.pallas_call(functools.partial(_ar_kernel, float(cell_total)), out_shap...  24.3 us
    pallas_call x1, Pallas kernels, from_lines_with_halo(): pl.pallas_call(functools.partial(_from_lines_kernel, (n_ax, n)), out_shap...  16.3 us
    pallas_call x1, Pallas kernels, _exchange(): pl.pallas_call(functools.partial(body, n), out_shape=jax.ShapeDtypeStruct...  15.8 us
    ppermute x2, starting transfers between devices, with_halo(): after = lax.ppermute(first, axis, down)  5.97 us
    dot_general x1, matrix products, shards(): jnp.dot(lines.reshape(-1, around_cells), dft_table(around_cells), precisi...  4.31 us
    ppermute x2, starting transfers between devices, with_halo(): before = lax.ppermute(last, axis, up)  3.19 us
    sub x1, other arithmetic, shards(): residual_new = residual - alpha * jnp.transpose(image_t, (1, 0, 2))  2.79 us
    transpose x1, other arithmetic, shards(): stiffness_t = jnp.transpose(stiffness, (1, 0, 2))  2.7 us
  transfers between devices with their start and end apart: 4, of which 0 were waited for; matrix products, arithmetic and copies ran while one was open for 10% of the time, Pallas kernels for 0%

profile of v8, /device:TPU:4, one launch (start us, length us, event | category | flops | bytes accessed | tf_op | source)
XLA Modules:
  0.0 104.6 jit_solution(10898591580464406374)
XLA Ops:
  0.7 1.3 %fusion.28 = (f32[128,6,1]{2,0,1:T(8,128)S(1)}, f32[128,6,1]{2,0,1:T(8,128)S(1)}) fusion(f32[128,6,256]{2,0,1:T(8,128)} %param.9), kind=kLoop, calls=%fused_computation.73 | loop fusion | bytes 12288 | tf_op jit(solution)/shard_map/slice | solution.py:334
  2.0 3.2 %collective-permute-start.2 = (f32[128,6,1]{2,0,1:T(8,128)S(1)}, f32[128,6,1]{2,0,1:T(8,128)}, u32[]{:S(2)}, u32[]{:S(2)}) collective-permute-start(f32[128,6,1]{2,0,1:T(8,128)S(1)} %get-tuple-element.23), channel_id=1, source_target_pairs={{1,0},{2,1},{3,2},{0,3},{5,4},{6,5},{7,6},{4,7},{9,8},{10,9},{11,1... | collective-permute-start | bytes 9224 | tf_op jit(solution)/shard_map/ppermute | solution.py:336
  5.3 0.8 fusion.27
  6.1 3.1 %collective-permute-start.1 = (f32[1,6,256]{2,0,1:T(1,128)S(1)}, f32[1,6,256]{2,0,1:T(1,128)S(1)}, u32[]{:S(2)}, u32[]{:S(2)}) collective-permute-start(f32[1,6,256]{2,0,1:T(1,128)S(1)} %get-tuple-element.22), channel_id=1, source_target_pairs={{0,4},{4,8},{8,12},{12,16},{16,20},{20,24},{24,28},{28,32},{32,36}... | collective-permute-start | bytes 18440 | tf_op jit(solution)/shard_map/ppermute | solution.py:335
  9.2 2.7 %collective-permute-start = (f32[1,6,256]{2,0,1:T(1,128)S(1)}, f32[1,6,256]{2,0,1:T(1,128)S(1)}, u32[]{:S(2)}, u32[]{:S(2)}) collective-permute-start(f32[1,6,256]{2,0,1:T(1,128)S(1)} %get-tuple-element.21), channel_id=1, source_target_pairs={{4,0},{8,4},{12,8},{16,12},{20,16},{24,20},{28,24},{32,28},{36,32}... | collective-permute-start | bytes 18440 | tf_op jit(solution)/shard_map/ppermute | solution.py:336
  12.0 1.6 %subtract_convert_fusion = (f32[128,256]{1,0:T(8,128)S(1)}, f32[1,128,256]{2,1,0:T(8,128)}) fusion(s32[128,256]{1,0:T(8,128)} %param.11), kind=kLoop, calls=%fused_computation.42 | loop fusion | flops 65536 | bytes 393216 | tf_op jit(solution)/shard_map/convert_element_type | solution.py:373
  13.6 1.3 %reverse_multiply_fusion = f32[128,3,2,256]{3,0,2,1:T(8,128)S(1)} fusion(f32[128,3,2,256]{3,0,2,1:T(8,128)} %bitcast.54), kind=kLoop, calls=%fused_computation.20 | loop fusion | flops 196608 | bytes 1572864 | tf_op jit(solution)/shard_map/mul | solution.py:358
  14.9 1.0 slice.87
  16.3 1.0 maximum_add_fusion
  17.7 1.1 %fusion.20 = (f32[32,1024]{1,0:T(8,128)S(1)}, f32[32,1024]{1,0:T(8,128)S(1)}, f32[32,1024]{1,0:T(8,128)S(1)}, f32[32,1024]{1,0:T(8,128)S(1)}) fusion(s32[1024]{0:T(1024)S(1)} %pad_add_fusion, s32[32]{0:T(128)S(1)} %iota_multiply_fusion, f32[1024]{0:T(1024)S(1)} %fusion.25), kind=kLoop, calls=%fused_computation.48 | loop fusion | flops 950272 | bytes 532608 | tf_op jit(solution)/shard_map/cos | solution.py:314
  18.9 2.6 %multiply_subtract_fusion = f32[32,32,1024]{2,1,0:T(8,128)} fusion(f32[32,1024]{1,0:T(8,128)S(1)} %get-tuple-element.31, f32[32,1024]{1,0:T(8,128)S(1)} %get-tuple-element.30, f32[32,1024]{1,0:T(8,128)S(1)} %get-tuple-element.32, f32[32,1024]{1,0:T(8,128)S(1)} %get-tuple-element.29), kind=kLoop, calls=%fused_computation.1 | loop fusion | flops 3145728 | bytes 4718592 | tf_op jit(solution)/shard_map/sub | solution.py:314
  21.6 2.7 %multiply_bitcast_fusion = (f32[6,128,256]{2,1,0:T(8,128)}, f32[128,6,256]{2,0,1:T(8,128)S(1)}) fusion(f32[128,6,256]{2,0,1:T(8,128)S(1)} %copy-done.8, f32[128,6]{0,1:T(8,128)S(1)} %convolution_multiply_fusion.1, f32[128,6,256]{2,0,1:T(8,128)} %param.8, f32[128,3,2,256]{3,0,2,1:T(8,128)S(1)} %reverse_multiply_fusion, f32[128,6,256]{2,0,1:T(8,128)S(1)} %copy-done.2, ...), kind=kLoop, calls=%fused_computation.21 | loop fusion | flops 2752512 | bytes 4871168 | tf_op jit(solution)/shard_map/transpose | solution.py:421
  24.3 2.1 %pad_maximum_fusion.x_ref = f32[7,128,256]{2,1,0:T(8,128)} fusion(f32[1,128,256]{2,1,0:T(8,128)} %get-tuple-element.26, f32[6,128,256]{2,1,0:T(8,128)S(1)} %bitcast.55), kind=kLoop, calls=%fused_computation.5 | loop fusion | flops 229376 | bytes 1835008 | tf_op jit(solution)/shard_map/concatenate | solution.py:377
  26.4 15.8 %shard_map.103 = f32[7,32,1024]{2,1,0:T(8,128)} custom-call(f32[7,128,256]{2,1,0:T(8,128)} %pad_maximum_fusion.x_ref), custom_call_target="tpu_custom_call" | custom-call | tf_op jit(solution)/shard_map/pallas_call | solution.py:287
  42.2 1.1 %slice_bitcast_fusion = f32[32,1024]{1,0:T(8,128)S(1)} fusion(f32[7,32,1024]{2,1,0:T(8,128)} %shard_map.103), kind=kLoop, calls=%fused_computation.41 | loop fusion | bytes 262144 | tf_op jit(solution)/shard_map/mul | solution.py:389
  43.3 4.3 %fusion.29 = f32[6,32,1024]{2,1,0:T(8,128)S(1)} fusion(f32[7,32,1024]{2,1,0:T(8,128)} %shard_map.103, f32[1024,1024,1]{1,0,2:T(8,128)} %bitcast.52), kind=kOutput, calls=%fused_computation.74 | convolution fusion | flops 1207959552 | bytes 5898240 | tf_op jit(solution)/shard_map/dot_general | solution.py:379
  47.6 0.3 multiply_reduce_fusion
  48.0 2.4 %bitcast_multiply_fusion = (f32[192,1024]{1,0:T(8,128)S(1)}, f32[192,1024]{1,0:T(8,128)S(1)}) fusion(f32[32,1024]{1,0:T(8,128)S(1)} %slice_bitcast_fusion, f32[192,1024]{1,0:T(8,128)S(1)} %bitcast.57, f32[1024,1024]{1,0:T(8,128)S(1)} %bitcast.53), kind=kOutput, calls=%fused_computation.19 | convolution fusion | flops 1208352768 | bytes 6684672 | tf_op jit(solution)/shard_map/dot_general | solution.py:383
  50.5 0.9 convolution_bitcast_fusion
  51.5 0.6 pad.15.cpk_ref
  52.3 0.6 pad.16.last_ref
  52.9 0.6 pad.17.first_ref
  53.5 16.3 %shard_map.104 = (f32[6,128,256]{2,1,0:T(8,128)}, f32[4,8,128]{2,1,0:T(8,128)}, f32[4,8,256]{2,1,0:T(8,128)}, f32[4,8,256]{2,1,0:T(8,128)}) custom-call(f32[6,32,1024]{2,1,0:T(8,128)} %copy-done.5, f32[4,8,128]{2,1,0:T(8,128)} %pad.15.cpk_ref, f32[4,8,256]{2,1,0:T(8,128)} %pad.16.last_ref, f32[4,8,256]{2,1,0:T(8,128)} %pad.17.first_ref), custom_call_target="tpu_custom_call" | custom-call | tf_op jit(solution)/shard_map/pallas_call | solution.py:272
  69.8 0.8 slice_bitcast_fusion.1
  71.0 1.2 %copy.25.hc_ref = f32[2,6,128,1]{3,2,1,0:T(8,128)} copy(f32[2,6,128,1]{2,0,1,3:T(2,128)S(1)} %maximum_bitcast_fusion) | data formatting | bytes 12288 | tf_op jit(solution)/shard_map/broadcast_in_dim | solution.py:423
  72.1 0.7 slice_select_fusion
  72.9 0.6 select_maximum_fusion.hr_ref
  73.5 24.3 %shard_map.105 = (f32[8,128]{1,0:T(8,128)}, f32[6,128,256]{2,1,0:T(8,128)}) custom-call(f32[6,128,256]{2,1,0:T(8,128)} %bitcast.56, f32[6,128,256]{2,1,0:T(8,128)} %get-tuple-element.9.p_ref, f32[6,128,256]{2,1,0:T(8,128)} %get-tuple-element.19.s_ref, f32[128,256]{1,0:T(8,128)} %copy-done.7, f32[2,8,256]{2,1,0:T(8,128)} %select_maximum_fusion.hr_ref, ...), custom_call_target="tpu_custom_call" | custom-call | tf_op jit(solution)/shard_map/pallas_call | solution.py:122
  97.7 1.2 %slice.97 = f32[1,1]{1,0:T(1,128)} slice(f32[8,128]{1,0:T(8,128)} %get-tuple-element.13), slice={[0:1], [0:1]} | slice | bytes 8 | tf_op jit(solution)/shard_map/slice | solution.py:429
  98.9 1.2 %slice_bitcast_fusion.2 = f32[3]{0:T(128)} fusion(f32[8,128]{1,0:T(8,128)} %get-tuple-element.13), kind=kLoop, calls=%fused_computation.68 | loop fusion | bytes 24 | tf_op jit(solution)/shard_map/slice | solution.py:432
  100.2 1.6 %bitcast_add_fusion = f32[128,6,256]{2,0,1:T(8,128)} fusion(f32[128,6,256]{2,0,1:T(8,128)S(1)} %copy-done.2, f32[6,128,256]{2,1,0:T(8,128)S(1)} %copy-done.6, f32[]{:T(128)} %bitcast.21), kind=kLoop, calls=%fused_computation.18 | loop fusion | flops 393216 | bytes 2359300 | tf_op jit(solution)/shard_map/add | solution.py:431
  101.8 2.8 %bitcast_subtract_fusion = f32[128,6,256]{2,0,1:T(8,128)} fusion(f32[128,6,256]{2,0,1:T(8,128)S(1)} %copy-done.4, f32[6,128,256]{2,1,0:T(8,128)} %get-tuple-element.14, f32[]{:T(128)} %bitcast.21), kind=kLoop, calls=%fused_computation.17 | loop fusion | flops 393216 | bytes 2359300 | tf_op jit(solution)/shard_map/sub | solution.py:430
  (49 shorter events, 1.7 us)
Async XLA Ops:
  0.6 16.9 %copy-start = (f32[4,6]{1,0:T(4,128)S(1)}, f32[4,6]{1,0:T(4,128)}, u32[]{:S(2)}) copy-start(f32[4,6]{1,0:T(4,128)} %param.13) | copy-start | bytes 292
  0.6 16.9 %copy-start.10 = (s32[128]{0:T(128)S(1)}, s32[128]{0:T(128)}, u32[]{:S(2)}) copy-start(s32[128]{0:T(128)} %param.12) | copy-start | bytes 1540
  1.9 19.6 %collective-permute-start.3 = (f32[128,6,1]{2,0,1:T(8,128)S(1)}, f32[128,6,1]{2,0,1:T(8,128)}, u32[]{:S(2)}, u32[]{:S(2)}) collective-permute-start(f32[128,6,1]{2,0,1:T(8,128)S(1)} %get-tuple-element.24), channel_id=1, source_target_pairs={{0,1},{1,2},{2,3},{3,0},{4,5},{5,6},{6,7},{7,4},{8,9},{9,10},{10,1... | collective-permute-start | bytes 9224 | tf_op jit(solution)/shard_map/ppermute | solution.py:335
  2.0 19.5 %collective-permute-start.2 = (f32[128,6,1]{2,0,1:T(8,128)S(1)}, f32[128,6,1]{2,0,1:T(8,128)}, u32[]{:S(2)}, u32[]{:S(2)}) collective-permute-start(f32[128,6,1]{2,0,1:T(8,128)S(1)} %get-tuple-element.23), channel_id=1, source_target_pairs={{1,0},{2,1},{3,2},{0,3},{5,4},{6,5},{7,6},{4,7},{9,8},{10,9},{11,1... | collective-permute-start | bytes 9224 | tf_op jit(solution)/shard_map/ppermute | solution.py:336
  6.1 15.5 %collective-permute-start.1 = (f32[1,6,256]{2,0,1:T(1,128)S(1)}, f32[1,6,256]{2,0,1:T(1,128)S(1)}, u32[]{:S(2)}, u32[]{:S(2)}) collective-permute-start(f32[1,6,256]{2,0,1:T(1,128)S(1)} %get-tuple-element.22), channel_id=1, source_target_pairs={{0,4},{4,8},{8,12},{12,16},{16,20},{20,24},{24,28},{28,32},{32,36}... | collective-permute-start | bytes 18440 | tf_op jit(solution)/shard_map/ppermute | solution.py:335
  9.2 12.4 %collective-permute-start = (f32[1,6,256]{2,0,1:T(1,128)S(1)}, f32[1,6,256]{2,0,1:T(1,128)S(1)}, u32[]{:S(2)}, u32[]{:S(2)}) collective-permute-start(f32[1,6,256]{2,0,1:T(1,128)S(1)} %get-tuple-element.21), channel_id=1, source_target_pairs={{4,0},{8,4},{12,8},{16,12},{20,16},{24,20},{28,24},{32,28},{36,32}... | collective-permute-start | bytes 18440 | tf_op jit(solution)/shard_map/ppermute | solution.py:336
  13.6 8.0 %copy-start.7 = (f32[128,256]{1,0:T(8,128)}, f32[128,256]{1,0:T(8,128)S(1)}, u32[]{:S(2)}) copy-start(f32[128,256]{1,0:T(8,128)S(1)} %get-tuple-element.25.m_ref) | copy-start | bytes 393220
  13.6 8.0 %copy-start.2 = (f32[128,6,256]{2,0,1:T(8,128)S(1)}, f32[128,6,256]{2,0,1:T(8,128)}, u32[]{:S(2)}) copy-start(f32[128,6,256]{2,0,1:T(8,128)} %param.9) | copy-start | bytes 2359300
  13.6 8.0 %copy-start.8 = (f32[128,6,256]{2,0,1:T(8,128)S(1)}, f32[128,6,256]{2,0,1:T(8,128)}, u32[]{:S(2)}) copy-start(f32[128,6,256]{2,0,1:T(8,128)} %param.10) | copy-start | bytes 2359300
  24.3 23.2 %copy-start.3 = (f32[128,6,256]{2,0,1:T(8,128)}, f32[128,6,256]{2,0,1:T(8,128)S(1)}, u32[]{:S(2)}) copy-start(f32[128,6,256]{2,0,1:T(8,128)S(1)} %get-tuple-element.20) | copy-start | bytes 2359300
  42.2 5.8 %copy-start.1 = (f32[32,32,1024]{2,1,0:T(8,128)S(1)}, f32[32,32,1024]{2,1,0:T(8,128)}, u32[]{:S(2)}) copy-start(f32[32,32,1024]{2,1,0:T(8,128)} %multiply_subtract_fusion) | copy-start | bytes 12582916
  47.9 2.5 %copy-start.9 = (s32[2,4]{1,0:T(2,128)S(1)}, s32[2,4]{1,0:T(2,128)}, u32[]{:S(2)}) copy-start(s32[2,4]{1,0:T(2,128)} %constant.77) | copy-start | bytes 100
  50.4 3.1 %copy-start.5 = (f32[6,32,1024]{2,1,0:T(8,128)}, f32[6,32,1024]{2,1,0:T(8,128)S(1)}, u32[]{:S(2)}) copy-start(f32[6,32,1024]{2,1,0:T(8,128)S(1)} %broadcast_multiply_fusion.x_ref) | copy-start | bytes 2359300
  50.5 51.4 %copy-start.4 = (f32[128,6,256]{2,0,1:T(8,128)S(1)}, f32[128,6,256]{2,0,1:T(8,128)}, u32[]{:S(2)}) copy-start(f32[128,6,256]{2,0,1:T(8,128)} %copy-done.3) | copy-start | bytes 2359300
  69.8 30.4 %copy-start.6 = (f32[6,128,256]{2,1,0:T(8,128)S(1)}, f32[6,128,256]{2,1,0:T(8,128)}, u32[]{:S(2)}) copy-start(f32[6,128,256]{2,1,0:T(8,128)} %get-tuple-element.9.p_ref) | copy-start | bytes 2359300

commit v9 on v8

--- a/solution.py
+++ b/solution.py
@@ -74,7 +74,8 @@
     return out
 
 
-def _ar_kernel(cell_total, r_ref, p_ref, s_ref, m_ref, hr_ref, hc_ref, o_ref, img_ref, recv_a, recv_b, own, send_sems, recv_sems):
+def _ar_kernel(cell_total, r_ref, p_ref, s_ref, m_ref, hr_ref, hc_ref, d_ref, o_ref, img_ref, dn_ref,
+               rn_ref, recv_a, recv_b, own, send_sems, recv_sems):
     recvs = (recv_a, recv_b)
     groups = _groups()
     for r in recvs:
@@ -115,18 +116,25 @@
         if g + 1 < len(groups):
             own[g + 1] = total
         else:
-            o_ref[...] = _finish(total, cell_total)
-
-
-def image_and_totals(residual, prec, stiffness, solid, halo_rows, halo_cols, cell_total, cid):
+            finished = _finish(total, cell_total)
+            o_ref[...] = finished
+            alpha = finished[0:1, 0:1]
+            for q in range(p_ref.shape[0]):
+                dn_ref[q] = d_ref[q] + alpha * p_ref[q]
+                rn_ref[q] = r_ref[q] - alpha * img_ref[q]
+
+
+def image_and_totals(residual, prec, stiffness, solid, halo_rows, halo_cols, disp, cell_total, cid):
     return pl.pallas_call(
         functools.partial(_ar_kernel, float(cell_total)),
         out_shape=[
             jax.ShapeDtypeStruct((8, 128), jnp.float32),
             jax.ShapeDtypeStruct(prec.shape, jnp.float32),
+            jax.ShapeDtypeStruct(prec.shape, jnp.float32),
+            jax.ShapeDtypeStruct(prec.shape, jnp.float32),
         ],
-        in_specs=[pl.BlockSpec(memory_space=pltpu.VMEM)] * 6,
-        out_specs=[pl.BlockSpec(memory_space=pltpu.VMEM)] * 2,
+        in_specs=[pl.BlockSpec(memory_space=pltpu.VMEM)] * 7,
+        out_specs=[pl.BlockSpec(memory_space=pltpu.VMEM)] * 4,
         scratch_shapes=[
             pltpu.VMEM((32, 8, 128), jnp.float32),
             pltpu.VMEM((8, 8, 128), jnp.float32),
@@ -135,38 +143,61 @@
             pltpu.SemaphoreType.DMA((40,)),
         ],
         compiler_params=pltpu.CompilerParams(collective_id=cid, has_side_effects=True),
-    )(residual, prec, stiffness, solid, halo_rows, halo_cols)
-
-
-def _to_lines_kernel(n, x_ref, o_ref, send_sems, recv_sems, local_sem):
+    )(residual, prec, stiffness, solid, halo_rows, halo_cols, disp)
+
+
+def _to_lines_kernel(n, count, *refs):
+    x_refs, o_refs = refs[:count], refs[count : 2 * count]
+    send_sems, recv_sems, local_sems = refs[2 * count :]
     me = lax.axis_index("sec")
     ax = lax.axis_index("ax")
-    rows, width = o_ref.shape[1], x_ref.shape[2]
     barrier = pltpu.get_barrier_semaphore()
     for d in range(1, n):
         pl.semaphore_signal(barrier, inc=1, device_id=(ax, (me + d) % n), device_id_type=MESH)
     pl.semaphore_wait(barrier, n - 1)
-    dst = o_ref.at[:, :, pl.ds(pl.multiple_of(me * width, width), width)]
-    copies = []
-    for d in range(1, n):
-        peer = (me + d) % n
-        cp = pltpu.make_async_remote_copy(
-            src_ref=x_ref.at[:, pl.ds(pl.multiple_of(peer * rows, rows), rows), :],
-            dst_ref=dst,
-            send_sem=send_sems.at[d],
-            recv_sem=recv_sems.at[d],
-            device_id=(ax, peer),
-            device_id_type=MESH,
+    copies, local = [], []
+    for i, (x_ref, o_ref) in enumerate(zip(x_refs, o_refs)):
+        rows, width = o_ref.shape[1], x_ref.shape[2]
+        dst = o_ref.at[:, :, pl.ds(pl.multiple_of(me * width, width), width)]
+        for d in range(1, n):
+            peer = (me + d) % n
+            cp = pltpu.make_async_remote_copy(
+                src_ref=x_ref.at[:, pl.ds(pl.multiple_of(peer * rows, rows), rows), :],
+                dst_ref=dst,
+                send_sem=send_sems.at[i * n + d],
+                recv_sem=recv_sems.at[i * n + d],
+                device_id=(ax, peer),
+                device_id_type=MESH,
+            )
+            cp.start()
+            copies.append(cp)
+        local.append(
+            pltpu.make_async_copy(
+                x_ref.at[:, pl.ds(pl.multiple_of(me * rows, rows), rows), :], dst, local_sems.at[i]
+            )
         )
-        cp.start()
-        copies.append(cp)
-    local = pltpu.make_async_copy(
-        x_ref.at[:, pl.ds(pl.multiple_of(me * rows, rows), rows), :], dst, local_sem
-    )
-    local.start()
-    local.wait()
+        local[-1].start()
+    for cp in local:
+        cp.wait()
     for cp in copies:
         cp.wait()
+
+
+def to_lines(arrays, n):
+    count = len(arrays)
+    shapes = [(x.shape[0], x.shape[1] // n, x.shape[2] * n) for x in arrays]
+    return pl.pallas_call(
+        functools.partial(_to_lines_kernel, n, count),
+        out_shape=[jax.ShapeDtypeStruct(s, x.dtype) for s, x in zip(shapes, arrays)],
+        in_specs=[pl.BlockSpec(memory_space=pltpu.VMEM)] * count,
+        out_specs=[pl.BlockSpec(memory_space=pltpu.VMEM)] * count,
+        scratch_shapes=[
+            pltpu.SemaphoreType.DMA((count * n,)),
+            pltpu.SemaphoreType.DMA((count * n,)),
+            pltpu.SemaphoreType.DMA((count,)),
+        ],
+        compiler_params=pltpu.CompilerParams(collective_id=1, has_side_effects=True),
+    )(*arrays)
 
 
 def _from_lines_kernel(sizes, x_ref, cpk_ref, last_ref, first_ref, o_ref, cols_ref, before_ref,
@@ -283,26 +314,6 @@
     )(x, cpk, last, first)
 
 
-def _exchange(body, out_shape, cid, n, x):
-    return pl.pallas_call(
-        functools.partial(body, n),
-        out_shape=jax.ShapeDtypeStruct(out_shape, x.dtype),
-        in_specs=[pl.BlockSpec(memory_space=pltpu.VMEM)],
-        out_specs=pl.BlockSpec(memory_space=pltpu.VMEM),
-        scratch_shapes=[
-            pltpu.SemaphoreType.DMA((n,)),
-            pltpu.SemaphoreType.DMA((n,)),
-            pltpu.SemaphoreType.DMA,
-        ],
-        compiler_params=pltpu.CompilerParams(collective_id=cid, has_side_effects=True),
-    )(x)
-
-
-def to_lines(x, n):
-    comps, rows, width = x.shape
-    return _exchange(_to_lines_kernel, (comps, rows // n, width * n), 1, n, x)
-
-
 def dft_table(length):
     half = length // 2
     root = int(round(math.sqrt(length)))
@@ -374,8 +385,7 @@
     residual = solid * (load - apply_operator(disp, stiffness))
     residual_t = jnp.transpose(residual, (1, 0, 2))
     solid_t = jnp.transpose(solid, (1, 0, 2))
-    lines_all = to_lines(jnp.concatenate([residual_t, solid_t], axis=0), sector_count)
-    lines = lines_all[:comp_count]
+    lines, solid_lines = to_lines([residual_t, solid_t], sector_count)
     spectrum = jnp.dot(
         lines.reshape(-1, around_cells), dft_table(around_cells), precision=lax.Precision.HIGH
     ).reshape(lines.shape)
@@ -386,7 +396,7 @@
         (((1,), (1,)), ((), ())),
         precision=lax.Precision.HIGH,
     ) / around_cells
-    prec_lines = lines_all[comp_count:] * smoothed_lines.reshape(lines.shape)
+    prec_lines = solid_lines * smoothed_lines.reshape(lines.shape)
     group_rows = lines.shape[1]
     lanes = -(-2 * group_rows // 128) * 128
     subl = -(-comp_count // 8) * 8
@@ -422,14 +432,22 @@
     halo_rows = jnp.pad(jnp.stack([before_row, after_row]), ((0, 0), (0, subl - comp_count), (0, 0)))
     halo_cols = jnp.stack([before_col, after_col])[..., None]
     cell_total = slab_count * lax.axis_size("ax") * comp_count * around_cells
-    finished, image_t = image_and_totals(
-        residual_t, prec_t, stiffness_t, solid_t[0], halo_rows, halo_cols, cell_total, 0
-    )
-    finished = finished[0]
-    alpha = finished[0]
-    residual_new = residual - alpha * jnp.transpose(image_t, (1, 0, 2))
-    disp_new = disp + alpha * jnp.transpose(prec_t, (1, 0, 2))
-    return (disp_new, residual_new, finished[1:4])
+    finished, _, disp_new_t, residual_new_t = image_and_totals(
+        residual_t,
+        prec_t,
+        stiffness_t,
+        solid_t[0],
+        halo_rows,
+        halo_cols,
+        jnp.transpose(disp, (1, 0, 2)),
+        cell_total,
+        0,
+    )
+    return (
+        jnp.transpose(disp_new_t, (1, 0, 2)),
+        jnp.transpose(residual_new_t, (1, 0, 2)),
+        finished[0, 1:4],
+    )
 
 
 def solution(mesh):

time: 107 us -> 105 us (0.981); the launches traced: 105 us -> 104 us
  other arithmetic: 18.7 us -> 12.5 us
  Pallas kernels: 56.3 us -> 59.8 us
  local copies, waits for them, and re-layouts: 11.6 us -> 14.4 us
    unnamed x24, local copies, waits for them, and re-layouts: 0.47 us -> 4.66 us
    sub x1 -> x0, other arithmetic: 2.79 us -> none  [shards(): residual_new = residual - alpha * jnp.transpose(image_t, (1, 0, 2))]
    slice x2 -> x0, local copies, waits for them, and re-layouts: 2.45 us -> none  [the longest x1 1.25 us: shards(): return (disp_new, residual_new, finished[1:4])]
    concatenate x1 -> x0, other arithmetic: 2.05 us -> none  [shards(): jnp.concatenate([residual_t, solid_t], axis=0)]
    pallas_call x1, Pallas kernels: 24.3 us -> 26.2 us  [image_and_totals(): pl.pallas_call(functools.partial(_ar_kernel, float(cell_total)), out_shap...]
    add x1 -> x0, other arithmetic: 1.61 us -> none  [shards(): disp_new = disp + alpha * jnp.transpose(prec_t, (1, 0, 2))]
    convert_element_type x1 -> x0, other arithmetic: 1.58 us -> none  [shards(): solid = (1 - hole).astype(jnp.float32)[:, None, :]]
    another operation x0 -> x1, other arithmetic: none -> 1.56 us  [shards(): solid_t = jnp.transpose(solid, (1, 0, 2))]
where the time goes in v9:
time: 105 us; the launch traced here: 104 us
  Pallas kernels  59.8 us (57%)
  local copies, waits for them, and re-layouts  14.4 us (14%)
  other arithmetic  12.5 us (12%)
  starting transfers between devices  8.48 us (8%)
  matrix products  7.73 us (7%)
    pallas_call x1, Pallas kernels, image_and_totals(): pl.pallas_call(functools.partial(_ar_kernel, float(cell_total)), out_shap...  26.2 us
    pallas_call x1, Pallas kernels, from_lines_with_halo(): pl.pallas_call(functools.partial(_from_lines_kernel, (n_ax, n)), out_shap...  17.3 us
    pallas_call x1, Pallas kernels, to_lines(): pl.pallas_call(functools.partial(_to_lines_kernel, n, count), out_shape=[...  16.2 us
    ppermute x2, starting transfers between devices, with_halo(): after = lax.ppermute(first, axis, down)  5.08 us
    unnamed x24, local copies, waits for them, and re-layouts  4.66 us
    dot_general x1, matrix products, shards(): jnp.dot(lines.reshape(-1, around_cells), dft_table(around_cells), precisi...  4.22 us
    ppermute x2, starting transfers between devices, with_halo(): before = lax.ppermute(last, axis, up)  3.4 us
    transpose x1, other arithmetic, shards(): stiffness_t = jnp.transpose(stiffness, (1, 0, 2))  2.96 us
  transfers between devices with their start and end apart: 4, of which 0 were waited for; matrix products, arithmetic and copies ran while one was open for 10% of the time, Pallas kernels for 0%

profile of v9, /device:TPU:4, one launch (start us, length us, event | category | flops | bytes accessed | tf_op | source)
XLA Modules:
  0.0 103.9 jit_solution(7254879337701782097)
XLA Ops:
  0.7 2.1 %fusion.29 = (f32[128,6,1]{2,0,1:T(8,128)}, f32[128,6,1]{2,0,1:T(8,128)}) fusion(f32[128,6,256]{2,0,1:T(8,128)} %param.9), kind=kLoop, calls=%fused_computation.70 | loop fusion | bytes 12288 | tf_op jit(solution)/shard_map/slice | solution.py:345
  2.8 2.6 %collective-permute-start.2 = (f32[128,6,1]{2,0,1:T(8,128)}, f32[128,6,1]{2,0,1:T(8,128)}, u32[]{:S(2)}, u32[]{:S(2)}) collective-permute-start(f32[128,6,1]{2,0,1:T(8,128)} %get-tuple-element.29), channel_id=1, source_target_pairs={{1,0},{2,1},{3,2},{0,3},{5,4},{6,5},{7,6},{4,7},{9,8},{10,9},{11,1... | collective-permute-start | bytes 9224 | tf_op jit(solution)/shard_map/ppermute | solution.py:347
  5.4 0.8 fusion.28
  6.2 2.4 %collective-permute-start = (f32[1,6,256]{2,0,1:T(1,128)S(1)}, f32[1,6,256]{2,0,1:T(1,128)S(1)}, u32[]{:S(2)}, u32[]{:S(2)}) collective-permute-start(f32[1,6,256]{2,0,1:T(1,128)S(1)} %get-tuple-element.27), channel_id=1, source_target_pairs={{4,0},{8,4},{12,8},{16,12},{20,16},{24,20},{28,24},{32,28},{36,32}... | collective-permute-start | bytes 18440 | tf_op jit(solution)/shard_map/ppermute | solution.py:347
  8.7 3.4 %collective-permute-start.1 = (f32[1,6,256]{2,0,1:T(1,128)S(1)}, f32[1,6,256]{2,0,1:T(1,128)S(1)}, u32[]{:S(2)}, u32[]{:S(2)}) collective-permute-start(f32[1,6,256]{2,0,1:T(1,128)S(1)} %get-tuple-element.28), channel_id=1, source_target_pairs={{0,4},{4,8},{8,12},{12,16},{16,20},{20,24},{24,28},{28,32},{32,36}... | collective-permute-start | bytes 18440 | tf_op jit(solution)/shard_map/ppermute | solution.py:346
  12.1 1.6 %fusion.27 = (f32[1,128,256]{2,1,0:T(8,128)}, f32[128,256]{1,0:T(8,128)S(1)}) fusion(s32[128,256]{1,0:T(8,128)} %param.11), kind=kLoop, calls=%fused_computation.68 | loop fusion | flops 65536 | bytes 393216 | tf_op jit(solution)/shard_map/transpose;broadcast_in_dim | solution.py:387
  13.7 1.3 %reverse_multiply_fusion = f32[128,3,2,256]{3,0,2,1:T(8,128)S(1)} fusion(f32[128,3,2,256]{3,0,2,1:T(8,128)} %bitcast.52), kind=kLoop, calls=%fused_computation.18 | loop fusion | flops 196608 | bytes 1572864 | tf_op jit(solution)/shard_map/mul | solution.py:369
  15.1 1.0 slice.70
  16.1 0.3 reverse
  16.5 1.0 maximum_add_fusion
  17.7 1.1 %fusion.21 = (f32[32,1024]{1,0:T(8,128)S(1)}, f32[32,1024]{1,0:T(8,128)S(1)}, f32[32,1024]{1,0:T(8,128)S(1)}, f32[32,1024]{1,0:T(8,128)S(1)}) fusion(s32[1024]{0:T(1024)S(1)} %pad_add_fusion, s32[32]{0:T(128)S(1)} %iota_multiply_fusion, f32[1024]{0:T(1024)S(1)} %fusion.26), kind=kLoop, calls=%fused_computation.45 | loop fusion | flops 950272 | bytes 532608 | tf_op jit(solution)/shard_map/cos | solution.py:325
  18.8 0.2 convolution_multiply_fusion.1
  19.0 2.7 %multiply_subtract_fusion = f32[32,32,1024]{2,1,0:T(8,128)} fusion(f32[32,1024]{1,0:T(8,128)S(1)} %get-tuple-element.37, f32[32,1024]{1,0:T(8,128)S(1)} %get-tuple-element.36, f32[32,1024]{1,0:T(8,128)S(1)} %get-tuple-element.38, f32[32,1024]{1,0:T(8,128)S(1)} %get-tuple-element.35), kind=kLoop, calls=%fused_computation.1 | loop fusion | flops 3145728 | bytes 4718592 | tf_op jit(solution)/shard_map/sub | solution.py:325
  21.8 3.0 %multiply_bitcast_fusion = (f32[6,128,256]{2,1,0:T(8,128)}, f32[6,128,256]{2,1,0:T(8,128)}) fusion(f32[128,6,256]{2,0,1:T(8,128)S(1)} %copy-done.5, f32[128,6]{0,1:T(8,128)S(1)} %convolution_multiply_fusion.1, f32[128,6,256]{2,0,1:T(8,128)S(1)} %copy-done.6, f32[128,3,2,256]{3,0,2,1:T(8,128)S(1)} %reverse_multiply_fusion, f32[128,6,256]{2,0,1:T(8,128)S(1)} %copy-done.2, ...), kind=kLoop, calls=%fused_computation.19 | loop fusion | flops 2752512 | bytes 4871168 | tf_op jit(solution)/shard_map/transpose | solution.py:431
  24.8 16.2 %shard_map.103 = (f32[6,32,1024]{2,1,0:T(8,128)}, f32[1,32,1024]{2,1,0:T(8,128)}) custom-call(f32[6,128,256]{2,1,0:T(8,128)} %get-tuple-element.26.refs_0_.r_ref, f32[1,128,256]{2,1,0:T(8,128)} %get-tuple-element.31.refs_1_), custom_call_target="tpu_custom_call" | custom-call | tf_op jit(solution)/shard_map/pallas_call | solution.py:189
  41.0 4.2 %fusion.30 = f32[6,32,1024]{2,1,0:T(8,128)S(1)} fusion(f32[6,32,1024]{2,1,0:T(8,128)} %get-tuple-element.13, f32[1024,1024,1]{1,0,2:T(8,128)} %bitcast.50), kind=kOutput, calls=%fused_computation.71 | convolution fusion | flops 1207959552 | bytes 5767168 | tf_op jit(solution)/shard_map/dot_general | solution.py:389
  45.3 0.3 multiply_reduce_fusion
  45.7 2.4 %bitcast_multiply_fusion = (f32[192,1024]{1,0:T(8,128)S(1)}, f32[192,1024]{1,0:T(8,128)S(1)}) fusion(f32[32,1024]{1,0:T(8,128)S(1)} %bitcast.59, f32[192,1024]{1,0:T(8,128)S(1)} %bitcast.54, f32[1024,1024]{1,0:T(8,128)S(1)} %bitcast.51), kind=kOutput, calls=%fused_computation.17 | convolution fusion | flops 1208352768 | bytes 6684672 | tf_op jit(solution)/shard_map/dot_general | solution.py:393
  48.1 0.1 slice_reduce_fusion
  48.3 0.8 pad.16.last_ref
  49.0 0.6 pad.17.first_ref
  49.6 0.9 convolution_bitcast_fusion
  50.7 0.6 pad.15.cpk_ref
  51.3 17.3 %shard_map.104 = (f32[6,128,256]{2,1,0:T(8,128)}, f32[4,8,128]{2,1,0:T(8,128)}, f32[4,8,256]{2,1,0:T(8,128)}, f32[4,8,256]{2,1,0:T(8,128)}) custom-call(f32[6,32,1024]{2,1,0:T(8,128)} %copy-done.3, f32[4,8,128]{2,1,0:T(8,128)} %pad.15.cpk_ref, f32[4,8,256]{2,1,0:T(8,128)} %pad.16.last_ref, f32[4,8,256]{2,1,0:T(8,128)} %pad.17.first_ref), custom_call_target="tpu_custom_call" | custom-call | tf_op jit(solution)/shard_map/pallas_call | solution.py:303
  68.6 0.7 slice_bitcast_fusion
  69.7 1.2 %copy.25.hc_ref = f32[2,6,128,1]{3,2,1,0:T(8,128)} copy(f32[2,6,128,1]{2,0,1,3:T(2,128)S(1)} %maximum_bitcast_fusion) | data formatting | bytes 12288 | tf_op jit(solution)/shard_map/broadcast_in_dim | solution.py:433
  70.9 0.7 slice_select_fusion
  71.7 0.6 select_maximum_fusion.hr_ref
  72.3 26.2 %shard_map.105 = (f32[8,128]{1,0:T(8,128)}, f32[6,128,256]{2,1,0:T(8,128)}, f32[6,128,256]{2,1,0:T(8,128)}, f32[6,128,256]{2,1,0:T(8,128)}) custom-call(f32[6,128,256]{2,1,0:T(8,128)} %get-tuple-element.26.refs_0_.r_ref, f32[6,128,256]{2,1,0:T(8,128)} %get-tuple-element.14.p_ref, f32[6,128,256]{2,1,0:T(8,128)} %get-tuple-element.25.s_ref, ...), custom_call_target="tpu_custom_call" | custom-call | tf_op jit(solution)/shard_map/pallas_call | solution.py:128
  98.5 1.3 %slice_bitcast_fusion.1 = f32[3]{0:T(128)} fusion(f32[8,128]{1,0:T(8,128)} %get-tuple-element.20), kind=kLoop, calls=%fused_computation.65 | loop fusion | bytes 24 | tf_op jit(solution)/shard_map/squeeze | solution.py:449
  99.8 2.1 %copy.31 = f32[128,6,256]{2,0,1:T(8,128)} copy(f32[128,6,256]{2,0,1:T(8,128)} %bitcast.58) | data formatting | bytes 1572864
  101.8 2.1 %copy.32 = f32[128,6,256]{2,0,1:T(8,128)} copy(f32[128,6,256]{2,0,1:T(8,128)} %bitcast.57) | data formatting | bytes 1572864
  (44 shorter events, 1.0 us)
Async XLA Ops:
  0.6 18.1 %copy-start = (f32[4,6]{1,0:T(4,128)S(1)}, f32[4,6]{1,0:T(4,128)}, u32[]{:S(2)}) copy-start(f32[4,6]{1,0:T(4,128)} %param.13) | copy-start | bytes 292
  0.6 18.1 %copy-start.9 = (s32[128]{0:T(128)S(1)}, s32[128]{0:T(128)}, u32[]{:S(2)}) copy-start(s32[128]{0:T(128)} %param.12) | copy-start | bytes 1540
  2.8 19.0 %collective-permute-start.2 = (f32[128,6,1]{2,0,1:T(8,128)}, f32[128,6,1]{2,0,1:T(8,128)}, u32[]{:S(2)}, u32[]{:S(2)}) collective-permute-start(f32[128,6,1]{2,0,1:T(8,128)} %get-tuple-element.29), channel_id=1, source_target_pairs={{1,0},{2,1},{3,2},{0,3},{5,4},{6,5},{7,6},{4,7},{9,8},{10,9},{11,1... | collective-permute-start | bytes 9224 | tf_op jit(solution)/shard_map/ppermute | solution.py:347
  5.4 16.3 %collective-permute-start.3 = (f32[128,6,1]{2,0,1:T(8,128)}, f32[128,6,1]{2,0,1:T(8,128)}, u32[]{:S(2)}, u32[]{:S(2)}) collective-permute-start(f32[128,6,1]{2,0,1:T(8,128)} %get-tuple-element.30), channel_id=1, source_target_pairs={{0,1},{1,2},{2,3},{3,0},{4,5},{5,6},{6,7},{7,4},{8,9},{9,10},{10,1... | collective-permute-start | bytes 9224 | tf_op jit(solution)/shard_map/ppermute | solution.py:346
  6.2 15.5 %collective-permute-start = (f32[1,6,256]{2,0,1:T(1,128)S(1)}, f32[1,6,256]{2,0,1:T(1,128)S(1)}, u32[]{:S(2)}, u32[]{:S(2)}) collective-permute-start(f32[1,6,256]{2,0,1:T(1,128)S(1)} %get-tuple-element.27), channel_id=1, source_target_pairs={{4,0},{8,4},{12,8},{16,12},{20,16},{24,20},{28,24},{32,28},{36,32}... | collective-permute-start | bytes 18440 | tf_op jit(solution)/shard_map/ppermute | solution.py:347
  8.7 13.1 %collective-permute-start.1 = (f32[1,6,256]{2,0,1:T(1,128)S(1)}, f32[1,6,256]{2,0,1:T(1,128)S(1)}, u32[]{:S(2)}, u32[]{:S(2)}) collective-permute-start(f32[1,6,256]{2,0,1:T(1,128)S(1)} %get-tuple-element.28), channel_id=1, source_target_pairs={{0,4},{4,8},{8,12},{12,16},{16,20},{20,24},{24,28},{28,32},{32,36}... | collective-permute-start | bytes 18440 | tf_op jit(solution)/shard_map/ppermute | solution.py:346
  13.7 8.1 %copy-start.4 = (f32[128,256]{1,0:T(8,128)}, f32[128,256]{1,0:T(8,128)S(1)}, u32[]{:S(2)}) copy-start(f32[128,256]{1,0:T(8,128)S(1)} %get-tuple-element.32.m_ref) | copy-start | bytes 393220
  13.7 8.1 %copy-start.2 = (f32[128,6,256]{2,0,1:T(8,128)S(1)}, f32[128,6,256]{2,0,1:T(8,128)}, u32[]{:S(2)}) copy-start(f32[128,6,256]{2,0,1:T(8,128)} %param.9) | copy-start | bytes 2359300
  13.7 8.1 %copy-start.5 = (f32[128,6,256]{2,0,1:T(8,128)S(1)}, f32[128,6,256]{2,0,1:T(8,128)}, u32[]{:S(2)}) copy-start(f32[128,6,256]{2,0,1:T(8,128)} %param.10) | copy-start | bytes 2359300
  13.7 8.1 %copy-start.6 = (f32[128,6,256]{2,0,1:T(8,128)S(1)}, f32[128,6,256]{2,0,1:T(8,128)}, u32[]{:S(2)}) copy-start(f32[128,6,256]{2,0,1:T(8,128)} %param.8) | copy-start | bytes 2359300
  41.0 4.6 %copy-start.1 = (f32[32,32,1024]{2,1,0:T(8,128)S(1)}, f32[32,32,1024]{2,1,0:T(8,128)}, u32[]{:S(2)}) copy-start(f32[32,32,1024]{2,1,0:T(8,128)} %multiply_subtract_fusion) | copy-start | bytes 12582916
  41.0 4.6 %copy-start.7 = (f32[1,32,1024]{2,1,0:T(8,128)S(1)}, f32[1,32,1024]{2,1,0:T(8,128)}, u32[]{:S(2)}) copy-start(f32[1,32,1024]{2,1,0:T(8,128)} %get-tuple-element.12) | copy-start | bytes 393220
  45.6 4.0 %copy-start.8 = (s32[2,4]{1,0:T(2,128)S(1)}, s32[2,4]{1,0:T(2,128)}, u32[]{:S(2)}) copy-start(s32[2,4]{1,0:T(2,128)} %constant.77) | copy-start | bytes 100
  48.1 3.2 %copy-start.3 = (f32[6,32,1024]{2,1,0:T(8,128)}, f32[6,32,1024]{2,1,0:T(8,128)S(1)}, u32[]{:S(2)}) copy-start(f32[6,32,1024]{2,1,0:T(8,128)S(1)} %broadcast_multiply_fusion.x_ref) | copy-start | bytes 2359300

commit v10 on v9

--- a/solution.py
+++ b/solution.py
@@ -356,16 +356,29 @@
 
 
 def swap_radial(field):
-    extent = field.shape
-    folded = field.reshape(extent[0], extent[1] // 2, 2, extent[2])
-    return jnp.flip(folded, axis=2).reshape(extent)
+    comps = field.shape[1]
+    return jnp.concatenate([field[:, q ^ 1 : (q ^ 1) + 1] for q in range(comps)], axis=1)
 
 
 def apply_operator(field, stiffness):
+    rows, comps, width = field.shape
     axial_pad = with_halo(field, (("ax", 0),), 1, False)
-    sector_pad = with_halo(field, (("sec", 2),), 1, True)
+    pick = (jnp.arange(width)[None, :] == jnp.array([0, width - 1])[:, None]).astype(jnp.float32)
+    edges = lax.dot_general(
+        pick, field.reshape(-1, width), (((1,), (1,)), ((), ())), precision=lax.Precision.HIGHEST
+    )
+    size = lax.axis_size("sec")
+    up = [(i, (i + 1) % size) for i in range(size)]
+    down = [(j, i) for i, j in up]
+    before_col = lax.ppermute(edges[1:], "sec", up).reshape(rows, comps, 1)
+    after_col = lax.ppermute(edges[:1], "sec", down).reshape(rows, comps, 1)
+    lane = lax.broadcasted_iota(jnp.int32, field.shape, 2)
+    left = jnp.where(lane == 0, jnp.broadcast_to(before_col, field.shape), jnp.roll(field, 1, axis=2))
+    right = jnp.where(
+        lane == width - 1, jnp.broadcast_to(after_col, field.shape), jnp.roll(field, -1, axis=2)
+    )
     beside = axial_pad[2:] + axial_pad[:-2]
-    beside = beside + sector_pad[:, :, 2:] + sector_pad[:, :, :-2]
+    beside = beside + right + left
     return (stiffness + 4.5) * field - beside - 0.5 * swap_radial(field)
 
 

time: 105 us -> 110 us (1.048)
  local copies, waits for them, and re-layouts: 14.4 us -> 18.9 us
    unnamed x24 -> x28, local copies, waits for them, and re-layouts: 4.66 us -> 9.88 us
    ppermute x0 -> x2, starting transfers between devices: none -> 2.71 us  [the longest x1 2.71 us: apply_operator(): after_col = lax.ppermute(edges[:1], 'sec', down).reshape(rows, comps, 1)]
    ppermute x2 -> x1, starting transfers between devices: 5.08 us -> 2.43 us  [with_halo(): after = lax.ppermute(first, axis, down)]
    slice x2 -> x1, local copies, waits for them, and re-layouts: 2.95 us -> 0.61 us  [with_halo(): first = lax.slice_in_dim(x, 0, width, axis=dim)]
    mul x1 -> x0, other arithmetic: 1.34 us -> none  [apply_operator(): return (stiffness + 4.5) * field - beside - 0.5 * swap_radial(field)]
    ppermute x2 -> x1, starting transfers between devices: 3.4 us -> 3.4 us  [with_halo(): before = lax.ppermute(last, axis, up)]
  transfers between devices with their start and end apart: 4 -> 4, of which waited for: 0 -> 0; matrix products, arithmetic and copies ran while one was open for 10% -> 13% of each run, Pallas kernels for 0% -> 0%
where the time goes in v10:
time: 110 us; the launch traced here: 109 us
  Pallas kernels  59.8 us (54%)
  local copies, waits for them, and re-layouts  18.9 us (17%)
  other arithmetic  12.9 us (12%)
  starting transfers between devices  8.55 us (8%)
  matrix products  8.21 us (7%)
    pallas_call x1, Pallas kernels, image_and_totals(): pl.pallas_call(functools.partial(_ar_kernel, float(cell_total)), out_shap...  26.2 us
    pallas_call x1, Pallas kernels, from_lines_with_halo(): pl.pallas_call(functools.partial(_from_lines_kernel, (n_ax, n)), out_shap...  17.3 us
    pallas_call x1, Pallas kernels, to_lines(): pl.pallas_call(functools.partial(_to_lines_kernel, n, count), out_shape=[...  16.2 us
    unnamed x28, local copies, waits for them, and re-layouts  9.88 us
    dot_general x1, matrix products, shards(): jnp.dot(lines.reshape(-1, around_cells), dft_table(around_cells), precisi...  4.22 us
    transpose x1, other arithmetic, shards(): stiffness_t = jnp.transpose(stiffness, (1, 0, 2))  3.58 us
    ppermute x1, starting transfers between devices, with_halo(): before = lax.ppermute(last, axis, up)  3.4 us
    ppermute x1, starting transfers between devices, apply_operator(): after_col = lax.ppermute(edges[:1], 'sec', down).reshape(rows, comps, 1)  2.71 us
  transfers between devices with their start and end apart: 4, of which 0 were waited for; matrix products, arithmetic and copies ran while one was open for 13% of the time, Pallas kernels for 0%

profile of v10, /device:TPU:4, one launch (start us, length us, event | category | flops | bytes accessed | tf_op | source)
XLA Modules:
  0.0 109.3 jit_solution(7498124157804193146)
XLA Ops:
  0.7 1.7 %copy.26 = f32[128,6,256]{2,1,0:T(8,128)S(1)} copy(f32[128,6,256]{2,0,1:T(8,128)} %param.10) | data formatting | bytes 1572864 | tf_op args[1]
  3.0 2.7 %collective-permute-start.2 = (f32[1,768]{1,0:T(1,128)S(1)}, f32[1,768]{1,0:T(1,128)S(1)}, u32[]{:S(2)}, u32[]{:S(2)}) collective-permute-start(f32[1,768]{1,0:T(1,128)S(1)} %get-tuple-element.37), channel_id=1, source_target_pairs={{1,0},{2,1},{3,2},{0,3},{5,4},{6,5},{7,6},{4,7},{9,8},{10,9},{11,1... | collective-permute-start | bytes 9224 | tf_op jit(solution)/shard_map/ppermute | solution.py:374
  6.3 2.4 %collective-permute-start = (f32[1,6,256]{2,0,1:T(1,128)}, f32[1,6,256]{2,0,1:T(1,128)}, u32[]{:S(2)}, u32[]{:S(2)}) collective-permute-start(f32[1,6,256]{2,0,1:T(1,128)} %get-tuple-element.31), channel_id=1, source_target_pairs={{4,0},{8,4},{12,8},{16,12},{20,16},{24,20},{28,24},{32,28},{36,32}... | collective-permute-start | bytes 18440 | tf_op jit(solution)/shard_map/ppermute | solution.py:347
  8.8 3.4 %collective-permute-start.1 = (f32[1,6,256]{2,0,1:T(1,128)}, f32[1,6,256]{2,0,1:T(1,128)}, u32[]{:S(2)}, u32[]{:S(2)}) collective-permute-start(f32[1,6,256]{2,0,1:T(1,128)} %get-tuple-element.32), channel_id=1, source_target_pairs={{0,4},{4,8},{8,12},{12,16},{16,20},{20,24},{24,28},{28,32},{32,36}... | collective-permute-start | bytes 18440 | tf_op jit(solution)/shard_map/ppermute | solution.py:346
  12.6 0.7 slice_dynamic-update-slice_fusion.5
  13.3 0.7 fusion.31
  14.0 0.7 slice_dynamic-update-slice_fusion.4
  14.7 0.7 slice_dynamic-update-slice_fusion.3
  15.4 0.7 slice_dynamic-update-slice_fusion.2
  16.0 0.7 slice_dynamic-update-slice_fusion.1
  16.7 0.7 slice_dynamic-update-slice_fusion
  17.4 1.0 slice.104
  19.0 1.0 maximum_add_fusion
  20.4 1.1 %fusion.21 = (f32[32,1024]{1,0:T(8,128)S(1)}, f32[32,1024]{1,0:T(8,128)S(1)}, f32[32,1024]{1,0:T(8,128)S(1)}, f32[32,1024]{1,0:T(8,128)S(1)}) fusion(s32[1024]{0:T(1024)S(1)} %pad_add_fusion, s32[32]{0:T(128)S(1)} %iota_multiply_fusion, f32[1024]{0:T(1024)S(1)} %fusion.26), kind=kLoop, calls=%fused_computation.50 | loop fusion | flops 950272 | bytes 532608 | tf_op jit(solution)/shard_map/cos | solution.py:325
  21.6 2.6 %multiply_subtract_fusion = f32[32,32,1024]{2,1,0:T(8,128)} fusion(f32[32,1024]{1,0:T(8,128)S(1)} %get-tuple-element.41, f32[32,1024]{1,0:T(8,128)S(1)} %get-tuple-element.40, f32[32,1024]{1,0:T(8,128)S(1)} %get-tuple-element.42, f32[32,1024]{1,0:T(8,128)S(1)} %get-tuple-element.39), kind=kLoop, calls=%fused_computation.1 | loop fusion | flops 3145728 | bytes 4718592 | tf_op jit(solution)/shard_map/sub | solution.py:325
  25.0 0.7 reduce.1
  25.9 3.6 %multiply_bitcast_fusion = (f32[6,128,256]{2,1,0:T(8,128)}, f32[6,128,256]{2,1,0:T(8,128)}) fusion(f32[128,6,256]{2,0,1:T(8,128)} %param.11, f32[128,6]{0,1:T(8,128)S(1)} %convolution_multiply_fusion.1, f32[128,6,256]{2,0,1:T(8,128)} %param.9, f32[128,6,256]{2,0,1:T(8,128)} %slice_dynamic-update-slice_fusion, f32[128,6,255]{2,0,1:T(8,128)S(1)} %get-tuple-element.29, ...), kind=kLoop, calls=%fused_computation.18 | loop fusion | flops 3342336 | bytes 6444544 | tf_op jit(solution)/shard_map/transpose | solution.py:444
  29.5 16.2 %shard_map.112 = (f32[6,32,1024]{2,1,0:T(8,128)}, f32[1,32,1024]{2,1,0:T(8,128)}) custom-call(f32[6,128,256]{2,1,0:T(8,128)} %get-tuple-element.26.refs_0_.r_ref, f32[1,128,256]{2,1,0:T(8,128)} %get-tuple-element.33.refs_1_), custom_call_target="tpu_custom_call" | custom-call | tf_op jit(solution)/shard_map/pallas_call | solution.py:189
  45.8 4.2 %fusion.36 = f32[6,32,1024]{2,1,0:T(8,128)S(1)} fusion(f32[6,32,1024]{2,1,0:T(8,128)} %get-tuple-element.13, f32[1024,1024,1]{1,0,2:T(8,128)} %bitcast.49), kind=kOutput, calls=%fused_computation.85 | convolution fusion | flops 1207959552 | bytes 5767168 | tf_op jit(solution)/shard_map/dot_general | solution.py:402
  50.4 2.4 %bitcast_multiply_fusion = (f32[192,1024]{1,0:T(8,128)S(1)}, f32[192,1024]{1,0:T(8,128)S(1)}) fusion(f32[32,1024]{1,0:T(8,128)S(1)} %bitcast.56, f32[192,1024]{1,0:T(8,128)S(1)} %bitcast.51, f32[1024,1024]{1,0:T(8,128)S(1)} %bitcast.50), kind=kOutput, calls=%fused_computation.17 | convolution fusion | flops 1208352768 | bytes 6684672 | tf_op jit(solution)/shard_map/dot_general | solution.py:406
  53.0 0.8 pad.16.last_ref
  53.7 0.6 pad.17.first_ref
  54.4 0.9 convolution_bitcast_fusion
  56.0 17.3 %shard_map.113 = (f32[6,128,256]{2,1,0:T(8,128)}, f32[4,8,128]{2,1,0:T(8,128)}, f32[4,8,256]{2,1,0:T(8,128)}, f32[4,8,256]{2,1,0:T(8,128)}) custom-call(f32[6,32,1024]{2,1,0:T(8,128)} %copy-done.3, f32[4,8,128]{2,1,0:T(8,128)} %pad.15.cpk_ref, f32[4,8,256]{2,1,0:T(8,128)} %pad.16.last_ref, f32[4,8,256]{2,1,0:T(8,128)} %pad.17.first_ref), custom_call_target="tpu_custom_call" | custom-call | tf_op jit(solution)/shard_map/pallas_call | solution.py:303
  73.4 0.7 slice_bitcast_fusion
  74.5 1.2 %copy.34.hc_ref = f32[2,6,128,1]{3,2,1,0:T(8,128)} copy(f32[2,6,128,1]{2,0,1,3:T(2,128)S(1)} %maximum_bitcast_fusion) | data formatting | bytes 12288 | tf_op jit(solution)/shard_map/broadcast_in_dim | solution.py:446
  75.6 0.7 slice_select_fusion.1
  76.3 0.7 slice_select_fusion
  77.7 26.2 %shard_map.114 = (f32[8,128]{1,0:T(8,128)}, f32[6,128,256]{2,1,0:T(8,128)}, f32[6,128,256]{2,1,0:T(8,128)}, f32[6,128,256]{2,1,0:T(8,128)}) custom-call(f32[6,128,256]{2,1,0:T(8,128)} %get-tuple-element.26.refs_0_.r_ref, f32[6,128,256]{2,1,0:T(8,128)} %get-tuple-element.14.p_ref, f32[6,128,256]{2,1,0:T(8,128)} %get-tuple-element.25.s_ref, ...), custom_call_target="tpu_custom_call" | custom-call | tf_op jit(solution)/shard_map/pallas_call | solution.py:128
  103.9 1.3 %slice_bitcast_fusion.1 = f32[3]{0:T(128)} fusion(f32[8,128]{1,0:T(8,128)} %get-tuple-element.20), kind=kLoop, calls=%fused_computation.76 | loop fusion | bytes 24 | tf_op jit(solution)/shard_map/squeeze | solution.py:462
  105.2 2.1 %copy.45 = f32[128,6,256]{2,0,1:T(8,128)} copy(f32[128,6,256]{2,0,1:T(8,128)} %bitcast.55) | data formatting | bytes 1572864
  107.2 2.1 %copy.46 = f32[128,6,256]{2,0,1:T(8,128)} copy(f32[128,6,256]{2,0,1:T(8,128)} %bitcast.54) | data formatting | bytes 1572864
  (61 shorter events, 6.0 us)
Async XLA Ops:
  0.6 19.6 %copy-start = (f32[4,6]{1,0:T(4,128)S(1)}, f32[4,6]{1,0:T(4,128)}, u32[]{:S(2)}) copy-start(f32[4,6]{1,0:T(4,128)} %param.14) | copy-start | bytes 292
  0.6 5.1 %copy-start.1 = (f32[128,6,256]{2,0,1:T(8,128)S(1)}, f32[128,6,256]{2,0,1:T(8,128)}, u32[]{:S(2)}) copy-start(f32[128,6,256]{2,0,1:T(8,128)} %param.10) | copy-start | bytes 2359300
  2.4 11.0 %copy-start.6 = (s32[128,256]{1,0:T(8,128)S(1)}, s32[128,256]{1,0:T(8,128)}, u32[]{:S(2)}) copy-start(s32[128,256]{1,0:T(8,128)} %param.12) | copy-start | bytes 393220
  3.0 17.3 %copy-start.8 = (s32[128]{0:T(128)S(1)}, s32[128]{0:T(128)}, u32[]{:S(2)}) copy-start(s32[128]{0:T(128)} %param.13) | copy-start | bytes 1540
  3.0 21.7 %collective-permute-start.2 = (f32[1,768]{1,0:T(1,128)S(1)}, f32[1,768]{1,0:T(1,128)S(1)}, u32[]{:S(2)}, u32[]{:S(2)}) collective-permute-start(f32[1,768]{1,0:T(1,128)S(1)} %get-tuple-element.37), channel_id=1, source_target_pairs={{1,0},{2,1},{3,2},{0,3},{5,4},{6,5},{7,6},{4,7},{9,8},{10,9},{11,1... | collective-permute-start | bytes 9224 | tf_op jit(solution)/shard_map/ppermute | solution.py:374
  5.7 19.2 %collective-permute-start.3 = (f32[1,768]{1,0:T(1,128)S(1)}, f32[1,768]{1,0:T(1,128)}, u32[]{:S(2)}, u32[]{:S(2)}) collective-permute-start(f32[1,768]{1,0:T(1,128)S(1)} %get-tuple-element.38), channel_id=1, source_target_pairs={{0,1},{1,2},{2,3},{3,0},{4,5},{5,6},{6,7},{7,4},{8,9},{9,10},{10,1... | collective-permute-start | bytes 9224 | tf_op jit(solution)/shard_map/ppermute | solution.py:373
  6.3 19.6 %collective-permute-start = (f32[1,6,256]{2,0,1:T(1,128)}, f32[1,6,256]{2,0,1:T(1,128)}, u32[]{:S(2)}, u32[]{:S(2)}) collective-permute-start(f32[1,6,256]{2,0,1:T(1,128)} %get-tuple-element.31), channel_id=1, source_target_pairs={{4,0},{8,4},{12,8},{16,12},{20,16},{24,20},{28,24},{32,28},{36,32}... | collective-permute-start | bytes 18440 | tf_op jit(solution)/shard_map/ppermute | solution.py:347
  8.8 17.1 %collective-permute-start.1 = (f32[1,6,256]{2,0,1:T(1,128)}, f32[1,6,256]{2,0,1:T(1,128)}, u32[]{:S(2)}, u32[]{:S(2)}) collective-permute-start(f32[1,6,256]{2,0,1:T(1,128)} %get-tuple-element.32), channel_id=1, source_target_pairs={{0,4},{4,8},{8,12},{12,16},{16,20},{20,24},{24,28},{28,32},{32,36}... | collective-permute-start | bytes 18440 | tf_op jit(solution)/shard_map/ppermute | solution.py:346
  14.0 11.9 %copy-start.4 = (f32[128,256]{1,0:T(8,128)}, f32[128,256]{1,0:T(8,128)S(1)}, u32[]{:S(2)}) copy-start(f32[128,256]{1,0:T(8,128)S(1)} %get-tuple-element.34.m_ref) | copy-start | bytes 393220
  45.7 4.6 %copy-start.2 = (f32[32,32,1024]{2,1,0:T(8,128)S(1)}, f32[32,32,1024]{2,1,0:T(8,128)}, u32[]{:S(2)}) copy-start(f32[32,32,1024]{2,1,0:T(8,128)} %multiply_subtract_fusion) | copy-start | bytes 12582916
  45.8 4.6 %copy-start.5 = (f32[1,32,1024]{2,1,0:T(8,128)S(1)}, f32[1,32,1024]{2,1,0:T(8,128)}, u32[]{:S(2)}) copy-start(f32[1,32,1024]{2,1,0:T(8,128)} %get-tuple-element.12) | copy-start | bytes 393220
  50.4 4.0 %copy-start.7 = (s32[2,4]{1,0:T(2,128)S(1)}, s32[2,4]{1,0:T(2,128)}, u32[]{:S(2)}) copy-start(s32[2,4]{1,0:T(2,128)} %constant.84) | copy-start | bytes 100
  52.8 3.2 %copy-start.3 = (f32[6,32,1024]{2,1,0:T(8,128)}, f32[6,32,1024]{2,1,0:T(8,128)S(1)}, u32[]{:S(2)}) copy-start(f32[6,32,1024]{2,1,0:T(8,128)S(1)} %broadcast_multiply_fusion.x_ref) | copy-start | bytes 2359300

commit v11 on v9

--- a/solution.py
+++ b/solution.py
@@ -74,8 +74,7 @@
     return out
 
 
-def _ar_kernel(cell_total, r_ref, p_ref, s_ref, m_ref, hr_ref, hc_ref, d_ref, o_ref, img_ref, dn_ref,
-               rn_ref, recv_a, recv_b, own, send_sems, recv_sems):
+def _ar_kernel(cell_total, r_ref, p_ref, s_ref, m_ref, hr_ref, hc_ref, o_ref, img_ref, recv_a, recv_b, own, send_sems, recv_sems):
     recvs = (recv_a, recv_b)
     groups = _groups()
     for r in recvs:
@@ -118,23 +117,17 @@
         else:
             finished = _finish(total, cell_total)
             o_ref[...] = finished
-            alpha = finished[0:1, 0:1]
-            for q in range(p_ref.shape[0]):
-                dn_ref[q] = d_ref[q] + alpha * p_ref[q]
-                rn_ref[q] = r_ref[q] - alpha * img_ref[q]
-
-
-def image_and_totals(residual, prec, stiffness, solid, halo_rows, halo_cols, disp, cell_total, cid):
+
+
+def image_and_totals(residual, prec, stiffness, solid, halo_rows, halo_cols, cell_total, cid):
     return pl.pallas_call(
         functools.partial(_ar_kernel, float(cell_total)),
         out_shape=[
             jax.ShapeDtypeStruct((8, 128), jnp.float32),
             jax.ShapeDtypeStruct(prec.shape, jnp.float32),
-            jax.ShapeDtypeStruct(prec.shape, jnp.float32),
-            jax.ShapeDtypeStruct(prec.shape, jnp.float32),
         ],
-        in_specs=[pl.BlockSpec(memory_space=pltpu.VMEM)] * 7,
-        out_specs=[pl.BlockSpec(memory_space=pltpu.VMEM)] * 4,
+        in_specs=[pl.BlockSpec(memory_space=pltpu.VMEM)] * 6,
+        out_specs=[pl.BlockSpec(memory_space=pltpu.VMEM)] * 2,
         scratch_shapes=[
             pltpu.VMEM((32, 8, 128), jnp.float32),
             pltpu.VMEM((8, 8, 128), jnp.float32),
@@ -143,7 +136,25 @@
             pltpu.SemaphoreType.DMA((40,)),
         ],
         compiler_params=pltpu.CompilerParams(collective_id=cid, has_side_effects=True),
-    )(residual, prec, stiffness, solid, halo_rows, halo_cols, disp)
+    )(residual, prec, stiffness, solid, halo_rows, halo_cols)
+
+
+def _update_kernel(f_ref, d_ref, p_ref, r_ref, i_ref, dn_ref, rn_ref):
+    alpha = f_ref[0:1, 0:1]
+    dn_ref[0] = d_ref[0] + alpha * p_ref[0]
+    rn_ref[0] = r_ref[0] - alpha * i_ref[0]
+
+
+def apply_step(finished, disp, prec, residual, image):
+    comps, rows, width = prec.shape
+    plane = pl.BlockSpec((1, rows, width), lambda q: (q, 0, 0))
+    return pl.pallas_call(
+        _update_kernel,
+        grid=(comps,),
+        out_shape=[jax.ShapeDtypeStruct(prec.shape, jnp.float32)] * 2,
+        in_specs=[pl.BlockSpec((8, 128), lambda q: (0, 0))] + [plane] * 4,
+        out_specs=[plane] * 2,
+    )(finished, disp, prec, residual, image)
 
 
 def _to_lines_kernel(n, count, *refs):
@@ -432,16 +443,11 @@
     halo_rows = jnp.pad(jnp.stack([before_row, after_row]), ((0, 0), (0, subl - comp_count), (0, 0)))
     halo_cols = jnp.stack([before_col, after_col])[..., None]
     cell_total = slab_count * lax.axis_size("ax") * comp_count * around_cells
-    finished, _, disp_new_t, residual_new_t = image_and_totals(
-        residual_t,
-        prec_t,
-        stiffness_t,
-        solid_t[0],
-        halo_rows,
-        halo_cols,
-        jnp.transpose(disp, (1, 0, 2)),
-        cell_total,
-        0,
+    finished, image_t = image_and_totals(
+        residual_t, prec_t, stiffness_t, solid_t[0], halo_rows, halo_cols, cell_total, 0
+    )
+    disp_new_t, residual_new_t = apply_step(
+        finished, jnp.transpose(disp, (1, 0, 2)), prec_t, residual_t, image_t
     )
     return (
         jnp.transpose(disp_new_t, (1, 0, 2)),

time: 105 us -> 105 us (level)
  Pallas kernels: 59.8 us -> 64 us
  local copies, waits for them, and re-layouts: 14.4 us -> 10.2 us
    pallas_call x0 -> x1, Pallas kernels: none -> 4.97 us  [apply_step(): pl.pallas_call(_update_kernel, grid=(comps,), out_shape=[jax.ShapeDtypeSt...]
    unnamed x24 -> x22, local copies, waits for them, and re-layouts: 4.66 us -> 0.47 us
where the time goes in v11:
time: 105 us; the launch traced here: 104 us
  Pallas kernels  64 us (61%)
  other arithmetic  12.6 us (12%)
  local copies, waits for them, and re-layouts  10.2 us (10%)
  starting transfers between devices  8.48 us (8%)
  matrix products  7.73 us (7%)
    pallas_call x1, Pallas kernels, image_and_totals(): pl.pallas_call(functools.partial(_ar_kernel, float(cell_total)), out_shap...  25.4 us
    pallas_call x1, Pallas kernels, from_lines_with_halo(): pl.pallas_call(functools.partial(_from_lines_kernel, (n_ax, n)), out_shap...  17.3 us
    pallas_call x1, Pallas kernels, to_lines(): pl.pallas_call(functools.partial(_to_lines_kernel, n, count), out_shape=[...  16.3 us
    ppermute x2, starting transfers between devices, with_halo(): after = lax.ppermute(first, axis, down)  5.08 us
    pallas_call x1, Pallas kernels, apply_step(): pl.pallas_call(_update_kernel, grid=(comps,), out_shape=[jax.ShapeDtypeSt...  4.97 us
    dot_general x1, matrix products, shards(): jnp.dot(lines.reshape(-1, around_cells), dft_table(around_cells), precisi...  4.22 us
    ppermute x2, starting transfers between devices, with_halo(): before = lax.ppermute(last, axis, up)  3.4 us
    transpose x1, other arithmetic, shards(): stiffness_t = jnp.transpose(stiffness, (1, 0, 2))  2.97 us
  transfers between devices with their start and end apart: 4, of which 0 were waited for; matrix products, arithmetic and copies ran while one was open for 10% of the time, Pallas kernels for 0%

profile of v11, /device:TPU:4, one launch (start us, length us, event | category | flops | bytes accessed | tf_op | source)
XLA Modules:
  0.0 104.0 jit_solution(14513150399043050597)
XLA Ops:
  0.7 2.1 %fusion.29 = (f32[128,6,1]{2,0,1:T(8,128)}, f32[128,6,1]{2,0,1:T(8,128)}) fusion(f32[128,6,256]{2,0,1:T(8,128)} %param.9), kind=kLoop, calls=%fused_computation.70 | loop fusion | bytes 12288 | tf_op jit(solution)/shard_map/slice | solution.py:356
  2.8 2.6 %collective-permute-start.2 = (f32[128,6,1]{2,0,1:T(8,128)}, f32[128,6,1]{2,0,1:T(8,128)}, u32[]{:S(2)}, u32[]{:S(2)}) collective-permute-start(f32[128,6,1]{2,0,1:T(8,128)} %get-tuple-element.31), channel_id=1, source_target_pairs={{1,0},{2,1},{3,2},{0,3},{5,4},{6,5},{7,6},{4,7},{9,8},{10,9},{11,1... | collective-permute-start | bytes 9224 | tf_op jit(solution)/shard_map/ppermute | solution.py:358
  5.4 0.8 fusion.28
  6.2 2.4 %collective-permute-start = (f32[1,6,256]{2,0,1:T(1,128)S(1)}, f32[1,6,256]{2,0,1:T(1,128)S(1)}, u32[]{:S(2)}, u32[]{:S(2)}) collective-permute-start(f32[1,6,256]{2,0,1:T(1,128)S(1)} %get-tuple-element.29), channel_id=1, source_target_pairs={{4,0},{8,4},{12,8},{16,12},{20,16},{24,20},{28,24},{32,28},{36,32}... | collective-permute-start | bytes 18440 | tf_op jit(solution)/shard_map/ppermute | solution.py:358
  8.7 3.4 %collective-permute-start.1 = (f32[1,6,256]{2,0,1:T(1,128)S(1)}, f32[1,6,256]{2,0,1:T(1,128)S(1)}, u32[]{:S(2)}, u32[]{:S(2)}) collective-permute-start(f32[1,6,256]{2,0,1:T(1,128)S(1)} %get-tuple-element.30), channel_id=1, source_target_pairs={{0,4},{4,8},{8,12},{12,16},{16,20},{20,24},{24,28},{28,32},{32,36}... | collective-permute-start | bytes 18440 | tf_op jit(solution)/shard_map/ppermute | solution.py:357
  12.1 1.6 %fusion.27 = (f32[1,128,256]{2,1,0:T(8,128)}, f32[128,256]{1,0:T(8,128)S(1)}) fusion(s32[128,256]{1,0:T(8,128)} %param.11), kind=kLoop, calls=%fused_computation.68 | loop fusion | flops 65536 | bytes 393216 | tf_op jit(solution)/shard_map/transpose;broadcast_in_dim | solution.py:398
  13.8 1.3 %reverse_multiply_fusion = f32[128,3,2,256]{3,0,2,1:T(8,128)S(1)} fusion(f32[128,3,2,256]{3,0,2,1:T(8,128)} %bitcast.52), kind=kLoop, calls=%fused_computation.18 | loop fusion | flops 196608 | bytes 1572864 | tf_op jit(solution)/shard_map/mul | solution.py:380
  15.1 1.0 slice.70
  16.1 0.3 reverse
  16.5 1.0 maximum_add_fusion
  17.7 1.1 %fusion.21 = (f32[32,1024]{1,0:T(8,128)S(1)}, f32[32,1024]{1,0:T(8,128)S(1)}, f32[32,1024]{1,0:T(8,128)S(1)}, f32[32,1024]{1,0:T(8,128)S(1)}) fusion(s32[1024]{0:T(1024)S(1)} %pad_add_fusion, s32[32]{0:T(128)S(1)} %iota_multiply_fusion, f32[1024]{0:T(1024)S(1)} %fusion.26), kind=kLoop, calls=%fused_computation.45 | loop fusion | flops 950272 | bytes 532608 | tf_op jit(solution)/shard_map/cos | solution.py:336
  18.8 0.2 convolution_multiply_fusion.1
  19.0 2.7 %multiply_subtract_fusion = f32[32,32,1024]{2,1,0:T(8,128)} fusion(f32[32,1024]{1,0:T(8,128)S(1)} %get-tuple-element.39, f32[32,1024]{1,0:T(8,128)S(1)} %get-tuple-element.38, f32[32,1024]{1,0:T(8,128)S(1)} %get-tuple-element.40, f32[32,1024]{1,0:T(8,128)S(1)} %get-tuple-element.37), kind=kLoop, calls=%fused_computation.1 | loop fusion | flops 3145728 | bytes 4718592 | tf_op jit(solution)/shard_map/sub | solution.py:336
  21.7 0.1 pad_maximum_fusion.4
  21.8 3.0 %multiply_bitcast_fusion = (f32[6,128,256]{2,1,0:T(8,128)}, f32[6,128,256]{2,1,0:T(8,128)}) fusion(f32[128,6,256]{2,0,1:T(8,128)S(1)} %copy-done.5, f32[128,6]{0,1:T(8,128)S(1)} %convolution_multiply_fusion.1, f32[128,6,256]{2,0,1:T(8,128)S(1)} %copy-done.6, f32[128,3,2,256]{3,0,2,1:T(8,128)S(1)} %reverse_multiply_fusion, f32[128,6,256]{2,0,1:T(8,128)S(1)} %copy-done.2, ...), kind=kLoop, calls=%fused_computation.19 | loop fusion | flops 2752512 | bytes 4871168 | tf_op jit(solution)/shard_map/transpose | solution.py:442
  24.8 16.3 %shard_map.103 = (f32[6,32,1024]{2,1,0:T(8,128)}, f32[1,32,1024]{2,1,0:T(8,128)}) custom-call(f32[6,128,256]{2,1,0:T(8,128)} %get-tuple-element.28.refs_0_.r_ref, f32[1,128,256]{2,1,0:T(8,128)} %get-tuple-element.33.refs_1_), custom_call_target="tpu_custom_call" | custom-call | tf_op jit(solution)/shard_map/pallas_call | solution.py:200
  41.1 4.2 %fusion.30 = f32[6,32,1024]{2,1,0:T(8,128)S(1)} fusion(f32[6,32,1024]{2,1,0:T(8,128)} %get-tuple-element.14, f32[1024,1024,1]{1,0,2:T(8,128)} %bitcast.50), kind=kOutput, calls=%fused_computation.71 | convolution fusion | flops 1207959552 | bytes 5767168 | tf_op jit(solution)/shard_map/dot_general | solution.py:400
  45.3 0.3 multiply_reduce_fusion
  45.7 2.4 %bitcast_multiply_fusion = (f32[192,1024]{1,0:T(8,128)S(1)}, f32[192,1024]{1,0:T(8,128)S(1)}) fusion(f32[32,1024]{1,0:T(8,128)S(1)} %bitcast.57, f32[192,1024]{1,0:T(8,128)S(1)} %bitcast.54, f32[1024,1024]{1,0:T(8,128)S(1)} %bitcast.51), kind=kOutput, calls=%fused_computation.17 | convolution fusion | flops 1208352768 | bytes 6684672 | tf_op jit(solution)/shard_map/dot_general | solution.py:404
  48.2 0.1 slice_reduce_fusion
  48.3 0.7 pad.16.last_ref
  49.1 0.6 pad.17.first_ref
  49.7 0.9 convolution_bitcast_fusion
  50.7 0.6 pad.15.cpk_ref
  51.3 17.3 %shard_map.104 = (f32[6,128,256]{2,1,0:T(8,128)}, f32[4,8,128]{2,1,0:T(8,128)}, f32[4,8,256]{2,1,0:T(8,128)}, f32[4,8,256]{2,1,0:T(8,128)}) custom-call(f32[6,32,1024]{2,1,0:T(8,128)} %copy-done.3, f32[4,8,128]{2,1,0:T(8,128)} %pad.15.cpk_ref, f32[4,8,256]{2,1,0:T(8,128)} %pad.16.last_ref, f32[4,8,256]{2,1,0:T(8,128)} %pad.17.first_ref), custom_call_target="tpu_custom_call" | custom-call | tf_op jit(solution)/shard_map/pallas_call | solution.py:314
  68.7 0.7 slice_bitcast_fusion
  69.8 1.2 %copy.25.hc_ref = f32[2,6,128,1]{3,2,1,0:T(8,128)} copy(f32[2,6,128,1]{2,0,1,3:T(2,128)S(1)} %maximum_bitcast_fusion) | data formatting | bytes 12288 | tf_op jit(solution)/shard_map/broadcast_in_dim | solution.py:444
  71.0 0.7 slice_select_fusion
  71.7 0.6 select_maximum_fusion.hr_ref
  72.3 25.4 %shard_map.105 = (f32[8,128]{1,0:T(8,128)}, f32[6,128,256]{2,1,0:T(8,128)}) custom-call(f32[6,128,256]{2,1,0:T(8,128)} %get-tuple-element.28.refs_0_.r_ref, f32[6,128,256]{2,1,0:T(8,128)} %get-tuple-element.15.p_ref, f32[6,128,256]{2,1,0:T(8,128)} %get-tuple-element.27.s_ref, f32[128,256]{1,0:T(8,128)} %copy-done.4, f32[2,8,256]{2,1,0:T(8,128)} %select_maximum_fusion.hr_ref, ...), custom_call_target="tpu_custom_call" | custom-call | tf_op jit(solution)/shard_map/pallas_call | solution.py:123
  97.7 1.3 %slice_bitcast_fusion.1 = f32[3]{0:T(128)} fusion(f32[8,128]{1,0:T(8,128)} %get-tuple-element.19.f_ref), kind=kLoop, calls=%fused_computation.65 | loop fusion | bytes 24 | tf_op jit(solution)/shard_map/squeeze | solution.py:455
  99.0 5.0 %shard_map.106 = (f32[6,128,256]{2,1,0:T(8,128)}, f32[6,128,256]{2,1,0:T(8,128)}) custom-call(f32[8,128]{1,0:T(8,128)} %get-tuple-element.19.f_ref, f32[6,128,256]{2,1,0:T(8,128)} %bitcast.53, f32[6,128,256]{2,1,0:T(8,128)} %get-tuple-element.15.p_ref, f32[6,128,256]{2,1,0:T(8,128)} %get-tuple-element.28.refs_0_.r_ref, f32[6,128,256]{2,1,0:T(8,128)} %get-tuple-element.20.i_ref), custom_call_target="tpu_custom_call" | custom-call | tf_op jit(solution)/shard_map/pallas_call | solution.py:151
  (43 shorter events, 0.9 us)
Async XLA Ops:
  0.6 18.2 %copy-start = (f32[4,6]{1,0:T(4,128)S(1)}, f32[4,6]{1,0:T(4,128)}, u32[]{:S(2)}) copy-start(f32[4,6]{1,0:T(4,128)} %param.13) | copy-start | bytes 292
  0.6 18.2 %copy-start.9 = (s32[128]{0:T(128)S(1)}, s32[128]{0:T(128)}, u32[]{:S(2)}) copy-start(s32[128]{0:T(128)} %param.12) | copy-start | bytes 1540
  2.8 19.0 %collective-permute-start.2 = (f32[128,6,1]{2,0,1:T(8,128)}, f32[128,6,1]{2,0,1:T(8,128)}, u32[]{:S(2)}, u32[]{:S(2)}) collective-permute-start(f32[128,6,1]{2,0,1:T(8,128)} %get-tuple-element.31), channel_id=1, source_target_pairs={{1,0},{2,1},{3,2},{0,3},{5,4},{6,5},{7,6},{4,7},{9,8},{10,9},{11,1... | collective-permute-start | bytes 9224 | tf_op jit(solution)/shard_map/ppermute | solution.py:358
  5.4 16.4 %collective-permute-start.3 = (f32[128,6,1]{2,0,1:T(8,128)}, f32[128,6,1]{2,0,1:T(8,128)}, u32[]{:S(2)}, u32[]{:S(2)}) collective-permute-start(f32[128,6,1]{2,0,1:T(8,128)} %get-tuple-element.32), channel_id=1, source_target_pairs={{0,1},{1,2},{2,3},{3,0},{4,5},{5,6},{6,7},{7,4},{8,9},{9,10},{10,1... | collective-permute-start | bytes 9224 | tf_op jit(solution)/shard_map/ppermute | solution.py:357
  6.2 15.5 %collective-permute-start = (f32[1,6,256]{2,0,1:T(1,128)S(1)}, f32[1,6,256]{2,0,1:T(1,128)S(1)}, u32[]{:S(2)}, u32[]{:S(2)}) collective-permute-start(f32[1,6,256]{2,0,1:T(1,128)S(1)} %get-tuple-element.29), channel_id=1, source_target_pairs={{4,0},{8,4},{12,8},{16,12},{20,16},{24,20},{28,24},{32,28},{36,32}... | collective-permute-start | bytes 18440 | tf_op jit(solution)/shard_map/ppermute | solution.py:358
  8.7 13.1 %collective-permute-start.1 = (f32[1,6,256]{2,0,1:T(1,128)S(1)}, f32[1,6,256]{2,0,1:T(1,128)S(1)}, u32[]{:S(2)}, u32[]{:S(2)}) collective-permute-start(f32[1,6,256]{2,0,1:T(1,128)S(1)} %get-tuple-element.30), channel_id=1, source_target_pairs={{0,4},{4,8},{8,12},{12,16},{16,20},{20,24},{24,28},{28,32},{32,36}... | collective-permute-start | bytes 18440 | tf_op jit(solution)/shard_map/ppermute | solution.py:357
  13.7 8.1 %copy-start.4 = (f32[128,256]{1,0:T(8,128)}, f32[128,256]{1,0:T(8,128)S(1)}, u32[]{:S(2)}) copy-start(f32[128,256]{1,0:T(8,128)S(1)} %get-tuple-element.34.m_ref) | copy-start | bytes 393220
  13.7 8.1 %copy-start.2 = (f32[128,6,256]{2,0,1:T(8,128)S(1)}, f32[128,6,256]{2,0,1:T(8,128)}, u32[]{:S(2)}) copy-start(f32[128,6,256]{2,0,1:T(8,128)} %param.9) | copy-start | bytes 2359300
  13.7 8.1 %copy-start.5 = (f32[128,6,256]{2,0,1:T(8,128)S(1)}, f32[128,6,256]{2,0,1:T(8,128)}, u32[]{:S(2)}) copy-start(f32[128,6,256]{2,0,1:T(8,128)} %param.10) | copy-start | bytes 2359300
  13.8 8.1 %copy-start.6 = (f32[128,6,256]{2,0,1:T(8,128)S(1)}, f32[128,6,256]{2,0,1:T(8,128)}, u32[]{:S(2)}) copy-start(f32[128,6,256]{2,0,1:T(8,128)} %param.8) | copy-start | bytes 2359300
  41.1 4.6 %copy-start.1 = (f32[32,32,1024]{2,1,0:T(8,128)S(1)}, f32[32,32,1024]{2,1,0:T(8,128)}, u32[]{:S(2)}) copy-start(f32[32,32,1024]{2,1,0:T(8,128)} %multiply_subtract_fusion) | copy-start | bytes 12582916
  41.1 4.6 %copy-start.7 = (f32[1,32,1024]{2,1,0:T(8,128)S(1)}, f32[1,32,1024]{2,1,0:T(8,128)}, u32[]{:S(2)}) copy-start(f32[1,32,1024]{2,1,0:T(8,128)} %get-tuple-element.13) | copy-start | bytes 393220
  45.7 4.0 %copy-start.8 = (s32[2,4]{1,0:T(2,128)S(1)}, s32[2,4]{1,0:T(2,128)}, u32[]{:S(2)}) copy-start(s32[2,4]{1,0:T(2,128)} %constant.77) | copy-start | bytes 100
  48.2 3.2 %copy-start.3 = (f32[6,32,1024]{2,1,0:T(8,128)}, f32[6,32,1024]{2,1,0:T(8,128)S(1)}, u32[]{:S(2)}) copy-start(f32[6,32,1024]{2,1,0:T(8,128)S(1)} %broadcast_multiply_fusion.x_ref) | copy-start | bytes 2359300

commit v12 on v11

--- a/solution.py
+++ b/solution.py
@@ -141,16 +141,18 @@
 
 def _update_kernel(f_ref, d_ref, p_ref, r_ref, i_ref, dn_ref, rn_ref):
     alpha = f_ref[0:1, 0:1]
-    dn_ref[0] = d_ref[0] + alpha * p_ref[0]
-    rn_ref[0] = r_ref[0] - alpha * i_ref[0]
+    for q in range(d_ref.shape[0]):
+        dn_ref[q] = d_ref[q] + alpha * p_ref[q]
+        rn_ref[q] = r_ref[q] - alpha * i_ref[q]
 
 
 def apply_step(finished, disp, prec, residual, image):
     comps, rows, width = prec.shape
-    plane = pl.BlockSpec((1, rows, width), lambda q: (q, 0, 0))
+    steps = 2 if comps % 2 == 0 else 1
+    plane = pl.BlockSpec((comps // steps, rows, width), lambda q: (q, 0, 0))
     return pl.pallas_call(
         _update_kernel,
-        grid=(comps,),
+        grid=(steps,),
         out_shape=[jax.ShapeDtypeStruct(prec.shape, jnp.float32)] * 2,
         in_specs=[pl.BlockSpec((8, 128), lambda q: (0, 0))] + [plane] * 4,
         out_specs=[plane] * 2,

time: 105 us -> 102 us (0.971)
  Pallas kernels: 64 us -> 61.9 us
    pallas_call x1, Pallas kernels: 4.97 us -> 2.82 us  [apply_step(): pl.pallas_call(_update_kernel, grid=(steps,), out_shape=[jax.ShapeDtypeSt...]
where the time goes in v12:
time: 102 us
  Pallas kernels  61.9 us (61%)
  other arithmetic  12.6 us (12%)
  local copies, waits for them, and re-layouts  10.2 us (10%)
  starting transfers between devices  8.48 us (8%)
  matrix products  7.73 us (8%)
    pallas_call x1, Pallas kernels, image_and_totals(): pl.pallas_call(functools.partial(_ar_kernel, float(cell_total)), out_shap...  25.4 us
    pallas_call x1, Pallas kernels, from_lines_with_halo(): pl.pallas_call(functools.partial(_from_lines_kernel, (n_ax, n)), out_shap...  17.3 us
    pallas_call x1, Pallas kernels, to_lines(): pl.pallas_call(functools.partial(_to_lines_kernel, n, count), out_shape=[...  16.3 us
    ppermute x2, starting transfers between devices, with_halo(): after = lax.ppermute(first, axis, down)  5.08 us
    dot_general x1, matrix products, shards(): jnp.dot(lines.reshape(-1, around_cells), dft_table(around_cells), precisi...  4.22 us
    ppermute x2, starting transfers between devices, with_halo(): before = lax.ppermute(last, axis, up)  3.4 us
    transpose x1, other arithmetic, shards(): stiffness_t = jnp.transpose(stiffness, (1, 0, 2))  2.97 us
    slice x2, local copies, waits for them, and re-layouts, with_halo(): first = lax.slice_in_dim(x, 0, width, axis=dim)  2.95 us
  transfers between devices with their start and end apart: 4, of which 0 were waited for; matrix products, arithmetic and copies ran while one was open for 10% of the time, Pallas kernels for 0%

profile of v12, /device:TPU:4, one launch (start us, length us, event | category | flops | bytes accessed | tf_op | source)
XLA Modules:
  0.0 101.8 jit_solution(11446366759135386402)
XLA Ops:
  0.7 2.1 %fusion.29 = (f32[128,6,1]{2,0,1:T(8,128)}, f32[128,6,1]{2,0,1:T(8,128)}) fusion(f32[128,6,256]{2,0,1:T(8,128)} %param.9), kind=kLoop, calls=%fused_computation.70 | loop fusion | bytes 12288 | tf_op jit(solution)/shard_map/slice | solution.py:358
  2.8 2.6 %collective-permute-start.2 = (f32[128,6,1]{2,0,1:T(8,128)}, f32[128,6,1]{2,0,1:T(8,128)}, u32[]{:S(2)}, u32[]{:S(2)}) collective-permute-start(f32[128,6,1]{2,0,1:T(8,128)} %get-tuple-element.31), channel_id=1, source_target_pairs={{1,0},{2,1},{3,2},{0,3},{5,4},{6,5},{7,6},{4,7},{9,8},{10,9},{11,1... | collective-permute-start | bytes 9224 | tf_op jit(solution)/shard_map/ppermute | solution.py:360
  5.4 0.8 fusion.28
  6.2 2.4 %collective-permute-start = (f32[1,6,256]{2,0,1:T(1,128)S(1)}, f32[1,6,256]{2,0,1:T(1,128)S(1)}, u32[]{:S(2)}, u32[]{:S(2)}) collective-permute-start(f32[1,6,256]{2,0,1:T(1,128)S(1)} %get-tuple-element.29), channel_id=1, source_target_pairs={{4,0},{8,4},{12,8},{16,12},{20,16},{24,20},{28,24},{32,28},{36,32}... | collective-permute-start | bytes 18440 | tf_op jit(solution)/shard_map/ppermute | solution.py:360
  8.7 3.4 %collective-permute-start.1 = (f32[1,6,256]{2,0,1:T(1,128)S(1)}, f32[1,6,256]{2,0,1:T(1,128)S(1)}, u32[]{:S(2)}, u32[]{:S(2)}) collective-permute-start(f32[1,6,256]{2,0,1:T(1,128)S(1)} %get-tuple-element.30), channel_id=1, source_target_pairs={{0,4},{4,8},{8,12},{12,16},{16,20},{20,24},{24,28},{28,32},{32,36}... | collective-permute-start | bytes 18440 | tf_op jit(solution)/shard_map/ppermute | solution.py:359
  12.1 1.6 %fusion.27 = (f32[1,128,256]{2,1,0:T(8,128)}, f32[128,256]{1,0:T(8,128)S(1)}) fusion(s32[128,256]{1,0:T(8,128)} %param.11), kind=kLoop, calls=%fused_computation.68 | loop fusion | flops 65536 | bytes 393216 | tf_op jit(solution)/shard_map/transpose;broadcast_in_dim | solution.py:400
  13.8 1.3 %reverse_multiply_fusion = f32[128,3,2,256]{3,0,2,1:T(8,128)S(1)} fusion(f32[128,3,2,256]{3,0,2,1:T(8,128)} %bitcast.52), kind=kLoop, calls=%fused_computation.18 | loop fusion | flops 196608 | bytes 1572864 | tf_op jit(solution)/shard_map/mul | solution.py:382
  15.1 1.0 slice.70
  16.1 0.3 reverse
  16.5 1.0 maximum_add_fusion
  17.7 1.1 %fusion.21 = (f32[32,1024]{1,0:T(8,128)S(1)}, f32[32,1024]{1,0:T(8,128)S(1)}, f32[32,1024]{1,0:T(8,128)S(1)}, f32[32,1024]{1,0:T(8,128)S(1)}) fusion(s32[1024]{0:T(1024)S(1)} %pad_add_fusion, s32[32]{0:T(128)S(1)} %iota_multiply_fusion, f32[1024]{0:T(1024)S(1)} %fusion.26), kind=kLoop, calls=%fused_computation.45 | loop fusion | flops 950272 | bytes 532608 | tf_op jit(solution)/shard_map/cos | solution.py:338
  18.8 0.2 convolution_multiply_fusion.1
  19.0 2.7 %multiply_subtract_fusion = f32[32,32,1024]{2,1,0:T(8,128)} fusion(f32[32,1024]{1,0:T(8,128)S(1)} %get-tuple-element.39, f32[32,1024]{1,0:T(8,128)S(1)} %get-tuple-element.38, f32[32,1024]{1,0:T(8,128)S(1)} %get-tuple-element.40, f32[32,1024]{1,0:T(8,128)S(1)} %get-tuple-element.37), kind=kLoop, calls=%fused_computation.1 | loop fusion | flops 3145728 | bytes 4718592 | tf_op jit(solution)/shard_map/sub | solution.py:338
  21.7 0.1 pad_maximum_fusion.4
  21.8 3.0 %multiply_bitcast_fusion = (f32[6,128,256]{2,1,0:T(8,128)}, f32[6,128,256]{2,1,0:T(8,128)}) fusion(f32[128,6,256]{2,0,1:T(8,128)S(1)} %copy-done.5, f32[128,6]{0,1:T(8,128)S(1)} %convolution_multiply_fusion.1, f32[128,6,256]{2,0,1:T(8,128)S(1)} %copy-done.6, f32[128,3,2,256]{3,0,2,1:T(8,128)S(1)} %reverse_multiply_fusion, f32[128,6,256]{2,0,1:T(8,128)S(1)} %copy-done.2, ...), kind=kLoop, calls=%fused_computation.19 | loop fusion | flops 2752512 | bytes 4871168 | tf_op jit(solution)/shard_map/transpose | solution.py:444
  24.8 16.3 %shard_map.103 = (f32[6,32,1024]{2,1,0:T(8,128)}, f32[1,32,1024]{2,1,0:T(8,128)}) custom-call(f32[6,128,256]{2,1,0:T(8,128)} %get-tuple-element.28.refs_0_.r_ref, f32[1,128,256]{2,1,0:T(8,128)} %get-tuple-element.33.refs_1_), custom_call_target="tpu_custom_call" | custom-call | tf_op jit(solution)/shard_map/pallas_call | solution.py:202
  41.1 4.2 %fusion.30 = f32[6,32,1024]{2,1,0:T(8,128)S(1)} fusion(f32[6,32,1024]{2,1,0:T(8,128)} %get-tuple-element.14, f32[1024,1024,1]{1,0,2:T(8,128)} %bitcast.50), kind=kOutput, calls=%fused_computation.71 | convolution fusion | flops 1207959552 | bytes 5767168 | tf_op jit(solution)/shard_map/dot_general | solution.py:402
  45.3 0.3 multiply_reduce_fusion
  45.7 2.4 %bitcast_multiply_fusion = (f32[192,1024]{1,0:T(8,128)S(1)}, f32[192,1024]{1,0:T(8,128)S(1)}) fusion(f32[32,1024]{1,0:T(8,128)S(1)} %bitcast.57, f32[192,1024]{1,0:T(8,128)S(1)} %bitcast.54, f32[1024,1024]{1,0:T(8,128)S(1)} %bitcast.51), kind=kOutput, calls=%fused_computation.17 | convolution fusion | flops 1208352768 | bytes 6684672 | tf_op jit(solution)/shard_map/dot_general | solution.py:406
  48.2 0.1 slice_reduce_fusion
  48.3 0.7 pad.16.last_ref
  49.1 0.6 pad.17.first_ref
  49.7 0.9 convolution_bitcast_fusion
  50.7 0.6 pad.15.cpk_ref
  51.3 17.3 %shard_map.104 = (f32[6,128,256]{2,1,0:T(8,128)}, f32[4,8,128]{2,1,0:T(8,128)}, f32[4,8,256]{2,1,0:T(8,128)}, f32[4,8,256]{2,1,0:T(8,128)}) custom-call(f32[6,32,1024]{2,1,0:T(8,128)} %copy-done.3, f32[4,8,128]{2,1,0:T(8,128)} %pad.15.cpk_ref, f32[4,8,256]{2,1,0:T(8,128)} %pad.16.last_ref, f32[4,8,256]{2,1,0:T(8,128)} %pad.17.first_ref), custom_call_target="tpu_custom_call" | custom-call | tf_op jit(solution)/shard_map/pallas_call | solution.py:316
  68.7 0.7 slice_bitcast_fusion
  69.8 1.2 %copy.25.hc_ref = f32[2,6,128,1]{3,2,1,0:T(8,128)} copy(f32[2,6,128,1]{2,0,1,3:T(2,128)S(1)} %maximum_bitcast_fusion) | data formatting | bytes 12288 | tf_op jit(solution)/shard_map/broadcast_in_dim | solution.py:446
  71.0 0.7 slice_select_fusion
  71.7 0.6 select_maximum_fusion.hr_ref
  72.3 25.4 %shard_map.105 = (f32[8,128]{1,0:T(8,128)}, f32[6,128,256]{2,1,0:T(8,128)}) custom-call(f32[6,128,256]{2,1,0:T(8,128)} %get-tuple-element.28.refs_0_.r_ref, f32[6,128,256]{2,1,0:T(8,128)} %get-tuple-element.15.p_ref, f32[6,128,256]{2,1,0:T(8,128)} %get-tuple-element.27.s_ref, f32[128,256]{1,0:T(8,128)} %copy-done.4, f32[2,8,256]{2,1,0:T(8,128)} %select_maximum_fusion.hr_ref, ...), custom_call_target="tpu_custom_call" | custom-call | tf_op jit(solution)/shard_map/pallas_call | solution.py:123
  97.7 1.3 %slice_bitcast_fusion.1 = f32[3]{0:T(128)} fusion(f32[8,128]{1,0:T(8,128)} %get-tuple-element.19.f_ref), kind=kLoop, calls=%fused_computation.65 | loop fusion | bytes 24 | tf_op jit(solution)/shard_map/squeeze | solution.py:457
  99.0 2.8 %shard_map.106 = (f32[6,128,256]{2,1,0:T(8,128)}, f32[6,128,256]{2,1,0:T(8,128)}) custom-call(f32[8,128]{1,0:T(8,128)} %get-tuple-element.19.f_ref, f32[6,128,256]{2,1,0:T(8,128)} %bitcast.53, f32[6,128,256]{2,1,0:T(8,128)} %get-tuple-element.15.p_ref, f32[6,128,256]{2,1,0:T(8,128)} %get-tuple-element.28.refs_0_.r_ref, f32[6,128,256]{2,1,0:T(8,128)} %get-tuple-element.20.i_ref), custom_call_target="tpu_custom_call" | custom-call | tf_op jit(solution)/shard_map/pallas_call | solution.py:153
  (43 shorter events, 0.9 us)
Async XLA Ops:
  0.6 18.2 %copy-start = (f32[4,6]{1,0:T(4,128)S(1)}, f32[4,6]{1,0:T(4,128)}, u32[]{:S(2)}) copy-start(f32[4,6]{1,0:T(4,128)} %param.13) | copy-start | bytes 292
  0.6 18.2 %copy-start.9 = (s32[128]{0:T(128)S(1)}, s32[128]{0:T(128)}, u32[]{:S(2)}) copy-start(s32[128]{0:T(128)} %param.12) | copy-start | bytes 1540
  2.8 19.0 %collective-permute-start.2 = (f32[128,6,1]{2,0,1:T(8,128)}, f32[128,6,1]{2,0,1:T(8,128)}, u32[]{:S(2)}, u32[]{:S(2)}) collective-permute-start(f32[128,6,1]{2,0,1:T(8,128)} %get-tuple-element.31), channel_id=1, source_target_pairs={{1,0},{2,1},{3,2},{0,3},{5,4},{6,5},{7,6},{4,7},{9,8},{10,9},{11,1... | collective-permute-start | bytes 9224 | tf_op jit(solution)/shard_map/ppermute | solution.py:360
  5.4 16.4 %collective-permute-start.3 = (f32[128,6,1]{2,0,1:T(8,128)}, f32[128,6,1]{2,0,1:T(8,128)}, u32[]{:S(2)}, u32[]{:S(2)}) collective-permute-start(f32[128,6,1]{2,0,1:T(8,128)} %get-tuple-element.32), channel_id=1, source_target_pairs={{0,1},{1,2},{2,3},{3,0},{4,5},{5,6},{6,7},{7,4},{8,9},{9,10},{10,1... | collective-permute-start | bytes 9224 | tf_op jit(solution)/shard_map/ppermute | solution.py:359
  6.2 15.5 %collective-permute-start = (f32[1,6,256]{2,0,1:T(1,128)S(1)}, f32[1,6,256]{2,0,1:T(1,128)S(1)}, u32[]{:S(2)}, u32[]{:S(2)}) collective-permute-start(f32[1,6,256]{2,0,1:T(1,128)S(1)} %get-tuple-element.29), channel_id=1, source_target_pairs={{4,0},{8,4},{12,8},{16,12},{20,16},{24,20},{28,24},{32,28},{36,32}... | collective-permute-start | bytes 18440 | tf_op jit(solution)/shard_map/ppermute | solution.py:360
  8.7 13.1 %collective-permute-start.1 = (f32[1,6,256]{2,0,1:T(1,128)S(1)}, f32[1,6,256]{2,0,1:T(1,128)S(1)}, u32[]{:S(2)}, u32[]{:S(2)}) collective-permute-start(f32[1,6,256]{2,0,1:T(1,128)S(1)} %get-tuple-element.30), channel_id=1, source_target_pairs={{0,4},{4,8},{8,12},{12,16},{16,20},{20,24},{24,28},{28,32},{32,36}... | collective-permute-start | bytes 18440 | tf_op jit(solution)/shard_map/ppermute | solution.py:359
  13.7 8.1 %copy-start.4 = (f32[128,256]{1,0:T(8,128)}, f32[128,256]{1,0:T(8,128)S(1)}, u32[]{:S(2)}) copy-start(f32[128,256]{1,0:T(8,128)S(1)} %get-tuple-element.34.m_ref) | copy-start | bytes 393220
  13.7 8.1 %copy-start.2 = (f32[128,6,256]{2,0,1:T(8,128)S(1)}, f32[128,6,256]{2,0,1:T(8,128)}, u32[]{:S(2)}) copy-start(f32[128,6,256]{2,0,1:T(8,128)} %param.9) | copy-start | bytes 2359300
  13.7 8.1 %copy-start.5 = (f32[128,6,256]{2,0,1:T(8,128)S(1)}, f32[128,6,256]{2,0,1:T(8,128)}, u32[]{:S(2)}) copy-start(f32[128,6,256]{2,0,1:T(8,128)} %param.10) | copy-start | bytes 2359300
  13.8 8.1 %copy-start.6 = (f32[128,6,256]{2,0,1:T(8,128)S(1)}, f32[128,6,256]{2,0,1:T(8,128)}, u32[]{:S(2)}) copy-start(f32[128,6,256]{2,0,1:T(8,128)} %param.8) | copy-start | bytes 2359300
  41.1 4.6 %copy-start.1 = (f32[32,32,1024]{2,1,0:T(8,128)S(1)}, f32[32,32,1024]{2,1,0:T(8,128)}, u32[]{:S(2)}) copy-start(f32[32,32,1024]{2,1,0:T(8,128)} %multiply_subtract_fusion) | copy-start | bytes 12582916
  41.1 4.6 %copy-start.7 = (f32[1,32,1024]{2,1,0:T(8,128)S(1)}, f32[1,32,1024]{2,1,0:T(8,128)}, u32[]{:S(2)}) copy-start(f32[1,32,1024]{2,1,0:T(8,128)} %get-tuple-element.13) | copy-start | bytes 393220
  45.7 4.0 %copy-start.8 = (s32[2,4]{1,0:T(2,128)S(1)}, s32[2,4]{1,0:T(2,128)}, u32[]{:S(2)}) copy-start(s32[2,4]{1,0:T(2,128)} %constant.77) | copy-start | bytes 100
  48.2 3.2 %copy-start.3 = (f32[6,32,1024]{2,1,0:T(8,128)}, f32[6,32,1024]{2,1,0:T(8,128)S(1)}, u32[]{:S(2)}) copy-start(f32[6,32,1024]{2,1,0:T(8,128)S(1)} %broadcast_multiply_fusion.x_ref) | copy-start | bytes 2359300

commit v13 on v12

--- a/solution.py
+++ b/solution.py
@@ -411,7 +411,6 @@
     ) / around_cells
     prec_lines = solid_lines * smoothed_lines.reshape(lines.shape)
     group_rows = lines.shape[1]
-    lanes = -(-2 * group_rows // 128) * 128
     subl = -(-comp_count // 8) * 8
     edge_at = [(p * sector_width - 1) % around_cells for p in range(sector_count)]
     edge_at += [((p + 1) * sector_width) % around_cells for p in range(sector_count)]
@@ -422,14 +421,10 @@
         (((1,), (1,)), ((), ())),
         precision=lax.Precision.HIGHEST,
     ).reshape(2, sector_count, comp_count, group_rows)
-    cpk = jnp.pad(
-        jnp.transpose(edges, (1, 2, 0, 3)).reshape(sector_count, comp_count, 2 * group_rows),
-        ((0, 0), (0, subl - comp_count), (0, lanes - 2 * group_rows)),
-    )
+    cpk = jnp.transpose(edges, (1, 2, 0, 3)).reshape(sector_count, comp_count, 2 * group_rows)
 
     def row_pack(row):
-        split = jnp.transpose(row.reshape(comp_count, sector_count, sector_width), (1, 0, 2))
-        return jnp.pad(split, ((0, 0), (0, subl - comp_count), (0, 0)))
+        return jnp.transpose(row.reshape(comp_count, sector_count, sector_width), (1, 0, 2))
 
     prec_t, halo_cols, before_rows, after_rows = from_lines_with_halo(
         prec_lines, cpk, row_pack(prec_lines[:, -1]), row_pack(prec_lines[:, 0]), sector_count

time: 102 us -> 102 us (level)
    pad x3 -> x0, local copies, waits for them, and re-layouts: 1.95 us -> none  [the longest x2 1.35 us: row_pack(): return jnp.pad(split, ((0, 0), (0, subl - comp_count), (0, 0)))]
where the time goes in v13:
time: 102 us; the launch traced here: 101 us
  Pallas kernels  61.8 us (61%)
  other arithmetic  12.6 us (12%)
  local copies, waits for them, and re-layouts  9.61 us (9%)
  starting transfers between devices  8.48 us (8%)
  matrix products  7.73 us (8%)
    pallas_call x1, Pallas kernels, image_and_totals(): pl.pallas_call(functools.partial(_ar_kernel, float(cell_total)), out_shap...  25.4 us
    pallas_call x1, Pallas kernels, from_lines_with_halo(): pl.pallas_call(functools.partial(_from_lines_kernel, (n_ax, n)), out_shap...  17.3 us
    pallas_call x1, Pallas kernels, to_lines(): pl.pallas_call(functools.partial(_to_lines_kernel, n, count), out_shape=[...  16.3 us
    ppermute x2, starting transfers between devices, with_halo(): after = lax.ppermute(first, axis, down)  5.08 us
    dot_general x1, matrix products, shards(): jnp.dot(lines.reshape(-1, around_cells), dft_table(around_cells), precisi...  4.22 us
    ppermute x2, starting transfers between devices, with_halo(): before = lax.ppermute(last, axis, up)  3.4 us
    transpose x1, other arithmetic, shards(): stiffness_t = jnp.transpose(stiffness, (1, 0, 2))  2.97 us
    slice x2, local copies, waits for them, and re-layouts, with_halo(): first = lax.slice_in_dim(x, 0, width, axis=dim)  2.95 us
  transfers between devices with their start and end apart: 4, of which 0 were waited for; matrix products, arithmetic and copies ran while one was open for 10% of the time, Pallas kernels for 0%

profile of v13, /device:TPU:4, one launch (start us, length us, event | category | flops | bytes accessed | tf_op | source)
XLA Modules:
  0.0 101.2 jit_solution(3576652691109550112)
XLA Ops:
  0.7 2.1 %fusion.29 = (f32[128,6,1]{2,0,1:T(8,128)}, f32[128,6,1]{2,0,1:T(8,128)}) fusion(f32[128,6,256]{2,0,1:T(8,128)} %param.9), kind=kLoop, calls=%fused_computation.69 | loop fusion | bytes 12288 | tf_op jit(solution)/shard_map/slice | solution.py:358
  2.8 2.6 %collective-permute-start.2 = (f32[128,6,1]{2,0,1:T(8,128)}, f32[128,6,1]{2,0,1:T(8,128)}, u32[]{:S(2)}, u32[]{:S(2)}) collective-permute-start(f32[128,6,1]{2,0,1:T(8,128)} %get-tuple-element.31), channel_id=1, source_target_pairs={{1,0},{2,1},{3,2},{0,3},{5,4},{6,5},{7,6},{4,7},{9,8},{10,9},{11,1... | collective-permute-start | bytes 9224 | tf_op jit(solution)/shard_map/ppermute | solution.py:360
  5.4 0.8 fusion.28
  6.2 2.4 %collective-permute-start = (f32[1,6,256]{2,0,1:T(1,128)S(1)}, f32[1,6,256]{2,0,1:T(1,128)S(1)}, u32[]{:S(2)}, u32[]{:S(2)}) collective-permute-start(f32[1,6,256]{2,0,1:T(1,128)S(1)} %get-tuple-element.29), channel_id=1, source_target_pairs={{4,0},{8,4},{12,8},{16,12},{20,16},{24,20},{28,24},{32,28},{36,32}... | collective-permute-start | bytes 18440 | tf_op jit(solution)/shard_map/ppermute | solution.py:360
  8.7 3.4 %collective-permute-start.1 = (f32[1,6,256]{2,0,1:T(1,128)S(1)}, f32[1,6,256]{2,0,1:T(1,128)S(1)}, u32[]{:S(2)}, u32[]{:S(2)}) collective-permute-start(f32[1,6,256]{2,0,1:T(1,128)S(1)} %get-tuple-element.30), channel_id=1, source_target_pairs={{0,4},{4,8},{8,12},{12,16},{16,20},{20,24},{24,28},{28,32},{32,36}... | collective-permute-start | bytes 18440 | tf_op jit(solution)/shard_map/ppermute | solution.py:359
  12.1 1.6 %fusion.27 = (f32[1,128,256]{2,1,0:T(8,128)}, f32[128,256]{1,0:T(8,128)S(1)}) fusion(s32[128,256]{1,0:T(8,128)} %param.11), kind=kLoop, calls=%fused_computation.67 | loop fusion | flops 65536 | bytes 393216 | tf_op jit(solution)/shard_map/transpose;broadcast_in_dim | solution.py:400
  13.8 1.3 %reverse_multiply_fusion = f32[128,3,2,256]{3,0,2,1:T(8,128)S(1)} fusion(f32[128,3,2,256]{3,0,2,1:T(8,128)} %bitcast.51), kind=kLoop, calls=%fused_computation.18 | loop fusion | flops 196608 | bytes 1572864 | tf_op jit(solution)/shard_map/mul | solution.py:382
  15.1 1.0 slice.67
  16.1 0.3 reverse
  16.4 0.1 slice.89
  16.5 1.0 maximum_add_fusion
  17.7 1.1 %fusion.21 = (f32[32,1024]{1,0:T(8,128)S(1)}, f32[32,1024]{1,0:T(8,128)S(1)}, f32[32,1024]{1,0:T(8,128)S(1)}, f32[32,1024]{1,0:T(8,128)S(1)}) fusion(s32[1024]{0:T(1024)S(1)} %pad_add_fusion, s32[32]{0:T(128)S(1)} %iota_multiply_fusion, f32[1024]{0:T(1024)S(1)} %fusion.26), kind=kLoop, calls=%fused_computation.45 | loop fusion | flops 950272 | bytes 532608 | tf_op jit(solution)/shard_map/cos | solution.py:338
  18.8 0.2 convolution_multiply_fusion.1
  19.0 2.7 %multiply_subtract_fusion = f32[32,32,1024]{2,1,0:T(8,128)} fusion(f32[32,1024]{1,0:T(8,128)S(1)} %get-tuple-element.39, f32[32,1024]{1,0:T(8,128)S(1)} %get-tuple-element.38, f32[32,1024]{1,0:T(8,128)S(1)} %get-tuple-element.40, f32[32,1024]{1,0:T(8,128)S(1)} %get-tuple-element.37), kind=kLoop, calls=%fused_computation.1 | loop fusion | flops 3145728 | bytes 4718592 | tf_op jit(solution)/shard_map/sub | solution.py:338
  21.7 0.1 pad_maximum_fusion.4
  21.8 3.0 %multiply_bitcast_fusion = (f32[6,128,256]{2,1,0:T(8,128)}, f32[6,128,256]{2,1,0:T(8,128)}) fusion(f32[128,6,256]{2,0,1:T(8,128)S(1)} %copy-done.5, f32[128,6]{0,1:T(8,128)S(1)} %convolution_multiply_fusion.1, f32[128,6,256]{2,0,1:T(8,128)S(1)} %copy-done.6, f32[128,3,2,256]{3,0,2,1:T(8,128)S(1)} %reverse_multiply_fusion, f32[128,6,256]{2,0,1:T(8,128)S(1)} %copy-done.2, ...), kind=kLoop, calls=%fused_computation.19 | loop fusion | flops 2752512 | bytes 4871168 | tf_op jit(solution)/shard_map/transpose | solution.py:439
  24.8 16.3 %shard_map.103 = (f32[6,32,1024]{2,1,0:T(8,128)}, f32[1,32,1024]{2,1,0:T(8,128)}) custom-call(f32[6,128,256]{2,1,0:T(8,128)} %get-tuple-element.28.refs_0_.r_ref, f32[1,128,256]{2,1,0:T(8,128)} %get-tuple-element.33.refs_1_), custom_call_target="tpu_custom_call" | custom-call | tf_op jit(solution)/shard_map/pallas_call | solution.py:202
  41.1 4.2 %fusion.30 = f32[6,32,1024]{2,1,0:T(8,128)S(1)} fusion(f32[6,32,1024]{2,1,0:T(8,128)} %get-tuple-element.14, f32[1024,1024,1]{1,0,2:T(8,128)} %bitcast.49), kind=kOutput, calls=%fused_computation.70 | convolution fusion | flops 1207959552 | bytes 5767168 | tf_op jit(solution)/shard_map/dot_general | solution.py:402
  45.3 0.3 multiply_reduce_fusion
  45.7 2.4 %bitcast_multiply_fusion = (f32[192,1024]{1,0:T(8,128)S(1)}, f32[192,1024]{1,0:T(8,128)S(1)}) fusion(f32[32,1024]{1,0:T(8,128)S(1)} %bitcast.56, f32[192,1024]{1,0:T(8,128)S(1)} %bitcast.53, f32[1024,1024]{1,0:T(8,128)S(1)} %bitcast.50), kind=kOutput, calls=%fused_computation.17 | convolution fusion | flops 1208352768 | bytes 6684672 | tf_op jit(solution)/shard_map/dot_general | solution.py:406
  48.2 0.9 slice_reduce_fusion
  49.1 0.9 convolution_bitcast_fusion
  50.1 0.7 reshape.252.cpk_ref
  50.8 17.3 %shard_map.104 = (f32[6,128,256]{2,1,0:T(8,128)}, f32[4,6,64]{2,1,0:T(8,128)}, f32[4,6,256]{2,1,0:T(8,128)}, f32[4,6,256]{2,1,0:T(8,128)}) custom-call(f32[6,32,1024]{2,1,0:T(8,128)} %copy-done.3, f32[4,6,64]{2,1,0:T(8,128)} %reshape.252.cpk_ref, f32[4,6,256]{2,1,0:T(8,128)} %bitcast.60, f32[4,6,256]{2,1,0:T(8,128)} %bitcast.59), custom_call_target="tpu_custom_call" | custom-call | tf_op jit(solution)/shard_map/pallas_call | solution.py:316
  68.1 0.7 copy.24
  68.8 0.1 reshape.248
  69.1 1.2 %copy.25.hc_ref = f32[2,6,128,1]{3,2,1,0:T(8,128)} copy(f32[2,6,128,1]{2,0,1,3:T(2,128)S(1)} %maximum_bitcast_fusion) | data formatting | bytes 12288 | tf_op jit(solution)/shard_map/broadcast_in_dim | solution.py:441
  70.3 0.7 slice_select_fusion
  71.1 0.6 select_maximum_fusion.hr_ref
  71.7 25.4 %shard_map.105 = (f32[8,128]{1,0:T(8,128)}, f32[6,128,256]{2,1,0:T(8,128)}) custom-call(f32[6,128,256]{2,1,0:T(8,128)} %get-tuple-element.28.refs_0_.r_ref, f32[6,128,256]{2,1,0:T(8,128)} %get-tuple-element.15.p_ref, f32[6,128,256]{2,1,0:T(8,128)} %get-tuple-element.27.s_ref, f32[128,256]{1,0:T(8,128)} %copy-done.4, f32[2,8,256]{2,1,0:T(8,128)} %select_maximum_fusion.hr_ref, ...), custom_call_target="tpu_custom_call" | custom-call | tf_op jit(solution)/shard_map/pallas_call | solution.py:123
  97.1 1.3 %slice_bitcast_fusion = f32[3]{0:T(128)} fusion(f32[8,128]{1,0:T(8,128)} %get-tuple-element.19.f_ref), kind=kLoop, calls=%fused_computation.64 | loop fusion | bytes 24 | tf_op jit(solution)/shard_map/squeeze | solution.py:452
  98.4 2.8 %shard_map.106 = (f32[6,128,256]{2,1,0:T(8,128)}, f32[6,128,256]{2,1,0:T(8,128)}) custom-call(f32[8,128]{1,0:T(8,128)} %get-tuple-element.19.f_ref, f32[6,128,256]{2,1,0:T(8,128)} %bitcast.52, f32[6,128,256]{2,1,0:T(8,128)} %get-tuple-element.15.p_ref, f32[6,128,256]{2,1,0:T(8,128)} %get-tuple-element.28.refs_0_.r_ref, f32[6,128,256]{2,1,0:T(8,128)} %get-tuple-element.20.i_ref), custom_call_target="tpu_custom_call" | custom-call | tf_op jit(solution)/shard_map/pallas_call | solution.py:153
  (39 shorter events, 0.6 us)
Async XLA Ops:
  0.6 18.2 %copy-start = (f32[4,6]{1,0:T(4,128)S(1)}, f32[4,6]{1,0:T(4,128)}, u32[]{:S(2)}) copy-start(f32[4,6]{1,0:T(4,128)} %param.13) | copy-start | bytes 292
  0.6 18.2 %copy-start.9 = (s32[128]{0:T(128)S(1)}, s32[128]{0:T(128)}, u32[]{:S(2)}) copy-start(s32[128]{0:T(128)} %param.12) | copy-start | bytes 1540
  2.8 19.0 %collective-permute-start.2 = (f32[128,6,1]{2,0,1:T(8,128)}, f32[128,6,1]{2,0,1:T(8,128)}, u32[]{:S(2)}, u32[]{:S(2)}) collective-permute-start(f32[128,6,1]{2,0,1:T(8,128)} %get-tuple-element.31), channel_id=1, source_target_pairs={{1,0},{2,1},{3,2},{0,3},{5,4},{6,5},{7,6},{4,7},{9,8},{10,9},{11,1... | collective-permute-start | bytes 9224 | tf_op jit(solution)/shard_map/ppermute | solution.py:360
  5.4 16.4 %collective-permute-start.3 = (f32[128,6,1]{2,0,1:T(8,128)}, f32[128,6,1]{2,0,1:T(8,128)}, u32[]{:S(2)}, u32[]{:S(2)}) collective-permute-start(f32[128,6,1]{2,0,1:T(8,128)} %get-tuple-element.32), channel_id=1, source_target_pairs={{0,1},{1,2},{2,3},{3,0},{4,5},{5,6},{6,7},{7,4},{8,9},{9,10},{10,1... | collective-permute-start | bytes 9224 | tf_op jit(solution)/shard_map/ppermute | solution.py:359
  6.2 15.5 %collective-permute-start = (f32[1,6,256]{2,0,1:T(1,128)S(1)}, f32[1,6,256]{2,0,1:T(1,128)S(1)}, u32[]{:S(2)}, u32[]{:S(2)}) collective-permute-start(f32[1,6,256]{2,0,1:T(1,128)S(1)} %get-tuple-element.29), channel_id=1, source_target_pairs={{4,0},{8,4},{12,8},{16,12},{20,16},{24,20},{28,24},{32,28},{36,32}... | collective-permute-start | bytes 18440 | tf_op jit(solution)/shard_map/ppermute | solution.py:360
  8.7 13.1 %collective-permute-start.1 = (f32[1,6,256]{2,0,1:T(1,128)S(1)}, f32[1,6,256]{2,0,1:T(1,128)S(1)}, u32[]{:S(2)}, u32[]{:S(2)}) collective-permute-start(f32[1,6,256]{2,0,1:T(1,128)S(1)} %get-tuple-element.30), channel_id=1, source_target_pairs={{0,4},{4,8},{8,12},{12,16},{16,20},{20,24},{24,28},{28,32},{32,36}... | collective-permute-start | bytes 18440 | tf_op jit(solution)/shard_map/ppermute | solution.py:359
  13.7 8.1 %copy-start.4 = (f32[128,256]{1,0:T(8,128)}, f32[128,256]{1,0:T(8,128)S(1)}, u32[]{:S(2)}) copy-start(f32[128,256]{1,0:T(8,128)S(1)} %get-tuple-element.34.m_ref) | copy-start | bytes 393220
  13.7 8.1 %copy-start.2 = (f32[128,6,256]{2,0,1:T(8,128)S(1)}, f32[128,6,256]{2,0,1:T(8,128)}, u32[]{:S(2)}) copy-start(f32[128,6,256]{2,0,1:T(8,128)} %param.9) | copy-start | bytes 2359300
  13.7 8.1 %copy-start.5 = (f32[128,6,256]{2,0,1:T(8,128)S(1)}, f32[128,6,256]{2,0,1:T(8,128)}, u32[]{:S(2)}) copy-start(f32[128,6,256]{2,0,1:T(8,128)} %param.10) | copy-start | bytes 2359300
  13.8 8.1 %copy-start.6 = (f32[128,6,256]{2,0,1:T(8,128)S(1)}, f32[128,6,256]{2,0,1:T(8,128)}, u32[]{:S(2)}) copy-start(f32[128,6,256]{2,0,1:T(8,128)} %param.8) | copy-start | bytes 2359300
  41.1 4.6 %copy-start.1 = (f32[32,32,1024]{2,1,0:T(8,128)S(1)}, f32[32,32,1024]{2,1,0:T(8,128)}, u32[]{:S(2)}) copy-start(f32[32,32,1024]{2,1,0:T(8,128)} %multiply_subtract_fusion) | copy-start | bytes 12582916
  41.1 4.6 %copy-start.7 = (f32[1,32,1024]{2,1,0:T(8,128)S(1)}, f32[1,32,1024]{2,1,0:T(8,128)}, u32[]{:S(2)}) copy-start(f32[1,32,1024]{2,1,0:T(8,128)} %get-tuple-element.13) | copy-start | bytes 393220
  45.7 3.4 %copy-start.8 = (s32[2,4]{1,0:T(2,128)S(1)}, s32[2,4]{1,0:T(2,128)}, u32[]{:S(2)}) copy-start(s32[2,4]{1,0:T(2,128)} %constant.71) | copy-start | bytes 100
  48.2 2.6 %copy-start.3 = (f32[6,32,1024]{2,1,0:T(8,128)}, f32[6,32,1024]{2,1,0:T(8,128)S(1)}, u32[]{:S(2)}) copy-start(f32[6,32,1024]{2,1,0:T(8,128)S(1)} %broadcast_multiply_fusion.x_ref) | copy-start | bytes 2359300

commit v14 on v13

--- a/solution.py
+++ b/solution.py
@@ -342,11 +342,12 @@
 def paired_inverse(precond):
     length = precond.shape[2]
     half = length // 2
-    low = precond[:, :, : half + 1]
-    mirror = jnp.flip(precond[:, :, half + 1 :], axis=2)
-    inner = jnp.concatenate([jnp.zeros_like(low[:, :, :1]), mirror, jnp.zeros_like(low[:, :, :1])], axis=2)
-    paired = low + inner
-    return jnp.concatenate([paired, paired[:, :, 1:half]], axis=2)
+    col = lax.broadcasted_iota(jnp.int32, precond.shape, 2)
+    mirror = jnp.flip(jnp.roll(precond, -1, axis=2), axis=2)
+    low = jnp.where(col <= half, precond, jnp.roll(precond, half, axis=2))
+    inner = (col >= 1) & (col < half)
+    high = jnp.where(col <= half, jnp.where(inner, mirror, 0.0), jnp.roll(mirror, half, axis=2))
+    return low + high
 
 
 def with_halo(x, sides, width, wrap):

time: 102 us -> 106 us (1.039)
  local copies, waits for them, and re-layouts: 9.61 us -> 15.2 us
  other arithmetic: 12.6 us -> 11.1 us
    slice x2 -> x5, local copies, waits for them, and re-layouts: 1.06 us -> 6.52 us  [the longest x3 4.74 us: paired_inverse(): jnp.roll(mirror, half, axis=2)]
    mul x1, other arithmetic: 1.34 us -> 0.07 us  [apply_operator(): return (stiffness + 4.5) * field - beside - 0.5 * swap_radial(field)]
  transfers between devices with their start and end apart: 4 -> 4, of which waited for: 0 -> 0; matrix products, arithmetic and copies ran while one was open for 10% -> 13% of each run, Pallas kernels for 0% -> 0%
where the time goes in v14:
time: 106 us; the launch traced here: 105 us
  Pallas kernels  61.8 us (58%)
  local copies, waits for them, and re-layouts  15.2 us (14%)
  other arithmetic  11.1 us (10%)
  starting transfers between devices  8.48 us (8%)
  matrix products  7.71 us (7%)
    pallas_call x1, Pallas kernels, image_and_totals(): pl.pallas_call(functools.partial(_ar_kernel, float(cell_total)), out_shap...  25.4 us
    pallas_call x1, Pallas kernels, from_lines_with_halo(): pl.pallas_call(functools.partial(_from_lines_kernel, (n_ax, n)), out_shap...  17.3 us
    pallas_call x1, Pallas kernels, to_lines(): pl.pallas_call(functools.partial(_to_lines_kernel, n, count), out_shape=[...  16.3 us
    ppermute x2, starting transfers between devices, with_halo(): after = lax.ppermute(first, axis, down)  5.08 us
    slice x3, local copies, waits for them, and re-layouts, paired_inverse(): jnp.roll(mirror, half, axis=2)  4.74 us
    dot_general x1, matrix products, shards(): jnp.dot(lines.reshape(-1, around_cells), dft_table(around_cells), precisi...  4.22 us
    ppermute x2, starting transfers between devices, with_halo(): before = lax.ppermute(last, axis, up)  3.4 us
    transpose x1, other arithmetic, shards(): stiffness_t = jnp.transpose(stiffness, (1, 0, 2))  2.99 us
  transfers between devices with their start and end apart: 4, of which 0 were waited for; matrix products, arithmetic and copies ran while one was open for 13% of the time, Pallas kernels for 0%

profile of v14, /device:TPU:4, one launch (start us, length us, event | category | flops | bytes accessed | tf_op | source)
XLA Modules:
  0.0 105.3 jit_solution(7499669536831524163)
XLA Ops:
  0.7 2.1 %fusion.32 = (f32[128,6,1]{2,0,1:T(8,128)}, f32[128,6,1]{2,0,1:T(8,128)}) fusion(f32[128,6,256]{2,0,1:T(8,128)} %param.9), kind=kLoop, calls=%fused_computation.78 | loop fusion | bytes 12288 | tf_op jit(solution)/shard_map/slice | solution.py:359
  2.8 2.6 %collective-permute-start.2 = (f32[128,6,1]{2,0,1:T(8,128)}, f32[128,6,1]{2,0,1:T(8,128)}, u32[]{:S(2)}, u32[]{:S(2)}) collective-permute-start(f32[128,6,1]{2,0,1:T(8,128)} %get-tuple-element.31), channel_id=1, source_target_pairs={{1,0},{2,1},{3,2},{0,3},{5,4},{6,5},{7,6},{4,7},{9,8},{10,9},{11,1... | collective-permute-start | bytes 9224 | tf_op jit(solution)/shard_map/ppermute | solution.py:361
  5.4 0.8 fusion.31
  6.2 2.4 %collective-permute-start = (f32[1,6,256]{2,0,1:T(1,128)S(1)}, f32[1,6,256]{2,0,1:T(1,128)S(1)}, u32[]{:S(2)}, u32[]{:S(2)}) collective-permute-start(f32[1,6,256]{2,0,1:T(1,128)S(1)} %get-tuple-element.29), channel_id=1, source_target_pairs={{4,0},{8,4},{12,8},{16,12},{20,16},{24,20},{28,24},{32,28},{36,32}... | collective-permute-start | bytes 18440 | tf_op jit(solution)/shard_map/ppermute | solution.py:361
  8.7 3.4 %collective-permute-start.1 = (f32[1,6,256]{2,0,1:T(1,128)S(1)}, f32[1,6,256]{2,0,1:T(1,128)S(1)}, u32[]{:S(2)}, u32[]{:S(2)}) collective-permute-start(f32[1,6,256]{2,0,1:T(1,128)S(1)} %get-tuple-element.30), channel_id=1, source_target_pairs={{0,4},{4,8},{8,12},{12,16},{16,20},{20,24},{24,28},{28,32},{32,36}... | collective-permute-start | bytes 18440 | tf_op jit(solution)/shard_map/ppermute | solution.py:360
  12.1 1.0 slice.89
  13.2 0.7 slice.90
  14.1 1.8 %fusion.33 = (f32[6,6,512]{2,1,0:T(8,128)S(1)}, f32[6,6,512]{2,1,0:T(8,128)}, f32[6,6,512]{2,1,0:T(8,128)}) fusion(f32[6,6,1024]{2,1,0:T(8,128)} %param.14), kind=kLoop, calls=%fused_computation.79 | loop fusion | bytes 442368 | tf_op jit(solution)/shard_map/jit(_roll_static)/slice | solution.py:349
  15.9 1.6 %fusion.30 = (f32[1,128,256]{2,1,0:T(8,128)}, f32[128,256]{1,0:T(8,128)S(1)}) fusion(s32[128,256]{1,0:T(8,128)} %param.11), kind=kLoop, calls=%fused_computation.76 | loop fusion | flops 65536 | bytes 393216 | tf_op jit(solution)/shard_map/transpose;broadcast_in_dim | solution.py:401
  17.4 0.6 rev.9
  18.1 1.5 %slice.94 = f32[6,6,512]{2,1,0:T(8,128)} reverse(f32[6,6,512]{2,1,0:T(8,128)S(1)} %fusion.19), dimensions={2} | reverse | bytes 147456 | tf_op jit(solution)/shard_map/jit(_roll_static)/slice | solution.py:349
  19.6 1.5 %slice.92 = f32[6,6,512]{2,1,0:T(8,128)} reverse(f32[6,6,512]{2,1,0:T(8,128)S(1)} %get-tuple-element.33), dimensions={2} | reverse | bytes 147456 | tf_op jit(solution)/shard_map/jit(_roll_static)/slice | solution.py:349
  21.2 1.1 %fusion.23 = (f32[32,1024]{1,0:T(8,128)S(1)}, f32[32,1024]{1,0:T(8,128)S(1)}, f32[32,1024]{1,0:T(8,128)S(1)}, f32[32,1024]{1,0:T(8,128)S(1)}) fusion(s32[1024]{0:T(1024)S(1)} %pad_add_fusion, s32[32]{0:T(128)S(1)} %iota_multiply_fusion, f32[1024]{0:T(1024)S(1)} %fusion.28), kind=kLoop, calls=%fused_computation.50 | loop fusion | flops 950272 | bytes 532608 | tf_op jit(solution)/shard_map/cos | solution.py:338
  22.2 0.2 convolution_multiply_fusion.1
  22.4 2.7 %multiply_subtract_fusion = f32[32,32,1024]{2,1,0:T(8,128)} fusion(f32[32,1024]{1,0:T(8,128)S(1)} %get-tuple-element.42, f32[32,1024]{1,0:T(8,128)S(1)} %get-tuple-element.41, f32[32,1024]{1,0:T(8,128)S(1)} %get-tuple-element.43, f32[32,1024]{1,0:T(8,128)S(1)} %get-tuple-element.40), kind=kLoop, calls=%fused_computation.1 | loop fusion | flops 3145728 | bytes 4718592 | tf_op jit(solution)/shard_map/sub | solution.py:338
  25.4 3.0 %multiply_bitcast_fusion = (f32[6,128,256]{2,1,0:T(8,128)}, f32[6,128,256]{2,1,0:T(8,128)}) fusion(f32[128,6,256]{2,0,1:T(8,128)S(1)} %copy-done.6, f32[128,6]{0,1:T(8,128)S(1)} %convolution_multiply_fusion.1, f32[128,6,256]{2,0,1:T(8,128)S(1)} %copy-done.7, f32[128,3,2,256]{3,0,2,1:T(8,128)S(1)} %reverse_multiply_fusion, f32[128,6,256]{2,0,1:T(8,128)S(1)} %copy-done.2, ...), kind=kLoop, calls=%fused_computation.19 | loop fusion | flops 2752512 | bytes 4871168 | tf_op jit(solution)/shard_map/transpose | solution.py:440
  28.3 16.3 %shard_map.103 = (f32[6,32,1024]{2,1,0:T(8,128)}, f32[1,32,1024]{2,1,0:T(8,128)}) custom-call(f32[6,128,256]{2,1,0:T(8,128)} %get-tuple-element.28.refs_0_.r_ref, f32[1,128,256]{2,1,0:T(8,128)} %get-tuple-element.36.refs_1_), custom_call_target="tpu_custom_call" | custom-call | tf_op jit(solution)/shard_map/pallas_call | solution.py:202
  44.7 4.2 %fusion.34 = f32[6,32,1024]{2,1,0:T(8,128)S(1)} fusion(f32[6,32,1024]{2,1,0:T(8,128)} %get-tuple-element.14, f32[1024,1024,1]{1,0,2:T(8,128)} %bitcast.48), kind=kOutput, calls=%fused_computation.80 | convolution fusion | flops 1207959552 | bytes 5767168 | tf_op jit(solution)/shard_map/dot_general | solution.py:403
  48.9 0.3 multiply_reduce_fusion
  49.3 2.4 %bitcast_multiply_fusion = (f32[192,1024]{1,0:T(8,128)S(1)}, f32[192,1024]{1,0:T(8,128)S(1)}) fusion(f32[32,1024]{1,0:T(8,128)S(1)} %bitcast.55, f32[192,1024]{1,0:T(8,128)S(1)} %bitcast.52, f32[1024,1024]{1,0:T(8,128)S(1)} %bitcast.49), kind=kOutput, calls=%fused_computation.17 | convolution fusion | flops 1208352768 | bytes 6684672 | tf_op jit(solution)/shard_map/dot_general | solution.py:407
  51.7 0.8 slice_reduce_fusion
  52.6 0.9 convolution_bitcast_fusion
  53.5 0.7 reshape.252.cpk_ref
  54.2 17.3 %shard_map.104 = (f32[6,128,256]{2,1,0:T(8,128)}, f32[4,6,64]{2,1,0:T(8,128)}, f32[4,6,256]{2,1,0:T(8,128)}, f32[4,6,256]{2,1,0:T(8,128)}) custom-call(f32[6,32,1024]{2,1,0:T(8,128)} %copy-done.3, f32[4,6,64]{2,1,0:T(8,128)} %reshape.252.cpk_ref, f32[4,6,256]{2,1,0:T(8,128)} %bitcast.58, f32[4,6,256]{2,1,0:T(8,128)} %bitcast.57), custom_call_target="tpu_custom_call" | custom-call | tf_op jit(solution)/shard_map/pallas_call | solution.py:316
  71.5 0.7 copy.24
  72.6 1.2 %copy.25.hc_ref = f32[2,6,128,1]{3,2,1,0:T(8,128)} copy(f32[2,6,128,1]{2,0,1,3:T(2,128)S(1)} %maximum_bitcast_fusion) | data formatting | bytes 12288 | tf_op jit(solution)/shard_map/broadcast_in_dim | solution.py:442
  73.8 0.7 slice_select_fusion.1
  74.5 0.7 slice_select_fusion
  75.2 0.6 select_maximum_fusion.hr_ref
  75.8 25.4 %shard_map.105 = (f32[8,128]{1,0:T(8,128)}, f32[6,128,256]{2,1,0:T(8,128)}) custom-call(f32[6,128,256]{2,1,0:T(8,128)} %get-tuple-element.28.refs_0_.r_ref, f32[6,128,256]{2,1,0:T(8,128)} %get-tuple-element.15.p_ref, f32[6,128,256]{2,1,0:T(8,128)} %get-tuple-element.27.s_ref, f32[128,256]{1,0:T(8,128)} %copy-done.5, f32[2,8,256]{2,1,0:T(8,128)} %select_maximum_fusion.hr_ref, ...), custom_call_target="tpu_custom_call" | custom-call | tf_op jit(solution)/shard_map/pallas_call | solution.py:123
  101.3 1.3 %slice_bitcast_fusion = f32[3]{0:T(128)} fusion(f32[8,128]{1,0:T(8,128)} %get-tuple-element.19.f_ref), kind=kLoop, calls=%fused_computation.73 | loop fusion | bytes 24 | tf_op jit(solution)/shard_map/squeeze | solution.py:453
  102.5 2.8 %shard_map.106 = (f32[6,128,256]{2,1,0:T(8,128)}, f32[6,128,256]{2,1,0:T(8,128)}) custom-call(f32[8,128]{1,0:T(8,128)} %get-tuple-element.19.f_ref, f32[6,128,256]{2,1,0:T(8,128)} %bitcast.50, f32[6,128,256]{2,1,0:T(8,128)} %get-tuple-element.15.p_ref, f32[6,128,256]{2,1,0:T(8,128)} %get-tuple-element.28.refs_0_.r_ref, f32[6,128,256]{2,1,0:T(8,128)} %get-tuple-element.20.i_ref), custom_call_target="tpu_custom_call" | custom-call | tf_op jit(solution)/shard_map/pallas_call | solution.py:153
  (53 shorter events, 0.9 us)
Async XLA Ops:
  0.6 21.6 %copy-start = (f32[4,6]{1,0:T(4,128)S(1)}, f32[4,6]{1,0:T(4,128)}, u32[]{:S(2)}) copy-start(f32[4,6]{1,0:T(4,128)} %param.13) | copy-start | bytes 292
  0.6 21.6 %copy-start.14 = (s32[128]{0:T(128)S(1)}, s32[128]{0:T(128)}, u32[]{:S(2)}) copy-start(s32[128]{0:T(128)} %param.12) | copy-start | bytes 1540
  2.8 22.3 %copy-start.4 = (f32[6,6,1024]{2,1,0:T(8,128)S(1)}, f32[6,6,1024]{2,1,0:T(8,128)}, u32[]{:S(2)}) copy-start(f32[6,6,1024]{2,1,0:T(8,128)} %param.14) | copy-start | bytes 442372
  2.8 22.5 %collective-permute-start.2 = (f32[128,6,1]{2,0,1:T(8,128)}, f32[128,6,1]{2,0,1:T(8,128)}, u32[]{:S(2)}, u32[]{:S(2)}) collective-permute-start(f32[128,6,1]{2,0,1:T(8,128)} %get-tuple-element.31), channel_id=1, source_target_pairs={{1,0},{2,1},{3,2},{0,3},{5,4},{6,5},{7,6},{4,7},{9,8},{10,9},{11,1... | collective-permute-start | bytes 9224 | tf_op jit(solution)/shard_map/ppermute | solution.py:361
  5.4 19.9 %collective-permute-start.3 = (f32[128,6,1]{2,0,1:T(8,128)}, f32[128,6,1]{2,0,1:T(8,128)}, u32[]{:S(2)}, u32[]{:S(2)}) collective-permute-start(f32[128,6,1]{2,0,1:T(8,128)} %get-tuple-element.32), channel_id=1, source_target_pairs={{0,1},{1,2},{2,3},{3,0},{4,5},{5,6},{6,7},{7,4},{8,9},{9,10},{10,1... | collective-permute-start | bytes 9224 | tf_op jit(solution)/shard_map/ppermute | solution.py:360
  6.2 19.1 %collective-permute-start = (f32[1,6,256]{2,0,1:T(1,128)S(1)}, f32[1,6,256]{2,0,1:T(1,128)S(1)}, u32[]{:S(2)}, u32[]{:S(2)}) collective-permute-start(f32[1,6,256]{2,0,1:T(1,128)S(1)} %get-tuple-element.29), channel_id=1, source_target_pairs={{4,0},{8,4},{12,8},{16,12},{20,16},{24,20},{28,24},{32,28},{36,32}... | collective-permute-start | bytes 18440 | tf_op jit(solution)/shard_map/ppermute | solution.py:361
  8.7 16.6 %collective-permute-start.1 = (f32[1,6,256]{2,0,1:T(1,128)S(1)}, f32[1,6,256]{2,0,1:T(1,128)S(1)}, u32[]{:S(2)}, u32[]{:S(2)}) collective-permute-start(f32[1,6,256]{2,0,1:T(1,128)S(1)} %get-tuple-element.30), channel_id=1, source_target_pairs={{0,4},{4,8},{8,12},{12,16},{16,20},{20,24},{24,28},{28,32},{32,36}... | collective-permute-start | bytes 18440 | tf_op jit(solution)/shard_map/ppermute | solution.py:360
  14.0 11.2 %copy-start.2 = (f32[128,6,256]{2,0,1:T(8,128)S(1)}, f32[128,6,256]{2,0,1:T(8,128)}, u32[]{:S(2)}) copy-start(f32[128,6,256]{2,0,1:T(8,128)} %param.9) | copy-start | bytes 2359300
  17.4 7.9 %copy-start.5 = (f32[128,256]{1,0:T(8,128)}, f32[128,256]{1,0:T(8,128)S(1)}, u32[]{:S(2)}) copy-start(f32[128,256]{1,0:T(8,128)S(1)} %get-tuple-element.37.m_ref) | copy-start | bytes 393220
  18.1 7.3 %copy-start.6 = (f32[128,6,256]{2,0,1:T(8,128)S(1)}, f32[128,6,256]{2,0,1:T(8,128)}, u32[]{:S(2)}) copy-start(f32[128,6,256]{2,0,1:T(8,128)} %param.10) | copy-start | bytes 2359300
  18.1 7.3 %copy-start.7 = (f32[128,6,256]{2,0,1:T(8,128)S(1)}, f32[128,6,256]{2,0,1:T(8,128)}, u32[]{:S(2)}) copy-start(f32[128,6,256]{2,0,1:T(8,128)} %param.8) | copy-start | bytes 2359300
  21.1 4.0 %copy-start.9 = (f32[6,6,512]{2,1,0:T(8,128)S(1)}, f32[6,6,512]{2,1,0:T(8,128)}, u32[]{:S(2)}) copy-start(f32[6,6,512]{2,1,0:T(8,128)} %get-tuple-element.34) | copy-start | bytes 221188
  21.1 4.0 %copy-start.10 = (f32[6,6,512]{2,1,0:T(8,128)S(1)}, f32[6,6,512]{2,1,0:T(8,128)}, u32[]{:S(2)}) copy-start(f32[6,6,512]{2,1,0:T(8,128)} %get-tuple-element.35) | copy-start | bytes 221188
  21.1 4.0 %copy-start.11 = (f32[6,6,512]{2,1,0:T(8,128)S(1)}, f32[6,6,512]{2,1,0:T(8,128)}, u32[]{:S(2)}) copy-start(f32[6,6,512]{2,1,0:T(8,128)} %slice.94) | copy-start | bytes 221188
  21.1 4.0 %copy-start.12 = (f32[6,6,512]{2,1,0:T(8,128)S(1)}, f32[6,6,512]{2,1,0:T(8,128)}, u32[]{:S(2)}) copy-start(f32[6,6,512]{2,1,0:T(8,128)} %slice.92) | copy-start | bytes 221188
  44.6 4.6 %copy-start.1 = (f32[32,32,1024]{2,1,0:T(8,128)S(1)}, f32[32,32,1024]{2,1,0:T(8,128)}, u32[]{:S(2)}) copy-start(f32[32,32,1024]{2,1,0:T(8,128)} %multiply_subtract_fusion) | copy-start | bytes 12582916
  44.7 4.6 %copy-start.8 = (f32[1,32,1024]{2,1,0:T(8,128)S(1)}, f32[1,32,1024]{2,1,0:T(8,128)}, u32[]{:S(2)}) copy-start(f32[1,32,1024]{2,1,0:T(8,128)} %get-tuple-element.13) | copy-start | bytes 393220
  49.3 3.3 %copy-start.13 = (s32[2,4]{1,0:T(2,128)S(1)}, s32[2,4]{1,0:T(2,128)}, u32[]{:S(2)}) copy-start(s32[2,4]{1,0:T(2,128)} %constant.72) | copy-start | bytes 100
  51.7 2.5 %copy-start.3 = (f32[6,32,1024]{2,1,0:T(8,128)}, f32[6,32,1024]{2,1,0:T(8,128)S(1)}, u32[]{:S(2)}) copy-start(f32[6,32,1024]{2,1,0:T(8,128)S(1)} %broadcast_multiply_fusion.x_ref) | copy-start | bytes 2359300

commit v15 on v13

--- a/solution.py
+++ b/solution.py
@@ -399,8 +399,12 @@
     residual_t = jnp.transpose(residual, (1, 0, 2))
     solid_t = jnp.transpose(solid, (1, 0, 2))
     lines, solid_lines = to_lines([residual_t, solid_t], sector_count)
-    spectrum = jnp.dot(
-        lines.reshape(-1, around_cells), dft_table(around_cells), precision=lax.Precision.HIGH
+    spectrum = lax.optimization_barrier(
+        jnp.dot(
+            lax.optimization_barrier(lines.reshape(-1, around_cells)),
+            dft_table(around_cells),
+            precision=lax.Precision.HIGH,
+        )
     ).reshape(lines.shape)
     mixed = jnp.sum(paired_inverse(precond)[:, :, None] * spectrum[None], axis=1)
     smoothed_lines = lax.dot_general(

time: 102 us -> 102 us (level)
  no operation moved by 1% of the time
where the time goes in v15:
time: 102 us; the launch traced here: 101 us
  Pallas kernels  61.8 us (61%)
  other arithmetic  12.6 us (12%)
  local copies, waits for them, and re-layouts  9.61 us (9%)
  starting transfers between devices  8.48 us (8%)
  matrix products  7.71 us (8%)
    pallas_call x1, Pallas kernels, image_and_totals(): pl.pallas_call(functools.partial(_ar_kernel, float(cell_total)), out_shap...  25.4 us
    pallas_call x1, Pallas kernels, from_lines_with_halo(): pl.pallas_call(functools.partial(_from_lines_kernel, (n_ax, n)), out_shap...  17.3 us
    pallas_call x1, Pallas kernels, to_lines(): pl.pallas_call(functools.partial(_to_lines_kernel, n, count), out_shape=[...  16.3 us
    ppermute x2, starting transfers between devices, with_halo(): after = lax.ppermute(first, axis, down)  5.08 us
    dot_general x1, matrix products, shards(): jnp.dot(lax.optimization_barrier(lines.reshape(-1, around_cells)), dft_ta...  4.22 us
    ppermute x2, starting transfers between devices, with_halo(): before = lax.ppermute(last, axis, up)  3.4 us
    transpose x1, other arithmetic, shards(): stiffness_t = jnp.transpose(stiffness, (1, 0, 2))  2.97 us
    slice x2, local copies, waits for them, and re-layouts, with_halo(): first = lax.slice_in_dim(x, 0, width, axis=dim)  2.95 us
  transfers between devices with their start and end apart: 4, of which 0 were waited for; matrix products, arithmetic and copies ran while one was open for 10% of the time, Pallas kernels for 0%

profile of v15, /device:TPU:4, one launch (start us, length us, event | category | flops | bytes accessed | tf_op | source)
XLA Modules:
  0.0 101.2 jit_solution(13986773736792545607)
XLA Ops:
  0.7 2.1 %fusion.29 = (f32[128,6,1]{2,0,1:T(8,128)}, f32[128,6,1]{2,0,1:T(8,128)}) fusion(f32[128,6,256]{2,0,1:T(8,128)} %param.9), kind=kLoop, calls=%fused_computation.69 | loop fusion | bytes 12288 | tf_op jit(solution)/shard_map/slice | solution.py:358
  2.8 2.6 %collective-permute-start.2 = (f32[128,6,1]{2,0,1:T(8,128)}, f32[128,6,1]{2,0,1:T(8,128)}, u32[]{:S(2)}, u32[]{:S(2)}) collective-permute-start(f32[128,6,1]{2,0,1:T(8,128)} %get-tuple-element.31), channel_id=1, source_target_pairs={{1,0},{2,1},{3,2},{0,3},{5,4},{6,5},{7,6},{4,7},{9,8},{10,9},{11,1... | collective-permute-start | bytes 9224 | tf_op jit(solution)/shard_map/ppermute | solution.py:360
  5.4 0.8 fusion.28
  6.2 2.4 %collective-permute-start = (f32[1,6,256]{2,0,1:T(1,128)S(1)}, f32[1,6,256]{2,0,1:T(1,128)S(1)}, u32[]{:S(2)}, u32[]{:S(2)}) collective-permute-start(f32[1,6,256]{2,0,1:T(1,128)S(1)} %get-tuple-element.29), channel_id=1, source_target_pairs={{4,0},{8,4},{12,8},{16,12},{20,16},{24,20},{28,24},{32,28},{36,32}... | collective-permute-start | bytes 18440 | tf_op jit(solution)/shard_map/ppermute | solution.py:360
  8.7 3.4 %collective-permute-start.1 = (f32[1,6,256]{2,0,1:T(1,128)S(1)}, f32[1,6,256]{2,0,1:T(1,128)S(1)}, u32[]{:S(2)}, u32[]{:S(2)}) collective-permute-start(f32[1,6,256]{2,0,1:T(1,128)S(1)} %get-tuple-element.30), channel_id=1, source_target_pairs={{0,4},{4,8},{8,12},{12,16},{16,20},{20,24},{24,28},{28,32},{32,36}... | collective-permute-start | bytes 18440 | tf_op jit(solution)/shard_map/ppermute | solution.py:359
  12.1 1.6 %fusion.27 = (f32[1,128,256]{2,1,0:T(8,128)}, f32[128,256]{1,0:T(8,128)S(1)}) fusion(s32[128,256]{1,0:T(8,128)} %param.11), kind=kLoop, calls=%fused_computation.67 | loop fusion | flops 65536 | bytes 393216 | tf_op jit(solution)/shard_map/transpose;broadcast_in_dim | solution.py:400
  13.8 1.3 %reverse_multiply_fusion = f32[128,3,2,256]{3,0,2,1:T(8,128)S(1)} fusion(f32[128,3,2,256]{3,0,2,1:T(8,128)} %bitcast.51), kind=kLoop, calls=%fused_computation.18 | loop fusion | flops 196608 | bytes 1572864 | tf_op jit(solution)/shard_map/mul | solution.py:382
  15.1 1.0 slice.67
  16.1 0.3 reverse
  16.4 0.1 slice.89
  16.5 1.0 maximum_add_fusion
  17.7 1.1 %fusion.21 = (f32[32,1024]{1,0:T(8,128)S(1)}, f32[32,1024]{1,0:T(8,128)S(1)}, f32[32,1024]{1,0:T(8,128)S(1)}, f32[32,1024]{1,0:T(8,128)S(1)}) fusion(s32[1024]{0:T(1024)S(1)} %pad_add_fusion, s32[32]{0:T(128)S(1)} %iota_multiply_fusion, f32[1024]{0:T(1024)S(1)} %fusion.26), kind=kLoop, calls=%fused_computation.45 | loop fusion | flops 950272 | bytes 532608 | tf_op jit(solution)/shard_map/cos | solution.py:338
  18.8 0.2 convolution_multiply_fusion.1
  19.0 2.7 %multiply_subtract_fusion = f32[32,32,1024]{2,1,0:T(8,128)} fusion(f32[32,1024]{1,0:T(8,128)S(1)} %get-tuple-element.39, f32[32,1024]{1,0:T(8,128)S(1)} %get-tuple-element.38, f32[32,1024]{1,0:T(8,128)S(1)} %get-tuple-element.40, f32[32,1024]{1,0:T(8,128)S(1)} %get-tuple-element.37), kind=kLoop, calls=%fused_computation.1 | loop fusion | flops 3145728 | bytes 4718592 | tf_op jit(solution)/shard_map/sub | solution.py:338
  21.7 0.1 pad_maximum_fusion.4
  21.8 3.0 %multiply_bitcast_fusion = (f32[6,128,256]{2,1,0:T(8,128)}, f32[6,128,256]{2,1,0:T(8,128)}) fusion(f32[128,6,256]{2,0,1:T(8,128)S(1)} %copy-done.5, f32[128,6]{0,1:T(8,128)S(1)} %convolution_multiply_fusion.1, f32[128,6,256]{2,0,1:T(8,128)S(1)} %copy-done.6, f32[128,3,2,256]{3,0,2,1:T(8,128)S(1)} %reverse_multiply_fusion, f32[128,6,256]{2,0,1:T(8,128)S(1)} %copy-done.2, ...), kind=kLoop, calls=%fused_computation.19 | loop fusion | flops 2752512 | bytes 4871168 | tf_op jit(solution)/shard_map/transpose | solution.py:443
  24.8 16.3 %shard_map.103 = (f32[6,32,1024]{2,1,0:T(8,128)}, f32[1,32,1024]{2,1,0:T(8,128)}) custom-call(f32[6,128,256]{2,1,0:T(8,128)} %get-tuple-element.28.refs_0_.r_ref, f32[1,128,256]{2,1,0:T(8,128)} %get-tuple-element.33.refs_1_), custom_call_target="tpu_custom_call" | custom-call | tf_op jit(solution)/shard_map/pallas_call | solution.py:202
  41.1 4.2 %fusion.30 = f32[192,1024]{1,0:T(8,128)S(1)} fusion(f32[192,1024]{1,0:T(8,128)} %bitcast.57, f32[1024,1024]{1,0:T(8,128)} %bitcast.49), kind=kOutput, calls=%fused_computation.70 | convolution fusion | flops 1207959552 | bytes 5767168 | tf_op jit(solution)/shard_map/dot_general | solution.py:403
  45.3 0.3 multiply_reduce_fusion
  45.7 2.4 %bitcast_multiply_fusion = (f32[192,1024]{1,0:T(8,128)S(1)}, f32[192,1024]{1,0:T(8,128)S(1)}) fusion(f32[32,1024]{1,0:T(8,128)S(1)} %bitcast.58, f32[192,1024]{1,0:T(8,128)S(1)} %bitcast.53, f32[1024,1024]{1,0:T(8,128)S(1)} %bitcast.50), kind=kOutput, calls=%fused_computation.17 | convolution fusion | flops 1208352768 | bytes 6684672 | tf_op jit(solution)/shard_map/dot_general | solution.py:410
  48.2 0.9 slice_reduce_fusion
  49.1 0.9 convolution_bitcast_fusion
  50.1 0.7 reshape.248.cpk_ref
  50.7 17.3 %shard_map.104 = (f32[6,128,256]{2,1,0:T(8,128)}, f32[4,6,64]{2,1,0:T(8,128)}, f32[4,6,256]{2,1,0:T(8,128)}, f32[4,6,256]{2,1,0:T(8,128)}) custom-call(f32[6,32,1024]{2,1,0:T(8,128)} %copy-done.3, f32[4,6,64]{2,1,0:T(8,128)} %reshape.248.cpk_ref, f32[4,6,256]{2,1,0:T(8,128)} %bitcast.62, f32[4,6,256]{2,1,0:T(8,128)} %bitcast.61), custom_call_target="tpu_custom_call" | custom-call | tf_op jit(solution)/shard_map/pallas_call | solution.py:316
  68.0 0.7 copy.24
  68.8 0.1 reshape.245
  69.1 1.2 %copy.25.hc_ref = f32[2,6,128,1]{3,2,1,0:T(8,128)} copy(f32[2,6,128,1]{2,0,1,3:T(2,128)S(1)} %maximum_bitcast_fusion) | data formatting | bytes 12288 | tf_op jit(solution)/shard_map/broadcast_in_dim | solution.py:445
  70.3 0.7 slice_select_fusion
  71.0 0.6 select_maximum_fusion.hr_ref
  71.6 25.4 %shard_map.105 = (f32[8,128]{1,0:T(8,128)}, f32[6,128,256]{2,1,0:T(8,128)}) custom-call(f32[6,128,256]{2,1,0:T(8,128)} %get-tuple-element.28.refs_0_.r_ref, f32[6,128,256]{2,1,0:T(8,128)} %get-tuple-element.15.p_ref, f32[6,128,256]{2,1,0:T(8,128)} %get-tuple-element.27.s_ref, f32[128,256]{1,0:T(8,128)} %copy-done.4, f32[2,8,256]{2,1,0:T(8,128)} %select_maximum_fusion.hr_ref, ...), custom_call_target="tpu_custom_call" | custom-call | tf_op jit(solution)/shard_map/pallas_call | solution.py:123
  97.1 1.3 %slice_bitcast_fusion = f32[3]{0:T(128)} fusion(f32[8,128]{1,0:T(8,128)} %get-tuple-element.19.f_ref), kind=kLoop, calls=%fused_computation.64 | loop fusion | bytes 24 | tf_op jit(solution)/shard_map/squeeze | solution.py:456
  98.3 2.8 %shard_map.106 = (f32[6,128,256]{2,1,0:T(8,128)}, f32[6,128,256]{2,1,0:T(8,128)}) custom-call(f32[8,128]{1,0:T(8,128)} %get-tuple-element.19.f_ref, f32[6,128,256]{2,1,0:T(8,128)} %bitcast.52, f32[6,128,256]{2,1,0:T(8,128)} %get-tuple-element.15.p_ref, f32[6,128,256]{2,1,0:T(8,128)} %get-tuple-element.28.refs_0_.r_ref, f32[6,128,256]{2,1,0:T(8,128)} %get-tuple-element.20.i_ref), custom_call_target="tpu_custom_call" | custom-call | tf_op jit(solution)/shard_map/pallas_call | solution.py:153
  (39 shorter events, 0.6 us)
Async XLA Ops:
  0.6 18.2 %copy-start = (f32[4,6]{1,0:T(4,128)S(1)}, f32[4,6]{1,0:T(4,128)}, u32[]{:S(2)}) copy-start(f32[4,6]{1,0:T(4,128)} %param.13) | copy-start | bytes 292
  0.6 18.2 %copy-start.9 = (s32[128]{0:T(128)S(1)}, s32[128]{0:T(128)}, u32[]{:S(2)}) copy-start(s32[128]{0:T(128)} %param.12) | copy-start | bytes 1540
  2.8 19.0 %collective-permute-start.2 = (f32[128,6,1]{2,0,1:T(8,128)}, f32[128,6,1]{2,0,1:T(8,128)}, u32[]{:S(2)}, u32[]{:S(2)}) collective-permute-start(f32[128,6,1]{2,0,1:T(8,128)} %get-tuple-element.31), channel_id=1, source_target_pairs={{1,0},{2,1},{3,2},{0,3},{5,4},{6,5},{7,6},{4,7},{9,8},{10,9},{11,1... | collective-permute-start | bytes 9224 | tf_op jit(solution)/shard_map/ppermute | solution.py:360
  5.4 16.4 %collective-permute-start.3 = (f32[128,6,1]{2,0,1:T(8,128)}, f32[128,6,1]{2,0,1:T(8,128)}, u32[]{:S(2)}, u32[]{:S(2)}) collective-permute-start(f32[128,6,1]{2,0,1:T(8,128)} %get-tuple-element.32), channel_id=1, source_target_pairs={{0,1},{1,2},{2,3},{3,0},{4,5},{5,6},{6,7},{7,4},{8,9},{9,10},{10,1... | collective-permute-start | bytes 9224 | tf_op jit(solution)/shard_map/ppermute | solution.py:359
  6.2 15.5 %collective-permute-start = (f32[1,6,256]{2,0,1:T(1,128)S(1)}, f32[1,6,256]{2,0,1:T(1,128)S(1)}, u32[]{:S(2)}, u32[]{:S(2)}) collective-permute-start(f32[1,6,256]{2,0,1:T(1,128)S(1)} %get-tuple-element.29), channel_id=1, source_target_pairs={{4,0},{8,4},{12,8},{16,12},{20,16},{24,20},{28,24},{32,28},{36,32}... | collective-permute-start | bytes 18440 | tf_op jit(solution)/shard_map/ppermute | solution.py:360
  8.7 13.1 %collective-permute-start.1 = (f32[1,6,256]{2,0,1:T(1,128)S(1)}, f32[1,6,256]{2,0,1:T(1,128)S(1)}, u32[]{:S(2)}, u32[]{:S(2)}) collective-permute-start(f32[1,6,256]{2,0,1:T(1,128)S(1)} %get-tuple-element.30), channel_id=1, source_target_pairs={{0,4},{4,8},{8,12},{12,16},{16,20},{20,24},{24,28},{28,32},{32,36}... | collective-permute-start | bytes 18440 | tf_op jit(solution)/shard_map/ppermute | solution.py:359
  13.7 8.1 %copy-start.4 = (f32[128,256]{1,0:T(8,128)}, f32[128,256]{1,0:T(8,128)S(1)}, u32[]{:S(2)}) copy-start(f32[128,256]{1,0:T(8,128)S(1)} %get-tuple-element.34.m_ref) | copy-start | bytes 393220
  13.7 8.1 %copy-start.2 = (f32[128,6,256]{2,0,1:T(8,128)S(1)}, f32[128,6,256]{2,0,1:T(8,128)}, u32[]{:S(2)}) copy-start(f32[128,6,256]{2,0,1:T(8,128)} %param.9) | copy-start | bytes 2359300
  13.7 8.1 %copy-start.5 = (f32[128,6,256]{2,0,1:T(8,128)S(1)}, f32[128,6,256]{2,0,1:T(8,128)}, u32[]{:S(2)}) copy-start(f32[128,6,256]{2,0,1:T(8,128)} %param.10) | copy-start | bytes 2359300
  13.8 8.1 %copy-start.6 = (f32[128,6,256]{2,0,1:T(8,128)S(1)}, f32[128,6,256]{2,0,1:T(8,128)}, u32[]{:S(2)}) copy-start(f32[128,6,256]{2,0,1:T(8,128)} %param.8) | copy-start | bytes 2359300
  41.1 4.6 %copy-start.1 = (f32[32,32,1024]{2,1,0:T(8,128)S(1)}, f32[32,32,1024]{2,1,0:T(8,128)}, u32[]{:S(2)}) copy-start(f32[32,32,1024]{2,1,0:T(8,128)} %multiply_subtract_fusion) | copy-start | bytes 12582916
  41.1 4.6 %copy-start.7 = (f32[1,32,1024]{2,1,0:T(8,128)S(1)}, f32[1,32,1024]{2,1,0:T(8,128)}, u32[]{:S(2)}) copy-start(f32[1,32,1024]{2,1,0:T(8,128)} %get-tuple-element.13) | copy-start | bytes 393220
  45.7 3.4 %copy-start.8 = (s32[2,4]{1,0:T(2,128)S(1)}, s32[2,4]{1,0:T(2,128)}, u32[]{:S(2)}) copy-start(s32[2,4]{1,0:T(2,128)} %constant.71) | copy-start | bytes 100
  48.2 2.6 %copy-start.3 = (f32[6,32,1024]{2,1,0:T(8,128)}, f32[6,32,1024]{2,1,0:T(8,128)S(1)}, u32[]{:S(2)}) copy-start(f32[6,32,1024]{2,1,0:T(8,128)S(1)} %broadcast_multiply_fusion.x_ref) | copy-start | bytes 2359300

commit v16 on v15

--- a/solution.py
+++ b/solution.py
@@ -327,26 +327,22 @@
     )(x, cpk, last, first)
 
 
-def dft_table(length):
-    half = length // 2
+def cas_table(length):
     root = int(round(math.sqrt(length)))
-    cols = jnp.concatenate([jnp.arange(half + 1), jnp.arange(1, half)])
-    phase = jnp.where(jnp.arange(length) > half, 0.5 * math.pi, 0.0).astype(jnp.float32)
+    index = jnp.arange(length)
     step = 2.0 * math.pi / length
-    coarse = step * ((root * jnp.arange(length // root)[:, None] * cols[None, :]) % length).astype(jnp.float32)
-    fine = step * ((jnp.arange(root)[:, None] * cols[None, :]) % length).astype(jnp.float32) - phase
-    table = jnp.cos(coarse)[:, None] * jnp.cos(fine)[None] - jnp.sin(coarse)[:, None] * jnp.sin(fine)[None]
+    coarse = step * ((root * jnp.arange(length // root)[:, None] * index[None, :]) % length).astype(jnp.float32)
+    fine = step * ((jnp.arange(root)[:, None] * index[None, :]) % length).astype(jnp.float32) - 0.25 * math.pi
+    scale = math.sqrt(2.0)
+    table = jnp.cos(coarse)[:, None] * (scale * jnp.cos(fine))[None] - jnp.sin(coarse)[:, None] * (
+        scale * jnp.sin(fine)
+    )[None]
     return table.reshape(length, length)
 
 
 def paired_inverse(precond):
-    length = precond.shape[2]
-    half = length // 2
-    low = precond[:, :, : half + 1]
-    mirror = jnp.flip(precond[:, :, half + 1 :], axis=2)
-    inner = jnp.concatenate([jnp.zeros_like(low[:, :, :1]), mirror, jnp.zeros_like(low[:, :, :1])], axis=2)
-    paired = low + inner
-    return jnp.concatenate([paired, paired[:, :, 1:half]], axis=2)
+    mirror = jnp.flip(jnp.roll(precond, -1, axis=2), axis=2)
+    return 0.5 * (precond + mirror)
 
 
 def with_halo(x, sides, width, wrap):
@@ -399,17 +395,19 @@
     residual_t = jnp.transpose(residual, (1, 0, 2))
     solid_t = jnp.transpose(solid, (1, 0, 2))
     lines, solid_lines = to_lines([residual_t, solid_t], sector_count)
+    table = cas_table(around_cells)
     spectrum = lax.optimization_barrier(
-        jnp.dot(
+        lax.dot_general(
             lax.optimization_barrier(lines.reshape(-1, around_cells)),
-            dft_table(around_cells),
+            table,
+            (((1,), (1,)), ((), ())),
             precision=lax.Precision.HIGH,
         )
     ).reshape(lines.shape)
     mixed = jnp.sum(paired_inverse(precond)[:, :, None] * spectrum[None], axis=1)
     smoothed_lines = lax.dot_general(
         mixed.reshape(-1, around_cells),
-        dft_table(around_cells),
+        table,
         (((1,), (1,)), ((), ())),
         precision=lax.Precision.HIGH,
     ) / around_cells

time: 102 us -> 104 us (1.020)
    mul x1 -> x3, other arithmetic: 0.01 us -> 1.53 us  [the longest x1 0.99 us: paired_inverse(): return 0.5 * (precond + mirror)]
    mul x1, other arithmetic: 1.34 us -> 0.07 us  [apply_operator(): return (stiffness + 4.5) * field - beside - 0.5 * swap_radial(field)]
  transfers between devices with their start and end apart: 4 -> 4, of which waited for: 0 -> 0; matrix products, arithmetic and copies ran while one was open for 10% -> 11% of each run, Pallas kernels for 0% -> 0%
where the time goes in v16:
time: 104 us
  Pallas kernels  61.8 us (59%)
  other arithmetic  13.6 us (13%)
  local copies, waits for them, and re-layouts  10.6 us (10%)
  starting transfers between devices  8.48 us (8%)
  matrix products  8.3 us (8%)
    pallas_call x1, Pallas kernels, image_and_totals(): pl.pallas_call(functools.partial(_ar_kernel, float(cell_total)), out_shap...  25.4 us
    pallas_call x1, Pallas kernels, from_lines_with_halo(): pl.pallas_call(functools.partial(_from_lines_kernel, (n_ax, n)), out_shap...  17.3 us
    pallas_call x1, Pallas kernels, to_lines(): pl.pallas_call(functools.partial(_to_lines_kernel, n, count), out_shape=[...  16.3 us
    ppermute x2, starting transfers between devices, with_halo(): after = lax.ppermute(first, axis, down)  5.08 us
    dot_general x1, matrix products, shards(): lax.dot_general(lax.optimization_barrier(lines.reshape(-1, around_cells))...  4.81 us
    sub x1, other arithmetic, cas_table(): jnp.cos(coarse)[:, None] * (scale * jnp.cos(fine))[None]  3.59 us
    ppermute x2, starting transfers between devices, with_halo(): before = lax.ppermute(last, axis, up)  3.4 us
    slice x2, local copies, waits for them, and re-layouts, with_halo(): first = lax.slice_in_dim(x, 0, width, axis=dim)  3.01 us
  transfers between devices with their start and end apart: 4, of which 0 were waited for; matrix products, arithmetic and copies ran while one was open for 11% of the time, Pallas kernels for 0%

profile of v16, /device:TPU:4, one launch (start us, length us, event | category | flops | bytes accessed | tf_op | source)
XLA Modules:
  0.0 103.7 jit_solution(2063647580116023827)
XLA Ops:
  0.7 2.2 %fusion.29 = (f32[128,6,1]{2,0,1:T(8,128)}, f32[128,6,1]{2,0,1:T(8,128)}) fusion(f32[128,6,256]{2,0,1:T(8,128)} %param.9), kind=kLoop, calls=%fused_computation.66 | loop fusion | bytes 12288 | tf_op jit(solution)/shard_map/slice | solution.py:354
  2.8 2.6 %collective-permute-start.2 = (f32[128,6,1]{2,0,1:T(8,128)}, f32[128,6,1]{2,0,1:T(8,128)}, u32[]{:S(2)}, u32[]{:S(2)}) collective-permute-start(f32[128,6,1]{2,0,1:T(8,128)} %get-tuple-element.31), channel_id=1, source_target_pairs={{1,0},{2,1},{3,2},{0,3},{5,4},{6,5},{7,6},{4,7},{9,8},{10,9},{11,1... | collective-permute-start | bytes 9224 | tf_op jit(solution)/shard_map/ppermute | solution.py:356
  5.5 0.8 fusion.28
  6.3 2.4 %collective-permute-start = (f32[1,6,256]{2,0,1:T(1,128)S(1)}, f32[1,6,256]{2,0,1:T(1,128)S(1)}, u32[]{:S(2)}, u32[]{:S(2)}) collective-permute-start(f32[1,6,256]{2,0,1:T(1,128)S(1)} %get-tuple-element.29), channel_id=1, source_target_pairs={{4,0},{8,4},{12,8},{16,12},{20,16},{24,20},{28,24},{32,28},{36,32}... | collective-permute-start | bytes 18440 | tf_op jit(solution)/shard_map/ppermute | solution.py:356
  8.8 3.4 %collective-permute-start.1 = (f32[1,6,256]{2,0,1:T(1,128)S(1)}, f32[1,6,256]{2,0,1:T(1,128)S(1)}, u32[]{:S(2)}, u32[]{:S(2)}) collective-permute-start(f32[1,6,256]{2,0,1:T(1,128)S(1)} %get-tuple-element.30), channel_id=1, source_target_pairs={{0,4},{4,8},{8,12},{12,16},{16,20},{20,24},{24,28},{28,32},{32,36}... | collective-permute-start | bytes 18440 | tf_op jit(solution)/shard_map/ppermute | solution.py:355
  12.2 0.5 sine_multiply_fusion
  12.7 1.0 slice.65
  13.8 0.7 slice.66
  14.5 1.7 %fusion.27 = (f32[1,128,256]{2,1,0:T(8,128)}, f32[128,256]{1,0:T(8,128)S(1)}) fusion(s32[128,256]{1,0:T(8,128)} %param.11), kind=kLoop, calls=%fused_computation.64 | loop fusion | flops 65536 | bytes 393216 | tf_op jit(solution)/shard_map/transpose;broadcast_in_dim | solution.py:396
  16.2 1.2 %fusion.22 = (f32[32,1024]{1,0:T(8,128)S(1)}, f32[32,1024]{1,0:T(8,128)}) fusion(s32[32]{0:T(128)S(1)} %iota_multiply_fusion), kind=kLoop, calls=%fused_computation.46 | loop fusion | flops 458752 | bytes 262272 | tf_op jit(solution)/shard_map/cos | solution.py:337
  17.6 0.6 rev.9
  18.2 1.0 add_multiply_fusion
  19.2 0.2 convolution_multiply_fusion.1
  19.4 3.6 %multiply_subtract_fusion = f32[32,32,1024]{2,1,0:T(8,128)} fusion(f32[32,1024]{1,0:T(8,128)S(1)} %get-tuple-element.39, f32[32,1024]{1,0:T(8,128)} %get-tuple-element.36, f32[32,1024]{1,0:T(8,128)S(1)} %get-tuple-element.40, f32[32,1024]{1,0:T(8,128)S(1)} %get-tuple-element.35), kind=kLoop, calls=%fused_computation.1 | loop fusion | flops 3145728 | bytes 4718592 | tf_op jit(solution)/shard_map/sub | solution.py:337
  23.1 3.0 %multiply_bitcast_fusion = (f32[6,128,256]{2,1,0:T(8,128)}, f32[6,128,256]{2,1,0:T(8,128)}) fusion(f32[128,6,256]{2,0,1:T(8,128)S(1)} %copy-done.5, f32[128,6]{0,1:T(8,128)S(1)} %convolution_multiply_fusion.1, f32[128,6,256]{2,0,1:T(8,128)S(1)} %copy-done.6, f32[128,3,2,256]{3,0,2,1:T(8,128)S(1)} %reverse_multiply_fusion, f32[128,6,256]{2,0,1:T(8,128)S(1)} %copy-done.2, ...), kind=kLoop, calls=%fused_computation.19 | loop fusion | flops 2752512 | bytes 4871168 | tf_op jit(solution)/shard_map/transpose | solution.py:441
  26.1 16.3 %shard_map.103 = (f32[6,32,1024]{2,1,0:T(8,128)}, f32[1,32,1024]{2,1,0:T(8,128)}) custom-call(f32[6,128,256]{2,1,0:T(8,128)} %get-tuple-element.28.refs_0_.r_ref, f32[1,128,256]{2,1,0:T(8,128)} %get-tuple-element.33.refs_1_), custom_call_target="tpu_custom_call" | custom-call | tf_op jit(solution)/shard_map/pallas_call | solution.py:202
  42.4 4.8 %fusion.30 = f32[192,1024]{1,0:T(8,128)S(1)} fusion(f32[192,1024]{1,0:T(8,128)} %bitcast.56, f32[1024,1024]{1,0:T(8,128)} %bitcast.48), kind=kOutput, calls=%fused_computation.67 | convolution fusion | flops 1207959552 | bytes 5767168 | tf_op jit(solution)/shard_map/dot_general | solution.py:400
  47.2 0.3 multiply_reduce_fusion
  47.6 2.4 %bitcast_multiply_fusion = (f32[192,1024]{1,0:T(8,128)S(1)}, f32[192,1024]{1,0:T(8,128)S(1)}) fusion(f32[32,1024]{1,0:T(8,128)S(1)} %bitcast.57, f32[192,1024]{1,0:T(8,128)S(1)} %bitcast.52, f32[1024,1024]{1,0:T(8,128)S(1)} %bitcast.49), kind=kOutput, calls=%fused_computation.17 | convolution fusion | flops 1208352768 | bytes 6684672 | tf_op jit(solution)/shard_map/dot_general | solution.py:408
  50.1 0.9 slice_reduce_fusion
  51.0 0.9 convolution_bitcast_fusion
  52.0 0.7 reshape.190.cpk_ref
  52.6 17.3 %shard_map.104 = (f32[6,128,256]{2,1,0:T(8,128)}, f32[4,6,64]{2,1,0:T(8,128)}, f32[4,6,256]{2,1,0:T(8,128)}, f32[4,6,256]{2,1,0:T(8,128)}) custom-call(f32[6,32,1024]{2,1,0:T(8,128)} %copy-done.3, f32[4,6,64]{2,1,0:T(8,128)} %reshape.190.cpk_ref, f32[4,6,256]{2,1,0:T(8,128)} %bitcast.60, f32[4,6,256]{2,1,0:T(8,128)} %bitcast.59), custom_call_target="tpu_custom_call" | custom-call | tf_op jit(solution)/shard_map/pallas_call | solution.py:316
  69.9 0.7 copy.24
  70.6 0.1 reshape.187
  71.0 1.2 %copy.25.hc_ref = f32[2,6,128,1]{3,2,1,0:T(8,128)} copy(f32[2,6,128,1]{2,0,1,3:T(2,128)S(1)} %maximum_bitcast_fusion) | data formatting | bytes 12288 | tf_op jit(solution)/shard_map/broadcast_in_dim | solution.py:443
  72.2 0.7 slice_select_fusion.1
  72.9 0.7 slice_select_fusion
  73.6 0.6 select_maximum_fusion.hr_ref
  74.2 25.4 %shard_map.105 = (f32[8,128]{1,0:T(8,128)}, f32[6,128,256]{2,1,0:T(8,128)}) custom-call(f32[6,128,256]{2,1,0:T(8,128)} %get-tuple-element.28.refs_0_.r_ref, f32[6,128,256]{2,1,0:T(8,128)} %get-tuple-element.15.p_ref, f32[6,128,256]{2,1,0:T(8,128)} %get-tuple-element.27.s_ref, f32[128,256]{1,0:T(8,128)} %copy-done.4, f32[2,8,256]{2,1,0:T(8,128)} %select_maximum_fusion.hr_ref, ...), custom_call_target="tpu_custom_call" | custom-call | tf_op jit(solution)/shard_map/pallas_call | solution.py:123
  99.6 1.3 %slice_bitcast_fusion = f32[3]{0:T(128)} fusion(f32[8,128]{1,0:T(8,128)} %get-tuple-element.19.f_ref), kind=kLoop, calls=%fused_computation.61 | loop fusion | bytes 24 | tf_op jit(solution)/shard_map/squeeze | solution.py:454
  100.9 2.8 %shard_map.106 = (f32[6,128,256]{2,1,0:T(8,128)}, f32[6,128,256]{2,1,0:T(8,128)}) custom-call(f32[8,128]{1,0:T(8,128)} %get-tuple-element.19.f_ref, f32[6,128,256]{2,1,0:T(8,128)} %bitcast.50, f32[6,128,256]{2,1,0:T(8,128)} %get-tuple-element.15.p_ref, f32[6,128,256]{2,1,0:T(8,128)} %get-tuple-element.28.refs_0_.r_ref, f32[6,128,256]{2,1,0:T(8,128)} %get-tuple-element.20.i_ref), custom_call_target="tpu_custom_call" | custom-call | tf_op jit(solution)/shard_map/pallas_call | solution.py:153
  (35 shorter events, 0.6 us)
Async XLA Ops:
  0.6 18.6 %copy-start = (f32[4,6]{1,0:T(4,128)S(1)}, f32[4,6]{1,0:T(4,128)}, u32[]{:S(2)}) copy-start(f32[4,6]{1,0:T(4,128)} %param.13) | copy-start | bytes 292
  0.6 22.3 %copy-start.2 = (f32[128,6,256]{2,0,1:T(8,128)S(1)}, f32[128,6,256]{2,0,1:T(8,128)}, u32[]{:S(2)}) copy-start(f32[128,6,256]{2,0,1:T(8,128)} %param.9) | copy-start | bytes 2359300
  0.7 18.5 %copy-start.9 = (s32[128]{0:T(128)S(1)}, s32[128]{0:T(128)}, u32[]{:S(2)}) copy-start(s32[128]{0:T(128)} %param.12) | copy-start | bytes 1540
  2.8 20.2 %collective-permute-start.2 = (f32[128,6,1]{2,0,1:T(8,128)}, f32[128,6,1]{2,0,1:T(8,128)}, u32[]{:S(2)}, u32[]{:S(2)}) collective-permute-start(f32[128,6,1]{2,0,1:T(8,128)} %get-tuple-element.31), channel_id=1, source_target_pairs={{1,0},{2,1},{3,2},{0,3},{5,4},{6,5},{7,6},{4,7},{9,8},{10,9},{11,1... | collective-permute-start | bytes 9224 | tf_op jit(solution)/shard_map/ppermute | solution.py:356
  5.5 17.6 %collective-permute-start.3 = (f32[128,6,1]{2,0,1:T(8,128)}, f32[128,6,1]{2,0,1:T(8,128)}, u32[]{:S(2)}, u32[]{:S(2)}) collective-permute-start(f32[128,6,1]{2,0,1:T(8,128)} %get-tuple-element.32), channel_id=1, source_target_pairs={{0,1},{1,2},{2,3},{3,0},{4,5},{5,6},{6,7},{7,4},{8,9},{9,10},{10,1... | collective-permute-start | bytes 9224 | tf_op jit(solution)/shard_map/ppermute | solution.py:355
  6.3 16.8 %collective-permute-start = (f32[1,6,256]{2,0,1:T(1,128)S(1)}, f32[1,6,256]{2,0,1:T(1,128)S(1)}, u32[]{:S(2)}, u32[]{:S(2)}) collective-permute-start(f32[1,6,256]{2,0,1:T(1,128)S(1)} %get-tuple-element.29), channel_id=1, source_target_pairs={{4,0},{8,4},{12,8},{16,12},{20,16},{24,20},{28,24},{32,28},{36,32}... | collective-permute-start | bytes 18440 | tf_op jit(solution)/shard_map/ppermute | solution.py:356
  8.8 14.3 %collective-permute-start.1 = (f32[1,6,256]{2,0,1:T(1,128)S(1)}, f32[1,6,256]{2,0,1:T(1,128)S(1)}, u32[]{:S(2)}, u32[]{:S(2)}) collective-permute-start(f32[1,6,256]{2,0,1:T(1,128)S(1)} %get-tuple-element.30), channel_id=1, source_target_pairs={{0,4},{4,8},{8,12},{12,16},{16,20},{20,24},{24,28},{28,32},{32,36}... | collective-permute-start | bytes 18440 | tf_op jit(solution)/shard_map/ppermute | solution.py:355
  14.5 8.6 %copy-start.5 = (f32[128,6,256]{2,0,1:T(8,128)S(1)}, f32[128,6,256]{2,0,1:T(8,128)}, u32[]{:S(2)}) copy-start(f32[128,6,256]{2,0,1:T(8,128)} %param.10) | copy-start | bytes 2359300
  14.5 8.6 %copy-start.6 = (f32[128,6,256]{2,0,1:T(8,128)S(1)}, f32[128,6,256]{2,0,1:T(8,128)}, u32[]{:S(2)}) copy-start(f32[128,6,256]{2,0,1:T(8,128)} %param.8) | copy-start | bytes 2359300
  16.2 9.9 %copy-start.4 = (f32[128,256]{1,0:T(8,128)}, f32[128,256]{1,0:T(8,128)S(1)}, u32[]{:S(2)}) copy-start(f32[128,256]{1,0:T(8,128)S(1)} %get-tuple-element.34.m_ref) | copy-start | bytes 393220
  42.4 5.2 %copy-start.1 = (f32[32,32,1024]{2,1,0:T(8,128)S(1)}, f32[32,32,1024]{2,1,0:T(8,128)}, u32[]{:S(2)}) copy-start(f32[32,32,1024]{2,1,0:T(8,128)} %multiply_subtract_fusion) | copy-start | bytes 12582916
  42.4 5.2 %copy-start.7 = (f32[1,32,1024]{2,1,0:T(8,128)S(1)}, f32[1,32,1024]{2,1,0:T(8,128)}, u32[]{:S(2)}) copy-start(f32[1,32,1024]{2,1,0:T(8,128)} %get-tuple-element.13) | copy-start | bytes 393220
  47.6 3.4 %copy-start.8 = (s32[2,4]{1,0:T(2,128)S(1)}, s32[2,4]{1,0:T(2,128)}, u32[]{:S(2)}) copy-start(s32[2,4]{1,0:T(2,128)} %constant.65) | copy-start | bytes 100
  50.1 2.6 %copy-start.3 = (f32[6,32,1024]{2,1,0:T(8,128)}, f32[6,32,1024]{2,1,0:T(8,128)S(1)}, u32[]{:S(2)}) copy-start(f32[6,32,1024]{2,1,0:T(8,128)S(1)} %broadcast_multiply_fusion.x_ref) | copy-start | bytes 2359300

commit v17 on v15

--- a/solution.py
+++ b/solution.py
@@ -31,16 +31,26 @@
     ]
 
 
-def _image_and_sums(r_ref, p_ref, s_ref, m_ref, hr_ref, hc_ref, img_ref):
+def _image_and_sums(r_ref, p_ref, s_ref, m_ref, br_ref, ar_ref, hc_ref, img_ref):
     comps, rows, width = p_ref.shape
+    ax = lax.axis_index("ax")
+    first_slab = ax == 0
+    last_slab = ax == lax.axis_size("ax") - 1
+
+    def before_row(q):
+        return jnp.where(first_slab, 0.0, br_ref[br_ref.shape[0] - 1, q : q + 1, :])
+
+    def after_row(q):
+        return jnp.where(last_slab, 0.0, ar_ref[0, q : q + 1, :])
+
     row = lax.broadcasted_iota(jnp.int32, (rows, width), 0)
     lane = lax.broadcasted_iota(jnp.int32, (rows, width), 1)
     solid = m_ref[...]
     acc = [jnp.zeros((1, width), jnp.float32) for _ in range(5)]
     for q in range(comps):
         field = p_ref[q]
-        up = jnp.where(row == 0, hr_ref[0, q : q + 1, :], pltpu.roll(field, 1, 0))
-        down = jnp.where(row == rows - 1, hr_ref[1, q : q + 1, :], pltpu.roll(field, rows - 1, 0))
+        up = jnp.where(row == 0, before_row(q), pltpu.roll(field, 1, 0))
+        down = jnp.where(row == rows - 1, after_row(q), pltpu.roll(field, rows - 1, 0))
         left = jnp.where(lane == 0, hc_ref[0, q], pltpu.roll(field, 1, 1))
         right = jnp.where(lane == width - 1, hc_ref[1, q], pltpu.roll(field, width - 1, 1))
         beside = down + up + right + left
@@ -74,7 +84,7 @@
     return out
 
 
-def _ar_kernel(cell_total, r_ref, p_ref, s_ref, m_ref, hr_ref, hc_ref, o_ref, img_ref, recv_a, recv_b, own, send_sems, recv_sems):
+def _ar_kernel(cell_total, r_ref, p_ref, s_ref, m_ref, br_ref, ar_ref, hc_ref, o_ref, img_ref, recv_a, recv_b, own, send_sems, recv_sems):
     recvs = (recv_a, recv_b)
     groups = _groups()
     for r in recvs:
@@ -85,7 +95,7 @@
         for d in range(1, n):
             pl.semaphore_signal(barrier, inc=1, device_id=dev((mine + d) % n), device_id_type=MESH)
             count += 1
-    own[0] = _image_and_sums(r_ref, p_ref, s_ref, m_ref, hr_ref, hc_ref, img_ref)
+    own[0] = _image_and_sums(r_ref, p_ref, s_ref, m_ref, br_ref, ar_ref, hc_ref, img_ref)
     pl.semaphore_wait(barrier, count)
     base = 0
     for g, (n, mine, dev) in enumerate(groups):
@@ -119,14 +129,14 @@
             o_ref[...] = finished
 
 
-def image_and_totals(residual, prec, stiffness, solid, halo_rows, halo_cols, cell_total, cid):
+def image_and_totals(residual, prec, stiffness, solid, before_rows, after_rows, halo_cols, cell_total, cid):
     return pl.pallas_call(
         functools.partial(_ar_kernel, float(cell_total)),
         out_shape=[
             jax.ShapeDtypeStruct((8, 128), jnp.float32),
             jax.ShapeDtypeStruct(prec.shape, jnp.float32),
         ],
-        in_specs=[pl.BlockSpec(memory_space=pltpu.VMEM)] * 6,
+        in_specs=[pl.BlockSpec(memory_space=pltpu.VMEM)] * 7,
         out_specs=[pl.BlockSpec(memory_space=pltpu.VMEM)] * 2,
         scratch_shapes=[
             pltpu.VMEM((32, 8, 128), jnp.float32),
@@ -136,7 +146,7 @@
             pltpu.SemaphoreType.DMA((40,)),
         ],
         compiler_params=pltpu.CompilerParams(collective_id=cid, has_side_effects=True),
-    )(residual, prec, stiffness, solid, halo_rows, halo_cols)
+    )(residual, prec, stiffness, solid, before_rows, after_rows, halo_cols)
 
 
 def _update_kernel(f_ref, d_ref, p_ref, r_ref, i_ref, dn_ref, rn_ref):
@@ -415,7 +425,6 @@
     ) / around_cells
     prec_lines = solid_lines * smoothed_lines.reshape(lines.shape)
     group_rows = lines.shape[1]
-    subl = -(-comp_count // 8) * 8
     edge_at = [(p * sector_width - 1) % around_cells for p in range(sector_count)]
     edge_at += [((p + 1) * sector_width) % around_cells for p in range(sector_count)]
     pick = (jnp.arange(around_cells)[None, :] == jnp.array(edge_at)[:, None]).astype(jnp.float32)
@@ -433,19 +442,15 @@
     prec_t, halo_cols, before_rows, after_rows = from_lines_with_halo(
         prec_lines, cpk, row_pack(prec_lines[:, -1]), row_pack(prec_lines[:, 0]), sector_count
     )
-    ax = lax.axis_index("ax")
-    before_row = jnp.where(ax == 0, 0.0, before_rows[sector_count - 1, :comp_count])
-    after_row = jnp.where(ax == lax.axis_size("ax") - 1, 0.0, after_rows[0, :comp_count])
     got_cols = jnp.transpose(halo_cols[:, :comp_count, : 2 * group_rows], (1, 0, 2))
     got_cols = got_cols.reshape(comp_count, sector_count, 2, group_rows)
     before_col = got_cols[:, :, 0].reshape(comp_count, slab_count)
     after_col = got_cols[:, :, 1].reshape(comp_count, slab_count)
     stiffness_t = jnp.transpose(stiffness, (1, 0, 2))
-    halo_rows = jnp.pad(jnp.stack([before_row, after_row]), ((0, 0), (0, subl - comp_count), (0, 0)))
     halo_cols = jnp.stack([before_col, after_col])[..., None]
     cell_total = slab_count * lax.axis_size("ax") * comp_count * around_cells
     finished, image_t = image_and_totals(
-        residual_t, prec_t, stiffness_t, solid_t[0], halo_rows, halo_cols, cell_total, 0
+        residual_t, prec_t, stiffness_t, solid_t[0], before_rows, after_rows, halo_cols, cell_total, 0
     )
     disp_new_t, residual_new_t = apply_step(
         finished, jnp.transpose(disp, (1, 0, 2)), prec_t, residual_t, image_t

time: 102 us -> 98.8 us (0.969)
  other arithmetic: 12.6 us -> 9.91 us
  waiting for transfers between devices: 0.01 us -> 1.41 us
    ppermute x2, waiting for transfers between devices: 0.01 us -> 1.4 us  [with_halo(): before = lax.ppermute(last, axis, up)]
    transpose x1, other arithmetic: 2.97 us -> 1.59 us  [shards(): stiffness_t = jnp.transpose(stiffness, (1, 0, 2))]
  transfers between devices with their start and end apart: 4 -> 4, of which waited for: 0 -> 1; matrix products, arithmetic and copies ran while one was open for 10% -> 11% of each run, Pallas kernels for 0% -> 0%
where the time goes in v17:
time: 98.8 us; the launch traced here: 98.3 us
  Pallas kernels  61.6 us (62%)
  other arithmetic  9.91 us (10%)
  local copies, waits for them, and re-layouts  8.8 us (9%)
  starting transfers between devices  8 us (8%)
  matrix products  7.71 us (8%)
  waiting for transfers between devices  1.41 us (1%)
    pallas_call x1, Pallas kernels, image_and_totals(): pl.pallas_call(functools.partial(_ar_kernel, float(cell_total)), out_shap...  25.5 us
    pallas_call x1, Pallas kernels, from_lines_with_halo(): pl.pallas_call(functools.partial(_from_lines_kernel, (n_ax, n)), out_shap...  17 us
    pallas_call x1, Pallas kernels, to_lines(): pl.pallas_call(functools.partial(_to_lines_kernel, n, count), out_shape=[...  16.3 us
    ppermute x2, starting transfers between devices, with_halo(): after = lax.ppermute(first, axis, down)  4.59 us
    dot_general x1, matrix products, shards(): jnp.dot(lax.optimization_barrier(lines.reshape(-1, around_cells)), dft_ta...  4.22 us
    ppermute x2, starting transfers between devices, with_halo(): before = lax.ppermute(last, axis, up)  3.4 us
    pallas_call x1, Pallas kernels, apply_step(): pl.pallas_call(_update_kernel, grid=(steps,), out_shape=[jax.ShapeDtypeSt...  2.82 us
    sub x1, other arithmetic, dft_table(): jnp.cos(coarse)[:, None] * jnp.cos(fine)[None]  2.59 us
  transfers between devices with their start and end apart: 4, of which 1 were waited for; matrix products, arithmetic and copies ran while one was open for 11% of the time, Pallas kernels for 0%

profile of v17, /device:TPU:4, one launch (start us, length us, event | category | flops | bytes accessed | tf_op | source)
XLA Modules:
  0.0 98.3 jit_solution(14816209621539046058)
XLA Ops:
  0.7 0.8 fusion.28
  1.5 2.4 %collective-permute-start = (f32[1,6,256]{2,0,1:T(1,128)S(1)}, f32[1,6,256]{2,0,1:T(1,128)S(1)}, u32[]{:S(2)}, u32[]{:S(2)}) collective-permute-start(f32[1,6,256]{2,0,1:T(1,128)S(1)} %get-tuple-element.29), channel_id=1, source_target_pairs={{4,0},{8,4},{12,8},{16,12},{20,16},{24,20},{28,24},{32,28},{36,32}... | collective-permute-start | bytes 18440 | tf_op jit(solution)/shard_map/ppermute | solution.py:370
  4.0 3.4 %collective-permute-start.1 = (f32[1,6,256]{2,0,1:T(1,128)S(1)}, f32[1,6,256]{2,0,1:T(1,128)S(1)}, u32[]{:S(2)}, u32[]{:S(2)}) collective-permute-start(f32[1,6,256]{2,0,1:T(1,128)S(1)} %get-tuple-element.30), channel_id=1, source_target_pairs={{0,4},{4,8},{8,12},{12,16},{16,20},{20,24},{24,28},{28,32},{32,36}... | collective-permute-start | bytes 18440 | tf_op jit(solution)/shard_map/ppermute | solution.py:369
  7.4 1.3 %fusion.29 = (f32[128,6,1]{2,0,1:T(8,128)S(1)}, f32[128,6,1]{2,0,1:T(8,128)S(1)}) fusion(f32[128,6,256]{2,0,1:T(8,128)} %param.9), kind=kLoop, calls=%fused_computation.65 | loop fusion | bytes 12288 | tf_op jit(solution)/shard_map/slice | solution.py:368
  8.6 2.1 %collective-permute-start.2 = (f32[128,6,1]{2,0,1:T(8,128)S(1)}, f32[128,6,1]{2,0,1:T(8,128)S(1)}, u32[]{:S(2)}, u32[]{:S(2)}) collective-permute-start(f32[128,6,1]{2,0,1:T(8,128)S(1)} %get-tuple-element.31), channel_id=1, source_target_pairs={{1,0},{2,1},{3,2},{0,3},{5,4},{6,5},{7,6},{4,7},{9,8},{10,9},{11,1... | collective-permute-start | bytes 9224 | tf_op jit(solution)/shard_map/ppermute | solution.py:370
  10.8 1.0 slice.61
  11.8 0.3 reverse
  12.1 0.1 slice.79
  12.3 1.1 %maximum_add_fusion = f32[6,6,513]{2,1,0:T(8,128)S(1)} fusion(f32[6,6,1]{2,1,0:T(8,128)S(1)} %broadcast.257, f32[6,6,511]{2,1,0:T(8,128)S(1)} %slice.79, f32[6,6,1024]{2,1,0:T(8,128)} %param.14), kind=kLoop, calls=%fused_computation.41 | loop fusion | flops 55404 | bytes 221472 | tf_op jit(solution)/shard_map/add | solution.py:358
  13.5 1.6 %fusion.27 = (f32[1,128,256]{2,1,0:T(8,128)}, f32[128,256]{1,0:T(8,128)S(1)}) fusion(s32[128,256]{1,0:T(8,128)} %param.11), kind=kLoop, calls=%fused_computation.63 | loop fusion | flops 65536 | bytes 393216 | tf_op jit(solution)/shard_map/transpose;broadcast_in_dim | solution.py:410
  15.1 1.3 %reverse_multiply_fusion = f32[128,3,2,256]{3,0,2,1:T(8,128)S(1)} fusion(f32[128,3,2,256]{3,0,2,1:T(8,128)} %bitcast.51), kind=kLoop, calls=%fused_computation.18 | loop fusion | flops 196608 | bytes 1572864 | tf_op jit(solution)/shard_map/mul | solution.py:392
  16.5 0.2 convolution_multiply_fusion.1
  16.7 1.1 %fusion.21 = (f32[32,1024]{1,0:T(8,128)S(1)}, f32[32,1024]{1,0:T(8,128)S(1)}, f32[32,1024]{1,0:T(8,128)S(1)}, f32[32,1024]{1,0:T(8,128)S(1)}) fusion(s32[1024]{0:T(1024)S(1)} %pad_add_fusion, s32[32]{0:T(128)S(1)} %iota_multiply_fusion, f32[1024]{0:T(1024)S(1)} %fusion.26), kind=kLoop, calls=%fused_computation.45 | loop fusion | flops 950272 | bytes 532608 | tf_op jit(solution)/shard_map/cos | solution.py:348
  17.8 2.6 %multiply_subtract_fusion = f32[32,32,1024]{2,1,0:T(8,128)} fusion(f32[32,1024]{1,0:T(8,128)S(1)} %get-tuple-element.39, f32[32,1024]{1,0:T(8,128)S(1)} %get-tuple-element.38, f32[32,1024]{1,0:T(8,128)S(1)} %get-tuple-element.40, f32[32,1024]{1,0:T(8,128)S(1)} %get-tuple-element.37), kind=kLoop, calls=%fused_computation.1 | loop fusion | flops 3145728 | bytes 4718592 | tf_op jit(solution)/shard_map/sub | solution.py:348
  20.4 0.1 pad_maximum_fusion.4
  20.5 1.4 %collective-permute-done.3 = f32[128,6,1]{2,0,1:T(8,128)S(1)} collective-permute-done((f32[128,6,1]{2,0,1:T(8,128)S(1)}, f32[128,6,1]{2,0,1:T(8,128)S(1)}, u32[]{:S(2)}, u32[]{:S(2)}) %collective-permute-start.3) | collective-permute-done | bytes 3104 | tf_op jit(solution)/shard_map/ppermute | solution.py:369
  21.9 1.6 %multiply_bitcast_fusion = (f32[6,128,256]{2,1,0:T(8,128)}, f32[6,128,256]{2,1,0:T(8,128)}) fusion(f32[128,6,256]{2,0,1:T(8,128)S(1)} %copy-done.5, f32[128,6]{0,1:T(8,128)S(1)} %convolution_multiply_fusion.1, f32[128,6,256]{2,0,1:T(8,128)S(1)} %copy-done.6, f32[128,3,2,256]{3,0,2,1:T(8,128)S(1)} %reverse_multiply_fusion, f32[128,6,256]{2,0,1:T(8,128)S(1)} %copy-done.2, ...), kind=kLoop, calls=%fused_computation.19 | loop fusion | flops 2752512 | bytes 4871168 | tf_op jit(solution)/shard_map/transpose | solution.py:449
  23.5 16.3 %shard_map.103 = (f32[6,32,1024]{2,1,0:T(8,128)}, f32[1,32,1024]{2,1,0:T(8,128)}) custom-call(f32[6,128,256]{2,1,0:T(8,128)} %get-tuple-element.28.refs_0_.r_ref, f32[1,128,256]{2,1,0:T(8,128)} %get-tuple-element.33.refs_1_), custom_call_target="tpu_custom_call" | custom-call | tf_op jit(solution)/shard_map/pallas_call | solution.py:212
  39.8 4.2 %fusion.30 = f32[192,1024]{1,0:T(8,128)S(1)} fusion(f32[192,1024]{1,0:T(8,128)} %bitcast.57, f32[1024,1024]{1,0:T(8,128)} %bitcast.49), kind=kOutput, calls=%fused_computation.66 | convolution fusion | flops 1207959552 | bytes 5767168 | tf_op jit(solution)/shard_map/dot_general | solution.py:413
  44.1 0.3 multiply_reduce_fusion
  44.4 2.4 %bitcast_multiply_fusion = (f32[192,1024]{1,0:T(8,128)S(1)}, f32[192,1024]{1,0:T(8,128)S(1)}) fusion(f32[32,1024]{1,0:T(8,128)S(1)} %bitcast.58, f32[192,1024]{1,0:T(8,128)S(1)} %bitcast.53, f32[1024,1024]{1,0:T(8,128)S(1)} %bitcast.50), kind=kOutput, calls=%fused_computation.17 | convolution fusion | flops 1208352768 | bytes 6684672 | tf_op jit(solution)/shard_map/dot_general | solution.py:420
  46.8 0.9 convolution_bitcast_fusion
  47.8 0.7 reshape.248.cpk_ref
  48.6 0.9 slice_reduce_fusion
  49.5 17.0 %shard_map.104 = (f32[6,128,256]{2,1,0:T(8,128)}, f32[4,6,64]{2,1,0:T(8,128)}, f32[4,6,256]{2,1,0:T(8,128)}, f32[4,6,256]{2,1,0:T(8,128)}) custom-call(f32[6,32,1024]{2,1,0:T(8,128)} %copy-done.3, f32[4,6,64]{2,1,0:T(8,128)} %reshape.248.cpk_ref, f32[4,6,256]{2,1,0:T(8,128)} %bitcast.62, f32[4,6,256]{2,1,0:T(8,128)} %bitcast.61), custom_call_target="tpu_custom_call" | custom-call | tf_op jit(solution)/shard_map/pallas_call | solution.py:326
  66.5 0.7 copy.24
  67.2 0.1 reshape.245
  67.4 0.1 stack_reshape_squeeze.6
  67.6 1.2 %copy.25.hc_ref = f32[2,6,128,1]{3,2,1,0:T(8,128)} copy(f32[2,6,128,1]{2,0,1,3:T(2,128)S(1)} %maximum_bitcast_fusion) | data formatting | bytes 12288 | tf_op jit(solution)/shard_map/broadcast_in_dim | solution.py:450
  68.8 25.5 %shard_map.105 = (f32[8,128]{1,0:T(8,128)}, f32[6,128,256]{2,1,0:T(8,128)}) custom-call(f32[6,128,256]{2,1,0:T(8,128)} %get-tuple-element.28.refs_0_.r_ref, f32[6,128,256]{2,1,0:T(8,128)} %get-tuple-element.15.p_ref, f32[6,128,256]{2,1,0:T(8,128)} %get-tuple-element.27.s_ref, f32[128,256]{1,0:T(8,128)} %copy-done.4, f32[4,6,256]{2,1,0:T(8,128)} %get-tuple-element.16.br_ref, ...), custom_call_target="tpu_custom_call" | custom-call | tf_op jit(solution)/shard_map/pallas_call | solution.py:133
  94.2 1.3 %slice_bitcast_fusion = f32[3]{0:T(128)} fusion(f32[8,128]{1,0:T(8,128)} %get-tuple-element.19.f_ref), kind=kLoop, calls=%fused_computation.60 | loop fusion | bytes 24 | tf_op jit(solution)/shard_map/squeeze | solution.py:461
  95.5 2.8 %shard_map.106 = (f32[6,128,256]{2,1,0:T(8,128)}, f32[6,128,256]{2,1,0:T(8,128)}) custom-call(f32[8,128]{1,0:T(8,128)} %get-tuple-element.19.f_ref, f32[6,128,256]{2,1,0:T(8,128)} %bitcast.52, f32[6,128,256]{2,1,0:T(8,128)} %get-tuple-element.15.p_ref, f32[6,128,256]{2,1,0:T(8,128)} %get-tuple-element.28.refs_0_.r_ref, f32[6,128,256]{2,1,0:T(8,128)} %get-tuple-element.20.i_ref), custom_call_target="tpu_custom_call" | custom-call | tf_op jit(solution)/shard_map/pallas_call | solution.py:163
  (37 shorter events, 0.5 us)
Async XLA Ops:
  0.6 15.8 %copy-start = (f32[4,6]{1,0:T(4,128)S(1)}, f32[4,6]{1,0:T(4,128)}, u32[]{:S(2)}) copy-start(f32[4,6]{1,0:T(4,128)} %param.13) | copy-start | bytes 292
  0.6 15.8 %copy-start.9 = (s32[128]{0:T(128)S(1)}, s32[128]{0:T(128)}, u32[]{:S(2)}) copy-start(s32[128]{0:T(128)} %param.12) | copy-start | bytes 1540
  1.5 20.4 %collective-permute-start = (f32[1,6,256]{2,0,1:T(1,128)S(1)}, f32[1,6,256]{2,0,1:T(1,128)S(1)}, u32[]{:S(2)}, u32[]{:S(2)}) collective-permute-start(f32[1,6,256]{2,0,1:T(1,128)S(1)} %get-tuple-element.29), channel_id=1, source_target_pairs={{4,0},{8,4},{12,8},{16,12},{20,16},{24,20},{28,24},{32,28},{36,32}... | collective-permute-start | bytes 18440 | tf_op jit(solution)/shard_map/ppermute | solution.py:370
  4.0 17.9 %collective-permute-start.1 = (f32[1,6,256]{2,0,1:T(1,128)S(1)}, f32[1,6,256]{2,0,1:T(1,128)S(1)}, u32[]{:S(2)}, u32[]{:S(2)}) collective-permute-start(f32[1,6,256]{2,0,1:T(1,128)S(1)} %get-tuple-element.30), channel_id=1, source_target_pairs={{0,4},{4,8},{8,12},{12,16},{16,20},{20,24},{24,28},{28,32},{32,36}... | collective-permute-start | bytes 18440 | tf_op jit(solution)/shard_map/ppermute | solution.py:369
  8.6 11.8 %collective-permute-start.2 = (f32[128,6,1]{2,0,1:T(8,128)S(1)}, f32[128,6,1]{2,0,1:T(8,128)S(1)}, u32[]{:S(2)}, u32[]{:S(2)}) collective-permute-start(f32[128,6,1]{2,0,1:T(8,128)S(1)} %get-tuple-element.31), channel_id=1, source_target_pairs={{1,0},{2,1},{3,2},{0,3},{5,4},{6,5},{7,6},{4,7},{9,8},{10,9},{11,1... | collective-permute-start | bytes 9224 | tf_op jit(solution)/shard_map/ppermute | solution.py:370
  10.8 11.1 %collective-permute-start.3 = (f32[128,6,1]{2,0,1:T(8,128)S(1)}, f32[128,6,1]{2,0,1:T(8,128)S(1)}, u32[]{:S(2)}, u32[]{:S(2)}) collective-permute-start(f32[128,6,1]{2,0,1:T(8,128)S(1)} %get-tuple-element.32), channel_id=1, source_target_pairs={{0,1},{1,2},{2,3},{3,0},{4,5},{5,6},{6,7},{7,4},{8,9},{9,10},{10,1... | collective-permute-start | bytes 9224 | tf_op jit(solution)/shard_map/ppermute | solution.py:369
  12.2 9.7 %copy-start.2 = (f32[128,6,256]{2,0,1:T(8,128)S(1)}, f32[128,6,256]{2,0,1:T(8,128)}, u32[]{:S(2)}) copy-start(f32[128,6,256]{2,0,1:T(8,128)} %param.9) | copy-start | bytes 2359300
  12.3 9.6 %copy-start.5 = (f32[128,6,256]{2,0,1:T(8,128)S(1)}, f32[128,6,256]{2,0,1:T(8,128)}, u32[]{:S(2)}) copy-start(f32[128,6,256]{2,0,1:T(8,128)} %param.10) | copy-start | bytes 2359300
  12.3 9.6 %copy-start.6 = (f32[128,6,256]{2,0,1:T(8,128)S(1)}, f32[128,6,256]{2,0,1:T(8,128)}, u32[]{:S(2)}) copy-start(f32[128,6,256]{2,0,1:T(8,128)} %param.8) | copy-start | bytes 2359300
  15.1 8.4 %copy-start.4 = (f32[128,256]{1,0:T(8,128)}, f32[128,256]{1,0:T(8,128)S(1)}, u32[]{:S(2)}) copy-start(f32[128,256]{1,0:T(8,128)S(1)} %get-tuple-element.34.m_ref) | copy-start | bytes 393220
  39.8 4.6 %copy-start.1 = (f32[32,32,1024]{2,1,0:T(8,128)S(1)}, f32[32,32,1024]{2,1,0:T(8,128)}, u32[]{:S(2)}) copy-start(f32[32,32,1024]{2,1,0:T(8,128)} %multiply_subtract_fusion) | copy-start | bytes 12582916
  39.8 4.6 %copy-start.7 = (f32[1,32,1024]{2,1,0:T(8,128)S(1)}, f32[1,32,1024]{2,1,0:T(8,128)}, u32[]{:S(2)}) copy-start(f32[1,32,1024]{2,1,0:T(8,128)} %get-tuple-element.13) | copy-start | bytes 393220
  44.1 2.7 %copy-start.8 = (s32[2,4]{1,0:T(2,128)S(1)}, s32[2,4]{1,0:T(2,128)}, u32[]{:S(2)}) copy-start(s32[2,4]{1,0:T(2,128)} %constant.65) | copy-start | bytes 100
  48.6 0.9 copy-start.3

commit v18 on v17

--- a/solution.py
+++ b/solution.py
@@ -43,6 +43,13 @@
     def after_row(q):
         return jnp.where(last_slab, 0.0, ar_ref[0, q : q + 1, :])
 
+    flipped = [hc_ref[g].T for g in range(hc_ref.shape[0])]
+    part = rows // len(flipped)
+
+    def column(w, q):
+        pieces = [t[w * part : (w + 1) * part, q : q + 1] for t in flipped]
+        return jnp.broadcast_to(jnp.concatenate(pieces, axis=0), (rows, width))
+
     row = lax.broadcasted_iota(jnp.int32, (rows, width), 0)
     lane = lax.broadcasted_iota(jnp.int32, (rows, width), 1)
     solid = m_ref[...]
@@ -51,8 +58,8 @@
         field = p_ref[q]
         up = jnp.where(row == 0, before_row(q), pltpu.roll(field, 1, 0))
         down = jnp.where(row == rows - 1, after_row(q), pltpu.roll(field, rows - 1, 0))
-        left = jnp.where(lane == 0, hc_ref[0, q], pltpu.roll(field, 1, 1))
-        right = jnp.where(lane == width - 1, hc_ref[1, q], pltpu.roll(field, width - 1, 1))
+        left = jnp.where(lane == 0, column(0, q), pltpu.roll(field, 1, 1))
+        right = jnp.where(lane == width - 1, column(1, q), pltpu.roll(field, width - 1, 1))
         beside = down + up + right + left
         image = solid * ((s_ref[q] + 4.5) * field - beside - 0.5 * p_ref[q ^ 1])
         img_ref[q] = image
@@ -434,7 +441,10 @@
         (((1,), (1,)), ((), ())),
         precision=lax.Precision.HIGHEST,
     ).reshape(2, sector_count, comp_count, group_rows)
-    cpk = jnp.transpose(edges, (1, 2, 0, 3)).reshape(sector_count, comp_count, 2 * group_rows)
+    cpk = jnp.pad(
+        jnp.transpose(edges, (1, 2, 0, 3)).reshape(sector_count, comp_count, 2 * group_rows),
+        ((0, 0), (0, -(-comp_count // 8) * 8 - comp_count), (0, -(-2 * group_rows // 128) * 128 - 2 * group_rows)),
+    )
 
     def row_pack(row):
         return jnp.transpose(row.reshape(comp_count, sector_count, sector_width), (1, 0, 2))
@@ -442,12 +452,7 @@
     prec_t, halo_cols, before_rows, after_rows = from_lines_with_halo(
         prec_lines, cpk, row_pack(prec_lines[:, -1]), row_pack(prec_lines[:, 0]), sector_count
     )
-    got_cols = jnp.transpose(halo_cols[:, :comp_count, : 2 * group_rows], (1, 0, 2))
-    got_cols = got_cols.reshape(comp_count, sector_count, 2, group_rows)
-    before_col = got_cols[:, :, 0].reshape(comp_count, slab_count)
-    after_col = got_cols[:, :, 1].reshape(comp_count, slab_count)
     stiffness_t = jnp.transpose(stiffness, (1, 0, 2))
-    halo_cols = jnp.stack([before_col, after_col])[..., None]
     cell_total = slab_count * lax.axis_size("ax") * comp_count * around_cells
     finished, image_t = image_and_totals(
         residual_t, prec_t, stiffness_t, solid_t[0], before_rows, after_rows, halo_cols, cell_total, 0

time: 98.8 us -> 96.4 us (0.976)
  local copies, waits for them, and re-layouts: 8.8 us -> 6.53 us
    broadcast_in_dim x1 -> x0, local copies, waits for them, and re-layouts: 1.18 us -> none  [shards(): halo_cols = jnp.stack([before_col, after_col])[..., None]]
where the time goes in v18:
time: 96.4 us; the launch traced here: 96 us
  Pallas kernels  61.5 us (64%)
  other arithmetic  9.92 us (10%)
  starting transfers between devices  8 us (8%)
  matrix products  7.72 us (8%)
  local copies, waits for them, and re-layouts  6.53 us (7%)
  waiting for transfers between devices  1.4 us (1%)
    pallas_call x1, Pallas kernels, image_and_totals(): pl.pallas_call(functools.partial(_ar_kernel, float(cell_total)), out_shap...  25.4 us
    pallas_call x1, Pallas kernels, from_lines_with_halo(): pl.pallas_call(functools.partial(_from_lines_kernel, (n_ax, n)), out_shap...  17.1 us
    pallas_call x1, Pallas kernels, to_lines(): pl.pallas_call(functools.partial(_to_lines_kernel, n, count), out_shape=[...  16.3 us
    ppermute x2, starting transfers between devices, with_halo(): after = lax.ppermute(first, axis, down)  4.59 us
    dot_general x1, matrix products, shards(): jnp.dot(lax.optimization_barrier(lines.reshape(-1, around_cells)), dft_ta...  4.22 us
    ppermute x2, starting transfers between devices, with_halo(): before = lax.ppermute(last, axis, up)  3.4 us
    pallas_call x1, Pallas kernels, apply_step(): pl.pallas_call(_update_kernel, grid=(steps,), out_shape=[jax.ShapeDtypeSt...  2.82 us
    sub x1, other arithmetic, dft_table(): jnp.cos(coarse)[:, None] * jnp.cos(fine)[None]  2.6 us
  transfers between devices with their start and end apart: 4, of which 1 were waited for; matrix products, arithmetic and copies ran while one was open for 11% of the time, Pallas kernels for 0%

profile of v18, /device:TPU:4, one launch (start us, length us, event | category | flops | bytes accessed | tf_op | source)
XLA Modules:
  0.0 96.0 jit_solution(9421962252237287006)
XLA Ops:
  0.7 0.8 fusion.28
  1.5 2.4 %collective-permute-start = (f32[1,6,256]{2,0,1:T(1,128)S(1)}, f32[1,6,256]{2,0,1:T(1,128)S(1)}, u32[]{:S(2)}, u32[]{:S(2)}) collective-permute-start(f32[1,6,256]{2,0,1:T(1,128)S(1)} %get-tuple-element.27), channel_id=1, source_target_pairs={{4,0},{8,4},{12,8},{16,12},{20,16},{24,20},{28,24},{32,28},{36,32}... | collective-permute-start | bytes 18440 | tf_op jit(solution)/shard_map/ppermute | solution.py:377
  4.0 3.4 %collective-permute-start.1 = (f32[1,6,256]{2,0,1:T(1,128)S(1)}, f32[1,6,256]{2,0,1:T(1,128)S(1)}, u32[]{:S(2)}, u32[]{:S(2)}) collective-permute-start(f32[1,6,256]{2,0,1:T(1,128)S(1)} %get-tuple-element.28), channel_id=1, source_target_pairs={{0,4},{4,8},{8,12},{12,16},{16,20},{20,24},{24,28},{28,32},{32,36}... | collective-permute-start | bytes 18440 | tf_op jit(solution)/shard_map/ppermute | solution.py:376
  7.4 1.3 %fusion.29 = (f32[128,6,1]{2,0,1:T(8,128)S(1)}, f32[128,6,1]{2,0,1:T(8,128)S(1)}) fusion(f32[128,6,256]{2,0,1:T(8,128)} %param.9), kind=kLoop, calls=%fused_computation.62 | loop fusion | bytes 12288 | tf_op jit(solution)/shard_map/slice | solution.py:375
  8.6 2.1 %collective-permute-start.2 = (f32[128,6,1]{2,0,1:T(8,128)S(1)}, f32[128,6,1]{2,0,1:T(8,128)S(1)}, u32[]{:S(2)}, u32[]{:S(2)}) collective-permute-start(f32[128,6,1]{2,0,1:T(8,128)S(1)} %get-tuple-element.29), channel_id=1, source_target_pairs={{1,0},{2,1},{3,2},{0,3},{5,4},{6,5},{7,6},{4,7},{9,8},{10,9},{11,1... | collective-permute-start | bytes 9224 | tf_op jit(solution)/shard_map/ppermute | solution.py:377
  10.8 1.0 %slice.55 = f32[6,6,511]{2,1,0:T(8,128)S(1)} slice(f32[6,6,1024]{2,1,0:T(8,128)} %param.14), slice={[0:6], [0:6], [513:1024]} | slice | bytes 147168 | tf_op jit(solution)/shard_map/slice | solution.py:363
  11.8 0.3 reverse
  12.1 0.1 slice.67
  12.3 1.1 %maximum_add_fusion = f32[6,6,513]{2,1,0:T(8,128)S(1)} fusion(f32[6,6,1]{2,1,0:T(8,128)S(1)} %broadcast.259, f32[6,6,511]{2,1,0:T(8,128)S(1)} %slice.67, f32[6,6,1024]{2,1,0:T(8,128)} %param.14), kind=kLoop, calls=%fused_computation.41 | loop fusion | flops 55404 | bytes 221472 | tf_op jit(solution)/shard_map/add | solution.py:365
  13.4 0.1 slice.60
  13.5 1.6 %fusion.27 = (f32[1,128,256]{2,1,0:T(8,128)}, f32[128,256]{1,0:T(8,128)S(1)}) fusion(s32[128,256]{1,0:T(8,128)} %param.11), kind=kLoop, calls=%fused_computation.60 | loop fusion | flops 65536 | bytes 393216 | tf_op jit(solution)/shard_map/transpose;broadcast_in_dim | solution.py:417
  15.1 1.3 %reverse_multiply_fusion = f32[128,3,2,256]{3,0,2,1:T(8,128)S(1)} fusion(f32[128,3,2,256]{3,0,2,1:T(8,128)} %bitcast.48), kind=kLoop, calls=%fused_computation.18 | loop fusion | flops 196608 | bytes 1572864 | tf_op jit(solution)/shard_map/mul | solution.py:399
  16.4 0.1 pad_add_fusion
  16.5 0.2 convolution_multiply_fusion.1
  16.7 1.1 %fusion.21 = (f32[32,1024]{1,0:T(8,128)S(1)}, f32[32,1024]{1,0:T(8,128)S(1)}, f32[32,1024]{1,0:T(8,128)S(1)}, f32[32,1024]{1,0:T(8,128)S(1)}) fusion(s32[1024]{0:T(1024)S(1)} %pad_add_fusion, s32[32]{0:T(128)S(1)} %iota_multiply_fusion, f32[1024]{0:T(1024)S(1)} %fusion.26), kind=kLoop, calls=%fused_computation.45 | loop fusion | flops 950272 | bytes 532608 | tf_op jit(solution)/shard_map/cos | solution.py:355
  17.8 2.6 %multiply_subtract_fusion = f32[32,32,1024]{2,1,0:T(8,128)} fusion(f32[32,1024]{1,0:T(8,128)S(1)} %get-tuple-element.37, f32[32,1024]{1,0:T(8,128)S(1)} %get-tuple-element.36, f32[32,1024]{1,0:T(8,128)S(1)} %get-tuple-element.38, f32[32,1024]{1,0:T(8,128)S(1)} %get-tuple-element.35), kind=kLoop, calls=%fused_computation.1 | loop fusion | flops 3145728 | bytes 4718592 | tf_op jit(solution)/shard_map/sub | solution.py:355
  20.4 0.1 pad_maximum_fusion.4
  20.5 1.4 %collective-permute-done.3 = f32[128,6,1]{2,0,1:T(8,128)S(1)} collective-permute-done((f32[128,6,1]{2,0,1:T(8,128)S(1)}, f32[128,6,1]{2,0,1:T(8,128)S(1)}, u32[]{:S(2)}, u32[]{:S(2)}) %collective-permute-start.3) | collective-permute-done | bytes 3104 | tf_op jit(solution)/shard_map/ppermute | solution.py:376
  21.9 1.6 %multiply_bitcast_fusion = (f32[6,128,256]{2,1,0:T(8,128)}, f32[6,128,256]{2,1,0:T(8,128)}) fusion(f32[128,6,256]{2,0,1:T(8,128)S(1)} %copy-done.5, f32[128,6]{0,1:T(8,128)S(1)} %convolution_multiply_fusion.1, f32[128,6,256]{2,0,1:T(8,128)S(1)} %copy-done.6, f32[128,3,2,256]{3,0,2,1:T(8,128)S(1)} %reverse_multiply_fusion, f32[128,6,256]{2,0,1:T(8,128)S(1)} %copy-done.2, ...), kind=kLoop, calls=%fused_computation.19 | loop fusion | flops 2752512 | bytes 4871168 | tf_op jit(solution)/shard_map/transpose | solution.py:455
  23.5 16.3 %shard_map.103 = (f32[6,32,1024]{2,1,0:T(8,128)}, f32[1,32,1024]{2,1,0:T(8,128)}) custom-call(f32[6,128,256]{2,1,0:T(8,128)} %get-tuple-element.26.refs_0_.r_ref, f32[1,128,256]{2,1,0:T(8,128)} %get-tuple-element.31.refs_1_), custom_call_target="tpu_custom_call" | custom-call | tf_op jit(solution)/shard_map/pallas_call | solution.py:219
  39.8 4.2 %fusion.30 = f32[192,1024]{1,0:T(8,128)S(1)} fusion(f32[192,1024]{1,0:T(8,128)} %bitcast.54, f32[1024,1024]{1,0:T(8,128)} %bitcast.46), kind=kOutput, calls=%fused_computation.63 | convolution fusion | flops 1207959552 | bytes 5767168 | tf_op jit(solution)/shard_map/dot_general | solution.py:420
  44.1 0.3 multiply_reduce_fusion
  44.4 2.4 %bitcast_multiply_fusion = (f32[192,1024]{1,0:T(8,128)S(1)}, f32[192,1024]{1,0:T(8,128)S(1)}) fusion(f32[32,1024]{1,0:T(8,128)S(1)} %bitcast.55, f32[192,1024]{1,0:T(8,128)S(1)} %bitcast.50, f32[1024,1024]{1,0:T(8,128)S(1)} %bitcast.47), kind=kOutput, calls=%fused_computation.17 | convolution fusion | flops 1208352768 | bytes 6684672 | tf_op jit(solution)/shard_map/dot_general | solution.py:427
  46.8 0.9 convolution_bitcast_fusion
  47.8 0.1 reshape.244
  47.9 0.6 pad.4.cpk_ref
  48.5 0.1 broadcast_multiply_fusion.x_ref
  48.6 0.8 slice_reduce_fusion
  49.5 17.1 %shard_map.104 = (f32[6,128,256]{2,1,0:T(8,128)}, f32[4,8,128]{2,1,0:T(8,128)}, f32[4,6,256]{2,1,0:T(8,128)}, f32[4,6,256]{2,1,0:T(8,128)}) custom-call(f32[6,32,1024]{2,1,0:T(8,128)} %copy-done.3, f32[4,8,128]{2,1,0:T(8,128)} %pad.4.cpk_ref, f32[4,6,256]{2,1,0:T(8,128)} %bitcast.59, f32[4,6,256]{2,1,0:T(8,128)} %bitcast.58), custom_call_target="tpu_custom_call" | custom-call | tf_op jit(solution)/shard_map/pallas_call | solution.py:333
  66.5 25.4 %shard_map.105 = (f32[8,128]{1,0:T(8,128)}, f32[6,128,256]{2,1,0:T(8,128)}) custom-call(f32[6,128,256]{2,1,0:T(8,128)} %get-tuple-element.26.refs_0_.r_ref, f32[6,128,256]{2,1,0:T(8,128)} %get-tuple-element.15.p_ref, f32[6,128,256]{2,1,0:T(8,128)} %get-tuple-element.25.s_ref, f32[128,256]{1,0:T(8,128)} %copy-done.4, f32[4,6,256]{2,1,0:T(8,128)} %get-tuple-element.16.br_ref, ...), custom_call_target="tpu_custom_call" | custom-call | tf_op jit(solution)/shard_map/pallas_call | solution.py:140
  91.9 1.3 %slice_bitcast_fusion = f32[3]{0:T(128)} fusion(f32[8,128]{1,0:T(8,128)} %get-tuple-element.19.f_ref), kind=kLoop, calls=%fused_computation.57 | loop fusion | bytes 24 | tf_op jit(solution)/shard_map/squeeze | solution.py:466
  93.2 2.8 %shard_map.106 = (f32[6,128,256]{2,1,0:T(8,128)}, f32[6,128,256]{2,1,0:T(8,128)}) custom-call(f32[8,128]{1,0:T(8,128)} %get-tuple-element.19.f_ref, f32[6,128,256]{2,1,0:T(8,128)} %bitcast.49, f32[6,128,256]{2,1,0:T(8,128)} %get-tuple-element.15.p_ref, f32[6,128,256]{2,1,0:T(8,128)} %get-tuple-element.26.refs_0_.r_ref, f32[6,128,256]{2,1,0:T(8,128)} %get-tuple-element.20.i_ref), custom_call_target="tpu_custom_call" | custom-call | tf_op jit(solution)/shard_map/pallas_call | solution.py:170
  (31 shorter events, 0.2 us)
Async XLA Ops:
  0.6 15.8 %copy-start = (f32[4,6]{1,0:T(4,128)S(1)}, f32[4,6]{1,0:T(4,128)}, u32[]{:S(2)}) copy-start(f32[4,6]{1,0:T(4,128)} %param.13) | copy-start | bytes 292
  0.6 15.8 %copy-start.9 = (s32[128]{0:T(128)S(1)}, s32[128]{0:T(128)}, u32[]{:S(2)}) copy-start(s32[128]{0:T(128)} %param.12) | copy-start | bytes 1540
  1.5 20.4 %collective-permute-start = (f32[1,6,256]{2,0,1:T(1,128)S(1)}, f32[1,6,256]{2,0,1:T(1,128)S(1)}, u32[]{:S(2)}, u32[]{:S(2)}) collective-permute-start(f32[1,6,256]{2,0,1:T(1,128)S(1)} %get-tuple-element.27), channel_id=1, source_target_pairs={{4,0},{8,4},{12,8},{16,12},{20,16},{24,20},{28,24},{32,28},{36,32}... | collective-permute-start | bytes 18440 | tf_op jit(solution)/shard_map/ppermute | solution.py:377
  4.0 17.9 %collective-permute-start.1 = (f32[1,6,256]{2,0,1:T(1,128)S(1)}, f32[1,6,256]{2,0,1:T(1,128)S(1)}, u32[]{:S(2)}, u32[]{:S(2)}) collective-permute-start(f32[1,6,256]{2,0,1:T(1,128)S(1)} %get-tuple-element.28), channel_id=1, source_target_pairs={{0,4},{4,8},{8,12},{12,16},{16,20},{20,24},{24,28},{28,32},{32,36}... | collective-permute-start | bytes 18440 | tf_op jit(solution)/shard_map/ppermute | solution.py:376
  8.6 11.8 %collective-permute-start.2 = (f32[128,6,1]{2,0,1:T(8,128)S(1)}, f32[128,6,1]{2,0,1:T(8,128)S(1)}, u32[]{:S(2)}, u32[]{:S(2)}) collective-permute-start(f32[128,6,1]{2,0,1:T(8,128)S(1)} %get-tuple-element.29), channel_id=1, source_target_pairs={{1,0},{2,1},{3,2},{0,3},{5,4},{6,5},{7,6},{4,7},{9,8},{10,9},{11,1... | collective-permute-start | bytes 9224 | tf_op jit(solution)/shard_map/ppermute | solution.py:377
  10.8 11.1 %collective-permute-start.3 = (f32[128,6,1]{2,0,1:T(8,128)S(1)}, f32[128,6,1]{2,0,1:T(8,128)S(1)}, u32[]{:S(2)}, u32[]{:S(2)}) collective-permute-start(f32[128,6,1]{2,0,1:T(8,128)S(1)} %get-tuple-element.30), channel_id=1, source_target_pairs={{0,1},{1,2},{2,3},{3,0},{4,5},{5,6},{6,7},{7,4},{8,9},{9,10},{10,1... | collective-permute-start | bytes 9224 | tf_op jit(solution)/shard_map/ppermute | solution.py:376
  12.2 9.7 %copy-start.2 = (f32[128,6,256]{2,0,1:T(8,128)S(1)}, f32[128,6,256]{2,0,1:T(8,128)}, u32[]{:S(2)}) copy-start(f32[128,6,256]{2,0,1:T(8,128)} %param.9) | copy-start | bytes 2359300
  12.3 9.6 %copy-start.5 = (f32[128,6,256]{2,0,1:T(8,128)S(1)}, f32[128,6,256]{2,0,1:T(8,128)}, u32[]{:S(2)}) copy-start(f32[128,6,256]{2,0,1:T(8,128)} %param.10) | copy-start | bytes 2359300
  12.3 9.6 %copy-start.6 = (f32[128,6,256]{2,0,1:T(8,128)S(1)}, f32[128,6,256]{2,0,1:T(8,128)}, u32[]{:S(2)}) copy-start(f32[128,6,256]{2,0,1:T(8,128)} %param.8) | copy-start | bytes 2359300
  15.1 8.4 %copy-start.4 = (f32[128,256]{1,0:T(8,128)}, f32[128,256]{1,0:T(8,128)S(1)}, u32[]{:S(2)}) copy-start(f32[128,256]{1,0:T(8,128)S(1)} %get-tuple-element.32.m_ref) | copy-start | bytes 393220
  39.8 4.6 %copy-start.1 = (f32[32,32,1024]{2,1,0:T(8,128)S(1)}, f32[32,32,1024]{2,1,0:T(8,128)}, u32[]{:S(2)}) copy-start(f32[32,32,1024]{2,1,0:T(8,128)} %multiply_subtract_fusion) | copy-start | bytes 12582916
  39.8 4.6 %copy-start.7 = (f32[1,32,1024]{2,1,0:T(8,128)S(1)}, f32[1,32,1024]{2,1,0:T(8,128)}, u32[]{:S(2)}) copy-start(f32[1,32,1024]{2,1,0:T(8,128)} %get-tuple-element.13) | copy-start | bytes 393220
  44.0 2.8 %copy-start.8 = (s32[2,4]{1,0:T(2,128)S(1)}, s32[2,4]{1,0:T(2,128)}, u32[]{:S(2)}) copy-start(s32[2,4]{1,0:T(2,128)} %constant.69) | copy-start | bytes 100
  48.6 0.9 copy-start.3

commit v19 on v18

--- a/solution.py
+++ b/solution.py
@@ -165,7 +165,7 @@
 
 def apply_step(finished, disp, prec, residual, image):
     comps, rows, width = prec.shape
-    steps = 2 if comps % 2 == 0 else 1
+    steps = 3 if comps % 3 == 0 else 1
     plane = pl.BlockSpec((comps // steps, rows, width), lambda q: (q, 0, 0))
     return pl.pallas_call(
         _update_kernel,

time: 96.4 us -> 97.4 us (1.010)
  no operation moved by 1% of the time
where the time goes in v19:
time: 97.4 us; the launch traced here: 96.9 us
  Pallas kernels  62.4 us (64%)
  other arithmetic  9.92 us (10%)
  starting transfers between devices  8 us (8%)
  matrix products  7.72 us (8%)
  local copies, waits for them, and re-layouts  6.53 us (7%)
  waiting for transfers between devices  1.4 us (1%)
    pallas_call x1, Pallas kernels, image_and_totals(): pl.pallas_call(functools.partial(_ar_kernel, float(cell_total)), out_shap...  25.4 us
    pallas_call x1, Pallas kernels, from_lines_with_halo(): pl.pallas_call(functools.partial(_from_lines_kernel, (n_ax, n)), out_shap...  17.1 us
    pallas_call x1, Pallas kernels, to_lines(): pl.pallas_call(functools.partial(_to_lines_kernel, n, count), out_shape=[...  16.3 us
    ppermute x2, starting transfers between devices, with_halo(): after = lax.ppermute(first, axis, down)  4.59 us
    dot_general x1, matrix products, shards(): jnp.dot(lax.optimization_barrier(lines.reshape(-1, around_cells)), dft_ta...  4.22 us
    pallas_call x1, Pallas kernels, apply_step(): pl.pallas_call(_update_kernel, grid=(steps,), out_shape=[jax.ShapeDtypeSt...  3.77 us
    ppermute x2, starting transfers between devices, with_halo(): before = lax.ppermute(last, axis, up)  3.4 us
    sub x1, other arithmetic, dft_table(): jnp.cos(coarse)[:, None] * jnp.cos(fine)[None]  2.6 us
  transfers between devices with their start and end apart: 4, of which 1 were waited for; matrix products, arithmetic and copies ran while one was open for 11% of the time, Pallas kernels for 0%

profile of v19, /device:TPU:4, one launch (start us, length us, event | category | flops | bytes accessed | tf_op | source)
XLA Modules:
  0.0 96.9 jit_solution(14008970830984722791)
XLA Ops:
  0.7 0.8 fusion.28
  1.5 2.4 %collective-permute-start = (f32[1,6,256]{2,0,1:T(1,128)S(1)}, f32[1,6,256]{2,0,1:T(1,128)S(1)}, u32[]{:S(2)}, u32[]{:S(2)}) collective-permute-start(f32[1,6,256]{2,0,1:T(1,128)S(1)} %get-tuple-element.27), channel_id=1, source_target_pairs={{4,0},{8,4},{12,8},{16,12},{20,16},{24,20},{28,24},{32,28},{36,32}... | collective-permute-start | bytes 18440 | tf_op jit(solution)/shard_map/ppermute | solution.py:377
  4.0 3.4 %collective-permute-start.1 = (f32[1,6,256]{2,0,1:T(1,128)S(1)}, f32[1,6,256]{2,0,1:T(1,128)S(1)}, u32[]{:S(2)}, u32[]{:S(2)}) collective-permute-start(f32[1,6,256]{2,0,1:T(1,128)S(1)} %get-tuple-element.28), channel_id=1, source_target_pairs={{0,4},{4,8},{8,12},{12,16},{16,20},{20,24},{24,28},{28,32},{32,36}... | collective-permute-start | bytes 18440 | tf_op jit(solution)/shard_map/ppermute | solution.py:376
  7.4 1.3 %fusion.29 = (f32[128,6,1]{2,0,1:T(8,128)S(1)}, f32[128,6,1]{2,0,1:T(8,128)S(1)}) fusion(f32[128,6,256]{2,0,1:T(8,128)} %param.9), kind=kLoop, calls=%fused_computation.62 | loop fusion | bytes 12288 | tf_op jit(solution)/shard_map/slice | solution.py:375
  8.6 2.1 %collective-permute-start.2 = (f32[128,6,1]{2,0,1:T(8,128)S(1)}, f32[128,6,1]{2,0,1:T(8,128)S(1)}, u32[]{:S(2)}, u32[]{:S(2)}) collective-permute-start(f32[128,6,1]{2,0,1:T(8,128)S(1)} %get-tuple-element.29), channel_id=1, source_target_pairs={{1,0},{2,1},{3,2},{0,3},{5,4},{6,5},{7,6},{4,7},{9,8},{10,9},{11,1... | collective-permute-start | bytes 9224 | tf_op jit(solution)/shard_map/ppermute | solution.py:377
  10.8 1.0 %slice.55 = f32[6,6,511]{2,1,0:T(8,128)S(1)} slice(f32[6,6,1024]{2,1,0:T(8,128)} %param.14), slice={[0:6], [0:6], [513:1024]} | slice | bytes 147168 | tf_op jit(solution)/shard_map/slice | solution.py:363
  11.8 0.3 reverse
  12.1 0.1 slice.67
  12.3 1.1 %maximum_add_fusion = f32[6,6,513]{2,1,0:T(8,128)S(1)} fusion(f32[6,6,1]{2,1,0:T(8,128)S(1)} %broadcast.259, f32[6,6,511]{2,1,0:T(8,128)S(1)} %slice.67, f32[6,6,1024]{2,1,0:T(8,128)} %param.14), kind=kLoop, calls=%fused_computation.41 | loop fusion | flops 55404 | bytes 221472 | tf_op jit(solution)/shard_map/add | solution.py:365
  13.4 0.1 slice.60
  13.5 1.6 %fusion.27 = (f32[1,128,256]{2,1,0:T(8,128)}, f32[128,256]{1,0:T(8,128)S(1)}) fusion(s32[128,256]{1,0:T(8,128)} %param.11), kind=kLoop, calls=%fused_computation.60 | loop fusion | flops 65536 | bytes 393216 | tf_op jit(solution)/shard_map/transpose;broadcast_in_dim | solution.py:417
  15.1 1.3 %reverse_multiply_fusion = f32[128,3,2,256]{3,0,2,1:T(8,128)S(1)} fusion(f32[128,3,2,256]{3,0,2,1:T(8,128)} %bitcast.48), kind=kLoop, calls=%fused_computation.18 | loop fusion | flops 196608 | bytes 1572864 | tf_op jit(solution)/shard_map/mul | solution.py:399
  16.4 0.1 pad_add_fusion
  16.5 0.2 convolution_multiply_fusion.1
  16.7 1.1 %fusion.21 = (f32[32,1024]{1,0:T(8,128)S(1)}, f32[32,1024]{1,0:T(8,128)S(1)}, f32[32,1024]{1,0:T(8,128)S(1)}, f32[32,1024]{1,0:T(8,128)S(1)}) fusion(s32[1024]{0:T(1024)S(1)} %pad_add_fusion, s32[32]{0:T(128)S(1)} %iota_multiply_fusion, f32[1024]{0:T(1024)S(1)} %fusion.26), kind=kLoop, calls=%fused_computation.45 | loop fusion | flops 950272 | bytes 532608 | tf_op jit(solution)/shard_map/cos | solution.py:355
  17.8 2.6 %multiply_subtract_fusion = f32[32,32,1024]{2,1,0:T(8,128)} fusion(f32[32,1024]{1,0:T(8,128)S(1)} %get-tuple-element.37, f32[32,1024]{1,0:T(8,128)S(1)} %get-tuple-element.36, f32[32,1024]{1,0:T(8,128)S(1)} %get-tuple-element.38, f32[32,1024]{1,0:T(8,128)S(1)} %get-tuple-element.35), kind=kLoop, calls=%fused_computation.1 | loop fusion | flops 3145728 | bytes 4718592 | tf_op jit(solution)/shard_map/sub | solution.py:355
  20.4 0.1 pad_maximum_fusion.4
  20.5 1.4 %collective-permute-done.3 = f32[128,6,1]{2,0,1:T(8,128)S(1)} collective-permute-done((f32[128,6,1]{2,0,1:T(8,128)S(1)}, f32[128,6,1]{2,0,1:T(8,128)S(1)}, u32[]{:S(2)}, u32[]{:S(2)}) %collective-permute-start.3) | collective-permute-done | bytes 3104 | tf_op jit(solution)/shard_map/ppermute | solution.py:376
  21.9 1.6 %multiply_bitcast_fusion = (f32[6,128,256]{2,1,0:T(8,128)}, f32[6,128,256]{2,1,0:T(8,128)}) fusion(f32[128,6,256]{2,0,1:T(8,128)S(1)} %copy-done.5, f32[128,6]{0,1:T(8,128)S(1)} %convolution_multiply_fusion.1, f32[128,6,256]{2,0,1:T(8,128)S(1)} %copy-done.6, f32[128,3,2,256]{3,0,2,1:T(8,128)S(1)} %reverse_multiply_fusion, f32[128,6,256]{2,0,1:T(8,128)S(1)} %copy-done.2, ...), kind=kLoop, calls=%fused_computation.19 | loop fusion | flops 2752512 | bytes 4871168 | tf_op jit(solution)/shard_map/transpose | solution.py:455
  23.5 16.3 %shard_map.103 = (f32[6,32,1024]{2,1,0:T(8,128)}, f32[1,32,1024]{2,1,0:T(8,128)}) custom-call(f32[6,128,256]{2,1,0:T(8,128)} %get-tuple-element.26.refs_0_.r_ref, f32[1,128,256]{2,1,0:T(8,128)} %get-tuple-element.31.refs_1_), custom_call_target="tpu_custom_call" | custom-call | tf_op jit(solution)/shard_map/pallas_call | solution.py:219
  39.8 4.2 %fusion.30 = f32[192,1024]{1,0:T(8,128)S(1)} fusion(f32[192,1024]{1,0:T(8,128)} %bitcast.54, f32[1024,1024]{1,0:T(8,128)} %bitcast.46), kind=kOutput, calls=%fused_computation.63 | convolution fusion | flops 1207959552 | bytes 5767168 | tf_op jit(solution)/shard_map/dot_general | solution.py:420
  44.1 0.3 multiply_reduce_fusion
  44.4 2.4 %bitcast_multiply_fusion = (f32[192,1024]{1,0:T(8,128)S(1)}, f32[192,1024]{1,0:T(8,128)S(1)}) fusion(f32[32,1024]{1,0:T(8,128)S(1)} %bitcast.55, f32[192,1024]{1,0:T(8,128)S(1)} %bitcast.50, f32[1024,1024]{1,0:T(8,128)S(1)} %bitcast.47), kind=kOutput, calls=%fused_computation.17 | convolution fusion | flops 1208352768 | bytes 6684672 | tf_op jit(solution)/shard_map/dot_general | solution.py:427
  46.8 0.9 convolution_bitcast_fusion
  47.8 0.1 reshape.244
  47.9 0.6 pad.4.cpk_ref
  48.5 0.1 broadcast_multiply_fusion.x_ref
  48.6 0.8 slice_reduce_fusion
  49.5 17.1 %shard_map.104 = (f32[6,128,256]{2,1,0:T(8,128)}, f32[4,8,128]{2,1,0:T(8,128)}, f32[4,6,256]{2,1,0:T(8,128)}, f32[4,6,256]{2,1,0:T(8,128)}) custom-call(f32[6,32,1024]{2,1,0:T(8,128)} %copy-done.3, f32[4,8,128]{2,1,0:T(8,128)} %pad.4.cpk_ref, f32[4,6,256]{2,1,0:T(8,128)} %bitcast.59, f32[4,6,256]{2,1,0:T(8,128)} %bitcast.58), custom_call_target="tpu_custom_call" | custom-call | tf_op jit(solution)/shard_map/pallas_call | solution.py:333
  66.5 25.4 %shard_map.105 = (f32[8,128]{1,0:T(8,128)}, f32[6,128,256]{2,1,0:T(8,128)}) custom-call(f32[6,128,256]{2,1,0:T(8,128)} %get-tuple-element.26.refs_0_.r_ref, f32[6,128,256]{2,1,0:T(8,128)} %get-tuple-element.15.p_ref, f32[6,128,256]{2,1,0:T(8,128)} %get-tuple-element.25.s_ref, f32[128,256]{1,0:T(8,128)} %copy-done.4, f32[4,6,256]{2,1,0:T(8,128)} %get-tuple-element.16.br_ref, ...), custom_call_target="tpu_custom_call" | custom-call | tf_op jit(solution)/shard_map/pallas_call | solution.py:140
  91.9 1.3 %slice_bitcast_fusion = f32[3]{0:T(128)} fusion(f32[8,128]{1,0:T(8,128)} %get-tuple-element.19.f_ref), kind=kLoop, calls=%fused_computation.57 | loop fusion | bytes 24 | tf_op jit(solution)/shard_map/squeeze | solution.py:466
  93.2 3.8 %shard_map.106 = (f32[6,128,256]{2,1,0:T(8,128)}, f32[6,128,256]{2,1,0:T(8,128)}) custom-call(f32[8,128]{1,0:T(8,128)} %get-tuple-element.19.f_ref, f32[6,128,256]{2,1,0:T(8,128)} %bitcast.49, f32[6,128,256]{2,1,0:T(8,128)} %get-tuple-element.15.p_ref, f32[6,128,256]{2,1,0:T(8,128)} %get-tuple-element.26.refs_0_.r_ref, f32[6,128,256]{2,1,0:T(8,128)} %get-tuple-element.20.i_ref), custom_call_target="tpu_custom_call" | custom-call | tf_op jit(solution)/shard_map/pallas_call | solution.py:170
  (31 shorter events, 0.2 us)
Async XLA Ops:
  0.6 15.8 %copy-start = (f32[4,6]{1,0:T(4,128)S(1)}, f32[4,6]{1,0:T(4,128)}, u32[]{:S(2)}) copy-start(f32[4,6]{1,0:T(4,128)} %param.13) | copy-start | bytes 292
  0.6 15.8 %copy-start.9 = (s32[128]{0:T(128)S(1)}, s32[128]{0:T(128)}, u32[]{:S(2)}) copy-start(s32[128]{0:T(128)} %param.12) | copy-start | bytes 1540
  1.5 20.4 %collective-permute-start = (f32[1,6,256]{2,0,1:T(1,128)S(1)}, f32[1,6,256]{2,0,1:T(1,128)S(1)}, u32[]{:S(2)}, u32[]{:S(2)}) collective-permute-start(f32[1,6,256]{2,0,1:T(1,128)S(1)} %get-tuple-element.27), channel_id=1, source_target_pairs={{4,0},{8,4},{12,8},{16,12},{20,16},{24,20},{28,24},{32,28},{36,32}... | collective-permute-start | bytes 18440 | tf_op jit(solution)/shard_map/ppermute | solution.py:377
  4.0 17.9 %collective-permute-start.1 = (f32[1,6,256]{2,0,1:T(1,128)S(1)}, f32[1,6,256]{2,0,1:T(1,128)S(1)}, u32[]{:S(2)}, u32[]{:S(2)}) collective-permute-start(f32[1,6,256]{2,0,1:T(1,128)S(1)} %get-tuple-element.28), channel_id=1, source_target_pairs={{0,4},{4,8},{8,12},{12,16},{16,20},{20,24},{24,28},{28,32},{32,36}... | collective-permute-start | bytes 18440 | tf_op jit(solution)/shard_map/ppermute | solution.py:376
  8.6 11.8 %collective-permute-start.2 = (f32[128,6,1]{2,0,1:T(8,128)S(1)}, f32[128,6,1]{2,0,1:T(8,128)S(1)}, u32[]{:S(2)}, u32[]{:S(2)}) collective-permute-start(f32[128,6,1]{2,0,1:T(8,128)S(1)} %get-tuple-element.29), channel_id=1, source_target_pairs={{1,0},{2,1},{3,2},{0,3},{5,4},{6,5},{7,6},{4,7},{9,8},{10,9},{11,1... | collective-permute-start | bytes 9224 | tf_op jit(solution)/shard_map/ppermute | solution.py:377
  10.8 11.1 %collective-permute-start.3 = (f32[128,6,1]{2,0,1:T(8,128)S(1)}, f32[128,6,1]{2,0,1:T(8,128)S(1)}, u32[]{:S(2)}, u32[]{:S(2)}) collective-permute-start(f32[128,6,1]{2,0,1:T(8,128)S(1)} %get-tuple-element.30), channel_id=1, source_target_pairs={{0,1},{1,2},{2,3},{3,0},{4,5},{5,6},{6,7},{7,4},{8,9},{9,10},{10,1... | collective-permute-start | bytes 9224 | tf_op jit(solution)/shard_map/ppermute | solution.py:376
  12.2 9.7 %copy-start.2 = (f32[128,6,256]{2,0,1:T(8,128)S(1)}, f32[128,6,256]{2,0,1:T(8,128)}, u32[]{:S(2)}) copy-start(f32[128,6,256]{2,0,1:T(8,128)} %param.9) | copy-start | bytes 2359300
  12.3 9.6 %copy-start.5 = (f32[128,6,256]{2,0,1:T(8,128)S(1)}, f32[128,6,256]{2,0,1:T(8,128)}, u32[]{:S(2)}) copy-start(f32[128,6,256]{2,0,1:T(8,128)} %param.10) | copy-start | bytes 2359300
  12.3 9.6 %copy-start.6 = (f32[128,6,256]{2,0,1:T(8,128)S(1)}, f32[128,6,256]{2,0,1:T(8,128)}, u32[]{:S(2)}) copy-start(f32[128,6,256]{2,0,1:T(8,128)} %param.8) | copy-start | bytes 2359300
  15.1 8.4 %copy-start.4 = (f32[128,256]{1,0:T(8,128)}, f32[128,256]{1,0:T(8,128)S(1)}, u32[]{:S(2)}) copy-start(f32[128,256]{1,0:T(8,128)S(1)} %get-tuple-element.32.m_ref) | copy-start | bytes 393220
  39.8 4.6 %copy-start.1 = (f32[32,32,1024]{2,1,0:T(8,128)S(1)}, f32[32,32,1024]{2,1,0:T(8,128)}, u32[]{:S(2)}) copy-start(f32[32,32,1024]{2,1,0:T(8,128)} %multiply_subtract_fusion) | copy-start | bytes 12582916
  39.8 4.6 %copy-start.7 = (f32[1,32,1024]{2,1,0:T(8,128)S(1)}, f32[1,32,1024]{2,1,0:T(8,128)}, u32[]{:S(2)}) copy-start(f32[1,32,1024]{2,1,0:T(8,128)} %get-tuple-element.13) | copy-start | bytes 393220
  44.0 2.8 %copy-start.8 = (s32[2,4]{1,0:T(2,128)S(1)}, s32[2,4]{1,0:T(2,128)}, u32[]{:S(2)}) copy-start(s32[2,4]{1,0:T(2,128)} %constant.69) | copy-start | bytes 100
  48.6 0.9 copy-start.3

commit v20 on v18

--- a/solution.py
+++ b/solution.py
@@ -86,7 +86,7 @@
     alpha = inner_rz / inner_zq
     square_new = (pick(2) - alpha * (2.0 * pick(3) - alpha * pick(4))) / cell_total
     out = jnp.zeros(total.shape, jnp.float32)
-    for k, v in enumerate((alpha, inner_rz, inner_zq, square_new)):
+    for k, v in enumerate((inner_rz, inner_zq, square_new, alpha)):
         out = jnp.where((row == 0) & (lane == k), v, out)
     return out
 
@@ -157,7 +157,7 @@
 
 
 def _update_kernel(f_ref, d_ref, p_ref, r_ref, i_ref, dn_ref, rn_ref):
-    alpha = f_ref[0:1, 0:1]
+    alpha = f_ref[0:1, 3:4]
     for q in range(d_ref.shape[0]):
         dn_ref[q] = d_ref[q] + alpha * p_ref[q]
         rn_ref[q] = r_ref[q] - alpha * i_ref[q]
@@ -463,7 +463,7 @@
     return (
         jnp.transpose(disp_new_t, (1, 0, 2)),
         jnp.transpose(residual_new_t, (1, 0, 2)),
-        finished[0, 1:4],
+        finished[0, 0:3],
     )
 
 

time: 96.4 us -> 96.4 us (level)
  no operation moved by 1% of the time
where the time goes in v20:
time: 96.4 us; the launch traced here: 96 us
  Pallas kernels  61.6 us (64%)
  other arithmetic  9.92 us (10%)
  starting transfers between devices  8 us (8%)
  matrix products  7.72 us (8%)
  local copies, waits for them, and re-layouts  6.46 us (7%)
  waiting for transfers between devices  1.4 us (1%)
    pallas_call x1, Pallas kernels, image_and_totals(): pl.pallas_call(functools.partial(_ar_kernel, float(cell_total)), out_shap...  25.4 us
    pallas_call x1, Pallas kernels, from_lines_with_halo(): pl.pallas_call(functools.partial(_from_lines_kernel, (n_ax, n)), out_shap...  17.1 us
    pallas_call x1, Pallas kernels, to_lines(): pl.pallas_call(functools.partial(_to_lines_kernel, n, count), out_shape=[...  16.3 us
    ppermute x2, starting transfers between devices, with_halo(): after = lax.ppermute(first, axis, down)  4.59 us
    dot_general x1, matrix products, shards(): jnp.dot(lax.optimization_barrier(lines.reshape(-1, around_cells)), dft_ta...  4.22 us
    ppermute x2, starting transfers between devices, with_halo(): before = lax.ppermute(last, axis, up)  3.4 us
    pallas_call x1, Pallas kernels, apply_step(): pl.pallas_call(_update_kernel, grid=(steps,), out_shape=[jax.ShapeDtypeSt...  2.89 us
    sub x1, other arithmetic, dft_table(): jnp.cos(coarse)[:, None] * jnp.cos(fine)[None]  2.6 us
  transfers between devices with their start and end apart: 4, of which 1 were waited for; matrix products, arithmetic and copies ran while one was open for 11% of the time, Pallas kernels for 0%

profile of v20, /device:TPU:4, one launch (start us, length us, event | category | flops | bytes accessed | tf_op | source)
XLA Modules:
  0.0 96.0 jit_solution(14332637581201988790)
XLA Ops:
  0.7 0.8 fusion.28
  1.5 2.4 %collective-permute-start = (f32[1,6,256]{2,0,1:T(1,128)S(1)}, f32[1,6,256]{2,0,1:T(1,128)S(1)}, u32[]{:S(2)}, u32[]{:S(2)}) collective-permute-start(f32[1,6,256]{2,0,1:T(1,128)S(1)} %get-tuple-element.27), channel_id=1, source_target_pairs={{4,0},{8,4},{12,8},{16,12},{20,16},{24,20},{28,24},{32,28},{36,32}... | collective-permute-start | bytes 18440 | tf_op jit(solution)/shard_map/ppermute | solution.py:377
  4.0 3.4 %collective-permute-start.1 = (f32[1,6,256]{2,0,1:T(1,128)S(1)}, f32[1,6,256]{2,0,1:T(1,128)S(1)}, u32[]{:S(2)}, u32[]{:S(2)}) collective-permute-start(f32[1,6,256]{2,0,1:T(1,128)S(1)} %get-tuple-element.28), channel_id=1, source_target_pairs={{0,4},{4,8},{8,12},{12,16},{16,20},{20,24},{24,28},{28,32},{32,36}... | collective-permute-start | bytes 18440 | tf_op jit(solution)/shard_map/ppermute | solution.py:376
  7.4 1.3 %fusion.29 = (f32[128,6,1]{2,0,1:T(8,128)S(1)}, f32[128,6,1]{2,0,1:T(8,128)S(1)}) fusion(f32[128,6,256]{2,0,1:T(8,128)} %param.9), kind=kLoop, calls=%fused_computation.62 | loop fusion | bytes 12288 | tf_op jit(solution)/shard_map/slice | solution.py:375
  8.6 2.1 %collective-permute-start.2 = (f32[128,6,1]{2,0,1:T(8,128)S(1)}, f32[128,6,1]{2,0,1:T(8,128)S(1)}, u32[]{:S(2)}, u32[]{:S(2)}) collective-permute-start(f32[128,6,1]{2,0,1:T(8,128)S(1)} %get-tuple-element.29), channel_id=1, source_target_pairs={{1,0},{2,1},{3,2},{0,3},{5,4},{6,5},{7,6},{4,7},{9,8},{10,9},{11,1... | collective-permute-start | bytes 9224 | tf_op jit(solution)/shard_map/ppermute | solution.py:377
  10.8 1.0 %slice.55 = f32[6,6,511]{2,1,0:T(8,128)S(1)} slice(f32[6,6,1024]{2,1,0:T(8,128)} %param.14), slice={[0:6], [0:6], [513:1024]} | slice | bytes 147168 | tf_op jit(solution)/shard_map/slice | solution.py:363
  11.8 0.3 reverse
  12.1 0.1 slice.67
  12.3 1.1 %maximum_add_fusion = f32[6,6,513]{2,1,0:T(8,128)S(1)} fusion(f32[6,6,1]{2,1,0:T(8,128)S(1)} %broadcast.259, f32[6,6,511]{2,1,0:T(8,128)S(1)} %slice.67, f32[6,6,1024]{2,1,0:T(8,128)} %param.14), kind=kLoop, calls=%fused_computation.41 | loop fusion | flops 55404 | bytes 221472 | tf_op jit(solution)/shard_map/add | solution.py:365
  13.4 0.1 slice.60
  13.5 1.6 %fusion.27 = (f32[1,128,256]{2,1,0:T(8,128)}, f32[128,256]{1,0:T(8,128)S(1)}) fusion(s32[128,256]{1,0:T(8,128)} %param.11), kind=kLoop, calls=%fused_computation.60 | loop fusion | flops 65536 | bytes 393216 | tf_op jit(solution)/shard_map/transpose;broadcast_in_dim | solution.py:417
  15.1 1.3 %reverse_multiply_fusion = f32[128,3,2,256]{3,0,2,1:T(8,128)S(1)} fusion(f32[128,3,2,256]{3,0,2,1:T(8,128)} %bitcast.48), kind=kLoop, calls=%fused_computation.18 | loop fusion | flops 196608 | bytes 1572864 | tf_op jit(solution)/shard_map/mul | solution.py:399
  16.4 0.1 pad_add_fusion
  16.5 0.2 convolution_multiply_fusion.1
  16.7 1.1 %fusion.21 = (f32[32,1024]{1,0:T(8,128)S(1)}, f32[32,1024]{1,0:T(8,128)S(1)}, f32[32,1024]{1,0:T(8,128)S(1)}, f32[32,1024]{1,0:T(8,128)S(1)}) fusion(s32[1024]{0:T(1024)S(1)} %pad_add_fusion, s32[32]{0:T(128)S(1)} %iota_multiply_fusion, f32[1024]{0:T(1024)S(1)} %fusion.26), kind=kLoop, calls=%fused_computation.45 | loop fusion | flops 950272 | bytes 532608 | tf_op jit(solution)/shard_map/cos | solution.py:355
  17.8 2.6 %multiply_subtract_fusion = f32[32,32,1024]{2,1,0:T(8,128)} fusion(f32[32,1024]{1,0:T(8,128)S(1)} %get-tuple-element.37, f32[32,1024]{1,0:T(8,128)S(1)} %get-tuple-element.36, f32[32,1024]{1,0:T(8,128)S(1)} %get-tuple-element.38, f32[32,1024]{1,0:T(8,128)S(1)} %get-tuple-element.35), kind=kLoop, calls=%fused_computation.1 | loop fusion | flops 3145728 | bytes 4718592 | tf_op jit(solution)/shard_map/sub | solution.py:355
  20.4 0.1 pad_maximum_fusion.4
  20.5 1.4 %collective-permute-done.3 = f32[128,6,1]{2,0,1:T(8,128)S(1)} collective-permute-done((f32[128,6,1]{2,0,1:T(8,128)S(1)}, f32[128,6,1]{2,0,1:T(8,128)S(1)}, u32[]{:S(2)}, u32[]{:S(2)}) %collective-permute-start.3) | collective-permute-done | bytes 3104 | tf_op jit(solution)/shard_map/ppermute | solution.py:376
  21.9 1.6 %multiply_bitcast_fusion = (f32[6,128,256]{2,1,0:T(8,128)}, f32[6,128,256]{2,1,0:T(8,128)}) fusion(f32[128,6,256]{2,0,1:T(8,128)S(1)} %copy-done.5, f32[128,6]{0,1:T(8,128)S(1)} %convolution_multiply_fusion.1, f32[128,6,256]{2,0,1:T(8,128)S(1)} %copy-done.6, f32[128,3,2,256]{3,0,2,1:T(8,128)S(1)} %reverse_multiply_fusion, f32[128,6,256]{2,0,1:T(8,128)S(1)} %copy-done.2, ...), kind=kLoop, calls=%fused_computation.19 | loop fusion | flops 2752512 | bytes 4871168 | tf_op jit(solution)/shard_map/transpose | solution.py:455
  23.5 16.3 %shard_map.103 = (f32[6,32,1024]{2,1,0:T(8,128)}, f32[1,32,1024]{2,1,0:T(8,128)}) custom-call(f32[6,128,256]{2,1,0:T(8,128)} %get-tuple-element.26.refs_0_.r_ref, f32[1,128,256]{2,1,0:T(8,128)} %get-tuple-element.31.refs_1_), custom_call_target="tpu_custom_call" | custom-call | tf_op jit(solution)/shard_map/pallas_call | solution.py:219
  39.8 4.2 %fusion.30 = f32[192,1024]{1,0:T(8,128)S(1)} fusion(f32[192,1024]{1,0:T(8,128)} %bitcast.54, f32[1024,1024]{1,0:T(8,128)} %bitcast.46), kind=kOutput, calls=%fused_computation.63 | convolution fusion | flops 1207959552 | bytes 5767168 | tf_op jit(solution)/shard_map/dot_general | solution.py:420
  44.1 0.3 multiply_reduce_fusion
  44.4 2.4 %bitcast_multiply_fusion = (f32[192,1024]{1,0:T(8,128)S(1)}, f32[192,1024]{1,0:T(8,128)S(1)}) fusion(f32[32,1024]{1,0:T(8,128)S(1)} %bitcast.55, f32[192,1024]{1,0:T(8,128)S(1)} %bitcast.50, f32[1024,1024]{1,0:T(8,128)S(1)} %bitcast.47), kind=kOutput, calls=%fused_computation.17 | convolution fusion | flops 1208352768 | bytes 6684672 | tf_op jit(solution)/shard_map/dot_general | solution.py:427
  46.8 0.9 convolution_bitcast_fusion
  47.8 0.1 reshape.244
  47.9 0.6 pad.4.cpk_ref
  48.5 0.1 broadcast_multiply_fusion.x_ref
  48.6 0.8 slice_reduce_fusion
  49.5 17.1 %shard_map.104 = (f32[6,128,256]{2,1,0:T(8,128)}, f32[4,8,128]{2,1,0:T(8,128)}, f32[4,6,256]{2,1,0:T(8,128)}, f32[4,6,256]{2,1,0:T(8,128)}) custom-call(f32[6,32,1024]{2,1,0:T(8,128)} %copy-done.3, f32[4,8,128]{2,1,0:T(8,128)} %pad.4.cpk_ref, f32[4,6,256]{2,1,0:T(8,128)} %bitcast.59, f32[4,6,256]{2,1,0:T(8,128)} %bitcast.58), custom_call_target="tpu_custom_call" | custom-call | tf_op jit(solution)/shard_map/pallas_call | solution.py:333
  66.5 25.4 %shard_map.105 = (f32[8,128]{1,0:T(8,128)}, f32[6,128,256]{2,1,0:T(8,128)}) custom-call(f32[6,128,256]{2,1,0:T(8,128)} %get-tuple-element.26.refs_0_.r_ref, f32[6,128,256]{2,1,0:T(8,128)} %get-tuple-element.15.p_ref, f32[6,128,256]{2,1,0:T(8,128)} %get-tuple-element.25.s_ref, f32[128,256]{1,0:T(8,128)} %copy-done.4, f32[4,6,256]{2,1,0:T(8,128)} %get-tuple-element.16.br_ref, ...), custom_call_target="tpu_custom_call" | custom-call | tf_op jit(solution)/shard_map/pallas_call | solution.py:140
  91.9 1.2 %slice_bitcast_fusion = f32[3]{0:T(128)} fusion(f32[8,128]{1,0:T(8,128)} %get-tuple-element.19.f_ref), kind=kLoop, calls=%fused_computation.57 | loop fusion | bytes 24 | tf_op jit(solution)/shard_map/squeeze | solution.py:466
  93.1 2.9 %shard_map.106 = (f32[6,128,256]{2,1,0:T(8,128)}, f32[6,128,256]{2,1,0:T(8,128)}) custom-call(f32[8,128]{1,0:T(8,128)} %get-tuple-element.19.f_ref, f32[6,128,256]{2,1,0:T(8,128)} %bitcast.49, f32[6,128,256]{2,1,0:T(8,128)} %get-tuple-element.15.p_ref, f32[6,128,256]{2,1,0:T(8,128)} %get-tuple-element.26.refs_0_.r_ref, f32[6,128,256]{2,1,0:T(8,128)} %get-tuple-element.20.i_ref), custom_call_target="tpu_custom_call" | custom-call | tf_op jit(solution)/shard_map/pallas_call | solution.py:170
  (31 shorter events, 0.2 us)
Async XLA Ops:
  0.6 15.8 %copy-start = (f32[4,6]{1,0:T(4,128)S(1)}, f32[4,6]{1,0:T(4,128)}, u32[]{:S(2)}) copy-start(f32[4,6]{1,0:T(4,128)} %param.13) | copy-start | bytes 292
  0.6 15.8 %copy-start.9 = (s32[128]{0:T(128)S(1)}, s32[128]{0:T(128)}, u32[]{:S(2)}) copy-start(s32[128]{0:T(128)} %param.12) | copy-start | bytes 1540
  1.5 20.4 %collective-permute-start = (f32[1,6,256]{2,0,1:T(1,128)S(1)}, f32[1,6,256]{2,0,1:T(1,128)S(1)}, u32[]{:S(2)}, u32[]{:S(2)}) collective-permute-start(f32[1,6,256]{2,0,1:T(1,128)S(1)} %get-tuple-element.27), channel_id=1, source_target_pairs={{4,0},{8,4},{12,8},{16,12},{20,16},{24,20},{28,24},{32,28},{36,32}... | collective-permute-start | bytes 18440 | tf_op jit(solution)/shard_map/ppermute | solution.py:377
  4.0 17.9 %collective-permute-start.1 = (f32[1,6,256]{2,0,1:T(1,128)S(1)}, f32[1,6,256]{2,0,1:T(1,128)S(1)}, u32[]{:S(2)}, u32[]{:S(2)}) collective-permute-start(f32[1,6,256]{2,0,1:T(1,128)S(1)} %get-tuple-element.28), channel_id=1, source_target_pairs={{0,4},{4,8},{8,12},{12,16},{16,20},{20,24},{24,28},{28,32},{32,36}... | collective-permute-start | bytes 18440 | tf_op jit(solution)/shard_map/ppermute | solution.py:376
  8.6 11.8 %collective-permute-start.2 = (f32[128,6,1]{2,0,1:T(8,128)S(1)}, f32[128,6,1]{2,0,1:T(8,128)S(1)}, u32[]{:S(2)}, u32[]{:S(2)}) collective-permute-start(f32[128,6,1]{2,0,1:T(8,128)S(1)} %get-tuple-element.29), channel_id=1, source_target_pairs={{1,0},{2,1},{3,2},{0,3},{5,4},{6,5},{7,6},{4,7},{9,8},{10,9},{11,1... | collective-permute-start | bytes 9224 | tf_op jit(solution)/shard_map/ppermute | solution.py:377
  10.8 11.1 %collective-permute-start.3 = (f32[128,6,1]{2,0,1:T(8,128)S(1)}, f32[128,6,1]{2,0,1:T(8,128)S(1)}, u32[]{:S(2)}, u32[]{:S(2)}) collective-permute-start(f32[128,6,1]{2,0,1:T(8,128)S(1)} %get-tuple-element.30), channel_id=1, source_target_pairs={{0,1},{1,2},{2,3},{3,0},{4,5},{5,6},{6,7},{7,4},{8,9},{9,10},{10,1... | collective-permute-start | bytes 9224 | tf_op jit(solution)/shard_map/ppermute | solution.py:376
  12.2 9.7 %copy-start.2 = (f32[128,6,256]{2,0,1:T(8,128)S(1)}, f32[128,6,256]{2,0,1:T(8,128)}, u32[]{:S(2)}) copy-start(f32[128,6,256]{2,0,1:T(8,128)} %param.9) | copy-start | bytes 2359300
  12.3 9.6 %copy-start.5 = (f32[128,6,256]{2,0,1:T(8,128)S(1)}, f32[128,6,256]{2,0,1:T(8,128)}, u32[]{:S(2)}) copy-start(f32[128,6,256]{2,0,1:T(8,128)} %param.10) | copy-start | bytes 2359300
  12.3 9.6 %copy-start.6 = (f32[128,6,256]{2,0,1:T(8,128)S(1)}, f32[128,6,256]{2,0,1:T(8,128)}, u32[]{:S(2)}) copy-start(f32[128,6,256]{2,0,1:T(8,128)} %param.8) | copy-start | bytes 2359300
  15.1 8.4 %copy-start.4 = (f32[128,256]{1,0:T(8,128)}, f32[128,256]{1,0:T(8,128)S(1)}, u32[]{:S(2)}) copy-start(f32[128,256]{1,0:T(8,128)S(1)} %get-tuple-element.32.m_ref) | copy-start | bytes 393220
  39.8 4.6 %copy-start.1 = (f32[32,32,1024]{2,1,0:T(8,128)S(1)}, f32[32,32,1024]{2,1,0:T(8,128)}, u32[]{:S(2)}) copy-start(f32[32,32,1024]{2,1,0:T(8,128)} %multiply_subtract_fusion) | copy-start | bytes 12582916
  39.8 4.6 %copy-start.7 = (f32[1,32,1024]{2,1,0:T(8,128)S(1)}, f32[1,32,1024]{2,1,0:T(8,128)}, u32[]{:S(2)}) copy-start(f32[1,32,1024]{2,1,0:T(8,128)} %get-tuple-element.13) | copy-start | bytes 393220
  44.0 2.8 %copy-start.8 = (s32[2,4]{1,0:T(2,128)S(1)}, s32[2,4]{1,0:T(2,128)}, u32[]{:S(2)}) copy-start(s32[2,4]{1,0:T(2,128)} %constant.69) | copy-start | bytes 100
  48.6 0.9 copy-start.3
